TPU v7x, 32 devices: a whole 2x2x4 slice. The times are simulated.
32 devices in a mesh: context: 4 (over y, x), expert: 8 (over z, core).
Axes of the slice: x: 2, y: 2, z: 4, core: 2. Of those that a mesh axis runs over, the one named last changes fastest.
Arguments:
- tokens: bfloat16 [8, 1024, 2048], P('expert', 'context'), may hold values from -6 to 6
- cotangent: bfloat16 [8, 1024, 2048], P('expert', 'context'), may hold values from -6 to 6
- lengths: int32 [8], P('expert'), may hold values from 257 to 1024, as said below
- expert_ids: int32 [8, 1024, 8], P('expert', 'context'), may hold values from 0 to 15, all different within a row; in each aligned block of 256 rows (0 to 255, 256 to 511, ..., all dimensions but the last counted through in order) at most 144 rows name the same one
- query_weight: bfloat16 [2048, 2048], P(('context', 'expert')), may hold values from -0.125 to 0.125
- key_weight: bfloat16 [2048, 2048], P(('context', 'expert')), may hold values from -0.125 to 0.125
- value_weight: bfloat16 [2048, 2048], P(('context', 'expert')), may hold values from -0.125 to 0.125
- out_weight: bfloat16 [2048, 2048], P(('context', 'expert')), may hold values from -0.5 to 0.5
- router_weight: bfloat16 [2048, 16], P(('context', 'expert')), may hold values from -0.0625 to 0.0625
- first_gain: bfloat16 [2048], P(('context', 'expert')), may hold values from 0.5 to 1.5
- second_gain: bfloat16 [2048], P(('context', 'expert')), may hold values from 0.5 to 1.5
- query_gain: bfloat16 [2048], P(('context', 'expert')), may hold values from 0.5 to 1.5
- key_gain: bfloat16 [2048], P(('context', 'expert')), may hold values from 0.5 to 1.5
- gate_weight: bfloat16 [16, 2048, 1024], P('expert', None, 'context'), may hold values from -0.125 to 0.125
- up_weight: bfloat16 [16, 2048, 1024], P('expert', None, 'context'), may hold values from -0.125 to 0.125
- down_weight: bfloat16 [16, 1024, 2048], P('expert', 'context'), may hold values from -4 to 4
Outputs:
- layer_out: bfloat16 [8, 1024, 2048], P('expert', 'context')
- input_grad: bfloat16 [8, 1024, 2048], P('expert', 'context')
- query_grad: float32 [2048, 2048], P(('context', 'expert'))
- key_grad: float32 [2048, 2048], P(('context', 'expert'))
- value_grad: float32 [2048, 2048], P(('context', 'expert'))
- out_grad: float32 [2048, 2048], P(('context', 'expert'))
- router_grad: float32 [2048, 16], P(('context', 'expert'))
- first_gain_grad: float32 [2048], P(('context', 'expert'))
- second_gain_grad: float32 [2048], P(('context', 'expert'))
- query_gain_grad: float32 [2048], P(('context', 'expert'))
- key_gain_grad: float32 [2048], P(('context', 'expert'))
- gate_grad: float32 [16, 2048, 1024], P('expert', None, 'context')
- up_grad: float32 [16, 2048, 1024], P('expert', None, 'context')
- down_grad: float32 [16, 1024, 2048], P('expert', 'context')
Inputs may be any that keep to these rules, and one draw needn't show every extreme that they name: `lengths`: the longest sequence has exactly 1024 positions. `expert_ids`: each token names 8 different experts. Among the tokens of one device's block, no expert is named more than 144 times, and some expert reaches 144.
All inputs are finite; a program needn't handle non-finite values.
Results may differ from a plain program's by a relative error of at most 0.02.
Values may be sent and summed in bfloat16 or wider, within the bound.
A program may use at most 384 MiB of HBM per device.

v0:
```python
import math

import jax
import jax.numpy as jnp
from jax import lax
from jax.sharding import PartitionSpec as P

HEADS = 16
HD = 128


EPSILON = 1e-06
ROPE_THETA = 10000.0
NEG_FILL = -1e30


def matmul(left, right):
    return jnp.dot(left, right, preferred_element_type=jnp.float32)


def times_transposed(left, right):
    return lax.dot_general(
        left, right, (((1,), (1,)), ((), ())), preferred_element_type=jnp.float32
    )


def transposed_times(left, right):
    return lax.dot_general(
        left, right, (((0,), (0,)), ((), ())), preferred_element_type=jnp.float32
    )


def norm_rows(values, gain):
    factor = lax.rsqrt(jnp.mean(values * values, axis=-1, keepdims=True) + EPSILON)
    return (values * factor * gain, factor)


def norm_back(grad, values, factor, gain):
    weighted = grad * gain
    inner = jnp.mean(weighted * values, axis=-1, keepdims=True)
    return (factor * weighted - values * factor**3 * inner, jnp.sum(grad * values * factor, axis=0))


def rotary_tables(positions, head_dim):
    half_dim = head_dim // 2
    frequency = jnp.exp(-math.log(ROPE_THETA) * jnp.arange(half_dim, dtype=jnp.float32) / half_dim)
    angles = positions.astype(jnp.float32)[:, None] * frequency[None, :]
    return (jnp.cos(angles), jnp.sin(angles))


def rotate(values, cosine, sine, direction):
    half_dim = values.shape[-1] // 2
    first = values[..., :half_dim]
    second = values[..., half_dim:]
    cos_rows = cosine[:, None, :]
    sin_rows = direction * sine[:, None, :]
    return jnp.concatenate(
        [first * cos_rows - second * sin_rows, second * cos_rows + first * sin_rows], axis=-1
    )


def scores_for(query_low, keys_all, key_valid, score_scale):
    scores = (
        jnp.einsum("qhd,khd->hqk", query_low, keys_all, preferred_element_type=jnp.float32)
        * score_scale
    )
    return jnp.where(key_valid[None, None, :], scores, NEG_FILL)


def expert_core(received, gate_matrix, up_matrix, down_matrix):
    gate_pre = jnp.einsum(
        "semd,edf->semf", received, gate_matrix, preferred_element_type=jnp.float32
    )
    up_pre = jnp.einsum("semd,edf->semf", received, up_matrix, preferred_element_type=jnp.float32)
    hidden_low = (gate_pre * jax.nn.sigmoid(gate_pre) * up_pre).astype(jnp.bfloat16)
    partial_out = jnp.einsum(
        "semf,efd->semd", hidden_low, down_matrix, preferred_element_type=jnp.float32
    )
    return (partial_out, gate_pre, up_pre)


def expert_backward(grad_out, received, gate_pre, up_pre, gate_matrix, up_matrix, down_matrix):
    gate_sigmoid = jax.nn.sigmoid(gate_pre)
    hidden_low = (gate_pre * gate_sigmoid * up_pre).astype(jnp.bfloat16)
    grad_hidden = jnp.einsum(
        "semd,efd->semf", grad_out, down_matrix, preferred_element_type=jnp.float32
    )
    grad_gate = (
        grad_hidden * up_pre * gate_sigmoid * (1.0 + gate_pre * (1.0 - gate_sigmoid))
    ).astype(jnp.bfloat16)
    grad_up = (grad_hidden * gate_pre * gate_sigmoid).astype(jnp.bfloat16)
    down_part = jnp.einsum(
        "semf,semd->efd", hidden_low, grad_out, preferred_element_type=jnp.float32
    )
    gate_part = jnp.einsum(
        "semd,semf->edf", received, grad_gate, preferred_element_type=jnp.float32
    )
    up_part = jnp.einsum("semd,semf->edf", received, grad_up, preferred_element_type=jnp.float32)
    grad_rows = jnp.einsum(
        "semf,edf->semd", grad_gate, gate_matrix, preferred_element_type=jnp.float32
    )
    grad_rows = grad_rows + jnp.einsum(
        "semf,edf->semd", grad_up, up_matrix, preferred_element_type=jnp.float32
    )
    return (grad_rows, (gate_part, up_part, down_part))


def local(
    tokens,
    cotangent,
    lengths,
    expert_ids,
    query_weight,
    key_weight,
    value_weight,
    out_weight,
    router_weight,
    first_gain,
    second_gain,
    query_gain,
    key_gain,
    gate_weight,
    up_weight,
    down_weight,
):
    token_count = tokens.shape[1]
    model_width = tokens.shape[2]
    heads = HEADS
    head_dim = HD
    top_count = expert_ids.shape[2]
    experts = router_weight.shape[1]
    local_experts = gate_weight.shape[0]
    sources = lax.axis_size("expert")
    capacity = max(2, -(-(token_count * top_count * 9) // (experts * 8)))
    score_scale = 1.0 / math.sqrt(head_dim)
    seq_len = token_count * lax.axis_size("context")
    (
        full_query,
        full_key,
        full_value,
        full_out,
        full_router,
        gain_first,
        gain_second,
        gain_queries,
        gain_keys,
    ) = (
        lax.all_gather(query_weight, ("context", "expert"), axis=0, tiled=True),
        lax.all_gather(key_weight, ("context", "expert"), axis=0, tiled=True),
        lax.all_gather(value_weight, ("context", "expert"), axis=0, tiled=True),
        lax.all_gather(out_weight, ("context", "expert"), axis=0, tiled=True),
        lax.all_gather(router_weight, ("context", "expert"), axis=0, tiled=True),
        lax.all_gather(first_gain, ("context", "expert"), axis=0, tiled=True),
        lax.all_gather(second_gain, ("context", "expert"), axis=0, tiled=True),
        lax.all_gather(query_gain, ("context", "expert"), axis=0, tiled=True),
        lax.all_gather(key_gain, ("context", "expert"), axis=0, tiled=True),
    )
    gain_first = gain_first.astype(jnp.float32)
    gain_second = gain_second.astype(jnp.float32)
    gain_queries = gain_queries.astype(jnp.float32)
    gain_keys = gain_keys.astype(jnp.float32)
    inputs = tokens[0].astype(jnp.float32)
    grads_out = cotangent[0].astype(jnp.float32)
    length = lengths[0]
    positions = lax.axis_index("context") * token_count + jnp.arange(token_count, dtype=jnp.int32)
    row_valid = (positions < length).astype(jnp.float32)[:, None]
    key_valid = jnp.arange(seq_len, dtype=jnp.int32) < length
    cosine, sine = rotary_tables(positions, head_dim)
    normed_one, factor_one = norm_rows(inputs, gain_first)
    normed_one_low = normed_one.astype(jnp.bfloat16)
    query_raw = matmul(normed_one_low, full_query)
    key_raw = matmul(normed_one_low, full_key)
    value_low = matmul(normed_one_low, full_value).astype(jnp.bfloat16)
    query_normed, query_factor = norm_rows(query_raw, gain_queries)
    key_normed, key_factor = norm_rows(key_raw, gain_keys)
    query_low = rotate(
        query_normed.reshape(token_count, heads, head_dim), cosine, sine, 1.0
    ).astype(jnp.bfloat16)
    key_low = rotate(key_normed.reshape(token_count, heads, head_dim), cosine, sine, 1.0).astype(
        jnp.bfloat16
    )
    keys_all, values_all = (
        lax.all_gather(key_low, "context", axis=0, tiled=True),
        lax.all_gather(
            value_low.reshape(token_count, heads, head_dim), "context", axis=0, tiled=True
        ),
    )
    scores = scores_for(query_low, keys_all, key_valid, score_scale)
    peak_score = jnp.max(scores, axis=-1, keepdims=True)
    log_total = peak_score + jnp.log(jnp.sum(jnp.exp(scores - peak_score), axis=-1, keepdims=True))
    softmax_low = jnp.exp(scores - log_total).astype(jnp.bfloat16)
    attended = jnp.einsum(
        "hqk,khd->qhd", softmax_low, values_all, preferred_element_type=jnp.float32
    )
    attended_low = attended.reshape(token_count, model_width).astype(jnp.bfloat16)
    hidden_state = inputs + matmul(attended_low, full_out)
    normed_two, factor_two = norm_rows(hidden_state, gain_second)
    normed_two_low = normed_two.astype(jnp.bfloat16)
    logits = matmul(normed_two_low, full_router)
    router_probs = jax.nn.softmax(logits, axis=-1)
    pick_table = (
        expert_ids[0][:, :, None] == jnp.arange(experts, dtype=jnp.int32)[None, None, :]
    ).astype(jnp.float32)
    gates = jnp.sum(pick_table * router_probs[:, None, :], axis=-1)
    pair_table = pick_table.reshape(-1, experts).astype(jnp.int32)
    pair_experts = expert_ids[0].reshape(-1)
    ranks = jnp.sum((jnp.cumsum(pair_table, axis=0) - pair_table) * pair_table, axis=1)
    slots = pair_experts * capacity + ranks
    send_rows = (
        jnp.zeros((experts * capacity, model_width), jnp.bfloat16)
        .at[slots]
        .set(jnp.repeat(normed_two_low, top_count, axis=0))
    )
    send_rows = send_rows.reshape(sources, local_experts, capacity, model_width)
    gate_all, up_all, down_all = (
        lax.all_gather(gate_weight, "context", axis=2, tiled=True),
        lax.all_gather(up_weight, "context", axis=2, tiled=True),
        lax.all_gather(down_weight, "context", axis=1, tiled=True),
    )
    received = lax.all_to_all(send_rows, "expert", split_axis=0, concat_axis=0, tiled=True)
    partial_out, gate_pre, up_pre = expert_core(received, gate_all, up_all, down_all)
    expert_out = partial_out.astype(jnp.bfloat16)
    returned = lax.all_to_all(
        expert_out, "expert", split_axis=0, concat_axis=0, tiled=True
    ).reshape(experts * capacity, model_width)
    pair_out = returned[slots].reshape(token_count, top_count, model_width).astype(jnp.float32)
    mixed = jnp.sum(gates[:, :, None] * pair_out, axis=1)
    layer_out = (row_valid * (hidden_state + mixed)).astype(jnp.bfloat16)
    grad_total = grads_out * row_valid
    grad_gates = jnp.sum(grad_total[:, None, :] * pair_out, axis=-1)
    grad_pairs = (
        (gates[:, :, None] * grad_total[:, None, :]).astype(jnp.bfloat16).reshape(-1, model_width)
    )
    grad_send = jnp.zeros((experts * capacity, model_width), jnp.bfloat16).at[slots].set(grad_pairs)
    grad_send = grad_send.reshape(sources, local_experts, capacity, model_width)
    grad_recv = lax.all_to_all(grad_send, "expert", split_axis=0, concat_axis=0, tiled=True)
    grad_rows_full, expert_parts = expert_backward(
        grad_recv, received, gate_pre, up_pre, gate_all, up_all, down_all
    )
    grad_rows_low = grad_rows_full.astype(jnp.bfloat16)
    gate_grad, up_grad, down_grad = (
        lax.psum_scatter(
            expert_parts[0].astype(jnp.bfloat16), "context", scatter_dimension=2, tiled=True
        ).astype(jnp.float32),
        lax.psum_scatter(
            expert_parts[1].astype(jnp.bfloat16), "context", scatter_dimension=2, tiled=True
        ).astype(jnp.float32),
        lax.psum_scatter(
            expert_parts[2].astype(jnp.bfloat16), "context", scatter_dimension=1, tiled=True
        ).astype(jnp.float32),
    )
    grad_back = lax.all_to_all(
        grad_rows_low, "expert", split_axis=0, concat_axis=0, tiled=True
    ).reshape(experts * capacity, model_width)
    grad_normed_two = jnp.sum(
        grad_back[slots].reshape(token_count, top_count, model_width).astype(jnp.float32), axis=1
    )
    grad_probs = jnp.sum(pick_table * grad_gates[:, :, None], axis=1)
    grad_logits = router_probs * (
        grad_probs - jnp.sum(grad_probs * router_probs, axis=-1, keepdims=True)
    )
    grad_logits_low = grad_logits.astype(jnp.bfloat16)
    grad_normed_two = grad_normed_two + times_transposed(grad_logits_low, full_router)
    router_part = transposed_times(normed_two_low, grad_logits_low)
    grad_hidden_norm, gain_second_part = norm_back(
        grad_normed_two, hidden_state, factor_two, gain_second
    )
    grad_hidden = grad_total + grad_hidden_norm
    grad_update_low = grad_hidden.astype(jnp.bfloat16)
    out_part = transposed_times(attended_low, grad_update_low)
    grad_attended = (
        times_transposed(grad_update_low, full_out)
        .astype(jnp.bfloat16)
        .reshape(token_count, heads, head_dim)
    )
    scores_again = scores_for(query_low, keys_all, key_valid, score_scale)
    softmax_again = jnp.exp(scores_again - log_total)
    grad_weights = jnp.einsum(
        "qhd,khd->hqk", grad_attended, values_all, preferred_element_type=jnp.float32
    )
    grad_values_part = jnp.einsum(
        "hqk,qhd->khd",
        softmax_again.astype(jnp.bfloat16),
        grad_attended,
        preferred_element_type=jnp.float32,
    )
    inner_sum = jnp.sum(grad_weights * softmax_again, axis=-1, keepdims=True)
    grad_scores = (softmax_again * (grad_weights - inner_sum)).astype(jnp.bfloat16)
    grad_query = (
        jnp.einsum("hqk,khd->qhd", grad_scores, keys_all, preferred_element_type=jnp.float32)
        * score_scale
    )
    grad_keys_part = (
        jnp.einsum("hqk,qhd->khd", grad_scores, query_low, preferred_element_type=jnp.float32)
        * score_scale
    )
    grad_keys_all, grad_values_all = (
        lax.psum_scatter(
            grad_keys_part.reshape(seq_len, model_width).astype(jnp.bfloat16),
            "context",
            scatter_dimension=0,
            tiled=True,
        ).astype(jnp.float32),
        lax.psum_scatter(
            grad_values_part.reshape(seq_len, model_width).astype(jnp.bfloat16),
            "context",
            scatter_dimension=0,
            tiled=True,
        ).astype(jnp.float32),
    )
    grad_value_low = grad_values_all.astype(jnp.bfloat16)
    grad_key_rot = rotate(
        grad_keys_all.reshape(token_count, heads, head_dim), cosine, sine, -1.0
    ).reshape(token_count, model_width)
    grad_key_raw, gain_keys_part = norm_back(grad_key_rot, key_raw, key_factor, gain_keys)
    grad_key_low = grad_key_raw.astype(jnp.bfloat16)
    grad_query_rot = rotate(grad_query, cosine, sine, -1.0).reshape(token_count, model_width)
    grad_query_raw, gain_queries_part = norm_back(
        grad_query_rot, query_raw, query_factor, gain_queries
    )
    grad_query_low = grad_query_raw.astype(jnp.bfloat16)
    grad_normed_one = times_transposed(grad_query_low, full_query) + times_transposed(
        grad_key_low, full_key
    )
    grad_normed_one = grad_normed_one + times_transposed(grad_value_low, full_value)
    query_part = transposed_times(normed_one_low, grad_query_low)
    key_part = transposed_times(normed_one_low, grad_key_low)
    value_part = transposed_times(normed_one_low, grad_value_low)
    grad_input_norm, gain_first_part = norm_back(grad_normed_one, inputs, factor_one, gain_first)
    input_grad = (grad_hidden + grad_input_norm).astype(jnp.bfloat16)
    (
        query_grad,
        key_grad,
        value_grad,
        out_grad,
        router_grad,
        first_gain_grad,
        second_gain_grad,
        query_gain_grad,
        key_gain_grad,
    ) = (
        lax.psum_scatter(query_part, ("context", "expert"), scatter_dimension=0, tiled=True),
        lax.psum_scatter(key_part, ("context", "expert"), scatter_dimension=0, tiled=True),
        lax.psum_scatter(value_part, ("context", "expert"), scatter_dimension=0, tiled=True),
        lax.psum_scatter(out_part, ("context", "expert"), scatter_dimension=0, tiled=True),
        lax.psum_scatter(router_part, ("context", "expert"), scatter_dimension=0, tiled=True),
        lax.psum_scatter(gain_first_part, ("context", "expert"), scatter_dimension=0, tiled=True),
        lax.psum_scatter(gain_second_part, ("context", "expert"), scatter_dimension=0, tiled=True),
        lax.psum_scatter(gain_queries_part, ("context", "expert"), scatter_dimension=0, tiled=True),
        lax.psum_scatter(gain_keys_part, ("context", "expert"), scatter_dimension=0, tiled=True),
    )
    return (
        layer_out[None],
        input_grad[None],
        query_grad,
        key_grad,
        value_grad,
        out_grad,
        router_grad,
        first_gain_grad,
        second_gain_grad,
        query_gain_grad,
        key_gain_grad,
        gate_grad,
        up_grad,
        down_grad,
    )


def solution(mesh):
    placed = (
        P("expert", "context", None),
        P("expert", "context", None),
        P("expert"),
        P("expert", "context", None),
        P(("context", "expert"), None),
        P(("context", "expert"), None),
        P(("context", "expert"), None),
        P(("context", "expert"), None),
        P(("context", "expert"), None),
        P(("context", "expert")),
        P(("context", "expert")),
        P(("context", "expert")),
        P(("context", "expert")),
        P("expert", None, "context"),
        P("expert", None, "context"),
        P("expert", "context", None),
    )
    return jax.shard_map(
        local,
        mesh=mesh,
        in_specs=placed,
        out_specs=(
            P("expert", "context", None),
            P("expert", "context", None),
            P(("context", "expert"), None),
            P(("context", "expert"), None),
            P(("context", "expert"), None),
            P(("context", "expert"), None),
            P(("context", "expert"), None),
            P(("context", "expert")),
            P(("context", "expert")),
            P(("context", "expert")),
            P(("context", "expert")),
            P("expert", None, "context"),
            P("expert", None, "context"),
            P("expert", "context", None),
        ),
        check_vma=False,
    )
```

profile of v0, /device:TPU:9, one launch (start us, length us, event | category | flops | bytes accessed | tf_op | source)
XLA Modules:
  0.0 2733.8 jit_solution(6935732502362821630)
XLA Ops:
  12.9 41.0 %all-reduce.9 = (bf16[2048]{0:T(1024)(128)(2,1)S(1)}, bf16[2048]{0:T(1024)(128)(2,1)S(1)}, bf16[2048]{0:T(1024)(128)(2,1)S(1)}, bf16[2048]{0:T(1024)(128)(2,1)S(1)}) all-reduce(bf16[2048]{0:T(1024)(128)(2,1)S(1)} %dynamic-update-slice, ...), channel_id=1, replica_groups=mesh['context'=4,'expert'=8] {'context','expert'}, use_global_device_ids=true, to_apply=%add | all-reduce | flops 8192 | bytes 32768
  57.3 33.3 %all-gather.17.cloned.1.call-done = bf16[2048,2048]{1,0:T(8,128)(2,1)} async-done(((bf16[64,2048]{1,0:T(8,128)(2,1)}), bf16[2048,2048]{1,0:T(8,128)(2,1)}) %all-gather.17.cloned.1.call-update) | async-done | bytes 8388624 | tf_op jit(solution)/shard_map/all_gather | solution.py:149
  100.0 69.4 %all-gather.15.cloned.1.call-done = bf16[2048,2048]{1,0:T(8,128)(2,1)} async-done(((bf16[64,2048]{1,0:T(8,128)(2,1)}), bf16[2048,2048]{1,0:T(8,128)(2,1)}) %all-gather.15.cloned.1.call-update) | async-done | bytes 8388624 | tf_op jit(solution)/shard_map/all_gather | solution.py:148
  184.6 63.7 %all-gather.11.cloned.1.call-done = bf16[2048,2048]{1,0:T(8,128)(2,1)} async-done(((bf16[64,2048]{1,0:T(8,128)(2,1)}), bf16[2048,2048]{1,0:T(8,128)(2,1)}) %all-gather.11.cloned.1.call-update) | async-done | bytes 8388624 | tf_op jit(solution)/shard_map/all_gather | solution.py:150
  265.4 36.0 %all-gather.19.cloned.1.call-done = bf16[1024,16,128]{2,0,1:T(8,128)(2,1)} async-done(((bf16[256,16,128]{2,0,1:T(8,128)(2,1)}), bf16[1024,16,128]{2,0,1:T(8,128)(2,1)}) %all-gather.19.cloned.1.call-update) | async-done | bytes 4194320 | tf_op jit(solution)/shard_map/all_gather | solution.py:183
  313.2 43.1 %all-gather.13.cloned.1.call-done = bf16[1024,16,128]{0,2,1:T(8,128)(2,1)} async-done(((bf16[256,16,128]{0,2,1:T(8,128)(2,1)}), bf16[1024,16,128]{0,2,1:T(8,128)(2,1)}) %all-gather.13.cloned.1.call-update) | async-done | bytes 4194320 | tf_op jit(solution)/shard_map/all_gather | solution.py:184
  356.3 9.4 convolution_convert_fusion.3
  365.8 71.3 %all-gather.21.cloned.1.call-done = bf16[2048,2048]{1,0:T(8,128)(2,1)} async-done(((bf16[64,2048]{1,0:T(8,128)(2,1)}), bf16[2048,2048]{1,0:T(8,128)(2,1)}) %all-gather.21.cloned.1.call-update) | async-done | bytes 8388624 | tf_op jit(solution)/shard_map/all_gather | solution.py:151
  444.5 26.9 scatter_custom_fusion
  477.7 232.0 %all-gather = bf16[32,64,16]{1,2,0:T(8,128)(2,1)S(1)} all-gather(bf16[1,64,16]{1,2,0:T(8,128)(2,1)S(1)} %bitcast.254), channel_id=1, replica_groups=mesh['context'=4,'expert'=8] {'context','expert'}, dimensions={0}, use_global_device_ids=true | all-gather | bytes 67584 | tf_op jit(solution)/shard_map/all_gather | solution.py:152
  713.0 18.6 scatter_custom_fusion.1
  731.7 8.3 all-to-all-start.2
  740.7 17.1 fusion.24
  757.9 17.2 fusion.20
  775.1 54.9 %all-gather.27.cloned.1.call-done = bf16[2,1024,2048]{2,1,0:T(8,128)(2,1)} async-done(((bf16[2,256,2048]{2,1,0:T(8,128)(2,1)}), bf16[2,1024,2048]{2,1,0:T(8,128)(2,1)}) %all-gather.27.cloned.1.call-update) | async-done | bytes 8388624 | tf_op jit(solution)/shard_map/all_gather | solution.py:218
  830.0 112.8 %all-to-all-done.2 = bf16[8,2,144,2048]{3,2,1,0:T(8,128)(2,1)} async-done(((bf16[8,2,144,2048]{3,2,1,0:T(8,128)(2,1)}), bf16[8,2,144,2048]{3,2,1,0:T(8,128)(2,1)}, u32[]{:S(2)}, u32[]{:S(2)}) %all-to-all-start.2) | async-done | bytes 9437216 | tf_op jit(solution)/shard_map/all_to_all | solution.py:236
  942.8 22.8 fusion.7
  965.6 16.5 convert_bitcast_fusion
  982.1 9.3 copy.140
  991.3 8.6 all-to-all-start.1
  999.9 17.4 fusion.18
  1017.3 18.6 fusion.4
  1035.9 9.3 copy.143
  1045.2 157.5 %all-to-all-done.1 = bf16[8,2,144,2048]{3,2,1,0:T(8,128)(2,1)} async-done(((bf16[8,2,144,2048]{3,2,1,0:T(8,128)(2,1)}), bf16[8,2,144,2048]{3,2,1,0:T(8,128)(2,1)}, u32[]{:S(2)}, u32[]{:S(2)}) %all-to-all-start.1) | async-done | bytes 9437216 | tf_op jit(solution)/shard_map/all_to_all | solution.py:223
  1202.7 8.6 all-to-all-start.3
  1211.4 21.8 gather_fusion
  1233.2 9.5 fusion.1
  1242.9 171.3 %all-to-all-done.3 = bf16[8,2,144,2048]{3,2,1,0:T(8,128)(2,1)} async-done(((bf16[8,2,144,2048]{3,2,1,0:T(8,128)(2,1)}), bf16[8,2,144,2048]{3,2,1,0:T(8,128)(2,1)}, u32[]{:S(2)}, u32[]{:S(2)}) %all-to-all-start.3) | async-done | bytes 9437216 | tf_op jit(solution)/shard_map/all_to_all | solution.py:252
  1414.1 21.3 gather_fusion.1
  1435.4 11.5 convert_reduce_fusion
  1456.3 9.4 convolution_convert_fusion
  1465.8 13.9 multiply_reduce_fusion
  1479.7 13.4 multiply_convert_fusion
  1500.8 18.1 bitcast_convert_fusion
  1518.9 17.0 bitcast_convert_fusion.2
  1536.0 17.7 bitcast_convert_fusion.1
  1555.6 8.6 fusion.66
  1565.4 9.5 fusion.82
  1599.6 8.3 fusion.84
  1623.1 79.7 %reduce-scatter.31.cloned.1.call-done = f32[64,16]{1,0:T(8,128)} async-done(((f32[2048,16]{1,0:T(8,128)}), f32[64,16]{1,0:T(8,128)}) %reduce-scatter.31.cloned.1.call-update) | async-done | bytes 4112
  1704.2 95.3 %reduce-scatter.29.cloned.1.call-done = bf16[2,256,2048]{2,1,0:T(8,128)(2,1)} async-done(((bf16[2,1024,2048]{2,1,0:T(8,128)(2,1)}), bf16[2,256,2048]{2,1,0:T(8,128)(2,1)}) %reduce-scatter.29.cloned.1.call-update) | async-done | bytes 2097168 | tf_op jit(solution)/shard_map/reduce_scatter | solution.py:248
  1803.6 85.2 %reduce-scatter.25.cloned.1.call-done = bf16[2,2048,256]{2,1,0:T(8,128)(2,1)} async-done(((bf16[2,2048,1024]{2,1,0:T(8,128)(2,1)}), bf16[2,2048,256]{2,1,0:T(8,128)(2,1)}) %reduce-scatter.25.cloned.1.call-update) | async-done | bytes 2097168 | tf_op jit(solution)/shard_map/reduce_scatter | solution.py:242
  1892.7 85.7 %reduce-scatter.27.cloned.1.call-done = bf16[2,2048,256]{2,1,0:T(8,128)(2,1)} async-done(((bf16[2,2048,1024]{2,1,0:T(8,128)(2,1)}), bf16[2,2048,256]{2,1,0:T(8,128)(2,1)}) %reduce-scatter.27.cloned.1.call-update) | async-done | bytes 2097168 | tf_op jit(solution)/shard_map/reduce_scatter | solution.py:245
  1998.4 41.6 %all-reduce.8 = (f32[2048]{0:T(1024)S(1)}, f32[2048]{0:T(1024)S(1)}, f32[2048]{0:T(1024)S(1)}, f32[2048]{0:T(1024)S(1)}) all-reduce(f32[2048]{0:T(1024)S(1)} %get-tuple-element.22, f32[2048]{0:T(1024)S(1)} %copy-done.55, f32[2048]{0:T(1024)S(1)} %get-tuple-element.18, ...), channel_id=9, replica_groups=mesh['context'=4,'expert'=8] {'context','expert'}, use_global_device_ids=true, to_apply=%region_32.33.clone | all-reduce | flops 8192 | bytes 65536
  2045.6 119.9 %reduce-scatter.23.cloned.1.call-done = f32[64,2048]{1,0:T(8,128)} async-done(((f32[2048,2048]{1,0:T(8,128)}), f32[64,2048]{1,0:T(8,128)}) %reduce-scatter.23.cloned.1.call-update) | async-done | bytes 524304 | tf_op jit(solution)/shard_map/reduce_scatter | solution.py:345
  2165.5 187.1 %reduce-scatter.21.cloned.1.call-done = f32[64,2048]{1,0:T(8,128)} async-done(((f32[2048,2048]{1,0:T(8,128)}), f32[64,2048]{1,0:T(8,128)}) %reduce-scatter.21.cloned.1.call-update) | async-done | bytes 524304 | tf_op jit(solution)/shard_map/reduce_scatter | solution.py:344
  2352.6 187.1 %reduce-scatter.19.cloned.1.call-done = f32[64,2048]{1,0:T(8,128)} async-done(((f32[2048,2048]{1,0:T(8,128)}), f32[64,2048]{1,0:T(8,128)}) %reduce-scatter.19.cloned.1.call-update) | async-done | bytes 524304 | tf_op jit(solution)/shard_map/reduce_scatter | solution.py:343
  2539.8 187.2 %reduce-scatter.17.cloned.1.call-done = f32[64,2048]{1,0:T(8,128)} async-done(((f32[2048,2048]{1,0:T(8,128)}), f32[64,2048]{1,0:T(8,128)}) %reduce-scatter.17.cloned.1.call-update) | async-done | bytes 524304 | tf_op jit(solution)/shard_map/reduce_scatter | solution.py:342
  (310 shorter events, 174.2 us)
Async XLA Ops:
  7.2 83.3 %all-gather.17.cloned.1.call-start = ((), (), s32[]{:S(2)}) async-start(), calls=%async_computation.17 | async-start | bytes 8650752 | tf_op jit(solution)/shard_map/all_gather | solution.py:149
  7.9 161.5 %all-gather.15.cloned.1.call-start = ((), (), s32[]{:S(2)}) async-start(), calls=%async_computation.16 | async-start | bytes 8650752 | tf_op jit(solution)/shard_map/all_gather | solution.py:148
  8.7 239.6 %all-gather.11.cloned.1.call-start = ((), (), s32[]{:S(2)}) async-start(), calls=%async_computation.14 | async-start | bytes 8650752 | tf_op jit(solution)/shard_map/all_gather | solution.py:150
  9.4 292.0 %all-gather.19.cloned.1.call-start = ((), (), s32[]{:S(2)}) async-start(), calls=%async_computation.18 | async-start | bytes 5242880 | tf_op jit(solution)/shard_map/all_gather | solution.py:183
  53.9 194.4 %copy-start.41 = (f32[2048]{0:T(1024)}, f32[2048]{0:T(1024)S(1)}, u32[]{:S(2)}) copy-start(f32[2048]{0:T(1024)S(1)} %convert_element_type.189) | copy-start | bytes 24580
  53.9 43.5 %copy-start.47 = (f32[2048]{0:T(1024)}, f32[2048]{0:T(1024)S(1)}, u32[]{:S(2)}) copy-start(f32[2048]{0:T(1024)S(1)} %convert_element_type.194) | copy-start | bytes 24580
  53.9 122.0 %copy-start.45 = (f32[2048]{0:T(1024)}, f32[2048]{0:T(1024)S(1)}, u32[]{:S(2)}) copy-start(f32[2048]{0:T(1024)S(1)} %convert_element_type.192) | copy-start | bytes 24580
  56.1 192.2 %copy-start.53 = (f32[256]{0:T(256)}, f32[256]{0:T(256)S(1)}, u32[]{:S(2)}) copy-start(f32[256]{0:T(256)S(1)} %get-tuple-element.59) | copy-start | bytes 3076
  57.3 121.7 %copy-start.31 = (f32[256,64]{1,0:T(8,128)}, f32[256,64]{1,0:T(8,128)S(1)}, u32[]{:S(2)}) copy-start(f32[256,64]{1,0:T(8,128)S(1)} %get-tuple-element.57) | copy-start | bytes 196612
  98.1 71.3 %copy-start.1 = (bf16[1,256,2048]{2,1,0:T(8,128)(2,1)S(1)}, bf16[1,256,2048]{2,1,0:T(8,128)(2,1)}, u32[]{:S(2)}) copy-start(bf16[1,256,2048]{2,1,0:T(8,128)(2,1)} %param.16) | copy-start | bytes 3145732
  182.7 118.8 %copy-start.20 = (bf16[256,16,64]{2,0,1:T(8,128)(2,1)}, bf16[256,16,64]{2,0,1:T(8,128)(2,1)S(1)}, u32[]{:S(2)}) copy-start(bf16[256,16,64]{2,0,1:T(8,128)(2,1)S(1)} %get-tuple-element.37) | copy-start | bytes 1572868
  184.2 172.0 %all-gather.13.cloned.1.call-start = ((), (), s32[]{:S(2)}) async-start(), calls=%async_computation.15 | async-start | bytes 5242880 | tf_op jit(solution)/shard_map/all_gather | solution.py:184
  257.4 179.7 %all-gather.21.cloned.1.call-start = ((), (), s32[]{:S(2)}) async-start(), calls=%async_computation.19 | async-start | bytes 8650752 | tf_op jit(solution)/shard_map/all_gather | solution.py:151
  258.0 482.7 %all-gather.23.cloned.1.call-start = ((), (), s32[]{:S(2)}) async-start(), calls=%async_computation.20 | async-start | bytes 10485760 | tf_op jit(solution)/shard_map/all_gather | solution.py:216
  259.8 96.5 %copy-start.60 = (pred[1024]{0:T(1024)(128)(4,1)}, pred[1024]{0:T(1024)(128)(4,1)S(1)}, u32[]{:S(2)}) copy-start(pred[1024]{0:T(1024)(128)(4,1)S(1)} %iota_compare_fusion.3) | copy-start | bytes 3076
  259.8 183.8 %copy-start.51 = (f32[2048]{0:T(1024)}, f32[2048]{0:T(1024)S(1)}, u32[]{:S(2)}) copy-start(f32[2048]{0:T(1024)S(1)} %convert_element_type.199) | copy-start | bytes 24580
  265.4 447.6 %copy-start.56 = (s32[2048,1]{0,1:T(1,128)}, s32[2048,1]{0,1:T(1,128)S(1)}, u32[]{:S(2)}) copy-start(s32[2048,1]{0,1:T(1,128)S(1)} %compare_select_fusion) | copy-start | bytes 24580
  313.2 52.6 %copy-start.43 = (f32[16,256]{1,0:T(8,128)}, f32[16,256]{1,0:T(8,128)S(1)}, u32[]{:S(2)}) copy-start(f32[16,256]{1,0:T(8,128)S(1)} %log_add_fusion) | copy-start | bytes 49156
  365.8 77.2 %copy-start.24 = (bf16[16,128,256]{2,1,0:T(8,128)(2,1)}, bf16[16,128,256]{2,1,0:T(8,128)(2,1)S(1)}, u32[]{:S(2)}) copy-start(bf16[16,128,256]{2,1,0:T(8,128)(2,1)S(1)} %convolution_convert_fusion.3) | copy-start | bytes 3145732
  443.6 27.9 %copy-start.66 = (f32[256]{0:T(256)}, f32[256]{0:T(256)S(1)}, u32[]{:S(2)}) copy-start(f32[256]{0:T(256)S(1)} %get-tuple-element.65) | copy-start | bytes 3076
  444.5 266.9 %copy-start.18 = (bf16[256,2048]{1,0:T(8,128)(2,1)}, bf16[256,2048]{1,0:T(8,128)(2,1)S(1)}, u32[]{:S(2)}) copy-start(bf16[256,2048]{1,0:T(8,128)(2,1)S(1)} %multiply_convert_fusion.3) | copy-start | bytes 3145732
  471.4 260.3 %all-to-all-start = ((bf16[8,2,144,2048]{3,2,1,0:T(8,128)(2,1)}), bf16[8,2,144,2048]{3,2,1,0:T(8,128)(2,1)}, u32[]{:S(2)}, u32[]{:S(2)}) async-start(bf16[8,2,144,2048]{3,2,1,0:T(8,128)(2,1)} %bitcast.232), calls=%async_computation | async-start | bytes 18874368 | tf_op jit(solution)/shard_map/all_to_all | solution.py:220
  476.9 280.9 %all-gather.25.cloned.1.call-start = ((), (), s32[]{:S(2)}) async-start(), calls=%async_computation.21 | async-start | bytes 10485760 | tf_op jit(solution)/shard_map/all_gather | solution.py:217
  709.9 21.7 copy-start.36
  711.4 20.3 copy-start.6
  712.9 18.8 copy-start.33
  731.7 211.1 %all-to-all-start.2 = ((bf16[8,2,144,2048]{3,2,1,0:T(8,128)(2,1)}), bf16[8,2,144,2048]{3,2,1,0:T(8,128)(2,1)}, u32[]{:S(2)}, u32[]{:S(2)}) async-start(bf16[8,2,144,2048]{3,2,1,0:T(8,128)(2,1)} %bitcast.233), calls=%async_computation.2 | async-start | bytes 18874368 | tf_op jit(solution)/shard_map/all_to_all | solution.py:236
  740.0 90.0 %all-gather.27.cloned.1.call-start = ((), (), s32[]{:S(2)}) async-start(), calls=%async_computation.22 | async-start | bytes 10485760 | tf_op jit(solution)/shard_map/all_gather | solution.py:218
  991.3 211.4 %all-to-all-start.1 = ((bf16[8,2,144,2048]{3,2,1,0:T(8,128)(2,1)}), bf16[8,2,144,2048]{3,2,1,0:T(8,128)(2,1)}, u32[]{:S(2)}, u32[]{:S(2)}) async-start(bf16[8,2,144,2048]{3,2,1,0:T(8,128)(2,1)} %copy.140), calls=%async_computation.1 | async-start | bytes 18874368 | tf_op jit(solution)/shard_map/all_to_all | solution.py:223
  1045.2 166.2 %copy-start.57 = (s32[2048,1]{0,1:T(1,128)S(1)}, s32[2048,1]{0,1:T(1,128)}, u32[]{:S(2)}) copy-start(s32[2048,1]{0,1:T(1,128)} %copy-done.56) | copy-start | bytes 24580
  1202.7 211.4 %all-to-all-start.3 = ((bf16[8,2,144,2048]{3,2,1,0:T(8,128)(2,1)}), bf16[8,2,144,2048]{3,2,1,0:T(8,128)(2,1)}, u32[]{:S(2)}, u32[]{:S(2)}) async-start(bf16[8,2,144,2048]{3,2,1,0:T(8,128)(2,1)} %copy.143), calls=%async_computation.3 | async-start | bytes 18874368 | tf_op jit(solution)/shard_map/all_to_all | solution.py:252
  1211.3 352.9 %reduce-scatter.15.cloned.1.call-start = ((), (), s32[]{:S(2)}) async-start(), calls=%async_computation.24 | async-start | bytes 5242880 | tf_op jit(solution)/shard_map/reduce_scatter | solution.py:304
  1211.4 21.8 copy-start.7
  1211.4 21.8 copy-start.34
  1435.4 14.6 copy-start.30
  1465.7 116.4 %reduce-scatter.13.cloned.1.call-start = ((), (), s32[]{:S(2)}) async-start(), calls=%async_computation.23 | async-start | bytes 5242880 | tf_op jit(solution)/shard_map/reduce_scatter | solution.py:298
  1479.7 13.5 copy-start.22
  1498.0 204.8 %reduce-scatter.31.cloned.1.call-start = ((), (), s32[]{:S(2)}) async-start(), calls=%async_computation.32 | async-start | bytes 1081344
  1500.7 298.7 %reduce-scatter.29.cloned.1.call-start = ((), (), s32[]{:S(2)}) async-start(), calls=%async_computation.31 | async-start | bytes 10485760 | tf_op jit(solution)/shard_map/reduce_scatter | solution.py:248
  1518.9 369.9 %reduce-scatter.25.cloned.1.call-start = ((), (), s32[]{:S(2)}) async-start(), calls=%async_computation.29 | async-start | bytes 10485760 | tf_op jit(solution)/shard_map/reduce_scatter | solution.py:242
  1536.0 442.4 %reduce-scatter.27.cloned.1.call-start = ((), (), s32[]{:S(2)}) async-start(), calls=%async_computation.30 | async-start | bytes 10485760 | tf_op jit(solution)/shard_map/reduce_scatter | solution.py:245
  1553.8 611.8 %reduce-scatter.23.cloned.1.call-start = ((), (), s32[]{:S(2)}) async-start(), calls=%async_computation.28 | async-start | bytes 17301504 | tf_op jit(solution)/shard_map/reduce_scatter | solution.py:345
  1564.2 788.4 %reduce-scatter.21.cloned.1.call-start = ((), (), s32[]{:S(2)}) async-start(), calls=%async_computation.27 | async-start | bytes 17301504 | tf_op jit(solution)/shard_map/reduce_scatter | solution.py:344
  1574.9 964.8 %reduce-scatter.19.cloned.1.call-start = ((), (), s32[]{:S(2)}) async-start(), calls=%async_computation.26 | async-start | bytes 17301504 | tf_op jit(solution)/shard_map/reduce_scatter | solution.py:343
  1607.9 1119.1 %reduce-scatter.17.cloned.1.call-start = ((), (), s32[]{:S(2)}) async-start(), calls=%async_computation.25 | async-start | bytes 17301504 | tf_op jit(solution)/shard_map/reduce_scatter | solution.py:342
  1892.7 89.8 %copy-start.29 = (bf16[256,2048]{1,0:T(8,128)(2,1)S(1)}, bf16[256,2048]{1,0:T(8,128)(2,1)}, u32[]{:S(2)}) copy-start(bf16[256,2048]{1,0:T(8,128)(2,1)} %copy-done.28) | copy-start | bytes 3145732
  1994.2 48.2 %copy-start.14 = (f32[256,2048]{1,0:T(8,128)S(1)}, f32[256,2048]{1,0:T(8,128)}, u32[]{:S(2)}) copy-start(f32[256,2048]{1,0:T(8,128)} %copy-done.12) | copy-start | bytes 6291460
  1994.2 48.2 %copy-start.72 = (f32[256]{0:T(256)S(1)}, f32[256]{0:T(256)}, u32[]{:S(2)}) copy-start(f32[256]{0:T(256)} %get-tuple-element.58) | copy-start | bytes 3076
  (58 other events, 268.3 us)
Sparse Core Ops, SparseCore 0:
  11.0 79.4 all-gather.16
  93.5 75.8 all-gather.14
  172.4 75.8 all-gather.10
  250.6 50.8 all-gather.18
  303.7 52.5 all-gather.12
  359.1 77.9 all-gather.20
  438.9 85.5 all-gather.22
  526.4 87.4 all-gather.24
  742.6 87.2 all-gather.26
  1465.9 53.4 reduce-scatter.14
  1523.2 52.6 reduce-scatter.12
  1578.5 124.2 reduce-scatter.30
  1706.1 93.2 reduce-scatter.28
  1802.4 86.3 reduce-scatter.24
  1892.0 86.3 reduce-scatter.26
  1981.1 184.4 reduce-scatter.22
  2168.3 184.3 reduce-scatter.20
  2355.4 184.3 reduce-scatter.18
  2542.6 184.3 reduce-scatter.16
where the time goes:
time: 2740 us; the launch traced here: 2730 us
  waiting for transfers between devices  1850 us (68%)
  blocking collectives  315 us (11%)
  matrix products  295 us (11%)
  local copies, waits for them, and re-layouts  127 us (5%)
  other arithmetic  104 us (4%)
  starting transfers between devices  32.2 us (1%)
    all_gather x1, blocking collectives, local(): lax.all_gather(router_weight, ('context', 'expert'), axis=0, tiled=True)  232 us
    reduce_scatter x1, waiting for transfers between devices, local(): lax.psum_scatter(query_part, ('context', 'expert'), scatter_dimension=0,...  187 us
    reduce_scatter x1, waiting for transfers between devices, local(): lax.psum_scatter(key_part, ('context', 'expert'), scatter_dimension=0, ti...  187 us
    reduce_scatter x1, waiting for transfers between devices, local(): lax.psum_scatter(value_part, ('context', 'expert'), scatter_dimension=0,...  187 us
    all_to_all x1, waiting for transfers between devices, local(): lax.all_to_all(grad_rows_low, 'expert', split_axis=0, concat_axis=0, tile...  171 us
    all_to_all x1, waiting for transfers between devices, local(): lax.all_to_all(expert_out, 'expert', split_axis=0, concat_axis=0, tiled=T...  158 us
    reduce_scatter x1, waiting for transfers between devices, local(): lax.psum_scatter(out_part, ('context', 'expert'), scatter_dimension=0, ti...  120 us
    all_to_all x1, waiting for transfers between devices, local(): lax.all_to_all(grad_send, 'expert', split_axis=0, concat_axis=0, tiled=True)  113 us
  transfers between devices with their start and end apart: 23, of which 18 were waited for; matrix products, arithmetic and copies ran while one was open for 15% of the time, Pallas kernels for 0%

commit v1 on v0

v1 whole, which is shorter than its diff:
```python
import functools
import math

import jax
import jax.numpy as jnp
from jax import lax
from jax.experimental import pallas as pl
from jax.experimental.pallas import tpu as pltpu
from jax.sharding import Mesh
from jax.sharding import PartitionSpec as P

HEADS = 16
HD = 128
EPSILON = 1e-06
ROPE_THETA = 10000.0
NEG_FILL = -1e30

CTX = ("ca", "cb")
EXP = ("ring", "core")
ALL = CTX + EXP


MESH = pl.DeviceIdType.MESH


def turn(name, by):
    size = lax.axis_size(name)
    return lax.rem(lax.axis_index(name) + by, size)


def await_bytes(ref, sem):
    pltpu.make_async_copy(ref, ref, sem).wait()


def greet(peers):
    barrier = pltpu.get_barrier_semaphore()
    for peer in peers:
        pl.semaphore_signal(barrier, inc=1, device_id=peer, device_id_type=MESH)
    pl.semaphore_wait(barrier, len(peers))


RING, SIDE_B, SIDE_A, FIRST, SECOND, CORE_OWN, CORE_B, CORE_A, CORE_FIRST, CORE_SECOND = range(10)


def spread_kernel(count, *refs):
    ring = lax.axis_size("ring")
    shards, ids, outs, ids_out = refs[:count], refs[count], refs[count + 1 : 2 * count + 1], refs[2 * count + 1]
    send, got_ring, got_b, got_a, got, place, ids_send, ids_got, ids_place = refs[2 * count + 2 :]
    a, b, r, c = (lax.axis_index(n) for n in ALL)
    na, nb, nc = turn("ca", 1), turn("cb", 1), turn("core", 1)
    to_a, to_b, to_core = {"ca": na}, {"cb": nb}, {"core": nc}
    greet([to_a, to_b, to_core] + [{"ring": turn("ring", k)} for k in range(1, ring)])

    def push(src, dst, ssem, rsem, to):
        pltpu.make_async_remote_copy(
            src_ref=src, dst_ref=dst, send_sem=ssem, recv_sem=rsem, device_id=to, device_id_type=MESH
        ).start()

    def half(ref, which):
        rows, cols = ref.shape[-2:]
        if rows * 8 < cols:
            return ref.at[..., pl.ds(which * (cols // 2), cols // 2)]
        return ref.at[..., pl.ds(which * (rows // 2), rows // 2), :]

    def halves(ref, which):
        rows, cols = ref.shape[-2:]
        if rows * 8 < cols:
            return ref.at[:, :, pl.ds(which * (cols // 2), cols // 2)]
        return ref.at[:, pl.ds(which * (rows // 2), rows // 2), :]

    for w in range(count):
        out = outs[w]
        pltpu.make_async_copy(shards[w], out.at[a, b, r, c], place.at[w]).start()
    pltpu.make_async_copy(ids, ids_out.at[r, c], ids_place).start()
    push(ids, ids_out.at[r, c], ids_send.at[ring], ids_got.at[ring], to_core)
    for w in reversed(range(count)):
        out = outs[w]
        for k in range(1, ring):
            push(shards[w], out.at[a, b, r, c], send.at[w, RING], got_ring.at[w, k], {"ring": turn("ring", k)})
        push(shards[w], out.at[a, b, r, c], send.at[w, SIDE_B], got_b.at[w, 0], to_b)
        push(shards[w], out.at[a, b, r, c], send.at[w, SIDE_A], got_a.at[w, 0], to_a)
        push(shards[w], out.at[a, b, r, c], send.at[w, CORE_OWN], got.at[w, CORE_OWN], to_core)
    for k in range(1, ring):
        push(ids, ids_out.at[r, c], ids_send.at[k], ids_got.at[k], {"ring": turn("ring", k)})

    def sides(w):
        out = outs[w]

        def one(k, carry):
            at = lax.rem(r + ring - k, ring)
            block = out.at[a, b, at, c]
            await_bytes(block, got_ring.at[w, k])
            push(block, block, send.at[w, SIDE_B], got_b.at[w, k], to_b)
            push(block, block, send.at[w, SIDE_A], got_a.at[w, k], to_a)
            push(block, block, send.at[w, CORE_OWN], got.at[w, CORE_OWN], to_core)
            return carry

        lax.fori_loop(1, ring, one, 0)

    def diagonal(w):
        out = outs[w]

        def one(k, carry):
            at = lax.rem(r + ring - k, ring)
            block = out.at[a, nb, at, c]
            await_bytes(block, got_b.at[w, k])
            push(half(block, 0), half(block, 0), send.at[w, FIRST], got.at[w, FIRST], to_a)
            push(block, block, send.at[w, CORE_B], got.at[w, CORE_B], to_core)
            block = out.at[na, b, at, c]
            await_bytes(block, got_a.at[w, k])
            push(half(block, 1), half(block, 1), send.at[w, SECOND], got.at[w, SECOND], to_b)
            push(block, block, send.at[w, CORE_A], got.at[w, CORE_A], to_core)
            return carry

        lax.fori_loop(0, ring, one, 0)

    def last(w):
        block = outs[w].at[na, nb, :, c]
        for which, kind, core_kind in ((0, FIRST, CORE_FIRST), (1, SECOND, CORE_SECOND)):
            part = halves(block, which)
            await_bytes(part, got.at[w, kind])
            push(part, part, send.at[w, core_kind], got.at[w, core_kind], to_core)

    order = list(reversed(range(count)))
    for step in range(count + 2):
        if step < count:
            sides(order[step])
        if 0 <= step - 1 < count:
            diagonal(order[step - 1])
        if 0 <= step - 2 < count:
            last(order[step - 2])

    def ids_on(k, carry):
        block = ids_out.at[lax.rem(r + ring - k, ring), c]
        await_bytes(block, ids_got.at[k])
        push(block, block, ids_send.at[ring], ids_got.at[ring], to_core)
        return carry

    lax.fori_loop(1, ring, ids_on, 0)
    for w in range(count):
        out = outs[w]
        pltpu.make_async_copy(shards[w], out.at[a, b, r, c], place.at[w]).wait()
        mine = lambda p, q: out.at[p, q, :, c]
        await_bytes(out.at[a, b, pl.ds(0, ring - 1), c], send.at[w, RING])
        for kind in (SIDE_B, SIDE_A, CORE_OWN, CORE_B, CORE_A):
            await_bytes(mine(a, b), send.at[w, kind])
        for which, kind in ((0, FIRST), (1, SECOND), (0, CORE_FIRST), (1, CORE_SECOND)):
            await_bytes(halves(mine(a, b), which), send.at[w, kind])
        for kind, p, q in ((CORE_OWN, a, b), (CORE_B, a, nb), (CORE_A, na, b)):
            await_bytes(out.at[p, q, :, nc], got.at[w, kind])
        for which, kind in ((0, CORE_FIRST), (1, CORE_SECOND)):
            await_bytes(halves(out.at[na, nb, :, nc], which), got.at[w, kind])
    pltpu.make_async_copy(ids, ids_out.at[r, c], ids_place).wait()
    for k in range(1, ring):
        await_bytes(ids, ids_send.at[k])
    await_bytes(ids_out.at[:, c], ids_send.at[ring])
    await_bytes(ids_out.at[:, nc], ids_got.at[ring])


def spread(shards, ids):
    count, ring = len(shards), lax.axis_size("ring")
    square = (lax.axis_size("ca"), lax.axis_size("cb"), ring, 2)
    dma = pltpu.SemaphoreType.DMA
    outs = pl.pallas_call(
        functools.partial(spread_kernel, count),
        out_shape=[jax.ShapeDtypeStruct(square + s.shape, s.dtype) for s in shards]
        + [jax.ShapeDtypeStruct((ring, 2) + ids.shape, ids.dtype)],
        in_specs=[pl.BlockSpec(memory_space=pltpu.VMEM)] * (count + 1),
        out_specs=[pl.BlockSpec(memory_space=pl.ANY)] * (count + 1),
        scratch_shapes=[
            dma((count, 10)), dma((count, ring)), dma((count, ring)), dma((count, ring)), dma((count, 10)), dma((count,)),
            dma((ring + 1,)), dma((ring + 1,)), dma,
        ],
        compiler_params=pltpu.CompilerParams(collective_id=0, has_side_effects=True),
        name="spread",
    )(*shards, ids)
    return outs[:count], outs[count]


def collect_kernel(count, *refs):
    ring = lax.axis_size("ring")
    parts, outs = refs[:count], refs[count : 2 * count]
    scratch = refs[2 * count :]
    a, b, r, c = (lax.axis_index(n) for n in ALL)
    na, nb, nc = turn("ca", 1), turn("cb", 1), turn("core", 1)
    to_a, to_b, to_core = {"ca": na}, {"cb": nb}, {"core": nc}
    send, got, ring_send, ring_got, load = scratch[-5:]
    bufs = [scratch[9 * w : 9 * w + 9] for w in range(count)]
    greet([to_a, to_b, to_core] + [{"ring": turn("ring", k)} for k in range(1, ring)])

    def push(src, dst, ssem, rsem, to):
        pltpu.make_async_remote_copy(
            src_ref=src, dst_ref=dst, send_sem=ssem, recv_sem=rsem, device_id=to, device_id_type=MESH
        ).start()

    def half(ref, which):
        rows, cols = ref.shape[-2:]
        lead = (slice(None),) * (len(ref.shape) - 2)
        if cols > 128:
            return ref.at[(*lead, slice(None), pl.ds(which * (cols // 2), cols // 2))]
        return ref.at[(*lead, pl.ds(which * (rows // 2), rows // 2), slice(None))]

    def loads(w):
        own_a, own_b = bufs[w][0:2]
        return (
            pltpu.make_async_copy(half(parts[w].at[a], 0), own_a, load.at[w, 0]),
            pltpu.make_async_copy(half(parts[w].at[:, b], 1), own_b, load.at[w, 1]),
        )

    def first(w):
        for copy in loads(w):
            copy.start()
        in_a, in_b = bufs[w][2:4]
        push(half(parts[w].at[na], 0), in_a, send.at[w, 0], got.at[w, 0], to_a)
        push(half(parts[w].at[:, nb], 1), in_b, send.at[w, 1], got.at[w, 1], to_b)

    def add(into, other):
        def one(k, carry):
            into[:, k] = (into[:, k].astype(jnp.float32) + other[:, k].astype(jnp.float32)).astype(into.dtype)
            return carry

        lax.fori_loop(0, ring, one, 0)

    def second(w):
        own_a, own_b, in_a, in_b, in_a2, in_b2 = bufs[w][:6]
        for copy in loads(w):
            copy.wait()
        await_bytes(in_a, got.at[w, 0])
        add(own_a, in_a)
        push(own_a.at[nb], in_a2, send.at[w, 2], got.at[w, 2], to_b)
        await_bytes(in_b, got.at[w, 1])
        add(own_b, in_b)
        push(own_b.at[na], in_b2, send.at[w, 3], got.at[w, 3], to_a)

    def third(w):
        own_a, own_b, _, _, in_a2, in_b2, total, in_ring = bufs[w][:8]
        await_bytes(in_a2, got.at[w, 2])
        await_bytes(in_b2, got.at[w, 3])

        def one(k, carry):
            sums = [
                own[own_at, k].astype(jnp.float32) + more[k].astype(jnp.float32)
                for own, own_at, more in ((own_a, b, in_a2), (own_b, a, in_b2))
            ]
            for which in range(2):
                half(total.at[k], which)[...] = sums[which].astype(total.dtype)
            return carry

        lax.fori_loop(0, ring, one, 0)
        for k in range(1, ring):
            at = turn("ring", k)
            push(total.at[at], in_ring.at[k - 1], ring_send.at[w, k - 1], ring_got.at[w, k - 1], {"ring": at})

    def fourth(w):
        total, in_ring, final = bufs[w][6:9]
        for k in range(1, ring):
            await_bytes(in_ring.at[k - 1], ring_got.at[w, k - 1])
        if final.shape[0] == 2:
            rows = final.shape[1]
            for core in range(2):
                at = pl.ds(core * rows, rows)
                value = total[r, at, :].astype(jnp.float32)
                for k in range(ring - 1):
                    value = value + in_ring[k, at, :].astype(jnp.float32)
                final[core] = value
            cols = final.shape[2]
            there = outs[w].at[:, pl.ds(pl.multiple_of(c * cols, cols), cols)]
            push(final.at[nc], there, send.at[w, 4], got.at[w, 4], to_core)
            pltpu.make_async_copy(final.at[c], there, load.at[w, 2]).start()
        else:
            value = total[r].astype(jnp.float32)
            for k in range(ring - 1):
                value = value + in_ring[k].astype(jnp.float32)
            outs[w][...] = value

    def finish(w):
        own_a, own_b, in_a, in_b, in_a2, in_b2, total, in_ring, final = bufs[w]
        await_bytes(in_a, send.at[w, 0])
        await_bytes(in_b, send.at[w, 1])
        await_bytes(in_a2, send.at[w, 2])
        await_bytes(in_b2, send.at[w, 3])
        for k in range(1, ring):
            await_bytes(in_ring.at[k - 1], ring_send.at[w, k - 1])
        if final.shape[0] == 2:
            await_bytes(final.at[0], send.at[w, 4])
            await_bytes(final.at[0], got.at[w, 4])
            await_bytes(final.at[0], load.at[w, 2])

    first(0)
    for step in range(count + 3):
        if step + 1 < count:
            first(step + 1)
        if step < count:
            second(step)
        if 0 <= step - 1 < count:
            third(step - 1)
        if 0 <= step - 2 < count:
            fourth(step - 2)
    for w in range(count):
        finish(w)


def collect(parts, small):
    count, ring = len(parts) + 1, lax.axis_size("ring")
    chips = lax.axis_size("ca") * lax.axis_size("cb") * ring
    square = (lax.axis_size("ca"), lax.axis_size("cb"), ring)
    views = [p.reshape(square + (p.shape[0] // chips, p.shape[1])) for p in parts]
    views = [small.reshape(square + small.shape[1:])] + views
    shapes, scratch = [], []
    for v in views:
        rows, cols = v.shape[3:]
        piece = (rows, cols // 2) if cols > 128 else (rows // 2, cols)
        big = cols > 128
        vm = lambda *shape: pltpu.VMEM(shape, v.dtype)
        scratch += [vm(2, ring, *piece)] * 4 + [vm(ring, *piece)] * 2
        scratch += [vm(ring, rows, cols), vm(ring - 1, rows, cols)]
        scratch += [pltpu.VMEM((2, rows // 2, cols) if big else (1, 8, 128), jnp.float32)]
        shapes.append(jax.ShapeDtypeStruct((rows // 2, 2 * cols) if big else (rows, cols), jnp.float32))
    dma = pltpu.SemaphoreType.DMA
    outs = pl.pallas_call(
        functools.partial(collect_kernel, count),
        out_shape=shapes,
        in_specs=[pl.BlockSpec(memory_space=pl.ANY)] * count,
        out_specs=[pl.BlockSpec(memory_space=pltpu.VMEM)] * count,
        scratch_shapes=scratch
        + [dma((count, 5)), dma((count, 5)), dma((count, ring - 1)), dma((count, ring - 1)), dma((count, 3))],
        compiler_params=pltpu.CompilerParams(collective_id=1, has_side_effects=True, vmem_limit_bytes=60 << 20),
        name="collect",
    )(*views)
    return outs[1:], outs[0]


def matmul(left, right):
    return jnp.dot(left, right, preferred_element_type=jnp.float32)


def times_transposed(left, right):
    return lax.dot_general(
        left, right, (((1,), (1,)), ((), ())), preferred_element_type=jnp.float32
    )


def transposed_times(left, right):
    return lax.dot_general(
        left, right, (((0,), (0,)), ((), ())), preferred_element_type=jnp.float32
    )


def norm_rows(values, gain):
    factor = lax.rsqrt(jnp.mean(values * values, axis=-1, keepdims=True) + EPSILON)
    return (values * factor * gain, factor)


def norm_back(grad, values, factor, gain):
    weighted = grad * gain
    inner = jnp.mean(weighted * values, axis=-1, keepdims=True)
    return (factor * weighted - values * factor**3 * inner, jnp.sum(grad * values * factor, axis=0))


def rotary_tables(positions, head_dim):
    half_dim = head_dim // 2
    frequency = jnp.exp(-math.log(ROPE_THETA) * jnp.arange(half_dim, dtype=jnp.float32) / half_dim)
    angles = positions.astype(jnp.float32)[:, None] * frequency[None, :]
    return (jnp.cos(angles), jnp.sin(angles))


def rotate(values, cosine, sine, direction):
    half_dim = values.shape[-1] // 2
    first = values[..., :half_dim]
    second = values[..., half_dim:]
    cos_rows = cosine[:, None, :]
    sin_rows = direction * sine[:, None, :]
    return jnp.concatenate(
        [first * cos_rows - second * sin_rows, second * cos_rows + first * sin_rows], axis=-1
    )


def to_heads(values):
    return lax.all_to_all(values, CTX, split_axis=1, concat_axis=0, tiled=True)


def to_rows(values):
    return lax.all_to_all(values, CTX, split_axis=0, concat_axis=1, tiled=True)


def local(
    tokens, cotangent, lengths, expert_ids, query_weight, key_weight, value_weight, out_weight,
    router_weight, first_gain, second_gain, query_gain, key_gain, gate_weight, up_weight, down_weight,
):
    token_count = tokens.shape[1]
    model_width = tokens.shape[2]
    head_dim = HD
    top_count = expert_ids.shape[2]
    experts = router_weight.shape[1]
    local_experts = gate_weight.shape[0]
    ctx_size = lax.axis_size(CTX)
    sources = lax.axis_size(EXP)
    capacity = max(2, -(-(token_count * top_count * 9) // (experts * 8)))
    score_scale = 1.0 / math.sqrt(head_dim)
    seq_len = token_count * ctx_size
    own_heads = HEADS // ctx_size

    rows_each = query_weight.shape[0]
    packed = jnp.concatenate(
        [g.reshape(-1) for g in (first_gain, second_gain, query_gain, key_gain)] + [router_weight.reshape(-1)]
    )
    small = jnp.pad(packed, (0, -packed.size % 2048)).reshape(-1, 128)
    ids_low = expert_ids[0].astype(jnp.bfloat16).reshape(-1, 128)
    gathered, ids_all = spread([query_weight, key_weight, value_weight, out_weight, small], ids_low)
    full_query, full_key, full_value, full_out = (w.reshape(model_width, -1) for w in gathered[:4])
    smalls = gathered[4].reshape(-1, small.size)
    gains = [smalls[:, i * rows_each : (i + 1) * rows_each].reshape(-1).astype(jnp.float32) for i in range(4)]
    gain_first, gain_second, gain_queries, gain_keys = gains
    full_router = smalls[:, 4 * rows_each : packed.size].reshape(model_width, experts)
    ids_all = ids_all.reshape(sources, token_count, top_count).astype(jnp.int32)
    inputs = tokens[0].astype(jnp.float32)
    length = lengths[0]
    positions = lax.axis_index(CTX) * token_count + jnp.arange(token_count, dtype=jnp.int32)
    row_valid = positions < length
    row_valid = row_valid.astype(jnp.float32)[:, None]
    key_valid = jnp.arange(seq_len, dtype=jnp.int32) < length
    grad_total_low = (cotangent[0].astype(jnp.float32) * row_valid).astype(jnp.bfloat16)
    grad_total = grad_total_low.astype(jnp.float32)

    g_all = lax.all_gather(grad_total_low, EXP, axis=0)
    gate_all, up_all, down_all = (
        lax.all_gather(gate_weight, CTX, axis=2, tiled=True),
        lax.all_gather(up_weight, CTX, axis=2, tiled=True),
        lax.all_gather(down_weight, CTX, axis=1, tiled=True),
    )

    cosine, sine = rotary_tables(positions, head_dim)
    normed_one, factor_one = norm_rows(inputs, gain_first)
    normed_one_low = normed_one.astype(jnp.bfloat16)
    query_raw = matmul(normed_one_low, full_query)
    key_raw = matmul(normed_one_low, full_key)
    value_low = matmul(normed_one_low, full_value).astype(jnp.bfloat16)
    query_normed, query_factor = norm_rows(query_raw, gain_queries)
    key_normed, key_factor = norm_rows(key_raw, gain_keys)
    by_head = lambda v: v.reshape(token_count, HEADS, head_dim)
    query_low = rotate(by_head(query_normed), cosine, sine, 1.0).astype(jnp.bfloat16)
    key_low = rotate(by_head(key_normed), cosine, sine, 1.0).astype(jnp.bfloat16)
    flat = lambda v: v.reshape(v.shape[0], -1)
    heads_of = lambda v: v.reshape(seq_len, own_heads, head_dim)
    q, k, v = (heads_of(to_heads(flat(a))) for a in (query_low, key_low, value_low))

    def scores_of():
        s = jnp.einsum("qhd,khd->hqk", q, k, preferred_element_type=jnp.float32) * score_scale
        return jnp.where(key_valid[None, None, :], s, NEG_FILL)

    scores = scores_of()
    peak = jnp.max(scores, axis=-1, keepdims=True)
    log_total = peak + jnp.log(jnp.sum(jnp.exp(scores - peak), axis=-1, keepdims=True))
    softmax_low = jnp.exp(scores - log_total).astype(jnp.bfloat16)
    attended = jnp.einsum("hqk,khd->qhd", softmax_low, v, preferred_element_type=jnp.float32)
    attended_low = to_rows(flat(attended.astype(jnp.bfloat16)))
    hidden_state = inputs + matmul(attended_low, full_out)
    normed_two, factor_two = norm_rows(hidden_state, gain_second)
    normed_two_low = normed_two.astype(jnp.bfloat16)

    n2_all = lax.all_gather(normed_two_low, EXP, axis=0)
    first_expert = lax.axis_index(EXP) * local_experts
    own_experts = first_expert + jnp.arange(local_experts, dtype=jnp.int32)
    mask = jnp.any(ids_all[:, None, :, :] == own_experts[None, :, None, None], axis=-1)
    before = (jnp.arange(token_count)[:, None] < jnp.arange(token_count)[None, :]).astype(jnp.bfloat16)
    ranks = jnp.einsum("seu,ut->set", mask.astype(jnp.bfloat16), before, preferred_element_type=jnp.float32)
    slots = jnp.arange(capacity, dtype=jnp.float32)
    hot = (mask[:, :, None, :] & (ranks[:, :, None, :] == slots[None, None, :, None])).astype(jnp.bfloat16)
    logits = matmul(n2_all.reshape(-1, model_width), full_router)
    probs = jax.nn.softmax(logits, axis=-1)
    own_probs = lax.dynamic_slice_in_dim(probs, first_expert, local_experts, 1).reshape(sources, token_count, local_experts)
    hot32 = hot.astype(jnp.float32)
    row_gate = jnp.sum(hot32 * own_probs.transpose(0, 2, 1)[:, :, None, :], axis=-1)
    x = jnp.einsum("sect,std->escd", hot, n2_all, preferred_element_type=jnp.float32).astype(jnp.bfloat16)
    g_rows = jnp.einsum("sect,std->escd", hot, g_all, preferred_element_type=jnp.float32)
    row_gate = row_gate.transpose(1, 0, 2)[..., None]
    de = (g_rows * row_gate).astype(jnp.bfloat16)
    ee = lambda eq, a, b: jnp.einsum(eq, a, b, preferred_element_type=jnp.float32)
    gp = ee("escd,edf->escf", x, gate_all)
    up = ee("escd,edf->escf", x, up_all)
    sig = jax.nn.sigmoid(gp)
    hid = (gp * sig * up).astype(jnp.bfloat16)
    eo = ee("escf,efd->escd", hid, down_all).astype(jnp.bfloat16)
    dgate_rows = jnp.sum(g_rows * eo.astype(jnp.float32), axis=-1)
    mixed_rows = (row_gate * eo.astype(jnp.float32)).astype(jnp.bfloat16)
    mixed_part = jnp.einsum("sect,escd->std", hot, mixed_rows, preferred_element_type=jnp.float32)
    mixed = lax.psum_scatter(mixed_part.astype(jnp.bfloat16).reshape(-1, model_width), EXP, scatter_dimension=0, tiled=True)
    layer_out = (row_valid * (hidden_state + mixed.astype(jnp.float32))).astype(jnp.bfloat16)

    dhid = ee("escd,efd->escf", de, down_all)
    dgp = (dhid * up * sig * (1.0 + gp * (1.0 - sig))).astype(jnp.bfloat16)
    dup = (dhid * gp * sig).astype(jnp.bfloat16)
    down_part = ee("escf,escd->efd", hid, de)
    gate_part = ee("escd,escf->edf", x, dgp)
    up_part = ee("escd,escf->edf", x, dup)
    dpair = (ee("escf,edf->escd", dgp, gate_all) + ee("escf,edf->escd", dup, up_all)).astype(jnp.bfloat16)
    rs_ctx = lambda v, a: lax.psum_scatter(v.astype(jnp.bfloat16), CTX, scatter_dimension=a, tiled=True).astype(jnp.float32)
    gate_grad, up_grad, down_grad = rs_ctx(gate_part, 2), rs_ctx(up_part, 2), rs_ctx(down_part, 1)

    dprobs_own = jnp.sum(hot32 * dgate_rows.transpose(1, 0, 2)[..., None], axis=2)
    dprobs_own = dprobs_own.transpose(0, 2, 1).reshape(-1, local_experts)
    onto = (jnp.arange(experts)[None, :] == own_experts[:, None]).astype(jnp.float32)
    dprobs = jnp.sum(dprobs_own[:, :, None] * onto[None], axis=1)
    dlogit_low = (probs * (dprobs - jnp.sum(dprobs * probs, axis=-1, keepdims=True))).astype(jnp.bfloat16)
    router_part = transposed_times(n2_all.reshape(-1, model_width), dlogit_low)
    dn2_part = jnp.einsum("sect,escd->std", hot, dpair, preferred_element_type=jnp.float32).reshape(-1, model_width)
    dn2_part = dn2_part + times_transposed(dlogit_low, full_router)
    dn2 = lax.psum_scatter(dn2_part.astype(jnp.bfloat16), EXP, scatter_dimension=0, tiled=True).astype(jnp.float32)

    dh_norm, gain_second_part = norm_back(dn2, hidden_state, factor_two, gain_second)
    grad_hidden = grad_total + dh_norm
    dh_low = grad_hidden.astype(jnp.bfloat16)
    out_part = transposed_times(attended_low, dh_low)
    d_att = heads_of(to_heads(times_transposed(dh_low, full_out).astype(jnp.bfloat16)))
    soft = jnp.exp(scores_of() - log_total)
    dp = jnp.einsum("qhd,khd->hqk", d_att, v, preferred_element_type=jnp.float32)
    dv = jnp.einsum("hqk,qhd->khd", soft.astype(jnp.bfloat16), d_att, preferred_element_type=jnp.float32)
    inner = jnp.sum(dp * soft, axis=-1, keepdims=True)
    ds = (soft * (dp - inner)).astype(jnp.bfloat16)
    dq = jnp.einsum("hqk,khd->qhd", ds, k, preferred_element_type=jnp.float32) * score_scale
    dk = jnp.einsum("hqk,qhd->khd", ds, q, preferred_element_type=jnp.float32) * score_scale
    dq, dk, dv = (to_rows(flat(a.astype(jnp.bfloat16))) for a in (dq, dk, dv))
    unrotate = lambda a: rotate(by_head(a.astype(jnp.float32)), cosine, sine, -1.0).reshape(token_count, model_width)
    dk_raw, gain_keys_part = norm_back(unrotate(dk), key_raw, key_factor, gain_keys)
    dq_raw, gain_queries_part = norm_back(unrotate(dq), query_raw, query_factor, gain_queries)
    dk_low, dq_low, dv_low = dk_raw.astype(jnp.bfloat16), dq_raw.astype(jnp.bfloat16), dv
    dn1 = times_transposed(dq_low, full_query) + times_transposed(dk_low, full_key)
    dn1 = dn1 + times_transposed(dv_low, full_value)
    input_norm, gain_first_part = norm_back(dn1, inputs, factor_one, gain_first)
    input_grad = (grad_hidden + input_norm).astype(jnp.bfloat16)
    core = lax.axis_index("core")
    swap = lambda v: lax.ppermute(v, "core", [(0, 1), (1, 0)])

    def columns_of_core(v):
        v = v.reshape(token_count, 2, -1)
        return jnp.concatenate([lax.dynamic_index_in_dim(v, core, 1, False), swap(lax.dynamic_index_in_dim(v, 1 - core, 1, False))], axis=0)

    both = lambda v: jnp.concatenate([v, swap(v)], axis=0)
    n1_both, att_both = both(normed_one_low), both(attended_low)
    parts = [
        transposed_times(l, columns_of_core(r)).astype(jnp.bfloat16)
        for l, r in ((att_both, dh_low), (n1_both, dq_low), (n1_both, dk_low), (n1_both, dv_low))
    ]
    split = lambda v: v.reshape(ctx_size * sources // 2, 2, -1)
    small_parts = jnp.concatenate(
        [split(v) for v in (gain_first_part, gain_second_part, gain_queries_part, gain_keys_part, router_part)], axis=2
    )
    small_parts = jnp.pad(small_parts, ((0, 0), (0, 0), (0, -small_parts.shape[2] % 2048)))
    small_parts = lax.dynamic_index_in_dim(small_parts, core, 1, False) + swap(lax.dynamic_index_in_dim(small_parts, 1 - core, 1, False))
    weight_grads, small_grads = collect(parts, small_parts.reshape(ctx_size * sources // 2, -1, 128))
    weight_grads = list(weight_grads[1:]) + [weight_grads[0]]
    small_grads = small_grads.reshape(-1)
    gain_grads = [small_grads[i * rows_each : (i + 1) * rows_each] for i in range(4)]
    router_grad = small_grads[4 * rows_each : packed.size].reshape(rows_each, experts)
    return (layer_out[None], input_grad[None], *weight_grads, router_grad, *gain_grads, gate_grad, up_grad, down_grad)


def solution(mesh):
    ctx, exp = mesh.devices.shape
    fine = Mesh(mesh.devices.reshape(2, ctx // 2, exp // 2, 2), ("ca", "cb", "ring", "core"))
    rows = P(EXP, CTX, None)
    flat2, flat1 = P(ALL, None), P(ALL)
    placed = (rows, rows, P(EXP), rows) + (flat2,) * 5 + (flat1,) * 4 + (P(EXP, None, CTX),) * 2 + (P(EXP, CTX, None),)
    outs = (rows, rows) + (flat2,) * 5 + (flat1,) * 4 + (P(EXP, None, CTX),) * 2 + (P(EXP, CTX, None),)
    return jax.shard_map(local, mesh=fine, in_specs=placed, out_specs=outs, check_vma=False)
```

time: 2740 us -> 1580 us (0.58)
  waiting for transfers between devices: 1850 us -> 608 us
  Pallas kernels: 0 us -> 392 us
  blocking collectives: 315 us -> 29.1 us
  local copies, waits for them, and re-layouts: 127 us -> 84.7 us
  matrix products: 295 us -> 337 us
  other arithmetic: 104 us -> 72.6 us
    reduce_scatter x9 -> x5, waiting for transfers between devices: 948 us -> 270 us  [the longest x3 159 us: local(): lax.psum_scatter(v.astype(jnp.bfloat16), CTX, scatter_dimension=a, tiled=...]
    pallas_call x0 -> x2, Pallas kernels: none -> 392 us  [the longest x1 212 us: spread(): pl.pallas_call(functools.partial(spread_kernel, count), out_shape=[jax.Sh...]
    all_to_all x4 -> x7, waiting for transfers between devices: 442 us -> 49.6 us  [the longest x4 26.7 us: to_rows(): return lax.all_to_all(values, CTX, split_axis=0, concat_axis=1, tiled=True)]
    all_gather x1 -> x0, blocking collectives: 232 us -> none  [local(): lax.all_gather(router_weight, ('context', 'expert'), axis=0, tiled=True)]
    all_gather x9 -> x5, waiting for transfers between devices: 372 us -> 286 us  [the longest x1 75.5 us: local(): lax.all_gather(gate_weight, CTX, axis=2, tiled=True)]
    unnamed x20 -> x10, waiting for transfers between devices: 84.6 us -> 1.85 us
    unnamed x2 -> x0, blocking collectives: 82.6 us -> none
    gather x2 -> x0, local copies, waits for them, and re-layouts: 43 us -> none  [the longest x1 21.8 us: local(): returned[slots].reshape(token_count, top_count, model_width)]
  transfers between devices with their start and end apart: 23 -> 24, of which waited for: 18 -> 13; matrix products, arithmetic and copies ran while one was open for 15% -> 23% of each run, Pallas kernels for 0% -> 13%
where the time goes in v1:
time: 1580 us; the launch traced here: 1570 us
  waiting for transfers between devices  608 us (38%)
  Pallas kernels  392 us (25%)
  matrix products  337 us (21%)
  local copies, waits for them, and re-layouts  84.7 us (5%)
  other arithmetic  72.6 us (5%)
  starting transfers between devices  32.9 us (2%)
  blocking collectives  29.1 us (2%)
  between operations  16.4 us (1%)
    pallas_call x1, Pallas kernels, spread(): pl.pallas_call(functools.partial(spread_kernel, count), out_shape=[jax.Sh...  212 us
    pallas_call x1, Pallas kernels, collect(): pl.pallas_call(functools.partial(collect_kernel, count), out_shape=shapes...  180 us
    reduce_scatter x3, waiting for transfers between devices, local(): lax.psum_scatter(v.astype(jnp.bfloat16), CTX, scatter_dimension=a, tiled=...  159 us
    dot_general x8, matrix products, local(): jnp.einsum(eq, a, b, preferred_element_type=jnp.float32)  154 us
    reduce_scatter x1, waiting for transfers between devices, local(): lax.psum_scatter(mixed_part.astype(jnp.bfloat16).reshape(-1, model_width)...  88.4 us
    all_gather x1, waiting for transfers between devices, local(): lax.all_gather(gate_weight, CTX, axis=2, tiled=True)  75.5 us
    all_gather x1, waiting for transfers between devices, local(): lax.all_gather(up_weight, CTX, axis=2, tiled=True)  72.2 us
    all_gather x1, waiting for transfers between devices, local(): n2_all = lax.all_gather(normed_two_low, EXP, axis=0)  69.4 us
  transfers between devices with their start and end apart: 24, of which 13 were waited for; matrix products, arithmetic and copies ran while one was open for 23% of the time, Pallas kernels for 13%

profile of v1, /device:TPU:9, one launch (start us, length us, event | category | flops | bytes accessed | tf_op | source)
XLA Modules:
  0.0 1573.0 jit_solution(6144620116542386484)
XLA Ops:
  16.8 212.4 %spread.1 = (bf16[2,2,4,2,64,2048]{5,4,3,2,1,0:T(8,128)(2,1)}, bf16[2,2,4,2,64,2048]{5,4,3,2,1,0:T(8,128)(2,1)}, bf16[2,2,4,2,64,2048]{5,4,3,2,1,0:T(8,128)(2,1)...) custom-call(bf16[64,2048]{1,0:T(8,128)(2,1)} %refs_0_.1, ...), custom_call_target="tpu_custom_call" | custom-call | tf_op jit(solution)/shard_map/spread/pallas_call | solution.py:164
  231.2 5.9 multiply_reduce_fusion.7
  242.0 5.9 multiply_reduce_fusion.6
  265.1 12.4 all-to-all-done.2
  281.0 5.8 convolution_convert_fusion.5
  287.9 6.2 all-to-all-done.1
  294.1 4.4 all-to-all-start
  307.3 4.4 all-to-all-done
  339.9 12.7 all-to-all-done.3
  352.6 6.2 multiply_reduce_fusion.5
  365.0 12.1 fusion.17
  377.1 69.4 %all-gather.15.cloned.1.call-done = bf16[2048,2048]{1,0:T(8,128)(2,1)} async-done(((bf16[256,2048]{1,0:T(8,128)(2,1)}), bf16[2048,2048]{1,0:T(8,128)(2,1)}) %all-gather.15.cloned.1.call-update) | async-done | bytes 8388624 | tf_op jit(solution)/shard_map/all_gather | solution.py:461
  446.5 5.7 fusion.121
  452.3 8.8 convert_bitcast_fusion
  461.1 75.5 %all-gather.7.cloned.1.call-done = bf16[2,2048,1024]{2,1,0:T(8,128)(2,1)} async-done(((bf16[2,2048,256]{2,1,0:T(8,128)(2,1)}), bf16[2,2048,1024]{2,1,0:T(8,128)(2,1)}) %all-gather.7.cloned.1.call-update) | async-done | bytes 8388624 | tf_op jit(solution)/shard_map/all_gather | solution.py:427
  536.6 17.0 %fusion.11 = f32[2,8,144,1024]{3,2,1,0:T(8,128)} fusion(bf16[2,2048,1024]{2,1,0:T(8,128)(2,1)} %all-gather.7.cloned.1.call-done, bf16[2,8,144,2048]{3,2,0,1:T(8,128)(2,1)} %convert_bitcast_fusion), kind=kOutput, calls=%fused_computation.30 | convolution fusion | flops 9663676416 | bytes 27262976 | tf_op jit(solution)/shard_map/escd,edf->escf/dot_general | solution.py:478
  553.6 72.2 %all-gather.9.cloned.1.call-done = bf16[2,2048,1024]{2,1,0:T(8,128)(2,1)} async-done(((bf16[2,2048,256]{2,1,0:T(8,128)(2,1)}), bf16[2,2048,1024]{2,1,0:T(8,128)(2,1)}) %all-gather.9.cloned.1.call-update) | async-done | bytes 8388624 | tf_op jit(solution)/shard_map/all_gather | solution.py:428
  625.8 20.0 %multiply_convert_fusion.3 = (bf16[2,8,144,1024]{3,2,1,0:T(8,128)(2,1)}, f32[2,8,144,1024]{3,2,1,0:T(8,128)}) fusion(f32[2,8,144,1024]{3,2,1,0:T(8,128)} %fusion.11, bf16[2,2048,1024]{2,1,0:T(8,128)(2,1)} %all-gather.9.cloned.1.call-done, bf16[2,8,144,2048]{3,2,0,1:T(8,128)(2,1)} %convert_bitcast_fusion), kind=kOutput, calls=%fused_computation.24 | convolution fusion | flops 9677832192 | bytes 41418752 | tf_op jit(solution)/shard_map/escd,edf->escf/dot_general | solution.py:478
  645.8 69.3 %all-gather.11.cloned.1.call-done = bf16[2,1024,2048]{2,1,0:T(8,128)(2,1)} async-done(((bf16[2,256,2048]{2,1,0:T(8,128)(2,1)}), bf16[2,1024,2048]{2,1,0:T(8,128)(2,1)}) %all-gather.11.cloned.1.call-update) | async-done | bytes 8388624 | tf_op jit(solution)/shard_map/all_gather | solution.py:429
  715.1 19.4 %fusion.1 = (f32[2,8,144]{2,1,0:T(8,128)S(1)}, bf16[2,8,144,2048]{3,2,1,0:T(8,128)(2,1)}) fusion(f32[8,2048,2,144]{1,3,0,2:T(8,128)} %fusion.17, bf16[2,8,144,1024]{3,2,1,0:T(8,128)(2,1)} %get-tuple-element.172, bf16[2,1024,2048]{2,1,0:T(8,128)(2,1)} %all-gather.11.cloned.1.call-done), kind=kOutput, calls=%fused_computation.3 | convolution fusion | flops 9682548736 | bytes 41427968 | tf_op jit(solution)/shard_map/escf,efd->escd/dot_general | solution.py:478
  736.2 24.2 %multiply_convert_fusion.2 = (bf16[2,8,144,1024]{3,2,1,0:T(8,128)(2,1)}, bf16[2,8,144,1024]{3,2,1,0:T(8,128)(2,1)}) fusion(f32[2,8,144,1024]{3,2,1,0:T(8,128)} %fusion.11, f32[2,8,144,1024]{3,2,1,0:T(8,128)} %get-tuple-element.173, bf16[2,1024,2048]{2,1,0:T(8,128)(2,1)} %all-gather.11.cloned.1.call-done, f32[8,2048,2,144]{1,3,0,2:T(8,128)} %fusion.17, ...), kind=kOutput, calls=%fused_computation.23 | convolution fusion | flops 9703784448 | bytes 55583744 | tf_op jit(solution)/shard_map/escd,efd->escf/dot_general | solution.py:478
  760.4 17.5 %fusion.19 = f32[2,8,144,2048]{3,2,0,1:T(8,128)} fusion(bf16[2,2048,1024]{2,1,0:T(8,128)(2,1)} %all-gather.9.cloned.1.call-done, bf16[2,8,144,1024]{3,2,1,0:T(8,128)(2,1)} %get-tuple-element.119), kind=kOutput, calls=%fused_computation.38 | convolution fusion | flops 9663676416 | bytes 31981568 | tf_op jit(solution)/shard_map/escf,edf->escd/dot_general | solution.py:478
  777.9 25.2 %fusion.5 = f32[8,256,2048,1]{2,1,3,0:T(8,128)} fusion(f32[2,8,144,2048]{3,2,0,1:T(8,128)} %fusion.19, bf16[2,2048,1024]{2,1,0:T(8,128)(2,1)} %all-gather.7.cloned.1.call-done, bf16[2,8,144,1024]{3,2,1,0:T(8,128)(2,1)} %get-tuple-element.118, f32[8,2,256]{2,1,0:T(2,128)S(1)} %copy.204, pred[8,2,256]{2,1,0:T(4,128)(4,1)S(1)} %compare_reduce_fusion), kind=kOutput, calls=%fused_computation.19 | convolution fusion | flops 12090212352 | bytes 48779264 | tf_op jit(solution)/shard_map/sect,escd->std/dot_general | solution.py:506
  803.1 11.5 fusion.3
  814.7 9.3 bitcast_convert_fusion.3
  824.1 21.1 %bitcast_convert_fusion = bf16[2,1024,2048]{2,1,0:T(8,128)(2,1)} fusion(bf16[2,8,144,1024]{3,2,1,0:T(8,128)(2,1)} %get-tuple-element.172, f32[8,2048,2,144]{1,3,0,2:T(8,128)} %fusion.17, f32[2,8,144]{2,1,0:T(8,128)S(1)} %copy.205), kind=kOutput, calls=%fused_computation.9 | convolution fusion | flops 9677307904 | bytes 31990784 | tf_op jit(solution)/shard_map/escf,escd->efd/dot_general | solution.py:478
  845.3 17.3 %bitcast_convert_fusion.2 = bf16[2,2048,1024]{2,1,0:T(8,128)(2,1)} fusion(bf16[2,8,144,2048]{3,2,0,1:T(8,128)(2,1)} %convert_bitcast_fusion, bf16[2,8,144,1024]{3,2,1,0:T(8,128)(2,1)} %get-tuple-element.118), kind=kOutput, calls=%fused_computation.11 | convolution fusion | flops 9667870720 | bytes 22544384 | tf_op jit(solution)/shard_map/escd,escf->edf/dot_general | solution.py:478
  862.7 17.2 %bitcast_convert_fusion.1 = bf16[2,2048,1024]{2,1,0:T(8,128)(2,1)} fusion(bf16[2,8,144,2048]{3,2,0,1:T(8,128)(2,1)} %convert_bitcast_fusion, bf16[2,8,144,1024]{3,2,1,0:T(8,128)(2,1)} %get-tuple-element.119), kind=kOutput, calls=%fused_computation.10 | convolution fusion | flops 9667870720 | bytes 22544384 | tf_op jit(solution)/shard_map/escd,escf->edf/dot_general | solution.py:478
  880.0 23.0 %reduce-scatter.8.cloned.1.call-done = bf16[256,2048]{1,0:T(8,128)(2,1)} async-done(((bf16[2048,2048]{1,0:T(8,128)(2,1)}), bf16[256,2048]{1,0:T(8,128)(2,1)}) %reduce-scatter.8.cloned.1.call-update) | async-done | bytes 1048592 | tf_op jit(solution)/shard_map/reduce_scatter | solution.py:508
  904.8 88.4 %reduce-scatter.6.cloned.1.call-done = bf16[256,2048]{1,0:T(8,128)(2,1)} async-done(((bf16[2048,2048]{1,0:T(8,128)(2,1)}), bf16[256,2048]{1,0:T(8,128)(2,1)}) %reduce-scatter.6.cloned.1.call-update) | async-done | bytes 1048592 | tf_op jit(solution)/shard_map/reduce_scatter | solution.py:487
  997.5 6.1 convolution_convert_fusion.4
  1003.7 29.1 %all_to_all.122 = bf16[256,4,512]{2,0,1:T(8,128)(2,1)S(1)} all-to-all(bf16[256,4,512]{2,0,1:T(8,128)(2,1)S(1)} %bitcast.296), channel_id=1, replica_groups=mesh['ca'=2,'cb'=2,'ring'=4,'core'=2] {'ca','cb'}, dimensions={1} | all-to-all | bytes 2097152 | tf_op jit(solution)/shard_map/all_to_all | solution.py:379
  1033.8 12.3 multiply_reduce_fusion
  1046.2 13.0 multiply_convert_fusion
  1074.8 7.5 fusion.74
  1085.4 14.0 all-to-all-done.5
  1099.3 4.4 all-to-all-start.6
  1103.8 5.9 fusion.123
  1121.7 73.1 %reduce-scatter.10.cloned.1.call-done = bf16[2,2048,256]{2,1,0:T(8,128)(2,1)} async-done(((bf16[2,2048,1024]{2,1,0:T(8,128)(2,1)}), bf16[2,2048,256]{2,1,0:T(8,128)(2,1)}) %reduce-scatter.10.cloned.1.call-update) | async-done | bytes 2097168 | tf_op jit(solution)/shard_map/reduce_scatter | solution.py:497
  1198.8 85.4 %reduce-scatter.12.cloned.1.call-done = bf16[2,2048,256]{2,1,0:T(8,128)(2,1)} async-done(((bf16[2,2048,1024]{2,1,0:T(8,128)(2,1)}), bf16[2,2048,256]{2,1,0:T(8,128)(2,1)}) %reduce-scatter.12.cloned.1.call-update) | async-done | bytes 2097168 | tf_op jit(solution)/shard_map/reduce_scatter | solution.py:497
  1288.1 6.3 fusion.72
  1316.9 6.6 fusion.122
  1327.9 7.3 fusion.60
  1338.4 5.8 convolution_convert_fusion.3
  1357.2 6.1 convolution_convert_fusion
  1363.3 6.1 convolution_convert_fusion.1
  1369.4 6.1 convolution_convert_fusion.2
  1375.5 180.1 %collect.1 = (f32[16,128]{1,0:T(8,128)}, f32[64,2048]{1,0:T(8,128)}, f32[64,2048]{1,0:T(8,128)}, f32[64,2048]{1,0:T(8,128)}, f32[64,2048]{1,0:T(8,128)}) custom-call(f32[2,2,4,16,128]{4,3,2,1,0:T(8,128)} %bitcast.304, bf16[2,2,4,128,1024]{4,3,2,1,0:T(8,128)(2,1)} %bitcast.298, bf16[2,2,4,128,1024]{4,3,2,1,0:T(8,128)(2,1)} %bitcast.301, ...), custom_call_target="tpu_custom_call" | custom-call | tf_op jit(solution)/shard_map/collect/pallas_call | solution.py:320
  (303 shorter events, 181.2 us)
Async XLA Ops:
  7.2 223.1 %copy-start.15 = (bf16[1,256,2048]{2,1,0:T(8,128)(2,1)S(1)}, bf16[1,256,2048]{2,1,0:T(8,128)(2,1)}, u32[]{:S(2)}) copy-start(bf16[1,256,2048]{2,1,0:T(8,128)(2,1)} %param.16) | copy-start | bytes 3145732
  7.2 357.8 %all-gather.13.cloned.1.call-start = ((), (), s32[]{:S(2)}) async-start(), calls=%async_computation.17 | async-start | bytes 9437184 | tf_op jit(solution)/shard_map/all_gather | solution.py:425
  230.2 50.8 %copy-start.46 = (f32[2048]{0:T(1024)}, f32[2048]{0:T(1024)S(1)}, u32[]{:S(2)}) copy-start(f32[2048]{0:T(1024)S(1)} %reshape.529) | copy-start | bytes 24580
  231.2 49.8 %copy-start.58 = (f32[256]{0:T(256)}, f32[256]{0:T(256)S(1)}, u32[]{:S(2)}) copy-start(f32[256]{0:T(256)S(1)} %get-tuple-element.157) | copy-start | bytes 3076
  248.5 9.2 copy-start.53
  258.8 18.7 %all-to-all-start.2 = ((bf16[256,4,512]{0,2,1:T(8,128)(2,1)}), bf16[256,4,512]{0,2,1:T(8,128)(2,1)S(1)}, u32[]{:S(2)}, u32[]{:S(2)}) async-start(bf16[256,4,512]{0,2,1:T(8,128)(2,1)} %bitcast.10), calls=%async_computation.2 | async-start | bytes 2097152 | tf_op jit(solution)/shard_map/all_to_all | solution.py:379
  277.5 16.6 %all-to-all-start.1 = ((bf16[256,4,512]{0,2,1:T(8,128)(2,1)}), bf16[256,4,512]{0,2,1:T(8,128)(2,1)S(1)}, u32[]{:S(2)}, u32[]{:S(2)}) async-start(bf16[256,4,512]{0,2,1:T(8,128)(2,1)} %bitcast.295), calls=%async_computation.1 | async-start | bytes 2097152 | tf_op jit(solution)/shard_map/all_to_all | solution.py:379
  294.1 17.6 %all-to-all-start = ((bf16[256,4,512]{2,0,1:T(8,128)(2,1)}), bf16[256,4,512]{2,0,1:T(8,128)(2,1)}, u32[]{:S(2)}, u32[]{:S(2)}) async-start(bf16[256,4,512]{2,0,1:T(8,128)(2,1)} %bitcast.294), calls=%async_computation | async-start | bytes 2097152 | tf_op jit(solution)/shard_map/all_to_all | solution.py:379
  298.5 25.2 %copy-start.44 = (pred[1024]{0:T(1024)(128)(4,1)}, pred[1024]{0:T(1024)(128)(4,1)S(1)}, u32[]{:S(2)}) copy-start(pred[1024]{0:T(1024)(128)(4,1)S(1)} %iota_compare_fusion.2) | copy-start | bytes 3076
  302.1 17.5 %copy-start.13 = (bf16[1024,4,128]{0,2,1:T(8,128)(2,1)}, bf16[1024,4,128]{0,2,1:T(8,128)(2,1)S(1)}, u32[]{:S(2)}) copy-start(bf16[1024,4,128]{0,2,1:T(8,128)(2,1)S(1)} %reshape.552) | copy-start | bytes 3145732
  307.3 12.3 copy-start.11
  336.0 16.6 %all-to-all-start.3 = ((bf16[4,256,512]{1,2,0:T(8,128)(2,1)}), bf16[4,256,512]{1,2,0:T(8,128)(2,1)S(1)}, u32[]{:S(2)}, u32[]{:S(2)}) async-start(bf16[4,256,512]{1,2,0:T(8,128)(2,1)} %copy.201), calls=%async_computation.3 | async-start | bytes 2097152 | tf_op jit(solution)/shard_map/all_to_all | solution.py:383
  339.5 107.0 %all-gather.15.cloned.1.call-start = ((), (), s32[]{:S(2)}) async-start(), calls=%async_computation.22 | async-start | bytes 9437184 | tf_op jit(solution)/shard_map/all_gather | solution.py:461
  339.9 19.6 %copy-start.42 = (f32[2048]{0:T(1024)}, f32[2048]{0:T(1024)S(1)}, u32[]{:S(2)}) copy-start(f32[2048]{0:T(1024)S(1)} %reshape.533) | copy-start | bytes 24580
  361.4 175.3 %all-gather.7.cloned.1.call-start = ((), (), s32[]{:S(2)}) async-start(), calls=%async_computation.13 | async-start | bytes 10485760 | tf_op jit(solution)/shard_map/all_gather | solution.py:427
  362.1 263.7 %all-gather.9.cloned.1.call-start = ((), (), s32[]{:S(2)}) async-start(), calls=%async_computation.14 | async-start | bytes 10485760 | tf_op jit(solution)/shard_map/all_gather | solution.py:428
  362.7 352.5 %all-gather.11.cloned.1.call-start = ((), (), s32[]{:S(2)}) async-start(), calls=%async_computation.15 | async-start | bytes 10485760 | tf_op jit(solution)/shard_map/all_gather | solution.py:429
  363.3 539.7 %reduce-scatter.8.cloned.1.call-start = ((), (), s32[]{:S(2)}) async-start(), calls=%async_computation.18 | async-start | bytes 9437184 | tf_op jit(solution)/shard_map/reduce_scatter | solution.py:508
  363.7 82.8 %copy-start.22 = (bf16[2048,16]{1,0:T(8,128)(2,1)}, bf16[2048,16]{1,0:T(8,128)(2,1)S(1)}, u32[]{:S(2)}) copy-start(bf16[2048,16]{1,0:T(8,128)(2,1)S(1)} %reshape.506) | copy-start | bytes 196612
  736.1 66.9 %copy-start.34 = (bf16[2048,16]{0,1:T(8,128)(2,1)}, bf16[2048,16]{0,1:T(8,128)(2,1)S(1)}, u32[]{:S(2)}) copy-start(bf16[2048,16]{0,1:T(8,128)(2,1)S(1)} %multiply_convert_fusion.8) | copy-start | bytes 196612
  777.9 25.2 %copy-start.23 = (bf16[2048,16]{1,0:T(8,128)(2,1)S(1)}, bf16[2048,16]{1,0:T(8,128)(2,1)}, u32[]{:S(2)}) copy-start(bf16[2048,16]{1,0:T(8,128)(2,1)} %copy-done.22) | copy-start | bytes 196612
  814.7 178.6 %reduce-scatter.6.cloned.1.call-start = ((), (), s32[]{:S(2)}) async-start(), calls=%async_computation.16 | async-start | bytes 9437184 | tf_op jit(solution)/shard_map/reduce_scatter | solution.py:487
  824.1 293.5 %reduce-scatter.14.cloned.1.call-start = ((), (), s32[]{:S(2)}) async-start(), calls=%async_computation.21 | async-start | bytes 10485760 | tf_op jit(solution)/shard_map/reduce_scatter | solution.py:497
  845.3 349.5 %reduce-scatter.10.cloned.1.call-start = ((), (), s32[]{:S(2)}) async-start(), calls=%async_computation.19 | async-start | bytes 10485760 | tf_op jit(solution)/shard_map/reduce_scatter | solution.py:497
  862.7 421.4 %reduce-scatter.12.cloned.1.call-start = ((), (), s32[]{:S(2)}) async-start(), calls=%async_computation.20 | async-start | bytes 10485760 | tf_op jit(solution)/shard_map/reduce_scatter | solution.py:497
  879.9 23.1 %copy-start.4 = (f32[256,2048]{1,0:T(8,128)S(1)}, f32[256,2048]{1,0:T(8,128)}, u32[]{:S(2)}) copy-start(f32[256,2048]{1,0:T(8,128)} %copy-done.3) | copy-start | bytes 6291460
  879.9 23.1 %copy-start.43 = (f32[2048]{0:T(1024)S(1)}, f32[2048]{0:T(1024)}, u32[]{:S(2)}) copy-start(f32[2048]{0:T(1024)} %copy-done.42) | copy-start | bytes 24580
  879.9 23.1 %copy-start.50 = (f32[256]{0:T(256)S(1)}, f32[256]{0:T(256)}, u32[]{:S(2)}) copy-start(f32[256]{0:T(256)} %copy-done.49) | copy-start | bytes 3076
  879.9 113.3 %copy-start.25 = (bf16[1,256,2048]{2,1,0:T(8,128)(2,1)S(1)}, bf16[1,256,2048]{2,1,0:T(8,128)(2,1)}, u32[]{:S(2)}) copy-start(bf16[1,256,2048]{2,1,0:T(8,128)(2,1)} %param.17) | copy-start | bytes 3145732
  879.9 113.3 %copy-start.56 = (f32[256]{0:T(256)S(1)}, f32[256]{0:T(256)}, u32[]{:S(2)}) copy-start(f32[256]{0:T(256)} %copy-done.55) | copy-start | bytes 3076
  879.9 113.3 %copy-start.60 = (f32[256]{0:T(256)S(1)}, f32[256]{0:T(256)}, u32[]{:S(2)}) copy-start(f32[256]{0:T(256)} %get-tuple-element.162) | copy-start | bytes 3076
  1003.6 30.2 %copy-start.18 = (bf16[1024,4,128]{0,2,1:T(8,128)(2,1)S(1)}, bf16[1024,4,128]{0,2,1:T(8,128)(2,1)}, u32[]{:S(2)}) copy-start(bf16[1024,4,128]{0,2,1:T(8,128)(2,1)} %copy.254) | copy-start | bytes 3145732
  1003.6 30.2 %copy-start.37 = (f32[4,1024]{1,0:T(4,128)S(1)}, f32[4,1024]{1,0:T(4,128)}, u32[]{:S(2)}) copy-start(f32[4,1024]{1,0:T(4,128)} %copy-done.36) | copy-start | bytes 49156
  1003.6 30.2 %copy-start.45 = (pred[1024]{0:T(1024)(128)(4,1)S(1)}, pred[1024]{0:T(1024)(128)(4,1)}, u32[]{:S(2)}) copy-start(pred[1024]{0:T(1024)(128)(4,1)} %copy-done.44) | copy-start | bytes 3076
  1046.2 16.2 %copy-start.14 = (bf16[1024,4,128]{0,2,1:T(8,128)(2,1)S(1)}, bf16[1024,4,128]{0,2,1:T(8,128)(2,1)}, u32[]{:S(2)}) copy-start(bf16[1024,4,128]{0,2,1:T(8,128)(2,1)} %copy-done.13) | copy-start | bytes 3145732
  1064.7 9.6 copy-start.21
  1064.7 10.2 copy-start.12
  1070.0 29.4 %all-to-all-start.5 = ((bf16[4,256,512]{1,2,0:T(8,128)(2,1)}), bf16[4,256,512]{1,2,0:T(8,128)(2,1)}, u32[]{:S(2)}, u32[]{:S(2)}) async-start(bf16[4,256,512]{1,2,0:T(8,128)(2,1)} %copy.218), calls=%async_computation.7 | async-start | bytes 2097152 | tf_op jit(solution)/shard_map/all_to_all | solution.py:383
  1074.3 264.1 %collective-permute-start.1 = (bf16[256,2048]{0,1:T(8,128)(2,1)S(1)}, bf16[256,2048]{0,1:T(8,128)(2,1)}, u32[]{:S(2)}, u32[]{:S(2)}) collective-permute-start(bf16[256,2048]{0,1:T(8,128)(2,1)S(1)} %bitcast.290), channel_id=1, source_target_pairs={{0,1},{1,0},{2,3},{3,2},{4,5},{5,4},{6,7},{7,6},{8,9},{9,8},{10,11... | collective-permute-start | bytes 3145736 | tf_op jit(solution)/shard_map/ppermute | solution.py:532
  1082.4 21.4 %copy-start.35 = (bf16[2048,16]{0,1:T(8,128)(2,1)S(1)}, bf16[2048,16]{0,1:T(8,128)(2,1)}, u32[]{:S(2)}) copy-start(bf16[2048,16]{0,1:T(8,128)(2,1)} %copy-done.34) | copy-start | bytes 196612
  1099.3 198.4 %all-to-all-start.6 = ((bf16[4,256,512]{1,2,0:T(8,128)(2,1)}), bf16[4,256,512]{1,2,0:T(8,128)(2,1)}, u32[]{:S(2)}, u32[]{:S(2)}) async-start(bf16[4,256,512]{1,2,0:T(8,128)(2,1)} %copy.222), calls=%async_computation.8 | async-start | bytes 2097152 | tf_op jit(solution)/shard_map/all_to_all | solution.py:383
  1115.2 223.2 %collective-permute-start.2 = (bf16[256,1024]{1,0:T(8,128)(2,1)}, bf16[256,1024]{1,0:T(8,128)(2,1)}, u32[]{:S(2)}, u32[]{:S(2)}) collective-permute-start(bf16[256,1024]{1,0:T(8,128)(2,1)} %bitcast.273), channel_id=1, source_target_pairs={{0,1},{1,0},{2,3},{3,2},{4,5},{5,4},{6,7},{7,6},{8,9},{9,8},{10,11... | collective-permute-start | bytes 1572872 | tf_op jit(solution)/shard_map/ppermute | solution.py:532
  1297.8 30.1 %all-to-all-start.7 = ((bf16[4,256,512]{1,2,0:T(8,128)(2,1)}), bf16[4,256,512]{1,2,0:T(8,128)(2,1)}, u32[]{:S(2)}, u32[]{:S(2)}) async-start(bf16[4,256,512]{1,2,0:T(8,128)(2,1)} %copy.226), calls=%async_computation.9 | async-start | bytes 2097152 | tf_op jit(solution)/shard_map/all_to_all | solution.py:383
  1337.6 19.5 %collective-permute-start.3 = (bf16[256,2048]{1,0:T(8,128)(2,1)}, bf16[256,2048]{1,0:T(8,128)(2,1)}, u32[]{:S(2)}, u32[]{:S(2)}) collective-permute-start(bf16[256,2048]{1,0:T(8,128)(2,1)} %get-tuple-element.129), channel_id=1, source_target_pairs={{0,1},{1,0},{2,3},{3,2},{4,5},{5,4},{6,7},{7,6},{8,9},{9,8},{10,11... | collective-permute-start | bytes 3145736 | tf_op jit(solution)/shard_map/ppermute | solution.py:532
  1349.2 8.0 collective-permute-start.6
  1351.8 11.5 collective-permute-start.5
  1353.3 3.2 collective-permute-start
  1355.7 13.7 collective-permute-start.4
  (41 other events, 202.3 us)
Sparse Core Ops, SparseCore 0:
  11.1 156.8 all-gather.12
  361.5 84.9 all-gather.14
  448.3 88.2 all-gather.6
  538.3 87.4 all-gather.8
  627.5 87.6 all-gather.10
  814.8 88.1 reduce-scatter.7
  905.3 87.9 reduce-scatter.5
  996.3 108.6 reduce-scatter.13
  1108.4 86.3 reduce-scatter.9
  1197.7 86.3 reduce-scatter.11

commit v2 on v1

--- a/solution.py
+++ b/solution.py
@@ -37,6 +37,12 @@
     for peer in peers:
         pl.semaphore_signal(barrier, inc=1, device_id=peer, device_id_type=MESH)
     pl.semaphore_wait(barrier, len(peers))
+
+
+def push(src, dst, ssem, rsem, to):
+    pltpu.make_async_remote_copy(
+        src_ref=src, dst_ref=dst, send_sem=ssem, recv_sem=rsem, device_id=to, device_id_type=MESH
+    ).start()
 
 
 RING, SIDE_B, SIDE_A, FIRST, SECOND, CORE_OWN, CORE_B, CORE_A, CORE_FIRST, CORE_SECOND = range(10)
@@ -50,11 +56,6 @@
     na, nb, nc = turn("ca", 1), turn("cb", 1), turn("core", 1)
     to_a, to_b, to_core = {"ca": na}, {"cb": nb}, {"core": nc}
     greet([to_a, to_b, to_core] + [{"ring": turn("ring", k)} for k in range(1, ring)])
-
-    def push(src, dst, ssem, rsem, to):
-        pltpu.make_async_remote_copy(
-            src_ref=src, dst_ref=dst, send_sem=ssem, recv_sem=rsem, device_id=to, device_id_type=MESH
-        ).start()
 
     def half(ref, which):
         rows, cols = ref.shape[-2:]
@@ -172,6 +173,7 @@
             dma((ring + 1,)), dma((ring + 1,)), dma,
         ],
         compiler_params=pltpu.CompilerParams(collective_id=0, has_side_effects=True),
+        cost_estimate=pl.CostEstimate(flops=150_000_000_000, bytes_accessed=300_000_000, transcendentals=0),
         name="spread",
     )(*shards, ids)
     return outs[:count], outs[count]
@@ -187,11 +189,6 @@
     send, got, ring_send, ring_got, load = scratch[-5:]
     bufs = [scratch[9 * w : 9 * w + 9] for w in range(count)]
     greet([to_a, to_b, to_core] + [{"ring": turn("ring", k)} for k in range(1, ring)])
-
-    def push(src, dst, ssem, rsem, to):
-        pltpu.make_async_remote_copy(
-            src_ref=src, dst_ref=dst, send_sem=ssem, recv_sem=rsem, device_id=to, device_id_type=MESH
-        ).start()
 
     def half(ref, which):
         rows, cols = ref.shape[-2:]
@@ -325,9 +322,185 @@
         scratch_shapes=scratch
         + [dma((count, 5)), dma((count, 5)), dma((count, ring - 1)), dma((count, ring - 1)), dma((count, 3))],
         compiler_params=pltpu.CompilerParams(collective_id=1, has_side_effects=True, vmem_limit_bytes=60 << 20),
+        cost_estimate=pl.CostEstimate(flops=160000000000, bytes_accessed=320000000, transcendentals=0),
         name="collect",
     )(*views)
     return outs[1:], outs[0]
+
+
+def dispatch_kernel(down, *refs):
+    ring, count = lax.axis_size("ring"), len(down)
+    rows, weights, rows_out, weights_out = refs[0], refs[1 : count + 1], refs[count + 1], refs[count + 2 : 2 * count + 2]
+    held_rows, held = refs[2 * count + 2], refs[2 * count + 3 : 3 * count + 3]
+    load, place, send_ring, got_ring, core_sem, send_side, got_side, send_diag, got_diag = refs[3 * count + 3 :]
+    a, b, r, c = (lax.axis_index(n) for n in ALL)
+    na, nb, nc = turn("ca", 1), turn("cb", 1), turn("core", 1)
+    to_a, to_b, to_core = {"ca": na}, {"cb": nb}, {"core": nc}
+    greet([to_a, to_b, to_core] + [{"ring": turn("ring", k)} for k in range(1, ring)])
+
+    def slot(w, e, p, q):
+        units = weights[w].shape[1 if down[w] else 2]
+        at = pl.ds(pl.multiple_of((2 * p + q) * units, units), units)
+        return weights_out[w].at[e, at, :] if down[w] else weights_out[w].at[e, :, at]
+
+    fetch_rows = pltpu.make_async_copy(rows, held_rows, load.at[count])
+    fetch_rows.start()
+    fetches = [pltpu.make_async_copy(weights[w], held[w], load.at[w]) for w in range(count)]
+    for fetch in fetches:
+        fetch.start()
+    fetch_rows.wait()
+    pltpu.make_async_copy(held_rows, rows_out.at[r, c], place.at[count]).start()
+    to_next, to_last = {"ring": turn("ring", 1)}, {"ring": turn("ring", ring - 1)}
+
+    def along(step):
+        return (
+            ((r + 1 < ring) & (r >= step), r >= step + 1, lax.rem(r + ring - step, ring), lax.rem(r + ring - 1 - step, ring), to_next, 0),
+            ((r >= 1) & (r + step < ring), r + 1 + step < ring, lax.rem(r + step, ring), lax.rem(r + 1 + step, ring), to_last, 1),
+        )
+
+    def send_along(step):
+        for sent, _, block, _, to, side in along(step):
+
+            @pl.when(sent)
+            def _(block=block, to=to, side=side):
+                src = held_rows if step == 0 else rows_out.at[block, c]
+                push(src, rows_out.at[block, c], send_ring.at[side, step], got_ring.at[side, step], to)
+
+    send_along(0)
+    push(held_rows, rows_out.at[r, c], core_sem.at[0], core_sem.at[1], to_core)
+    for w in range(count):
+        fetches[w].wait()
+        for e in range(weights[w].shape[0]):
+            mine, here = held[w].at[e], slot(w, e, a, b)
+            push(mine, here, send_side.at[w, 0, e], got_side.at[w, 0, e], to_b)
+            push(mine, here, send_side.at[w, 1, e], got_side.at[w, 1, e], to_a)
+            pltpu.make_async_copy(mine, here, place.at[w]).start()
+
+    for step in range(ring - 1):
+        for _, comes, _, block, _, side in along(step):
+
+            @pl.when(comes)
+            def _(block=block, side=side):
+                await_bytes(rows_out.at[block, c], got_ring.at[side, step])
+
+        if step + 1 < ring - 1:
+            send_along(step + 1)
+        for _, comes, _, block, _, side in along(step):
+
+            @pl.when(comes)
+            def _(block=block):
+                here = rows_out.at[block, c]
+                push(here, here, core_sem.at[0], core_sem.at[1], to_core)
+
+    for w in range(count):
+        experts = weights[w].shape[0]
+        for e in range(experts):
+            from_b, from_a = slot(w, e, a, nb), slot(w, e, na, b)
+            await_bytes(from_b, got_side.at[w, 0, e])
+            await_bytes(from_a, got_side.at[w, 1, e])
+            if 2 * e < experts:
+                push(from_b, from_b, send_diag.at[w, e], got_diag.at[w, e], to_a)
+            else:
+                push(from_a, from_a, send_diag.at[w, e], got_diag.at[w, e], to_b)
+
+    await_bytes(held_rows, place.at[count])
+    for step in range(ring - 1):
+        for sent, _, _, _, _, side in along(step):
+
+            @pl.when(sent)
+            def _(side=side):
+                await_bytes(held_rows, send_ring.at[side, step])
+
+    await_bytes(rows_out.at[:, c], core_sem.at[0])
+    await_bytes(rows_out.at[:, nc], core_sem.at[1])
+    for w in range(count):
+        await_bytes(held[w], place.at[w])
+        for e in range(weights[w].shape[0]):
+            await_bytes(held[w].at[e], send_side.at[w, 0, e])
+            await_bytes(held[w].at[e], send_side.at[w, 1, e])
+            await_bytes(held[w].at[e], send_diag.at[w, e])
+            await_bytes(slot(w, e, na, nb), got_diag.at[w, e])
+
+
+def dispatch(rows, weights, down):
+    ring, chips = lax.axis_size("ring"), lax.axis_size("ca") * lax.axis_size("cb")
+    experts, count = max([w.shape[0] for w in weights], default=1), len(weights)
+    full = [(w.shape[0], w.shape[1] * (chips if d else 1), w.shape[2] * (1 if d else chips)) for w, d in zip(weights, down)]
+    dma = pltpu.SemaphoreType.DMA
+    outs = pl.pallas_call(
+        functools.partial(dispatch_kernel, tuple(down)),
+        out_shape=[jax.ShapeDtypeStruct((ring, 2) + rows.shape, rows.dtype)]
+        + [jax.ShapeDtypeStruct(shape, rows.dtype) for shape in full],
+        in_specs=[pl.BlockSpec(memory_space=pl.ANY)] * (count + 1),
+        out_specs=[pl.BlockSpec(memory_space=pl.ANY)] * (count + 1),
+        scratch_shapes=[pltpu.VMEM(v.shape, v.dtype) for v in (rows, *weights)]
+        + [
+            dma((1 + count,)), dma((1 + count,)), dma((2, ring)), dma((2, ring)), dma((2,)),
+            dma((max(count, 1), 2, experts)), dma((max(count, 1), 2, experts)), dma((max(count, 1), experts)), dma((max(count, 1), experts)),
+        ],
+        compiler_params=pltpu.CompilerParams(collective_id=2, has_side_effects=True),
+        cost_estimate=pl.CostEstimate(flops=80_000_000_000, bytes_accessed=100_000_000, transcendentals=0),
+        name="dispatch",
+    )(rows, *weights)
+    return outs[0], outs[1:]
+
+
+def give_back_kernel(part, out, own, core_in, ring_in, load, core_send, core_got, ring_send, ring_got):
+    ring = lax.axis_size("ring")
+    r, c, nc = lax.axis_index("ring"), lax.axis_index("core"), turn("core", 1)
+    greet([{"core": nc}] + [{"ring": turn("ring", k)} for k in range(1, ring)])
+    order = list(range(1, ring)) + [0]
+    block_of = lambda k: lax.rem(r + k, ring)
+    for k in order:
+        push(part.at[block_of(k), nc], core_in.at[k], core_send.at[k], core_got.at[k], {"core": nc})
+        pltpu.make_async_copy(part.at[block_of(k), c], own.at[k], load.at[k]).start()
+    rows, cols = own.shape[1:]
+    tile = 32
+    for k in order:
+        await_bytes(own.at[k], load.at[k])
+        await_bytes(core_in.at[k], core_got.at[k])
+        if k == 0:
+            continue
+
+        def add(i, carry):
+            at = pl.ds(pl.multiple_of(i * tile, tile), tile)
+            own[k, at] = (own[k, at].astype(jnp.float32) + core_in[k, at].astype(jnp.float32)).astype(own.dtype)
+            return carry
+
+        lax.fori_loop(0, rows // tile, add, 0)
+        push(own.at[k], ring_in.at[k - 1], ring_send.at[k - 1], ring_got.at[k - 1], {"ring": block_of(k)})
+    for k in range(1, ring):
+        await_bytes(ring_in.at[k - 1], ring_got.at[k - 1])
+
+    def total(i, carry):
+        at = pl.ds(pl.multiple_of(i * tile, tile), tile)
+        value = own[0, at].astype(jnp.float32) + core_in[0, at].astype(jnp.float32)
+        for k in range(ring - 1):
+            value = value + ring_in[k, at].astype(jnp.float32)
+        out[at, :] = value
+        return carry
+
+    lax.fori_loop(0, rows // tile, total, 0)
+    for k in order:
+        await_bytes(core_in.at[k], core_send.at[k])
+        if k:
+            await_bytes(ring_in.at[k - 1], ring_send.at[k - 1])
+
+
+def give_back(part):
+    ring, dma = lax.axis_size("ring"), pltpu.SemaphoreType.DMA
+    rows, cols = part.shape[1:]
+    block = lambda n: pltpu.VMEM((n, rows, cols), part.dtype)
+    return pl.pallas_call(
+        give_back_kernel,
+        out_shape=jax.ShapeDtypeStruct((rows, cols), jnp.float32),
+        in_specs=[pl.BlockSpec(memory_space=pl.ANY)],
+        out_specs=pl.BlockSpec(memory_space=pltpu.VMEM),
+        scratch_shapes=[block(ring), block(ring), block(ring - 1), dma((ring,)), dma((ring,)), dma((ring,)), dma((ring,)), dma((ring,))],
+        compiler_params=pltpu.CompilerParams(collective_id=3, has_side_effects=True, vmem_limit_bytes=60 << 20),
+        cost_estimate=pl.CostEstimate(flops=100000000000, bytes_accessed=200000000, transcendentals=0),
+        name="give_back",
+    )(part.reshape(ring, 2, rows, cols))
 
 
 def matmul(left, right):
@@ -344,6 +517,164 @@
     return lax.dot_general(
         left, right, (((0,), (0,)), ((), ())), preferred_element_type=jnp.float32
     )
+
+
+def corners():
+    return ((0, 1), (1, 0), (1, 1))
+
+
+def corner(da, db):
+    pa, pb = turn("ca", da), turn("cb", db)
+    return 2 * pa + pb, {"ca": pa, "cb": pb}
+
+
+def rows_to_heads(src, dst, send, got, place):
+    rows, width = src.shape[0], dst.shape[1]
+    me, _ = corner(0, 0)
+    there = dst.at[pl.ds(pl.multiple_of(me * rows, rows), rows), :]
+    for i, (da, db) in enumerate(corners()):
+        peer, to = corner(da, db)
+        push(src.at[:, pl.ds(pl.multiple_of(peer * width, width), width)], there, send.at[i], got.at[i], to)
+    pltpu.make_async_copy(src.at[:, pl.ds(pl.multiple_of(me * width, width), width)], there, place).start()
+
+
+def wait_heads(src, dst, got, place):
+    rows = src.shape[0]
+    here = lambda at: dst.at[pl.ds(pl.multiple_of(at * rows, rows), rows), :]
+    await_bytes(here(corner(0, 0)[0]), place)
+    for i, (da, db) in enumerate(corners()):
+        await_bytes(here(corner(da, db)[0]), got.at[i])
+
+
+def attend_kernel(scale, q, k, v, keep, o, qh, kh, vh, logs, oh, send, got, place, send_o, got_o, place_o):
+    rows, width = q.shape[0], qh.shape[1]
+    greet([corner(da, db)[1] for da, db in corners()])
+    pairs = ((q, qh), (k, kh), (v, vh))
+    for i, (src, dst) in enumerate(pairs):
+        rows_to_heads(src, dst, send.at[i], got.at[i], place.at[i])
+    for i, (src, dst) in enumerate(pairs):
+        wait_heads(src, dst, got.at[i], place.at[i])
+    me, _ = corner(0, 0)
+    tile = 128
+    mine = pl.ds(pl.multiple_of(me * width, width), width)
+
+    def block(at_block):
+        def part(i, carry):
+            at = pl.ds(pl.multiple_of(at_block * rows + i * tile, tile), tile)
+            for h in range(width // HD):
+                lanes = pl.ds(h * HD, HD)
+                s = times_transposed(qh[at, lanes], kh[:, lanes]) * scale
+                s = jnp.where(keep[...] > 0.0, s, NEG_FILL)
+                peak = jnp.max(s, axis=-1, keepdims=True)
+                p = jnp.exp(s - peak)
+                total = jnp.sum(p, axis=-1, keepdims=True)
+                logs[h, at, :] = peak + jnp.log(total)
+                low = (p * (1.0 / total)).astype(jnp.bfloat16)
+                oh[at, lanes] = matmul(low, vh[:, lanes]).astype(jnp.bfloat16)
+            return carry
+
+        lax.fori_loop(0, rows // tile, part, 0)
+
+    for i, (da, db) in enumerate(corners()):
+        peer, to = corner(da, db)
+        block(peer)
+        push(oh.at[pl.ds(pl.multiple_of(peer * rows, rows), rows), :], o.at[:, mine], send_o.at[i], got_o.at[i], to)
+    block(me)
+    pltpu.make_async_copy(oh.at[pl.ds(pl.multiple_of(me * rows, rows), rows), :], o.at[:, mine], place_o).start()
+    pltpu.make_async_copy(oh.at[pl.ds(pl.multiple_of(me * rows, rows), rows), :], o.at[:, mine], place_o).wait()
+    piece = o.at[:, mine]
+    for i in range(3):
+        await_bytes(piece, got_o.at[i])
+        await_bytes(piece, send_o.at[i])
+        for j in range(3):
+            await_bytes(piece, send.at[j, i])
+
+
+def attend(q, k, v, keep, scale):
+    rows, width = q.shape
+    chips = lax.axis_size("ca") * lax.axis_size("cb")
+    heads = jax.ShapeDtypeStruct((rows * chips, width // chips), q.dtype)
+    vm, dma = pl.BlockSpec(memory_space=pltpu.VMEM), pltpu.SemaphoreType.DMA
+    return pl.pallas_call(
+        functools.partial(attend_kernel, scale),
+        out_shape=[jax.ShapeDtypeStruct(q.shape, q.dtype), heads, heads, heads]
+        + [jax.ShapeDtypeStruct((width // chips // HD, rows * chips, 1), jnp.float32)],
+        in_specs=[vm] * 4,
+        out_specs=[vm] * 5,
+        scratch_shapes=[pltpu.VMEM(heads.shape, q.dtype)]
+        + [dma((3, 3)), dma((3, 3)), dma((3,)), dma((3,)), dma((3,)), dma],
+        compiler_params=pltpu.CompilerParams(collective_id=4, has_side_effects=True, vmem_limit_bytes=48 << 20),
+        cost_estimate=pl.CostEstimate(flops=1_000_000, bytes_accessed=10_000, transcendentals=0),
+        name="attend",
+    )(q, k, v, keep)
+
+
+def attend_back_kernel(scale, do, qh, kh, vh, logs, keep, dq, dk, dv, doh, dqh, dkh, dvh, send, got, place, send_g, got_g, place_g):
+    rows, width = do.shape[0], qh.shape[1]
+    greet([corner(da, db)[1] for da, db in corners()])
+    rows_to_heads(do, doh, send, got, place)
+    wait_heads(do, doh, got, place)
+    me, _ = corner(0, 0)
+    tile, total_rows = 128, qh.shape[0]
+    grads = ((dqh, dq), (dkh, dk), (dvh, dv))
+
+    def one_head(h):
+        lanes = pl.ds(h * HD, HD)
+
+        def part(i, carry):
+            dk_sum, dv_sum = carry
+            at = pl.ds(pl.multiple_of(i * tile, tile), tile)
+            qb, db, kb, vb = qh[at, lanes], doh[at, lanes], kh[:, lanes], vh[:, lanes]
+            s = times_transposed(qb, kb) * scale
+            s = jnp.where(keep[...] > 0.0, s, NEG_FILL)
+            p = jnp.exp(s - logs[h, at, :])
+            dp = times_transposed(db, vb)
+            ds = (p * (dp - jnp.sum(dp * p, axis=-1, keepdims=True))).astype(jnp.bfloat16)
+            dqh[at, lanes] = (matmul(ds, kb) * scale).astype(jnp.bfloat16)
+            dk_sum = dk_sum + transposed_times(ds, qb)
+            dv_sum = dv_sum + transposed_times(p.astype(jnp.bfloat16), db)
+            return dk_sum, dv_sum
+
+        zero = jnp.zeros((total_rows, HD), jnp.float32)
+        dk_sum, dv_sum = lax.fori_loop(0, total_rows // tile, part, (zero, zero))
+        dkh[:, lanes] = (dk_sum * scale).astype(jnp.bfloat16)
+        dvh[:, lanes] = dv_sum.astype(jnp.bfloat16)
+
+    for h in range(width // HD):
+        one_head(h)
+        lanes = pl.ds(h * HD, HD)
+        here = pl.ds(pl.multiple_of(me * width + h * HD, HD), HD)
+        for g, (src, dst) in enumerate(grads):
+            for i, (da, db) in enumerate(corners()):
+                peer, to = corner(da, db)
+                push(src.at[pl.ds(pl.multiple_of(peer * rows, rows), rows), lanes], dst.at[:, here], send_g.at[g, i, h], got_g.at[g, i, h], to)
+            own = src.at[pl.ds(pl.multiple_of(me * rows, rows), rows), lanes]
+            pltpu.make_async_copy(own, dst.at[:, here], place_g.at[g, h]).start()
+    piece = dq.at[:, pl.ds(0, HD)]
+    for h in range(width // HD):
+        for g in range(3):
+            await_bytes(piece, place_g.at[g, h])
+            for i in range(3):
+                await_bytes(piece, send_g.at[g, i, h])
+                await_bytes(piece, got_g.at[g, i, h])
+    for i in range(3):
+        await_bytes(do.at[:, pl.ds(0, width)], send.at[i])
+
+
+def attend_back(do, qh, kh, vh, logs, keep, scale):
+    heads = qh.shape[1] // HD
+    vm, dma = pl.BlockSpec(memory_space=pltpu.VMEM), pltpu.SemaphoreType.DMA
+    return pl.pallas_call(
+        functools.partial(attend_back_kernel, scale),
+        out_shape=[jax.ShapeDtypeStruct(do.shape, do.dtype)] * 3,
+        in_specs=[vm] * 6,
+        out_specs=[vm] * 3,
+        scratch_shapes=[pltpu.VMEM(qh.shape, qh.dtype)] * 4
+        + [dma((3,)), dma((3,)), dma, dma((3, 3, heads)), dma((3, 3, heads)), dma((3, heads))],
+        compiler_params=pltpu.CompilerParams(collective_id=5, has_side_effects=True, vmem_limit_bytes=48 << 20),
+        cost_estimate=pl.CostEstimate(flops=50_000_000_000, bytes_accessed=10_000_000, transcendentals=0),
+        name="attend_back",
+    )(do, qh, kh, vh, logs, keep)
 
 
 def norm_rows(values, gain):
@@ -373,14 +704,6 @@
     return jnp.concatenate(
         [first * cos_rows - second * sin_rows, second * cos_rows + first * sin_rows], axis=-1
     )
-
-
-def to_heads(values):
-    return lax.all_to_all(values, CTX, split_axis=1, concat_axis=0, tiled=True)
-
-
-def to_rows(values):
-    return lax.all_to_all(values, CTX, split_axis=0, concat_axis=1, tiled=True)
 
 
 def local(
@@ -398,7 +721,6 @@
     capacity = max(2, -(-(token_count * top_count * 9) // (experts * 8)))
     score_scale = 1.0 / math.sqrt(head_dim)
     seq_len = token_count * ctx_size
-    own_heads = HEADS // ctx_size
 
     rows_each = query_weight.shape[0]
     packed = jnp.concatenate(
@@ -413,6 +735,8 @@
     gain_first, gain_second, gain_queries, gain_keys = gains
     full_router = smalls[:, 4 * rows_each : packed.size].reshape(model_width, experts)
     ids_all = ids_all.reshape(sources, token_count, top_count).astype(jnp.int32)
+    gate_all, up_all = (lax.all_gather(w, CTX, axis=2, tiled=True) for w in (gate_weight, up_weight))
+    down_all = lax.all_gather(down_weight, CTX, axis=1, tiled=True)
     inputs = tokens[0].astype(jnp.float32)
     length = lengths[0]
     positions = lax.axis_index(CTX) * token_count + jnp.arange(token_count, dtype=jnp.int32)
@@ -423,12 +747,6 @@
     grad_total = grad_total_low.astype(jnp.float32)
 
     g_all = lax.all_gather(grad_total_low, EXP, axis=0)
-    gate_all, up_all, down_all = (
-        lax.all_gather(gate_weight, CTX, axis=2, tiled=True),
-        lax.all_gather(up_weight, CTX, axis=2, tiled=True),
-        lax.all_gather(down_weight, CTX, axis=1, tiled=True),
-    )
-
     cosine, sine = rotary_tables(positions, head_dim)
     normed_one, factor_one = norm_rows(inputs, gain_first)
     normed_one_low = normed_one.astype(jnp.bfloat16)
@@ -441,24 +759,16 @@
     query_low = rotate(by_head(query_normed), cosine, sine, 1.0).astype(jnp.bfloat16)
     key_low = rotate(by_head(key_normed), cosine, sine, 1.0).astype(jnp.bfloat16)
     flat = lambda v: v.reshape(v.shape[0], -1)
-    heads_of = lambda v: v.reshape(seq_len, own_heads, head_dim)
-    q, k, v = (heads_of(to_heads(flat(a))) for a in (query_low, key_low, value_low))
-
-    def scores_of():
-        s = jnp.einsum("qhd,khd->hqk", q, k, preferred_element_type=jnp.float32) * score_scale
-        return jnp.where(key_valid[None, None, :], s, NEG_FILL)
-
-    scores = scores_of()
-    peak = jnp.max(scores, axis=-1, keepdims=True)
-    log_total = peak + jnp.log(jnp.sum(jnp.exp(scores - peak), axis=-1, keepdims=True))
-    softmax_low = jnp.exp(scores - log_total).astype(jnp.bfloat16)
-    attended = jnp.einsum("hqk,khd->qhd", softmax_low, v, preferred_element_type=jnp.float32)
-    attended_low = to_rows(flat(attended.astype(jnp.bfloat16)))
+    keep = key_valid.astype(jnp.float32)[None, :]
+    value_low, gate_all = lax.optimization_barrier((value_low, gate_all))
+    attended_low, *saved = attend(flat(query_low), flat(key_low), value_low, keep, score_scale)
     hidden_state = inputs + matmul(attended_low, full_out)
     normed_two, factor_two = norm_rows(hidden_state, gain_second)
     normed_two_low = normed_two.astype(jnp.bfloat16)
 
-    n2_all = lax.all_gather(normed_two_low, EXP, axis=0)
+    n2_sent, up_all = lax.optimization_barrier((normed_two_low, up_all))
+    n2_all, _ = dispatch(n2_sent, [], [])
+    n2_all = n2_all.reshape(sources, token_count, model_width)
     first_expert = lax.axis_index(EXP) * local_experts
     own_experts = first_expert + jnp.arange(local_experts, dtype=jnp.int32)
     mask = jnp.any(ids_all[:, None, :, :] == own_experts[None, :, None, None], axis=-1)
@@ -472,20 +782,20 @@
     hot32 = hot.astype(jnp.float32)
     row_gate = jnp.sum(hot32 * own_probs.transpose(0, 2, 1)[:, :, None, :], axis=-1)
     x = jnp.einsum("sect,std->escd", hot, n2_all, preferred_element_type=jnp.float32).astype(jnp.bfloat16)
-    g_rows = jnp.einsum("sect,std->escd", hot, g_all, preferred_element_type=jnp.float32)
     row_gate = row_gate.transpose(1, 0, 2)[..., None]
-    de = (g_rows * row_gate).astype(jnp.bfloat16)
     ee = lambda eq, a, b: jnp.einsum(eq, a, b, preferred_element_type=jnp.float32)
     gp = ee("escd,edf->escf", x, gate_all)
     up = ee("escd,edf->escf", x, up_all)
+    up, g_all = lax.optimization_barrier((up, g_all))
+    g_rows = jnp.einsum("sect,std->escd", hot, g_all, preferred_element_type=jnp.float32)
+    de = (g_rows * row_gate).astype(jnp.bfloat16)
     sig = jax.nn.sigmoid(gp)
     hid = (gp * sig * up).astype(jnp.bfloat16)
     eo = ee("escf,efd->escd", hid, down_all).astype(jnp.bfloat16)
     dgate_rows = jnp.sum(g_rows * eo.astype(jnp.float32), axis=-1)
     mixed_rows = (row_gate * eo.astype(jnp.float32)).astype(jnp.bfloat16)
     mixed_part = jnp.einsum("sect,escd->std", hot, mixed_rows, preferred_element_type=jnp.float32)
-    mixed = lax.psum_scatter(mixed_part.astype(jnp.bfloat16).reshape(-1, model_width), EXP, scatter_dimension=0, tiled=True)
-    layer_out = (row_valid * (hidden_state + mixed.astype(jnp.float32))).astype(jnp.bfloat16)
+    mixed_part = mixed_part.astype(jnp.bfloat16)
 
     dhid = ee("escd,efd->escf", de, down_all)
     dgp = (dhid * up * sig * (1.0 + gp * (1.0 - sig))).astype(jnp.bfloat16)
@@ -493,9 +803,11 @@
     down_part = ee("escf,escd->efd", hid, de)
     gate_part = ee("escd,escf->edf", x, dgp)
     up_part = ee("escd,escf->edf", x, dup)
+    parts = [v.astype(jnp.bfloat16) for v in (down_part, gate_part, up_part)]
+    dgp, dup, *_ = lax.optimization_barrier((dgp, dup, *parts))
+    rs_ctx = lambda v, a: lax.psum_scatter(v, CTX, scatter_dimension=a, tiled=True)
+    down_grad, gate_grad, up_grad = rs_ctx(parts[0], 1), rs_ctx(parts[1], 2), rs_ctx(parts[2], 2)
     dpair = (ee("escf,edf->escd", dgp, gate_all) + ee("escf,edf->escd", dup, up_all)).astype(jnp.bfloat16)
-    rs_ctx = lambda v, a: lax.psum_scatter(v.astype(jnp.bfloat16), CTX, scatter_dimension=a, tiled=True).astype(jnp.float32)
-    gate_grad, up_grad, down_grad = rs_ctx(gate_part, 2), rs_ctx(up_part, 2), rs_ctx(down_part, 1)
 
     dprobs_own = jnp.sum(hot32 * dgate_rows.transpose(1, 0, 2)[..., None], axis=2)
     dprobs_own = dprobs_own.transpose(0, 2, 1).reshape(-1, local_experts)
@@ -505,21 +817,20 @@
     router_part = transposed_times(n2_all.reshape(-1, model_width), dlogit_low)
     dn2_part = jnp.einsum("sect,escd->std", hot, dpair, preferred_element_type=jnp.float32).reshape(-1, model_width)
     dn2_part = dn2_part + times_transposed(dlogit_low, full_router)
-    dn2 = lax.psum_scatter(dn2_part.astype(jnp.bfloat16), EXP, scatter_dimension=0, tiled=True).astype(jnp.float32)
+    dn2_part = dn2_part.astype(jnp.bfloat16).reshape(sources, token_count, model_width)
+    dn2_part, down_grad = lax.optimization_barrier((dn2_part, down_grad))
+    dn2 = give_back(dn2_part)
+    dn2, gate_grad = lax.optimization_barrier((dn2, gate_grad))
+    dn2, mixed_part = lax.optimization_barrier((dn2, mixed_part))
+    mixed = lax.psum_scatter(mixed_part.reshape(-1, model_width), EXP, scatter_dimension=0, tiled=True)
 
     dh_norm, gain_second_part = norm_back(dn2, hidden_state, factor_two, gain_second)
     grad_hidden = grad_total + dh_norm
     dh_low = grad_hidden.astype(jnp.bfloat16)
     out_part = transposed_times(attended_low, dh_low)
-    d_att = heads_of(to_heads(times_transposed(dh_low, full_out).astype(jnp.bfloat16)))
-    soft = jnp.exp(scores_of() - log_total)
-    dp = jnp.einsum("qhd,khd->hqk", d_att, v, preferred_element_type=jnp.float32)
-    dv = jnp.einsum("hqk,qhd->khd", soft.astype(jnp.bfloat16), d_att, preferred_element_type=jnp.float32)
-    inner = jnp.sum(dp * soft, axis=-1, keepdims=True)
-    ds = (soft * (dp - inner)).astype(jnp.bfloat16)
-    dq = jnp.einsum("hqk,khd->qhd", ds, k, preferred_element_type=jnp.float32) * score_scale
-    dk = jnp.einsum("hqk,qhd->khd", ds, q, preferred_element_type=jnp.float32) * score_scale
-    dq, dk, dv = (to_rows(flat(a.astype(jnp.bfloat16))) for a in (dq, dk, dv))
+    d_att = times_transposed(dh_low, full_out).astype(jnp.bfloat16)
+    dq, dk, dv = attend_back(d_att, *saved, keep, score_scale)
+    dq, up_grad = lax.optimization_barrier((dq, up_grad))
     unrotate = lambda a: rotate(by_head(a.astype(jnp.float32)), cosine, sine, -1.0).reshape(token_count, model_width)
     dk_raw, gain_keys_part = norm_back(unrotate(dk), key_raw, key_factor, gain_keys)
     dq_raw, gain_queries_part = norm_back(unrotate(dq), query_raw, query_factor, gain_queries)
@@ -548,6 +859,11 @@
     small_parts = jnp.pad(small_parts, ((0, 0), (0, 0), (0, -small_parts.shape[2] % 2048)))
     small_parts = lax.dynamic_index_in_dim(small_parts, core, 1, False) + swap(lax.dynamic_index_in_dim(small_parts, 1 - core, 1, False))
     weight_grads, small_grads = collect(parts, small_parts.reshape(ctx_size * sources // 2, -1, 128))
+    weight_grads, mixed, gate_grad, up_grad, down_grad = lax.optimization_barrier(
+        (list(weight_grads), mixed, gate_grad, up_grad, down_grad)
+    )
+    layer_out = (row_valid * (hidden_state + mixed.astype(jnp.float32))).astype(jnp.bfloat16)
+    gate_grad, up_grad, down_grad = (v.astype(jnp.float32) for v in (gate_grad, up_grad, down_grad))
     weight_grads = list(weight_grads[1:]) + [weight_grads[0]]
     small_grads = small_grads.reshape(-1)
     gain_grads = [small_grads[i * rows_each : (i + 1) * rows_each] for i in range(4)]

time: 1580 us -> 1160 us (0.73)
  waiting for transfers between devices: 608 us -> 2.07 us
  Pallas kernels: 392 us -> 735 us
  local copies, waits for them, and re-layouts: 84.7 us -> 45.9 us
  matrix products: 337 us -> 306 us
  other arithmetic: 72.6 us -> 42 us
  blocking collectives: 29.1 us -> 0 us
  starting transfers between devices: 32.9 us -> 5.45 us
    pallas_call x0 -> x4, Pallas kernels: none -> 307 us  [the longest x1 104 us: give_back(): pl.pallas_call(give_back_kernel, out_shape=jax.ShapeDtypeStruct((rows, co...]
    all_gather x4 -> x3, waiting for transfers between devices: 286 us -> 0.02 us  [the longest x2 0.02 us: local(): lax.all_gather(w, CTX, axis=2, tiled=True)]
    reduce_scatter x5 -> x4, waiting for transfers between devices: 270 us -> 0.05 us  [the longest x3 0.04 us: local(): lax.psum_scatter(v, CTX, scatter_dimension=a, tiled=True)]
    all_to_all x7 -> x0, waiting for transfers between devices: 49.6 us -> none  [the longest x4 26.7 us: to_rows(): return lax.all_to_all(values, CTX, split_axis=0, concat_axis=1, tiled=True)]
    pallas_call x1, Pallas kernels: 212 us -> 250 us  [spread(): pl.pallas_call(functools.partial(spread_kernel, count), out_shape=[jax.Sh...]
    dot_general x6 -> x0, matrix products: 33.1 us -> none  [the longest x1 12.3 us: local(): jnp.einsum('qhd,khd->hqk', d_att, v, preferred_element_type=jnp.float32)]
    all_to_all x1 -> x0, blocking collectives: 29.1 us -> none  [to_heads(): return lax.all_to_all(values, CTX, split_axis=1, concat_axis=0, tiled=True)]
    all_to_all x7 -> x0, starting transfers between devices: 28.5 us -> none  [the longest x4 16.5 us: to_rows(): return lax.all_to_all(values, CTX, split_axis=0, concat_axis=1, tiled=True)]
  transfers between devices with their start and end apart: 24 -> 15, of which waited for: 13 -> 0; matrix products, arithmetic and copies ran while one was open for 23% -> 29% of each run, Pallas kernels for 13% -> 64%
where the time goes in v2:
time: 1160 us; the launch traced here: 1150 us
  Pallas kernels  735 us (63%)
  matrix products  306 us (26%)
  local copies, waits for them, and re-layouts  45.9 us (4%)
  other arithmetic  42 us (4%)
  between operations  16.5 us (1%)
    pallas_call x1, Pallas kernels, spread(): pl.pallas_call(functools.partial(spread_kernel, count), out_shape=[jax.Sh...  250 us
    pallas_call x1, Pallas kernels, collect(): pl.pallas_call(functools.partial(collect_kernel, count), out_shape=shapes...  178 us
    dot_general x8, matrix products, local(): jnp.einsum(eq, a, b, preferred_element_type=jnp.float32)  154 us
    pallas_call x1, Pallas kernels, give_back(): pl.pallas_call(give_back_kernel, out_shape=jax.ShapeDtypeStruct((rows, co...  104 us
    pallas_call x1, Pallas kernels, attend_back(): pl.pallas_call(functools.partial(attend_back_kernel, scale), out_shape=[j...  71.8 us
    pallas_call x1, Pallas kernels, dispatch(): pl.pallas_call(functools.partial(dispatch_kernel, tuple(down)), out_shape...  71.5 us
    pallas_call x1, Pallas kernels, attend(): pl.pallas_call(functools.partial(attend_kernel, scale), out_shape=[jax.Sh...  59.6 us
    dot_general x5, matrix products, times_transposed(): lax.dot_general(left, right, (((1,), (1,)), ((), ())), preferred_element_...  37 us
  transfers between devices with their start and end apart: 15, of which 0 were waited for; matrix products, arithmetic and copies ran while one was open for 29% of the time, Pallas kernels for 64%

profile of v2, /device:TPU:9, one launch (start us, length us, event | category | flops | bytes accessed | tf_op | source)
XLA Modules:
  0.0 1153.3 jit_solution(10946134214492299320)
XLA Ops:
  14.7 249.9 %spread.1 = (bf16[2,2,4,2,64,2048]{5,4,3,2,1,0:T(8,128)(2,1)}, bf16[2,2,4,2,64,2048]{5,4,3,2,1,0:T(8,128)(2,1)}, bf16[2,2,4,2,64,2048]{5,4,3,2,1,0:T(8,128)(2,1)...) custom-call(bf16[64,2048]{1,0:T(8,128)(2,1)} %refs_0_.1, ...), custom_call_target="tpu_custom_call" | custom-call | flops 149999992832 | bytes 300000000 | tf_op jit(solution)/shard_map/spread/pallas_call | solution.py:165
  266.6 5.9 multiply_reduce_fusion.6
  274.4 7.1 multiply_reduce_fusion.5
  290.5 3.4 convolution_convert_fusion.5.v
  298.0 59.6 %attend.1 = (bf16[256,2048]{1,0:T(8,128)(2,1)}, bf16[1024,512]{1,0:T(8,128)(2,1)S(1)}, bf16[1024,512]{1,0:T(8,128)(2,1)S(1)}, bf16[1024,512]{1,0:T(8,128)(2,1)S(1)}, f32[4,1024,1]{2,1,0:T(8,128)}) custom-call(bf16[256,2048]{1,0:T(8,128)(2,1)S(1)} %bitcast.267, bf16[256,2048]{1,0:T(8,128)(2,1)} %bitcast.281, bf16[256,2048]{1,0:T(8,128)(2,1)} %convolution_convert_fusion.5.v, ...), custom_call_target="tpu_custom_call" | custom-call | flops 1000000 | bytes 10000 | tf_op jit(solution)/shard_map/attend/pallas_call | solution.py:598
  357.6 7.3 multiply_reduce_fusion.4
  367.6 71.5 %dispatch.1 = bf16[4,2,256,2048]{3,2,1,0:T(8,128)(2,1)} custom-call(bf16[256,2048]{1,0:T(8,128)(2,1)} %multiply_convert_fusion.4.refs_0_), custom_call_target="tpu_custom_call" | custom-call | flops 80000000000 | bytes 100000000 | tf_op jit(solution)/shard_map/dispatch/pallas_call | solution.py:430
  439.1 5.7 fusion.117
  446.0 8.3 convert_bitcast_fusion
  454.3 17.0 %fusion.14 = f32[2,8,144,1024]{3,2,1,0:T(8,128)} fusion(bf16[2,2048,1024]{2,1,0:T(8,128)(2,1)} %all-gather.7.cloned.1.call-done, bf16[2,8,144,2048]{3,2,0,1:T(8,128)(2,1)} %convert_bitcast_fusion), kind=kOutput, calls=%fused_computation.27 | convolution fusion | flops 9663676416 | bytes 27262976 | tf_op jit(solution)/shard_map/escd,edf->escf/dot_general | solution.py:786
  471.4 11.2 fusion.12
  482.6 20.4 %multiply_convert_fusion = (bf16[2,8,144,1024]{3,2,1,0:T(8,128)(2,1)}, f32[2,8,144,1024]{3,2,1,0:T(8,128)}) fusion(f32[2,8,144,1024]{3,2,1,0:T(8,128)} %fusion.14, bf16[2,2048,1024]{2,1,0:T(8,128)(2,1)} %all-gather.5.cloned.1.call-done, bf16[2,8,144,2048]{3,2,0,1:T(8,128)(2,1)} %convert_bitcast_fusion), kind=kOutput, calls=%fused_computation.15 | convolution fusion | flops 9677832192 | bytes 41418752 | tf_op jit(solution)/shard_map/escd,edf->escf/dot_general | solution.py:786
  503.0 19.4 %fusion = (f32[2,8,144]{2,0,1:T(2,128)S(1)}, bf16[2,8,144,2048]{3,2,0,1:T(8,128)(2,1)}) fusion(f32[8,2048,2,144]{1,3,2,0:T(8,128)} %fusion.12, bf16[2,1024,2048]{2,1,0:T(8,128)(2,1)} %all-gather.11.cloned.1.call-done, bf16[2,8,144,1024]{3,2,1,0:T(8,128)(2,1)} %get-tuple-element.219), kind=kOutput, calls=%fused_computation.2 | convolution fusion | flops 9682548736 | bytes 41427968 | tf_op jit(solution)/shard_map/escf,efd->escd/dot_general | solution.py:786
  523.8 18.7 %bitcast_convert_fusion.3 = bf16[2,1024,2048]{2,1,0:T(8,128)(2,1)} fusion(bf16[2,8,144,1024]{3,2,1,0:T(8,128)(2,1)} %get-tuple-element.219, f32[8,2048,2,144]{1,3,2,0:T(8,128)} %fusion.12, f32[2,8,144]{2,0,1:T(2,128)S(1)} %bitcast.296), kind=kOutput, calls=%fused_computation.12 | convolution fusion | flops 9677307904 | bytes 31990784 | tf_op jit(solution)/shard_map/escf,escd->efd/dot_general | solution.py:786
  542.5 25.1 %multiply_convert_fusion.1 = (bf16[2,8,144,1024]{3,2,1,0:T(8,128)(2,1)}, bf16[2,8,144,1024]{3,2,1,0:T(8,128)(2,1)}) fusion(f32[2,8,144,1024]{3,2,1,0:T(8,128)} %get-tuple-element.220, f32[2,8,144,1024]{3,2,1,0:T(8,128)} %fusion.14, bf16[2,1024,2048]{2,1,0:T(8,128)(2,1)} %all-gather.11.cloned.1.call-done, f32[8,2048,2,144]{1,3,2,0:T(8,128)} %fusion.12, ...), kind=kOutput, calls=%fused_computation.16 | convolution fusion | flops 9703784448 | bytes 55583744 | tf_op jit(solution)/shard_map/escd,efd->escf/dot_general | solution.py:786
  567.6 17.3 %bitcast_convert_fusion.2 = bf16[2,2048,1024]{2,1,0:T(8,128)(2,1)} fusion(bf16[2,8,144,2048]{3,2,0,1:T(8,128)(2,1)} %convert_bitcast_fusion, bf16[2,8,144,1024]{3,2,1,0:T(8,128)(2,1)} %get-tuple-element.70), kind=kOutput, calls=%fused_computation.11 | convolution fusion | flops 9667870720 | bytes 22544384 | tf_op jit(solution)/shard_map/escd,escf->edf/dot_general | solution.py:786
  585.7 2.2 collective-permute-start.1
  587.9 17.8 %bitcast_convert_fusion.1 = bf16[2,2048,1024]{2,1,0:T(8,128)(2,1)} fusion(bf16[2,8,144,2048]{3,2,0,1:T(8,128)(2,1)} %convert_bitcast_fusion, bf16[2,8,144,1024]{3,2,1,0:T(8,128)(2,1)} %get-tuple-element.71), kind=kOutput, calls=%fused_computation.10 | convolution fusion | flops 9667870720 | bytes 22544384 | tf_op jit(solution)/shard_map/escd,escf->edf/dot_general | solution.py:786
  605.9 11.2 bitcast_convert_fusion
  617.1 17.8 %fusion.16 = f32[2,8,144,2048]{3,2,0,1:T(8,128)} fusion(bf16[2,2048,1024]{2,1,0:T(8,128)(2,1)} %all-gather.5.cloned.1.call-done, bf16[2,8,144,1024]{3,2,1,0:T(8,128)(2,1)} %get-tuple-element.70), kind=kOutput, calls=%fused_computation.29 | convolution fusion | flops 9663676416 | bytes 31981568 | tf_op jit(solution)/shard_map/escf,edf->escd/dot_general | solution.py:786
  635.1 5.9 fusion.127
  642.1 25.3 %fusion.4 = f32[8,256,2048,1]{2,1,3,0:T(8,128)} fusion(f32[2,8,144,2048]{3,2,0,1:T(8,128)} %fusion.16, f32[8,2,256]{2,1,0:T(2,128)S(1)} %copy-done.35, pred[8,2,256]{2,1,0:T(4,128)(4,1)S(1)} %copy-done.43, bf16[2,2048,1024]{2,1,0:T(8,128)(2,1)} %all-gather.7.cloned.1.call-done, bf16[2,8,144,1024]{3,2,1,0:T(8,128)(2,1)} %get-tuple-element.71), kind=kOutput, calls=%fused_computation.13 | convolution fusion | flops 12090212352 | bytes 48779264 | tf_op jit(solution)/shard_map/sect,escd->std/dot_general | solution.py:818
  667.4 11.9 %fusion.3 = bf16[2048,2048]{1,0:T(8,128)(2,1)} fusion(f32[8,256,2048,1]{2,1,3,0:T(8,128)} %fusion.4, bf16[2048,16]{0,1:T(8,128)(2,1)S(1)} %multiply_convert_fusion.5, bf16[2048,16]{1,0:T(8,128)(2,1)S(1)} %copy-done.17), kind=kOutput, calls=%fused_computation.8 | convolution fusion | flops 142606336 | bytes 25296896 | tf_op jit(solution)/shard_map/dot_general | solution.py:511
  679.4 104.5 %give_back.1 = f32[256,2048]{1,0:T(8,128)} custom-call(bf16[4,2,256,2048]{3,2,1,0:T(8,128)(2,1)} %bitcast.279), custom_call_target="tpu_custom_call" | custom-call | flops 99999997952 | bytes 200000000 | tf_op jit(solution)/shard_map/give_back/pallas_call | solution.py:494
  783.9 2.3 multiply_reduce_fusion
  786.5 2.1 fusion.115
  788.6 6.2 convolution_convert_fusion.4.do
  794.8 71.8 %attend_back.1 = (bf16[256,2048]{1,0:T(8,128)(2,1)S(1)}, bf16[256,2048]{1,0:T(8,128)(2,1)S(1)}, bf16[256,2048]{1,0:T(8,128)(2,1)S(1)}) custom-call(bf16[256,2048]{1,0:T(8,128)(2,1)S(1)} %convolution_convert_fusion.4.do, bf16[1024,512]{1,0:T(8,128)(2,1)S(1)} %copy-done.3, bf16[1024,512]{1,0:T(8,128)(2,1)} %copy-done.4, bf16[1024,512]{1,0:T(8,128)(2,1)} %copy-done.5, ...), custom_call_target="tpu_custom_call" | custom-call | flops 49999998976 | bytes 10000000 | tf_op jit(solution)/shard_map/attend_back/pallas_call | solution.py:667
  868.4 3.1 multiply_subtract_fusion
  876.1 3.7 fusion.126
  879.8 1.9 reshape.475
  883.3 3.0 pad_maximum_fusion.1
  887.4 1.9 subtract_convert_fusion
  891.2 8.0 convolution_add_fusion.1
  900.9 7.3 fusion.62
  908.3 2.4 fusion.85
  912.6 3.1 constant_dynamic-slice_fusion.1
  916.7 2.2 constant_dynamic-slice_fusion.7
  921.9 2.2 constant_dynamic-slice_fusion.3
  924.0 2.4 constant_dynamic-slice_fusion.5
  928.8 6.1 convolution_convert_fusion.3
  934.9 6.1 convolution_convert_fusion
  941.0 6.0 convolution_convert_fusion.1
  947.0 6.3 convolution_convert_fusion.2
  953.3 177.9 %collect.1 = (f32[16,128]{1,0:T(8,128)}, f32[64,2048]{1,0:T(8,128)}, f32[64,2048]{1,0:T(8,128)}, f32[64,2048]{1,0:T(8,128)}, f32[64,2048]{1,0:T(8,128)}) custom-call(f32[2,2,4,16,128]{4,3,2,1,0:T(8,128)} %bitcast.292, bf16[2,2,4,128,1024]{4,3,2,1,0:T(8,128)(2,1)} %bitcast.313, bf16[2,2,4,128,1024]{4,3,2,1,0:T(8,128)(2,1)} %bitcast.316, ...), custom_call_target="tpu_custom_call" | custom-call | flops 160000000000 | bytes 320000000 | tf_op jit(solution)/shard_map/collect/pallas_call | solution.py:317
  1134.1 2.3 convert_element_type.309
  1136.4 2.3 convert_element_type.310
  1138.8 2.5 convert_element_type.311
  (305 shorter events, 59.5 us)
Async XLA Ops:
  7.2 290.8 %all-gather.5.cloned.1.call-start = ((), (), s32[]{:S(2)}) async-start(), calls=%async_computation.4 | async-start | bytes 10485760 | tf_op jit(solution)/shard_map/all_gather | solution.py:738
  7.9 359.7 %all-gather.7.cloned.1.call-start = ((), (), s32[]{:S(2)}) async-start(), calls=%async_computation.5 | async-start | bytes 10485760 | tf_op jit(solution)/shard_map/all_gather | solution.py:738
  8.7 462.7 %all-gather.9.cloned.1.call-start = ((), (), s32[]{:S(2)}) async-start(), calls=%async_computation.6 | async-start | bytes 9437184 | tf_op jit(solution)/shard_map/all_gather | solution.py:749
  11.2 491.7 %all-gather.11.cloned.1.call-start = ((), (), s32[]{:S(2)}) async-start(), calls=%async_computation.7 | async-start | bytes 10485760 | tf_op jit(solution)/shard_map/all_gather | solution.py:739
  11.8 667.5 %reduce-scatter.5.cloned.1.call-start = ((), (), s32[]{:S(2)}) async-start(), calls=%async_computation.8 | async-start | bytes 10485760 | tf_op jit(solution)/shard_map/reduce_scatter | solution.py:808
  14.7 251.0 %copy-start.18 = (bf16[1,256,2048]{2,1,0:T(8,128)(2,1)S(1)}, bf16[1,256,2048]{2,1,0:T(8,128)(2,1)}, u32[]{:S(2)}) copy-start(bf16[1,256,2048]{2,1,0:T(8,128)(2,1)} %param.16) | copy-start | bytes 3145732
  265.7 24.8 %copy-start.55 = (f32[2048]{0:T(1024)}, f32[2048]{0:T(1024)S(1)}, u32[]{:S(2)}) copy-start(f32[2048]{0:T(1024)S(1)} %reshape.485) | copy-start | bytes 24580
  266.6 23.9 %copy-start.69 = (f32[256]{0:T(256)}, f32[256]{0:T(256)S(1)}, u32[]{:S(2)}) copy-start(f32[256]{0:T(256)S(1)} %get-tuple-element.206) | copy-start | bytes 3076
  284.1 6.4 slice-start
  294.0 63.6 %copy-start = (f32[1,1024]{1,0:T(1,128)}, f32[1,1024]{1,0:T(1,128)S(1)}, u32[]{:S(2)}) copy-start(f32[1,1024]{1,0:T(1,128)S(1)} %compare_convert_fusion.keep) | copy-start | bytes 12292
  294.1 71.6 %copy-start.50 = (f32[2048]{0:T(1024)}, f32[2048]{0:T(1024)S(1)}, u32[]{:S(2)}) copy-start(f32[2048]{0:T(1024)S(1)} %reshape.490) | copy-start | bytes 24580
  294.5 144.6 %copy-start.16 = (bf16[2048,16]{1,0:T(8,128)(2,1)}, bf16[2048,16]{1,0:T(8,128)(2,1)S(1)}, u32[]{:S(2)}) copy-start(bf16[2048,16]{1,0:T(8,128)(2,1)S(1)} %reshape.457) | copy-start | bytes 196612
  294.5 63.1 %copy-start.76 = (s32[2]{0:T(128)}, s32[2]{0:T(128)S(1)}, u32[]{:S(2)}) copy-start(s32[2]{0:T(128)S(1)} %iota_add_fusion.1) | copy-start | bytes 28
  297.8 224.6 %copy-start.42 = (pred[8,2,256]{2,1,0:T(4,128)(4,1)}, pred[8,2,256]{2,1,0:T(4,128)(4,1)S(1)}, u32[]{:S(2)}) copy-start(pred[8,2,256]{2,1,0:T(4,128)(4,1)S(1)} %compare_reduce_fusion) | copy-start | bytes 12292
  297.9 224.4 %copy-start.34 = (f32[8,2,256]{2,1,0:T(2,128)}, f32[8,2,256]{2,1,0:T(2,128)S(1)}, u32[]{:S(2)}) copy-start(f32[8,2,256]{2,1,0:T(2,128)S(1)} %copy.91) | copy-start | bytes 49156
  357.6 7.4 copy-start.2
  357.6 7.4 copy-start.4
  357.6 7.4 copy-start.5
  365.6 73.4 %copy-start.61 = (f32[256]{0:T(256)}, f32[256]{0:T(256)S(1)}, u32[]{:S(2)}) copy-start(f32[256]{0:T(256)S(1)} %get-tuple-element.212) | copy-start | bytes 3076
  542.5 241.4 %reduce-scatter.7.cloned.1.call-start = ((), (), s32[]{:S(2)}) async-start(), calls=%async_computation.9 | async-start | bytes 10485760 | tf_op jit(solution)/shard_map/reduce_scatter | solution.py:808
  585.0 281.6 %reduce-scatter.9.cloned.1.call-start = ((), (), s32[]{:S(2)}) async-start(), calls=%async_computation.10 | async-start | bytes 10485760 | tf_op jit(solution)/shard_map/reduce_scatter | solution.py:808
  585.7 343.1 %collective-permute-start.1 = (bf16[256,2048]{1,0:T(8,128)(2,1)}, bf16[256,2048]{1,0:T(8,128)(2,1)}, u32[]{:S(2)}, u32[]{:S(2)}) collective-permute-start(bf16[256,2048]{1,0:T(8,128)(2,1)} %get-tuple-element.62), channel_id=1, source_target_pairs={{0,1},{1,0},{2,3},{3,2},{4,5},{5,4},{6,7},{7,6},{8,9},{9,8},{10,11... | collective-permute-start | bytes 3145736 | tf_op jit(solution)/shard_map/ppermute | solution.py:843
  587.8 17.8 %copy-start.54 = (f32[8,2,256]{2,1,0:T(2,128)S(1)}, f32[8,2,256]{2,1,0:T(2,128)}, u32[]{:S(2)}) copy-start(f32[8,2,256]{2,1,0:T(2,128)} %get-tuple-element.164) | copy-start | bytes 49156
  587.8 17.9 %copy-start.27 = (f32[2048,16]{0,1:T(8,128)S(1)}, f32[2048,16]{0,1:T(8,128)}, u32[]{:S(2)}) copy-start(f32[2048,16]{0,1:T(8,128)} %copy-done.26) | copy-start | bytes 393220
  587.8 17.9 %copy-start.45 = (f32[2048]{0:T(1024)S(1)}, f32[2048]{0:T(1024)}, u32[]{:S(2)}) copy-start(f32[2048]{0:T(1024)} %copy-done.44) | copy-start | bytes 24580
  587.8 17.9 %copy-start.53 = (f32[2048]{0:T(1024)S(1)}, f32[2048]{0:T(1024)}, u32[]{:S(2)}) copy-start(f32[2048]{0:T(1024)} %copy-done.52) | copy-start | bytes 24580
  587.8 18.0 %copy-start.35 = (f32[8,2,256]{2,1,0:T(2,128)S(1)}, f32[8,2,256]{2,1,0:T(2,128)}, u32[]{:S(2)}) copy-start(f32[8,2,256]{2,1,0:T(2,128)} %copy-done.34) | copy-start | bytes 49156
  587.9 18.0 %copy-start.43 = (pred[8,2,256]{2,1,0:T(4,128)(4,1)S(1)}, pred[8,2,256]{2,1,0:T(4,128)(4,1)}, u32[]{:S(2)}) copy-start(pred[8,2,256]{2,1,0:T(4,128)(4,1)} %copy-done.42) | copy-start | bytes 12292
  635.0 499.0 %reduce-scatter.11.cloned.1.call-start = ((), (), s32[]{:S(2)}) async-start(), calls=%async_computation.11 | async-start | bytes 9437184 | tf_op jit(solution)/shard_map/reduce_scatter | solution.py:825
  642.1 25.3 %copy-start.17 = (bf16[2048,16]{1,0:T(8,128)(2,1)S(1)}, bf16[2048,16]{1,0:T(8,128)(2,1)}, u32[]{:S(2)}) copy-start(bf16[2048,16]{1,0:T(8,128)(2,1)} %copy-done.16) | copy-start | bytes 196612
  679.3 104.6 %copy-start.7 = (f32[256,2048]{1,0:T(8,128)S(1)}, f32[256,2048]{1,0:T(8,128)}, u32[]{:S(2)}) copy-start(f32[256,2048]{1,0:T(8,128)} %copy-done.6) | copy-start | bytes 6291460
  679.3 104.6 %copy-start.51 = (f32[2048]{0:T(1024)S(1)}, f32[2048]{0:T(1024)}, u32[]{:S(2)}) copy-start(f32[2048]{0:T(1024)} %copy-done.50) | copy-start | bytes 24580
  679.4 104.6 %copy-start.62 = (f32[256]{0:T(256)S(1)}, f32[256]{0:T(256)}, u32[]{:S(2)}) copy-start(f32[256]{0:T(256)} %copy-done.61) | copy-start | bytes 3076
  788.6 6.2 copy-start.21
  788.6 6.2 copy-start.1
  788.6 6.2 copy-start.3
  867.4 8.7 slice-start.2
  868.4 7.7 slice-start.3
  900.9 7.3 copy-start.14
  900.9 7.3 copy-start.19
  900.9 7.3 copy-start.68
  910.7 24.1 %collective-permute-start.3 = (bf16[256,2048]{1,0:T(8,128)(2,1)}, bf16[256,2048]{1,0:T(8,128)(2,1)}, u32[]{:S(2)}, u32[]{:S(2)}) collective-permute-start(bf16[256,2048]{1,0:T(8,128)(2,1)} %get-tuple-element.179), channel_id=1, source_target_pairs={{0,1},{1,0},{2,3},{3,2},{4,5},{5,4},{6,7},{7,6},{8,9},{9,8},{10,11... | collective-permute-start | bytes 3145736 | tf_op jit(solution)/shard_map/ppermute | solution.py:843
  916.7 18.2 %collective-permute-start.6 = (bf16[256,1024]{1,0:T(8,128)(2,1)}, bf16[256,1024]{1,0:T(8,128)(2,1)}, u32[]{:S(2)}, u32[]{:S(2)}) collective-permute-start(bf16[256,1024]{1,0:T(8,128)(2,1)} %bitcast.255), channel_id=1, source_target_pairs={{0,1},{1,0},{2,3},{3,2},{4,5},{5,4},{6,7},{7,6},{8,9},{9,8},{10,11... | collective-permute-start | bytes 1572872 | tf_op jit(solution)/shard_map/ppermute | solution.py:843
  919.8 9.0 collective-permute-start.2
  921.8 5.7 collective-permute-start
  927.5 13.5 %collective-permute-start.5 = (bf16[256,1024]{1,0:T(8,128)(2,1)S(1)}, bf16[256,1024]{1,0:T(8,128)(2,1)S(1)}, u32[]{:S(2)}, u32[]{:S(2)}) collective-permute-start(bf16[256,1024]{1,0:T(8,128)(2,1)S(1)} %bitcast.288), channel_id=1, source_target_pairs={{0,1},{1,0},{2,3},{3,2},{4,5},{5,4},{6,7},{7,6},{8,9},{9,8},{10,11... | collective-permute-start | bytes 1572872 | tf_op jit(solution)/shard_map/ppermute | solution.py:843
  928.8 18.2 %collective-permute-start.4 = (bf16[256,1024]{1,0:T(8,128)(2,1)S(1)}, bf16[256,1024]{1,0:T(8,128)(2,1)S(1)}, u32[]{:S(2)}, u32[]{:S(2)}) collective-permute-start(bf16[256,1024]{1,0:T(8,128)(2,1)S(1)} %bitcast.286), channel_id=1, source_target_pairs={{0,1},{1,0},{2,3},{3,2},{4,5},{5,4},{6,7},{7,6},{8,9},{9,8},{10,11... | collective-permute-start | bytes 1572872 | tf_op jit(solution)/shard_map/ppermute | solution.py:843
  953.3 180.8 %copy-start.29 = (bf16[2,2048,256]{2,1,0:T(8,128)(2,1)S(1)}, bf16[2,2048,256]{2,1,0:T(8,128)(2,1)}, u32[]{:S(2)}) copy-start(bf16[2,2048,256]{2,1,0:T(8,128)(2,1)} %reduce-scatter.7.cloned.1.call-done) | copy-start | bytes 6291460
  (54 other events, 112.7 us)
Sparse Core Ops, SparseCore 0:
  9.8 156.5 all-gather.4
  168.2 122.8 all-gather.6
  293.3 78.6 all-gather.8
  373.8 89.1 all-gather.10
  542.6 94.3 reduce-scatter.4
  640.2 86.3 reduce-scatter.6
  729.7 99.6 reduce-scatter.8
  922.0 87.7 reduce-scatter.10

commit v3 on v2

--- a/solution.py
+++ b/solution.py
@@ -48,10 +48,52 @@
 RING, SIDE_B, SIDE_A, FIRST, SECOND, CORE_OWN, CORE_B, CORE_A, CORE_FIRST, CORE_SECOND = range(10)
 
 
-def spread_kernel(count, *refs):
+def along(step):
+    ring, r = lax.axis_size("ring"), lax.axis_index("ring")
+    to_next, to_last = {"ring": turn("ring", 1)}, {"ring": turn("ring", ring - 1)}
+    return (
+        ((r + 1 < ring) & (r >= step), r >= step + 1, lax.rem(r + ring - step, ring), lax.rem(r + ring - 1 - step, ring), to_next, 0),
+        ((r >= 1) & (r + step < ring), r + 1 + step < ring, lax.rem(r + step, ring), lax.rem(r + 1 + step, ring), to_last, 1),
+    )
+
+
+def send_along(step, own, block_of, send, got):
+    for sent, _, block, _, to, side in along(step):
+
+        @pl.when(sent)
+        def _(block=block, to=to, side=side):
+            push(own if step == 0 else block_of(block), block_of(block), send.at[side, step], got.at[side, step], to)
+
+
+def take_along(step, block_of, got, then):
+    for _, comes, _, block, _, side in along(step):
+
+        @pl.when(comes)
+        def _(block=block, side=side):
+            await_bytes(block_of(block), got.at[side, step])
+
+    for _, comes, _, block, _, side in along(step):
+
+        @pl.when(comes)
+        def _(block=block):
+            then(block)
+
+
+def sent_along(own, send):
     ring = lax.axis_size("ring")
-    shards, ids, outs, ids_out = refs[:count], refs[count], refs[count + 1 : 2 * count + 1], refs[2 * count + 1]
-    send, got_ring, got_b, got_a, got, place, ids_send, ids_got, ids_place = refs[2 * count + 2 :]
+    for step in range(ring - 1):
+        for sent, _, _, _, _, side in along(step):
+
+            @pl.when(sent)
+            def _(side=side):
+                await_bytes(own, send.at[side, step])
+
+
+def spread_kernel(count, tables, *refs):
+    ring = lax.axis_size("ring")
+    ins, refs = refs[: count + tables], refs[count + tables :]
+    outs, sems = refs[: count + tables], refs[count + tables :]
+    send, send_ring, got_ring, got_b, got_a, got, place, core_sem = sems
     a, b, r, c = (lax.axis_index(n) for n in ALL)
     na, nb, nc = turn("ca", 1), turn("cb", 1), turn("core", 1)
     to_a, to_b, to_core = {"ca": na}, {"cb": nb}, {"core": nc}
@@ -69,34 +111,32 @@
             return ref.at[:, :, pl.ds(which * (cols // 2), cols // 2)]
         return ref.at[:, pl.ds(which * (rows // 2), rows // 2), :]
 
-    for w in range(count):
-        out = outs[w]
-        pltpu.make_async_copy(shards[w], out.at[a, b, r, c], place.at[w]).start()
-    pltpu.make_async_copy(ids, ids_out.at[r, c], ids_place).start()
-    push(ids, ids_out.at[r, c], ids_send.at[ring], ids_got.at[ring], to_core)
+    def place_of(w):
+        return (lambda at: outs[w].at[a, b, at, c]) if w < count else (lambda at: outs[w].at[at, c])
+
+    for w in range(count + tables):
+        pltpu.make_async_copy(ins[w], place_of(w)(r), place.at[w]).start()
     for w in reversed(range(count)):
-        out = outs[w]
-        for k in range(1, ring):
-            push(shards[w], out.at[a, b, r, c], send.at[w, RING], got_ring.at[w, k], {"ring": turn("ring", k)})
-        push(shards[w], out.at[a, b, r, c], send.at[w, SIDE_B], got_b.at[w, 0], to_b)
-        push(shards[w], out.at[a, b, r, c], send.at[w, SIDE_A], got_a.at[w, 0], to_a)
-        push(shards[w], out.at[a, b, r, c], send.at[w, CORE_OWN], got.at[w, CORE_OWN], to_core)
-    for k in range(1, ring):
-        push(ids, ids_out.at[r, c], ids_send.at[k], ids_got.at[k], {"ring": turn("ring", k)})
+        send_along(0, ins[w], place_of(w), send_ring.at[w], got_ring.at[w])
+        here = place_of(w)(r)
+        push(ins[w], here, send.at[w, SIDE_B], got_b.at[w, r], to_b)
+        push(ins[w], here, send.at[w, SIDE_A], got_a.at[w, r], to_a)
+        push(ins[w], here, send.at[w, CORE_OWN], got.at[w, CORE_OWN], to_core)
+    for t in range(tables):
+        push(ins[count + t], place_of(count + t)(r), core_sem.at[t, 0], core_sem.at[t, 1], to_core)
 
     def sides(w):
-        out = outs[w]
-
-        def one(k, carry):
-            at = lax.rem(r + ring - k, ring)
-            block = out.at[a, b, at, c]
-            await_bytes(block, got_ring.at[w, k])
-            push(block, block, send.at[w, SIDE_B], got_b.at[w, k], to_b)
-            push(block, block, send.at[w, SIDE_A], got_a.at[w, k], to_a)
-            push(block, block, send.at[w, CORE_OWN], got.at[w, CORE_OWN], to_core)
-            return carry
-
-        lax.fori_loop(1, ring, one, 0)
+        for step in range(ring - 1):
+
+            def on(at):
+                block = place_of(w)(at)
+                push(block, block, send.at[w, SIDE_B], got_b.at[w, at], to_b)
+                push(block, block, send.at[w, SIDE_A], got_a.at[w, at], to_a)
+                push(block, block, send.at[w, CORE_OWN], got.at[w, CORE_OWN], to_core)
+
+            take_along(step, place_of(w), got_ring.at[w], on)
+            if step + 1 < ring - 1:
+                send_along(step + 1, ins[w], place_of(w), send_ring.at[w], got_ring.at[w])
 
     def diagonal(w):
         out = outs[w]
@@ -104,11 +144,11 @@
         def one(k, carry):
             at = lax.rem(r + ring - k, ring)
             block = out.at[a, nb, at, c]
-            await_bytes(block, got_b.at[w, k])
+            await_bytes(block, got_b.at[w, at])
             push(half(block, 0), half(block, 0), send.at[w, FIRST], got.at[w, FIRST], to_a)
             push(block, block, send.at[w, CORE_B], got.at[w, CORE_B], to_core)
             block = out.at[na, b, at, c]
-            await_bytes(block, got_a.at[w, k])
+            await_bytes(block, got_a.at[w, at])
             push(half(block, 1), half(block, 1), send.at[w, SECOND], got.at[w, SECOND], to_b)
             push(block, block, send.at[w, CORE_A], got.at[w, CORE_A], to_core)
             return carry
@@ -122,27 +162,37 @@
             await_bytes(part, got.at[w, kind])
             push(part, part, send.at[w, core_kind], got.at[w, core_kind], to_core)
 
+    def table_step(t, step):
+        w = count + t
+
+        def on(at):
+            push(place_of(w)(at), place_of(w)(at), core_sem.at[t, 0], core_sem.at[t, 1], to_core)
+
+        if step >= 0:
+            take_along(step, place_of(w), got_ring.at[w], on)
+        if step + 1 < ring - 1:
+            send_along(step + 1, ins[w], place_of(w), send_ring.at[w], got_ring.at[w])
+
     order = list(reversed(range(count)))
     for step in range(count + 2):
         if step < count:
             sides(order[step])
+        if step >= count - 1:
+            for t in range(tables):
+                table_step(t, step - count)
         if 0 <= step - 1 < count:
             diagonal(order[step - 1])
         if 0 <= step - 2 < count:
             last(order[step - 2])
-
-    def ids_on(k, carry):
-        block = ids_out.at[lax.rem(r + ring - k, ring), c]
-        await_bytes(block, ids_got.at[k])
-        push(block, block, ids_send.at[ring], ids_got.at[ring], to_core)
-        return carry
-
-    lax.fori_loop(1, ring, ids_on, 0)
+    for step in range(2, ring - 1):
+        for t in range(tables):
+            table_step(t, step)
+
     for w in range(count):
         out = outs[w]
-        pltpu.make_async_copy(shards[w], out.at[a, b, r, c], place.at[w]).wait()
         mine = lambda p, q: out.at[p, q, :, c]
-        await_bytes(out.at[a, b, pl.ds(0, ring - 1), c], send.at[w, RING])
+        await_bytes(ins[w], place.at[w])
+        sent_along(ins[w], send_ring.at[w])
         for kind in (SIDE_B, SIDE_A, CORE_OWN, CORE_B, CORE_A):
             await_bytes(mine(a, b), send.at[w, kind])
         for which, kind in ((0, FIRST), (1, SECOND), (0, CORE_FIRST), (1, CORE_SECOND)):
@@ -151,44 +201,108 @@
             await_bytes(out.at[p, q, :, nc], got.at[w, kind])
         for which, kind in ((0, CORE_FIRST), (1, CORE_SECOND)):
             await_bytes(halves(out.at[na, nb, :, nc], which), got.at[w, kind])
-    pltpu.make_async_copy(ids, ids_out.at[r, c], ids_place).wait()
-    for k in range(1, ring):
-        await_bytes(ids, ids_send.at[k])
-    await_bytes(ids_out.at[:, c], ids_send.at[ring])
-    await_bytes(ids_out.at[:, nc], ids_got.at[ring])
-
-
-def spread(shards, ids):
-    count, ring = len(shards), lax.axis_size("ring")
+    for t in range(tables):
+        w = count + t
+        await_bytes(ins[w], place.at[w])
+        sent_along(ins[w], send_ring.at[w])
+        await_bytes(outs[w].at[:, c], core_sem.at[t, 0])
+        await_bytes(outs[w].at[:, nc], core_sem.at[t, 1])
+
+
+def spread(shards, tables):
+    count, more, ring = len(shards), len(tables), lax.axis_size("ring")
     square = (lax.axis_size("ca"), lax.axis_size("cb"), ring, 2)
     dma = pltpu.SemaphoreType.DMA
     outs = pl.pallas_call(
-        functools.partial(spread_kernel, count),
+        functools.partial(spread_kernel, count, more),
         out_shape=[jax.ShapeDtypeStruct(square + s.shape, s.dtype) for s in shards]
-        + [jax.ShapeDtypeStruct((ring, 2) + ids.shape, ids.dtype)],
-        in_specs=[pl.BlockSpec(memory_space=pltpu.VMEM)] * (count + 1),
-        out_specs=[pl.BlockSpec(memory_space=pl.ANY)] * (count + 1),
+        + [jax.ShapeDtypeStruct((ring, 2) + t.shape, t.dtype) for t in tables],
+        in_specs=[pl.BlockSpec(memory_space=pltpu.VMEM)] * (count + more),
+        out_specs=[pl.BlockSpec(memory_space=pl.ANY)] * (count + more),
         scratch_shapes=[
-            dma((count, 10)), dma((count, ring)), dma((count, ring)), dma((count, ring)), dma((count, 10)), dma((count,)),
-            dma((ring + 1,)), dma((ring + 1,)), dma,
+            dma((count, 10)), dma((count + more, 2, ring)), dma((count + more, 2, ring)), dma((count, ring)), dma((count, ring)),
+            dma((count, 10)), dma((count + more,)), dma((more, 2)),
         ],
         compiler_params=pltpu.CompilerParams(collective_id=0, has_side_effects=True),
         cost_estimate=pl.CostEstimate(flops=150_000_000_000, bytes_accessed=300_000_000, transcendentals=0),
         name="spread",
-    )(*shards, ids)
-    return outs[:count], outs[count]
+    )(*shards, *tables)
+    return outs[:count], outs[count:]
 
 
 def collect_kernel(count, *refs):
     ring = lax.axis_size("ring")
-    parts, outs = refs[:count], refs[count : 2 * count]
-    scratch = refs[2 * count :]
+    parts, refs = refs[:count], refs[count:]
+    grads, matrices, (x, gain, passed), refs = refs[:3], refs[3:6], refs[6:9], refs[9:]
+    outs, (input_grad, gain_out), refs = refs[:count], refs[count : count + 2], refs[count + 2 :]
+    scratch, refs = refs[: 9 * count], refs[9 * count :]
+    send, got, ring_send, ring_got, load, chunks, dn1, sums, arrived, ring_arrived, fetch, gain_send, gain_got = refs
     a, b, r, c = (lax.axis_index(n) for n in ALL)
     na, nb, nc = turn("ca", 1), turn("cb", 1), turn("core", 1)
     to_a, to_b, to_core = {"ca": na}, {"cb": nb}, {"core": nc}
-    send, got, ring_send, ring_got, load = scratch[-5:]
     bufs = [scratch[9 * w : 9 * w + 9] for w in range(count)]
     greet([to_a, to_b, to_core] + [{"ring": turn("ring", k)} for k in range(1, ring)])
+
+    def chunk(i, slot, w):
+        rows = chunks.shape[2]
+        return pltpu.make_async_copy(
+            matrices[w].at[pl.ds(pl.multiple_of(i * rows, rows), rows), :], chunks.at[slot, w], fetch.at[slot, w]
+        )
+
+    def input_side():
+        steps, rows = matrices[0].shape[0] // chunks.shape[2], chunks.shape[2]
+
+        def one(i, carry):
+            slot = lax.rem(i, 2)
+
+            @pl.when(i + 1 < steps)
+            def _():
+                for w in range(3):
+                    chunk(i + 1, 1 - slot, w).start()
+
+            value = jnp.zeros((x.shape[0], rows), jnp.float32)
+            for w in range(3):
+                chunk(i, slot, w).wait()
+                value = value + times_transposed(grads[w][...], chunks[slot, w])
+            dn1[:, pl.ds(pl.multiple_of(i * rows, rows), rows)] = value
+            return carry
+
+        lax.fori_loop(0, steps, one, 0)
+        tile = 32
+        sums[0] = jnp.zeros(sums.shape[1:], jnp.float32)
+
+        def back(i, carry):
+            at = pl.ds(pl.multiple_of(i * tile, tile), tile)
+            v, grad = x[at, :].astype(jnp.float32), dn1[at, :]
+            factor = lax.rsqrt(jnp.mean(v * v, axis=-1, keepdims=True) + EPSILON)
+            weighted = grad * gain[...]
+            inner = jnp.mean(weighted * v, axis=-1, keepdims=True)
+            total = passed[at, :] + factor * weighted - v * (factor * factor * factor * inner)
+            input_grad[at, :] = total.astype(input_grad.dtype)
+            gained = grad * v * factor
+            sums[0] += sum(gained[k : k + 8] for k in range(0, tile, 8))
+            return carry
+
+        lax.fori_loop(0, x.shape[0] // tile, back, 0)
+        push(sums.at[0], arrived.at[0], gain_send.at[0], gain_got.at[0], to_a)
+
+    def gain_stage(stage):
+        if stage < 3:
+            await_bytes(arrived.at[stage], gain_got.at[stage])
+            sums[stage + 1] = sums[stage] + arrived[stage]
+            if stage < 2:
+                push(sums.at[stage + 1], arrived.at[stage + 1], gain_send.at[stage + 1], gain_got.at[stage + 1], (to_b, to_core)[stage])
+            else:
+                for k in range(1, ring):
+                    push(sums.at[3], ring_arrived.at[k - 1], gain_send.at[2 + k], gain_got.at[2 + k], {"ring": turn("ring", k)})
+        else:
+            total = sums[3]
+            for k in range(1, ring):
+                await_bytes(ring_arrived.at[k - 1], gain_got.at[2 + k])
+                total = total + ring_arrived[k - 1]
+            gain_out[...] = total
+            for k in range(3 + ring - 1):
+                await_bytes(sums.at[0], gain_send.at[k])
 
     def half(ref, which):
         rows, cols = ref.shape[-2:]
@@ -283,21 +397,28 @@
             await_bytes(final.at[0], got.at[w, 4])
             await_bytes(final.at[0], load.at[w, 2])
 
+    for w in range(3):
+        chunk(0, 0, w).start()
     first(0)
+    first(1)
+    first(2)
+    input_side()
     for step in range(count + 3):
-        if step + 1 < count:
-            first(step + 1)
+        if 0 < step and step + 2 < count:
+            first(step + 2)
         if step < count:
             second(step)
         if 0 <= step - 1 < count:
             third(step - 1)
         if 0 <= step - 2 < count:
             fourth(step - 2)
+        if 1 <= step < 5:
+            gain_stage(step - 1)
     for w in range(count):
         finish(w)
 
 
-def collect(parts, small):
+def collect(parts, small, grads, matrices, x, gain, passed):
     count, ring = len(parts) + 1, lax.axis_size("ring")
     chips = lax.axis_size("ca") * lax.axis_size("cb") * ring
     square = (lax.axis_size("ca"), lax.axis_size("cb"), ring)
@@ -314,135 +435,64 @@
         scratch += [pltpu.VMEM((2, rows // 2, cols) if big else (1, 8, 128), jnp.float32)]
         shapes.append(jax.ShapeDtypeStruct((rows // 2, 2 * cols) if big else (rows, cols), jnp.float32))
     dma = pltpu.SemaphoreType.DMA
+    vm, anywhere = pl.BlockSpec(memory_space=pltpu.VMEM), pl.BlockSpec(memory_space=pl.ANY)
+    wide = (8, gain.shape[1])
+    f32 = lambda *shape: pltpu.VMEM(shape, jnp.float32)
     outs = pl.pallas_call(
         functools.partial(collect_kernel, count),
-        out_shape=shapes,
-        in_specs=[pl.BlockSpec(memory_space=pl.ANY)] * count,
-        out_specs=[pl.BlockSpec(memory_space=pltpu.VMEM)] * count,
+        out_shape=shapes + [jax.ShapeDtypeStruct(x.shape, x.dtype), jax.ShapeDtypeStruct(wide, jnp.float32)],
+        in_specs=[anywhere] * count + [vm] * 3 + [anywhere] * 3 + [vm] * 3,
+        out_specs=[vm] * (count + 2),
         scratch_shapes=scratch
-        + [dma((count, 5)), dma((count, 5)), dma((count, ring - 1)), dma((count, ring - 1)), dma((count, 3))],
-        compiler_params=pltpu.CompilerParams(collective_id=1, has_side_effects=True, vmem_limit_bytes=60 << 20),
-        cost_estimate=pl.CostEstimate(flops=160000000000, bytes_accessed=320000000, transcendentals=0),
+        + [dma((count, 5)), dma((count, 5)), dma((count, ring - 1)), dma((count, ring - 1)), dma((count, 3))]
+        + [pltpu.VMEM((2, 3, 256, x.shape[1]), x.dtype), f32(*x.shape), f32(4, *wide), f32(3, *wide), f32(ring - 1, *wide)]
+        + [dma((2, 3)), dma((2 + ring,)), dma((2 + ring,))],
+        compiler_params=pltpu.CompilerParams(collective_id=1, has_side_effects=True, vmem_limit_bytes=62 << 20),
+        cost_estimate=pl.CostEstimate(flops=160_000_000_000, bytes_accessed=320_000_000, transcendentals=0),
         name="collect",
-    )(*views)
-    return outs[1:], outs[0]
-
-
-def dispatch_kernel(down, *refs):
-    ring, count = lax.axis_size("ring"), len(down)
-    rows, weights, rows_out, weights_out = refs[0], refs[1 : count + 1], refs[count + 1], refs[count + 2 : 2 * count + 2]
-    held_rows, held = refs[2 * count + 2], refs[2 * count + 3 : 3 * count + 3]
-    load, place, send_ring, got_ring, core_sem, send_side, got_side, send_diag, got_diag = refs[3 * count + 3 :]
-    a, b, r, c = (lax.axis_index(n) for n in ALL)
-    na, nb, nc = turn("ca", 1), turn("cb", 1), turn("core", 1)
-    to_a, to_b, to_core = {"ca": na}, {"cb": nb}, {"core": nc}
-    greet([to_a, to_b, to_core] + [{"ring": turn("ring", k)} for k in range(1, ring)])
-
-    def slot(w, e, p, q):
-        units = weights[w].shape[1 if down[w] else 2]
-        at = pl.ds(pl.multiple_of((2 * p + q) * units, units), units)
-        return weights_out[w].at[e, at, :] if down[w] else weights_out[w].at[e, :, at]
-
-    fetch_rows = pltpu.make_async_copy(rows, held_rows, load.at[count])
-    fetch_rows.start()
-    fetches = [pltpu.make_async_copy(weights[w], held[w], load.at[w]) for w in range(count)]
-    for fetch in fetches:
-        fetch.start()
-    fetch_rows.wait()
-    pltpu.make_async_copy(held_rows, rows_out.at[r, c], place.at[count]).start()
-    to_next, to_last = {"ring": turn("ring", 1)}, {"ring": turn("ring", ring - 1)}
-
-    def along(step):
-        return (
-            ((r + 1 < ring) & (r >= step), r >= step + 1, lax.rem(r + ring - step, ring), lax.rem(r + ring - 1 - step, ring), to_next, 0),
-            ((r >= 1) & (r + step < ring), r + 1 + step < ring, lax.rem(r + step, ring), lax.rem(r + 1 + step, ring), to_last, 1),
-        )
-
-    def send_along(step):
-        for sent, _, block, _, to, side in along(step):
-
-            @pl.when(sent)
-            def _(block=block, to=to, side=side):
-                src = held_rows if step == 0 else rows_out.at[block, c]
-                push(src, rows_out.at[block, c], send_ring.at[side, step], got_ring.at[side, step], to)
-
-    send_along(0)
-    push(held_rows, rows_out.at[r, c], core_sem.at[0], core_sem.at[1], to_core)
-    for w in range(count):
-        fetches[w].wait()
-        for e in range(weights[w].shape[0]):
-            mine, here = held[w].at[e], slot(w, e, a, b)
-            push(mine, here, send_side.at[w, 0, e], got_side.at[w, 0, e], to_b)
-            push(mine, here, send_side.at[w, 1, e], got_side.at[w, 1, e], to_a)
-            pltpu.make_async_copy(mine, here, place.at[w]).start()
+    )(*views, *grads, *matrices, x, gain, passed)
+    return outs[1:count], outs[0], outs[count], outs[count + 1]
+
+
+def dispatch_kernel(rows, out, send, got, place, core_send, core_got):
+    ring, r, c, nc = lax.axis_size("ring"), lax.axis_index("ring"), lax.axis_index("core"), turn("core", 1)
+    to_core = {"core": nc}
+    greet([to_core] + [{"ring": turn("ring", k)} for k in range(1, ring)])
+    block_of = lambda at: out.at[at, c]
+    own = pltpu.make_async_copy(rows, block_of(r), place)
+    own.start()
+    send_along(0, rows, block_of, send, got)
+    push(rows, block_of(r), core_send, core_got, to_core)
+
+    def on(at):
+        push(block_of(at), block_of(at), core_send, core_got, to_core)
 
     for step in range(ring - 1):
-        for _, comes, _, block, _, side in along(step):
-
-            @pl.when(comes)
-            def _(block=block, side=side):
-                await_bytes(rows_out.at[block, c], got_ring.at[side, step])
-
         if step + 1 < ring - 1:
-            send_along(step + 1)
-        for _, comes, _, block, _, side in along(step):
-
-            @pl.when(comes)
-            def _(block=block):
-                here = rows_out.at[block, c]
-                push(here, here, core_sem.at[0], core_sem.at[1], to_core)
-
-    for w in range(count):
-        experts = weights[w].shape[0]
-        for e in range(experts):
-            from_b, from_a = slot(w, e, a, nb), slot(w, e, na, b)
-            await_bytes(from_b, got_side.at[w, 0, e])
-            await_bytes(from_a, got_side.at[w, 1, e])
-            if 2 * e < experts:
-                push(from_b, from_b, send_diag.at[w, e], got_diag.at[w, e], to_a)
-            else:
-                push(from_a, from_a, send_diag.at[w, e], got_diag.at[w, e], to_b)
-
-    await_bytes(held_rows, place.at[count])
-    for step in range(ring - 1):
-        for sent, _, _, _, _, side in along(step):
-
-            @pl.when(sent)
-            def _(side=side):
-                await_bytes(held_rows, send_ring.at[side, step])
-
-    await_bytes(rows_out.at[:, c], core_sem.at[0])
-    await_bytes(rows_out.at[:, nc], core_sem.at[1])
-    for w in range(count):
-        await_bytes(held[w], place.at[w])
-        for e in range(weights[w].shape[0]):
-            await_bytes(held[w].at[e], send_side.at[w, 0, e])
-            await_bytes(held[w].at[e], send_side.at[w, 1, e])
-            await_bytes(held[w].at[e], send_diag.at[w, e])
-            await_bytes(slot(w, e, na, nb), got_diag.at[w, e])
-
-
-def dispatch(rows, weights, down):
-    ring, chips = lax.axis_size("ring"), lax.axis_size("ca") * lax.axis_size("cb")
-    experts, count = max([w.shape[0] for w in weights], default=1), len(weights)
-    full = [(w.shape[0], w.shape[1] * (chips if d else 1), w.shape[2] * (1 if d else chips)) for w, d in zip(weights, down)]
-    dma = pltpu.SemaphoreType.DMA
-    outs = pl.pallas_call(
-        functools.partial(dispatch_kernel, tuple(down)),
-        out_shape=[jax.ShapeDtypeStruct((ring, 2) + rows.shape, rows.dtype)]
-        + [jax.ShapeDtypeStruct(shape, rows.dtype) for shape in full],
-        in_specs=[pl.BlockSpec(memory_space=pl.ANY)] * (count + 1),
-        out_specs=[pl.BlockSpec(memory_space=pl.ANY)] * (count + 1),
-        scratch_shapes=[pltpu.VMEM(v.shape, v.dtype) for v in (rows, *weights)]
-        + [
-            dma((1 + count,)), dma((1 + count,)), dma((2, ring)), dma((2, ring)), dma((2,)),
-            dma((max(count, 1), 2, experts)), dma((max(count, 1), 2, experts)), dma((max(count, 1), experts)), dma((max(count, 1), experts)),
-        ],
+            take_along(step, block_of, got, lambda at: None)
+            send_along(step + 1, rows, block_of, send, got)
+            for _, comes, _, block, _, _ in along(step):
+                pl.when(comes)(functools.partial(on, block))
+        else:
+            take_along(step, block_of, got, on)
+    own.wait()
+    sent_along(rows, send)
+    await_bytes(out.at[:, c], core_send)
+    await_bytes(out.at[:, nc], core_got)
+
+
+def dispatch(rows):
+    ring, dma = lax.axis_size("ring"), pltpu.SemaphoreType.DMA
+    return pl.pallas_call(
+        dispatch_kernel,
+        out_shape=jax.ShapeDtypeStruct((ring, 2) + rows.shape, rows.dtype),
+        in_specs=[pl.BlockSpec(memory_space=pltpu.VMEM)],
+        out_specs=pl.BlockSpec(memory_space=pl.ANY),
+        scratch_shapes=[dma((2, ring)), dma((2, ring)), dma, dma, dma],
         compiler_params=pltpu.CompilerParams(collective_id=2, has_side_effects=True),
-        cost_estimate=pl.CostEstimate(flops=80_000_000_000, bytes_accessed=100_000_000, transcendentals=0),
+        cost_estimate=pl.CostEstimate(flops=1_000_000, bytes_accessed=10_000, transcendentals=0),
         name="dispatch",
-    )(rows, *weights)
-    return outs[0], outs[1:]
+    )(rows)
 
 
 def give_back_kernel(part, out, own, core_in, ring_in, load, core_send, core_got, ring_send, ring_got):
@@ -546,12 +596,64 @@
         await_bytes(here(corner(da, db)[0]), got.at[i])
 
 
-def attend_kernel(scale, q, k, v, keep, o, qh, kh, vh, logs, oh, send, got, place, send_o, got_o, place_o):
-    rows, width = q.shape[0], qh.shape[1]
+def swap_halves(v):
+    return pltpu.roll(v, HD // 2, 1)
+
+
+def norm_and_turn(raw, gain, cosine, sine, out):
+    rows, width = raw.shape
+    tile = 32
+
+    def part(i, carry):
+        at = pl.ds(pl.multiple_of(i * tile, tile), tile)
+        value = raw[at, :]
+        factor = lax.rsqrt(jnp.mean(value * value, axis=-1, keepdims=True) + EPSILON)
+        for h in range(width // HD):
+            lanes = pl.ds(h * HD, HD)
+            v = raw[at, lanes] * factor * gain[:, lanes]
+            out[at, lanes] = (v * cosine[at, :] + swap_halves(v) * sine[at, :]).astype(out.dtype)
+        return carry
+
+    lax.fori_loop(0, rows // tile, part, 0)
+
+
+def norm_and_turn_back(grad, raw, gain, cosine, sine, out, gain_grad, turned):
+    rows, width = raw.shape
+    tile = 32
+    gain_grad[...] = jnp.zeros_like(gain_grad)
+
+    def part(i, carry):
+        at = pl.ds(pl.multiple_of(i * tile, tile), tile)
+        value = raw[at, :]
+        factor = lax.rsqrt(jnp.mean(value * value, axis=-1, keepdims=True) + EPSILON)
+        inner = jnp.zeros((tile, HD), jnp.float32)
+        for h in range(width // HD):
+            lanes = pl.ds(h * HD, HD)
+            g = grad[at, lanes].astype(jnp.float32)
+            g = g * cosine[at, :] - swap_halves(g) * sine[at, :]
+            turned[:, lanes] = g
+            inner = inner + g * gain[:, lanes] * raw[at, lanes]
+        inner = jnp.sum(inner, axis=-1, keepdims=True) * (factor * factor * factor / width)
+        for h in range(width // HD):
+            lanes = pl.ds(h * HD, HD)
+            g, v = turned[:, lanes], raw[at, lanes]
+            out[at, lanes] = (factor * (g * gain[:, lanes]) - v * inner).astype(out.dtype)
+            gained = g * v * factor
+            gain_grad[:, lanes] += sum(gained[k : k + 8] for k in range(0, tile, 8))
+        return carry
+
+    lax.fori_loop(0, rows // tile, part, 0)
+
+
+def attend_kernel(scale, q_raw, k_raw, v, q_gain, k_gain, cosine, sine, keep, o, qh, kh, vh, logs, q, k, oh, send, got, place, send_o, got_o, place_o):
+    rows, width = v.shape[0], qh.shape[1]
     greet([corner(da, db)[1] for da, db in corners()])
-    pairs = ((q, qh), (k, kh), (v, vh))
-    for i, (src, dst) in enumerate(pairs):
-        rows_to_heads(src, dst, send.at[i], got.at[i], place.at[i])
+    pairs = ((v, vh), (k, kh), (q, qh))
+    rows_to_heads(v, vh, send.at[0], got.at[0], place.at[0])
+    norm_and_turn(k_raw, k_gain, cosine, sine, k)
+    rows_to_heads(k, kh, send.at[1], got.at[1], place.at[1])
+    norm_and_turn(q_raw, q_gain, cosine, sine, q)
+    rows_to_heads(q, qh, send.at[2], got.at[2], place.at[2])
     for i, (src, dst) in enumerate(pairs):
         wait_heads(src, dst, got.at[i], place.at[i])
     me, _ = corner(0, 0)
@@ -590,26 +692,30 @@
             await_bytes(piece, send.at[j, i])
 
 
-def attend(q, k, v, keep, scale):
-    rows, width = q.shape
+def attend(q_raw, k_raw, v, q_gain, k_gain, cosine, sine, keep, scale):
+    rows, width = v.shape
     chips = lax.axis_size("ca") * lax.axis_size("cb")
-    heads = jax.ShapeDtypeStruct((rows * chips, width // chips), q.dtype)
+    heads = jax.ShapeDtypeStruct((rows * chips, width // chips), v.dtype)
     vm, dma = pl.BlockSpec(memory_space=pltpu.VMEM), pltpu.SemaphoreType.DMA
     return pl.pallas_call(
         functools.partial(attend_kernel, scale),
-        out_shape=[jax.ShapeDtypeStruct(q.shape, q.dtype), heads, heads, heads]
+        out_shape=[jax.ShapeDtypeStruct(v.shape, v.dtype), heads, heads, heads]
         + [jax.ShapeDtypeStruct((width // chips // HD, rows * chips, 1), jnp.float32)],
-        in_specs=[vm] * 4,
+        in_specs=[vm] * 8,
         out_specs=[vm] * 5,
-        scratch_shapes=[pltpu.VMEM(heads.shape, q.dtype)]
+        scratch_shapes=[pltpu.VMEM(v.shape, v.dtype)] * 2 + [pltpu.VMEM(heads.shape, v.dtype)]
         + [dma((3, 3)), dma((3, 3)), dma((3,)), dma((3,)), dma((3,)), dma],
         compiler_params=pltpu.CompilerParams(collective_id=4, has_side_effects=True, vmem_limit_bytes=48 << 20),
         cost_estimate=pl.CostEstimate(flops=1_000_000, bytes_accessed=10_000, transcendentals=0),
         name="attend",
-    )(q, k, v, keep)
-
-
-def attend_back_kernel(scale, do, qh, kh, vh, logs, keep, dq, dk, dv, doh, dqh, dkh, dvh, send, got, place, send_g, got_g, place_g):
+    )(q_raw, k_raw, v, q_gain, k_gain, cosine, sine, keep)
+
+
+def attend_back_kernel(
+    scale, do, qh, kh, vh, logs, keep, q_raw, k_raw, q_gain, k_gain, cosine, sine,
+    dq_raw, dk_raw, dv, q_gain_grad, k_gain_grad,
+    doh, dqh, dkh, dvh, dq, dk, turned, send, got, place, send_g, got_g, place_g,
+):
     rows, width = do.shape[0], qh.shape[1]
     greet([corner(da, db)[1] for da, db in corners()])
     rows_to_heads(do, doh, send, got, place)
@@ -659,22 +765,26 @@
                 await_bytes(piece, got_g.at[g, i, h])
     for i in range(3):
         await_bytes(do.at[:, pl.ds(0, width)], send.at[i])
-
-
-def attend_back(do, qh, kh, vh, logs, keep, scale):
+    norm_and_turn_back(dk, k_raw, k_gain, cosine, sine, dk_raw, k_gain_grad, turned)
+    norm_and_turn_back(dq, q_raw, q_gain, cosine, sine, dq_raw, q_gain_grad, turned)
+
+
+def attend_back(do, qh, kh, vh, logs, keep, q_raw, k_raw, q_gain, k_gain, cosine, sine, scale):
     heads = qh.shape[1] // HD
     vm, dma = pl.BlockSpec(memory_space=pltpu.VMEM), pltpu.SemaphoreType.DMA
     return pl.pallas_call(
         functools.partial(attend_back_kernel, scale),
-        out_shape=[jax.ShapeDtypeStruct(do.shape, do.dtype)] * 3,
-        in_specs=[vm] * 6,
-        out_specs=[vm] * 3,
+        out_shape=[jax.ShapeDtypeStruct(do.shape, do.dtype)] * 3 + [jax.ShapeDtypeStruct((8, do.shape[1]), jnp.float32)] * 2,
+        in_specs=[vm] * 12,
+        out_specs=[vm] * 5,
         scratch_shapes=[pltpu.VMEM(qh.shape, qh.dtype)] * 4
+        + [pltpu.VMEM(do.shape, do.dtype)] * 2
+        + [pltpu.VMEM((32, do.shape[1]), jnp.float32)]
         + [dma((3,)), dma((3,)), dma, dma((3, 3, heads)), dma((3, 3, heads)), dma((3, heads))],
-        compiler_params=pltpu.CompilerParams(collective_id=5, has_side_effects=True, vmem_limit_bytes=48 << 20),
+        compiler_params=pltpu.CompilerParams(collective_id=5, has_side_effects=True, vmem_limit_bytes=56 << 20),
         cost_estimate=pl.CostEstimate(flops=50_000_000_000, bytes_accessed=10_000_000, transcendentals=0),
         name="attend_back",
-    )(do, qh, kh, vh, logs, keep)
+    )(do, qh, kh, vh, logs, keep, q_raw, k_raw, q_gain, k_gain, cosine, sine)
 
 
 def norm_rows(values, gain):
@@ -693,17 +803,6 @@
     frequency = jnp.exp(-math.log(ROPE_THETA) * jnp.arange(half_dim, dtype=jnp.float32) / half_dim)
     angles = positions.astype(jnp.float32)[:, None] * frequency[None, :]
     return (jnp.cos(angles), jnp.sin(angles))
-
-
-def rotate(values, cosine, sine, direction):
-    half_dim = values.shape[-1] // 2
-    first = values[..., :half_dim]
-    second = values[..., half_dim:]
-    cos_rows = cosine[:, None, :]
-    sin_rows = direction * sine[:, None, :]
-    return jnp.concatenate(
-        [first * cos_rows - second * sin_rows, second * cos_rows + first * sin_rows], axis=-1
-    )
 
 
 def local(
@@ -722,21 +821,6 @@
     score_scale = 1.0 / math.sqrt(head_dim)
     seq_len = token_count * ctx_size
 
-    rows_each = query_weight.shape[0]
-    packed = jnp.concatenate(
-        [g.reshape(-1) for g in (first_gain, second_gain, query_gain, key_gain)] + [router_weight.reshape(-1)]
-    )
-    small = jnp.pad(packed, (0, -packed.size % 2048)).reshape(-1, 128)
-    ids_low = expert_ids[0].astype(jnp.bfloat16).reshape(-1, 128)
-    gathered, ids_all = spread([query_weight, key_weight, value_weight, out_weight, small], ids_low)
-    full_query, full_key, full_value, full_out = (w.reshape(model_width, -1) for w in gathered[:4])
-    smalls = gathered[4].reshape(-1, small.size)
-    gains = [smalls[:, i * rows_each : (i + 1) * rows_each].reshape(-1).astype(jnp.float32) for i in range(4)]
-    gain_first, gain_second, gain_queries, gain_keys = gains
-    full_router = smalls[:, 4 * rows_each : packed.size].reshape(model_width, experts)
-    ids_all = ids_all.reshape(sources, token_count, top_count).astype(jnp.int32)
-    gate_all, up_all = (lax.all_gather(w, CTX, axis=2, tiled=True) for w in (gate_weight, up_weight))
-    down_all = lax.all_gather(down_weight, CTX, axis=1, tiled=True)
     inputs = tokens[0].astype(jnp.float32)
     length = lengths[0]
     positions = lax.axis_index(CTX) * token_count + jnp.arange(token_count, dtype=jnp.int32)
@@ -746,28 +830,40 @@
     grad_total_low = (cotangent[0].astype(jnp.float32) * row_valid).astype(jnp.bfloat16)
     grad_total = grad_total_low.astype(jnp.float32)
 
-    g_all = lax.all_gather(grad_total_low, EXP, axis=0)
+    rows_each = query_weight.shape[0]
+    packed = jnp.concatenate(
+        [g.reshape(-1) for g in (first_gain, second_gain, query_gain, key_gain)] + [router_weight.reshape(-1)]
+    )
+    small = jnp.pad(packed, (0, -packed.size % 2048)).reshape(-1, 128)
+    ids_low = expert_ids[0].astype(jnp.bfloat16).reshape(-1, 128)
+    gathered, (ids_all, g_all) = spread([query_weight, key_weight, value_weight, out_weight, small], [ids_low, grad_total_low])
+    g_all = g_all.reshape(sources, token_count, model_width)
+    full_query, full_key, full_value, full_out = (w.reshape(model_width, -1) for w in gathered[:4])
+    smalls = gathered[4].reshape(-1, small.size)
+    gains = [smalls[:, i * rows_each : (i + 1) * rows_each].reshape(-1).astype(jnp.float32) for i in range(4)]
+    gain_first, gain_second, gain_queries, gain_keys = gains
+    full_router = smalls[:, 4 * rows_each : packed.size].reshape(model_width, experts)
+    ids_all = ids_all.reshape(sources, token_count, top_count).astype(jnp.int32)
+    full_value, gate_weight, up_weight, down_weight = lax.optimization_barrier((full_value, gate_weight, up_weight, down_weight))
+    gate_all, up_all = (lax.all_gather(w, CTX, axis=2, tiled=True) for w in (gate_weight, up_weight))
+    down_all = lax.all_gather(down_weight, CTX, axis=1, tiled=True)
     cosine, sine = rotary_tables(positions, head_dim)
     normed_one, factor_one = norm_rows(inputs, gain_first)
     normed_one_low = normed_one.astype(jnp.bfloat16)
     query_raw = matmul(normed_one_low, full_query)
     key_raw = matmul(normed_one_low, full_key)
     value_low = matmul(normed_one_low, full_value).astype(jnp.bfloat16)
-    query_normed, query_factor = norm_rows(query_raw, gain_queries)
-    key_normed, key_factor = norm_rows(key_raw, gain_keys)
-    by_head = lambda v: v.reshape(token_count, HEADS, head_dim)
-    query_low = rotate(by_head(query_normed), cosine, sine, 1.0).astype(jnp.bfloat16)
-    key_low = rotate(by_head(key_normed), cosine, sine, 1.0).astype(jnp.bfloat16)
-    flat = lambda v: v.reshape(v.shape[0], -1)
     keep = key_valid.astype(jnp.float32)[None, :]
-    value_low, gate_all = lax.optimization_barrier((value_low, gate_all))
-    attended_low, *saved = attend(flat(query_low), flat(key_low), value_low, keep, score_scale)
+    turns = (jnp.concatenate([cosine, cosine], axis=1), jnp.concatenate([-sine, sine], axis=1))
+    row = lambda g: g.reshape(1, model_width)
+    shared = (row(gain_queries), row(gain_keys), *turns)
+    attended_low, *saved = attend(query_raw, key_raw, value_low, *shared, keep, score_scale)
     hidden_state = inputs + matmul(attended_low, full_out)
     normed_two, factor_two = norm_rows(hidden_state, gain_second)
     normed_two_low = normed_two.astype(jnp.bfloat16)
 
-    n2_sent, up_all = lax.optimization_barrier((normed_two_low, up_all))
-    n2_all, _ = dispatch(n2_sent, [], [])
+    n2_all = dispatch(normed_two_low)
+    n2_all, gate_all = lax.optimization_barrier((n2_all, gate_all))
     n2_all = n2_all.reshape(sources, token_count, model_width)
     first_expert = lax.axis_index(EXP) * local_experts
     own_experts = first_expert + jnp.arange(local_experts, dtype=jnp.int32)
@@ -791,6 +887,8 @@
     de = (g_rows * row_gate).astype(jnp.bfloat16)
     sig = jax.nn.sigmoid(gp)
     hid = (gp * sig * up).astype(jnp.bfloat16)
+    down_part = ee("escf,escd->efd", hid, de).astype(jnp.bfloat16)
+    down_all, down_part = lax.optimization_barrier((down_all, down_part))
     eo = ee("escf,efd->escd", hid, down_all).astype(jnp.bfloat16)
     dgate_rows = jnp.sum(g_rows * eo.astype(jnp.float32), axis=-1)
     mixed_rows = (row_gate * eo.astype(jnp.float32)).astype(jnp.bfloat16)
@@ -800,7 +898,6 @@
     dhid = ee("escd,efd->escf", de, down_all)
     dgp = (dhid * up * sig * (1.0 + gp * (1.0 - sig))).astype(jnp.bfloat16)
     dup = (dhid * gp * sig).astype(jnp.bfloat16)
-    down_part = ee("escf,escd->efd", hid, de)
     gate_part = ee("escd,escf->edf", x, dgp)
     up_part = ee("escd,escf->edf", x, dup)
     parts = [v.astype(jnp.bfloat16) for v in (down_part, gate_part, up_part)]
@@ -829,22 +926,17 @@
     dh_low = grad_hidden.astype(jnp.bfloat16)
     out_part = transposed_times(attended_low, dh_low)
     d_att = times_transposed(dh_low, full_out).astype(jnp.bfloat16)
-    dq, dk, dv = attend_back(d_att, *saved, keep, score_scale)
-    dq, up_grad = lax.optimization_barrier((dq, up_grad))
-    unrotate = lambda a: rotate(by_head(a.astype(jnp.float32)), cosine, sine, -1.0).reshape(token_count, model_width)
-    dk_raw, gain_keys_part = norm_back(unrotate(dk), key_raw, key_factor, gain_keys)
-    dq_raw, gain_queries_part = norm_back(unrotate(dq), query_raw, query_factor, gain_queries)
-    dk_low, dq_low, dv_low = dk_raw.astype(jnp.bfloat16), dq_raw.astype(jnp.bfloat16), dv
-    dn1 = times_transposed(dq_low, full_query) + times_transposed(dk_low, full_key)
-    dn1 = dn1 + times_transposed(dv_low, full_value)
-    input_norm, gain_first_part = norm_back(dn1, inputs, factor_one, gain_first)
-    input_grad = (grad_hidden + input_norm).astype(jnp.bfloat16)
+    dq_low, dk_low, dv_low, *gain_parts = attend_back(d_att, *saved, keep, query_raw, key_raw, *shared, score_scale)
+    dv_low, up_grad = lax.optimization_barrier((dv_low, up_grad))
+    gain_queries_part, gain_keys_part = (jnp.sum(g, axis=0) for g in gain_parts)
     core = lax.axis_index("core")
     swap = lambda v: lax.ppermute(v, "core", [(0, 1), (1, 0)])
 
     def columns_of_core(v):
-        v = v.reshape(token_count, 2, -1)
-        return jnp.concatenate([lax.dynamic_index_in_dim(v, core, 1, False), swap(lax.dynamic_index_in_dim(v, 1 - core, 1, False))], axis=0)
+        width = model_width // 2
+        mine = lax.dynamic_slice_in_dim(v, core * width, width, 1)
+        other = lax.dynamic_slice_in_dim(v, (1 - core) * width, width, 1)
+        return jnp.concatenate([mine, swap(other)], axis=0)
 
     both = lambda v: jnp.concatenate([v, swap(v)], axis=0)
     n1_both, att_both = both(normed_one_low), both(attended_low)
@@ -854,11 +946,14 @@
     ]
     split = lambda v: v.reshape(ctx_size * sources // 2, 2, -1)
     small_parts = jnp.concatenate(
-        [split(v) for v in (gain_first_part, gain_second_part, gain_queries_part, gain_keys_part, router_part)], axis=2
+        [split(v) for v in (gain_second_part, gain_queries_part, gain_keys_part, router_part)], axis=2
     )
     small_parts = jnp.pad(small_parts, ((0, 0), (0, 0), (0, -small_parts.shape[2] % 2048)))
     small_parts = lax.dynamic_index_in_dim(small_parts, core, 1, False) + swap(lax.dynamic_index_in_dim(small_parts, 1 - core, 1, False))
-    weight_grads, small_grads = collect(parts, small_parts.reshape(ctx_size * sources // 2, -1, 128))
+    weight_grads, small_grads, input_grad, gain_first_sums = collect(
+        parts, small_parts.reshape(ctx_size * sources // 2, -1, 128), (dq_low, dk_low, dv_low),
+        (full_query, full_key, full_value), tokens[0], row(gain_first), grad_hidden,
+    )
     weight_grads, mixed, gate_grad, up_grad, down_grad = lax.optimization_barrier(
         (list(weight_grads), mixed, gate_grad, up_grad, down_grad)
     )
@@ -866,8 +961,9 @@
     gate_grad, up_grad, down_grad = (v.astype(jnp.float32) for v in (gate_grad, up_grad, down_grad))
     weight_grads = list(weight_grads[1:]) + [weight_grads[0]]
     small_grads = small_grads.reshape(-1)
-    gain_grads = [small_grads[i * rows_each : (i + 1) * rows_each] for i in range(4)]
-    router_grad = small_grads[4 * rows_each : packed.size].reshape(rows_each, experts)
+    gain_grads = [lax.dynamic_slice_in_dim(jnp.sum(gain_first_sums, axis=0), lax.axis_index(ALL) * rows_each, rows_each)]
+    gain_grads += [small_grads[i * rows_each : (i + 1) * rows_each] for i in range(3)]
+    router_grad = small_grads[3 * rows_each : packed.size - rows_each].reshape(rows_each, experts)
     return (layer_out[None], input_grad[None], *weight_grads, router_grad, *gain_grads, gate_grad, up_grad, down_grad)
 
 

time: 1160 us -> 1080 us (0.931)
  Pallas kernels: 735 us -> 676 us
  waiting for transfers between devices: 2.07 us -> 33.3 us
  local copies, waits for them, and re-layouts: 45.9 us -> 27.6 us
  matrix products: 306 us -> 289 us
  other arithmetic: 42 us -> 26.3 us
    pallas_call x2, Pallas kernels: 321 us -> 229 us  [the longest x1 154 us: spread(): pl.pallas_call(functools.partial(spread_kernel, count, more), out_shape=[...]
    pallas_call x1, Pallas kernels: 59.6 us -> 82.1 us  [attend(): pl.pallas_call(functools.partial(attend_kernel, scale), out_shape=[jax.Sh...]
    pallas_call x1, Pallas kernels: 178 us -> 200 us  [collect(): pl.pallas_call(functools.partial(collect_kernel, count), out_shape=shapes...]
    all_gather x2, waiting for transfers between devices: 0.02 us -> 21.7 us  [local(): lax.all_gather(w, CTX, axis=2, tiled=True)]
    dot_general x5 -> x2, matrix products: 37 us -> 19 us  [times_transposed(): lax.dot_general(left, right, (((1,), (1,)), ((), ())), preferred_element_...]
  transfers between devices with their start and end apart: 15 -> 14, of which waited for: 0 -> 2; matrix products, arithmetic and copies ran while one was open for 29% -> 29% of each run, Pallas kernels for 64% -> 49%
where the time goes in v3:
time: 1080 us; the launch traced here: 1070 us
  Pallas kernels  676 us (63%)
  matrix products  289 us (27%)
  waiting for transfers between devices  33.3 us (3%)
  local copies, waits for them, and re-layouts  27.6 us (3%)
  other arithmetic  26.3 us (2%)
  between operations  16.1 us (1%)
    pallas_call x1, Pallas kernels, collect(): pl.pallas_call(functools.partial(collect_kernel, count), out_shape=shapes...  200 us
    pallas_call x1, Pallas kernels, spread(): pl.pallas_call(functools.partial(spread_kernel, count, more), out_shape=[...  154 us
    dot_general x8, matrix products, local(): jnp.einsum(eq, a, b, preferred_element_type=jnp.float32)  149 us
    pallas_call x1, Pallas kernels, give_back(): pl.pallas_call(give_back_kernel, out_shape=jax.ShapeDtypeStruct((rows, co...  98.8 us
    pallas_call x1, Pallas kernels, attend(): pl.pallas_call(functools.partial(attend_kernel, scale), out_shape=[jax.Sh...  82.1 us
    pallas_call x1, Pallas kernels, dispatch(): pl.pallas_call(dispatch_kernel, out_shape=jax.ShapeDtypeStruct((ring, 2)...  74.9 us
    pallas_call x1, Pallas kernels, attend_back(): pl.pallas_call(functools.partial(attend_back_kernel, scale), out_shape=[j...  66.2 us
    dot_general x5, matrix products, matmul(): return jnp.dot(left, right, preferred_element_type=jnp.float32)  31 us
  transfers between devices with their start and end apart: 14, of which 2 were waited for; matrix products, arithmetic and copies ran while one was open for 29% of the time, Pallas kernels for 49%

profile of v3, /device:TPU:9, one launch (start us, length us, event | category | flops | bytes accessed | tf_op | source)
XLA Modules:
  0.0 1073.0 jit_solution(5447367243055108545)
XLA Ops:
  10.3 2.8 concatenate.30
  14.2 2.4 fusion.53.refs_6_
  16.7 154.2 %spread.1 = (bf16[2,2,4,2,64,2048]{5,4,3,2,1,0:T(8,128)(2,1)}, bf16[2,2,4,2,64,2048]{5,4,3,2,1,0:T(8,128)(2,1)}, bf16[2,2,4,2,64,2048]{5,4,3,2,1,0:T(8,128)(2,1)...) custom-call(bf16[64,2048]{1,0:T(8,128)(2,1)} %refs_0_.1, ...), custom_call_target="tpu_custom_call" | custom-call | flops 149999992832 | bytes 300000000 | tf_op jit(solution)/shard_map/spread/pallas_call | solution.py:216
  173.0 1.3 fusion.49
  174.3 7.4 fusion.76.k_raw
  181.7 3.8 fusion.78.q_raw
  185.7 6.8 convolution_convert_fusion.5.v
  193.2 82.1 %attend.1 = (bf16[256,2048]{1,0:T(8,128)(2,1)}, bf16[1024,512]{1,0:T(8,128)(2,1)S(1)}, bf16[1024,512]{1,0:T(8,128)(2,1)S(1)}, bf16[1024,512]{1,0:T(8,128)(2,1)S(1)}, f32[4,1024,1]{2,1,0:T(8,128)}) custom-call(f32[256,2048]{1,0:T(8,128)} %fusion.78.q_raw, f32[256,2048]{1,0:T(8,128)} %fusion.76.k_raw, bf16[256,2048]{1,0:T(8,128)(2,1)S(1)} %convolution_convert_fusion.5.v, ...), custom_call_target="tpu_custom_call" | custom-call | flops 1000000 | bytes 10000 | tf_op jit(solution)/shard_map/attend/pallas_call | solution.py:700
  275.3 7.3 multiply_reduce_fusion.2
  283.3 1.2 multiply_convert_fusion.4.rows
  284.5 74.9 %dispatch.1 = bf16[4,2,256,2048]{3,2,1,0:T(8,128)(2,1)} custom-call(bf16[256,2048]{1,0:T(8,128)(2,1)} %multiply_convert_fusion.4.rows), custom_call_target="tpu_custom_call" | custom-call | flops 1000000 | bytes 10000 | tf_op jit(solution)/shard_map/dispatch/pallas_call | solution.py:486
  361.1 8.4 convert_bitcast_fusion
  369.5 21.7 %all-gather.6.cloned.1.call-done = bf16[2,2048,1024]{2,1,0:T(8,128)(2,1)} async-done(((bf16[2,2048,256]{2,1,0:T(8,128)(2,1)}), bf16[2,2048,1024]{2,1,0:T(8,128)(2,1)}) %all-gather.6.cloned.1.call-update) | async-done | bytes 8388624 | tf_op jit(solution)/shard_map/all_gather | solution.py:848
  391.2 17.5 %fusion.14 = f32[2,8,144,1024]{3,2,1,0:T(8,128)} fusion(bf16[2,2048,1024]{2,1,0:T(8,128)(2,1)} %all-gather.6.cloned.1.call-done, bf16[2,8,144,2048]{3,2,0,1:T(8,128)(2,1)} %convert_bitcast_fusion), kind=kOutput, calls=%fused_computation.27 | convolution fusion | flops 9663676416 | bytes 27262976 | tf_op jit(solution)/shard_map/escd,edf->escf/dot_general | solution.py:882
  408.7 5.7 fusion.95
  416.4 14.2 %fusion.2 = (bf16[2,8,144,2048]{3,2,0,1:T(8,128)(2,1)}, f32[8,2048,2,144]{1,3,2,0:T(8,128)}) fusion(f32[2,8,144]{2,0,1:T(2,128)S(1)} %bitcast.164, f32[8,2,256]{2,1,0:T(2,128)S(1)} %copy.75, pred[8,2,256]{2,1,0:T(4,128)(4,1)S(1)} %compare_reduce_fusion, bf16[8,256,2048]{2,1,0:T(8,128)(2,1)} %bitcast.154), kind=kOutput, calls=%fused_computation.5 | convolution fusion | flops 2426535936 | bytes 36729856 | tf_op jit(solution)/shard_map/sect,std->escd/dot_general | solution.py:886
  430.6 21.1 %multiply_convert_fusion.2 = (bf16[2,8,144,1024]{3,2,1,0:T(8,128)(2,1)S(1)}, f32[2,8,144,1024]{3,2,1,0:T(8,128)}) fusion(f32[2,8,144,1024]{3,2,1,0:T(8,128)} %fusion.14, bf16[2,2048,1024]{2,1,0:T(8,128)(2,1)} %all-gather.4.cloned.1.call-done, bf16[2,8,144,2048]{3,2,0,1:T(8,128)(2,1)} %convert_bitcast_fusion), kind=kOutput, calls=%fused_computation.17 | convolution fusion | flops 9677832192 | bytes 41418752 | tf_op jit(solution)/shard_map/escd,edf->escf/dot_general | solution.py:882
  451.6 2.1 copy-done.55
  453.7 16.9 %bitcast_convert_fusion.3 = bf16[2,1024,2048]{2,1,0:T(8,128)(2,1)} fusion(bf16[2,8,144,1024]{3,2,1,0:T(8,128)(2,1)S(1)} %get-tuple-element.190, bf16[2,8,144,2048]{3,2,0,1:T(8,128)(2,1)} %get-tuple-element.194), kind=kOutput, calls=%fused_computation.12 | convolution fusion | flops 9667870720 | bytes 22544384 | tf_op jit(solution)/shard_map/escf,escd->efd/dot_general | solution.py:882
  470.6 10.1 all-gather.8.cloned.1.call-done
  480.8 21.2 %multiply_convert_fusion = (bf16[2,8,144,1024]{3,2,1,0:T(8,128)(2,1)}, bf16[2,8,144,1024]{3,2,1,0:T(8,128)(2,1)}) fusion(f32[2,8,144,1024]{3,2,1,0:T(8,128)} %get-tuple-element.191, f32[2,8,144,1024]{3,2,1,0:T(8,128)} %fusion.14, bf16[2,1024,2048]{2,1,0:T(8,128)(2,1)} %all-gather.8.cloned.1.call-done, bf16[2,8,144,2048]{3,2,0,1:T(8,128)(2,1)} %get-tuple-element.194), kind=kOutput, calls=%fused_computation.15 | convolution fusion | flops 9694347264 | bytes 46137344 | tf_op jit(solution)/shard_map/escd,efd->escf/dot_general | solution.py:882
  501.9 17.4 %bitcast_convert_fusion.2 = bf16[2,2048,1024]{2,1,0:T(8,128)(2,1)} fusion(bf16[2,8,144,2048]{3,2,0,1:T(8,128)(2,1)} %convert_bitcast_fusion, bf16[2,8,144,1024]{3,2,1,0:T(8,128)(2,1)} %get-tuple-element.84), kind=kOutput, calls=%fused_computation.11 | convolution fusion | flops 9667870720 | bytes 22544384 | tf_op jit(solution)/shard_map/escd,escf->edf/dot_general | solution.py:882
  521.2 17.4 %bitcast_convert_fusion.1 = bf16[2,2048,1024]{2,1,0:T(8,128)(2,1)} fusion(bf16[2,8,144,2048]{3,2,0,1:T(8,128)(2,1)} %convert_bitcast_fusion, bf16[2,8,144,1024]{3,2,1,0:T(8,128)(2,1)} %get-tuple-element.85), kind=kOutput, calls=%fused_computation.10 | convolution fusion | flops 9667870720 | bytes 22544384 | tf_op jit(solution)/shard_map/escd,escf->edf/dot_general | solution.py:882
  538.6 20.0 %fusion = (f32[2,8,144]{2,0,1:T(2,128)S(1)}, bf16[2,8,144,2048]{3,2,0,1:T(8,128)(2,1)}) fusion(f32[8,2048,2,144]{1,3,2,0:T(8,128)} %get-tuple-element.195, bf16[2,1024,2048]{2,1,0:T(8,128)(2,1)} %all-gather.8.cloned.1.call-done, bf16[2,8,144,1024]{3,2,1,0:T(8,128)(2,1)} %copy-done.55), kind=kOutput, calls=%fused_computation.2 | convolution fusion | flops 9682548736 | bytes 41427968 | tf_op jit(solution)/shard_map/escf,efd->escd/dot_general | solution.py:882
  559.5 11.7 %bitcast_convert_fusion = bf16[8,256,2048]{2,1,0:T(8,128)(2,1)} fusion(bf16[2,8,144,2048]{3,2,0,1:T(8,128)(2,1)} %get-tuple-element.197, f32[2,8,144]{2,0,1:T(2,128)S(1)} %bitcast.165, f32[8,2,256]{2,1,0:T(2,128)S(1)} %copy-done.26, pred[8,2,256]{2,1,0:T(4,128)(4,1)S(1)} %copy-done.34), kind=kOutput, calls=%fused_computation.9 | convolution fusion | flops 2435448832 | bytes 17855488 | tf_op jit(solution)/shard_map/sect,escd->std/dot_general | solution.py:895
  571.2 17.4 %fusion.18 = f32[2,8,144,2048]{3,2,0,1:T(8,128)} fusion(bf16[2,2048,1024]{2,1,0:T(8,128)(2,1)} %all-gather.4.cloned.1.call-done, bf16[2,8,144,1024]{3,2,1,0:T(8,128)(2,1)} %get-tuple-element.84), kind=kOutput, calls=%fused_computation.31 | convolution fusion | flops 9663676416 | bytes 31981568 | tf_op jit(solution)/shard_map/escf,edf->escd/dot_general | solution.py:882
  588.7 5.9 fusion.104
  594.7 1.2 reshape.301
  595.9 25.7 %fusion.4 = f32[8,256,2048,1]{2,1,3,0:T(8,128)} fusion(f32[2,8,144,2048]{3,2,0,1:T(8,128)} %fusion.18, f32[8,2,256]{2,1,0:T(2,128)S(1)} %copy-done.26, pred[8,2,256]{2,1,0:T(4,128)(4,1)S(1)} %copy-done.34, bf16[2,2048,1024]{2,1,0:T(8,128)(2,1)} %all-gather.6.cloned.1.call-done, bf16[2,8,144,1024]{3,2,1,0:T(8,128)(2,1)} %get-tuple-element.85), kind=kOutput, calls=%fused_computation.13 | convolution fusion | flops 12090212352 | bytes 48779264 | tf_op jit(solution)/shard_map/sect,escd->std/dot_general | solution.py:915
  621.7 11.7 %fusion.3 = bf16[2048,2048]{1,0:T(8,128)(2,1)} fusion(f32[8,256,2048,1]{2,1,3,0:T(8,128)} %fusion.4, bf16[2048,16]{0,1:T(8,128)(2,1)S(1)} %multiply_convert_fusion.6, bf16[2048,16]{1,0:T(8,128)(2,1)S(1)} %copy-done.13), kind=kOutput, calls=%fused_computation.8 | convolution fusion | flops 142606336 | bytes 25296896 | tf_op jit(solution)/shard_map/dot_general | solution.py:561
  633.4 98.8 %give_back.1 = f32[256,2048]{1,0:T(8,128)} custom-call(bf16[4,2,256,2048]{3,2,1,0:T(8,128)(2,1)} %bitcast.155), custom_call_target="tpu_custom_call" | custom-call | flops 99999997952 | bytes 200000000 | tf_op jit(solution)/shard_map/give_back/pallas_call | solution.py:544
  732.2 2.3 multiply_reduce_fusion
  734.7 2.1 fusion.93
  736.8 7.3 convolution_convert_fusion.4.do
  744.1 66.2 %attend_back.1 = (bf16[256,2048]{1,0:T(8,128)(2,1)}, bf16[256,2048]{1,0:T(8,128)(2,1)}, bf16[256,2048]{1,0:T(8,128)(2,1)}, f32[8,2048]{1,0:T(8,128)}, f32[8,2048]{1,0:T(8,128)}) custom-call(bf16[256,2048]{1,0:T(8,128)(2,1)} %convolution_convert_fusion.4.do, bf16[1024,512]{1,0:T(8,128)(2,1)} %copy-done.5, bf16[1024,512]{1,0:T(8,128)(2,1)} %copy-done.6, ...), custom_call_target="tpu_custom_call" | custom-call | flops 49999998976 | bytes 10000000 | tf_op jit(solution)/shard_map/attend_back/pallas_call | solution.py:775
  810.3 2.2 constant_dynamic-slice_fusion.1
  812.6 2.0 collective-permute-start.6
  814.5 2.1 constant_dynamic-slice_fusion.3
  822.4 6.2 convolution_convert_fusion
  828.6 6.1 convolution_convert_fusion.1
  834.7 6.0 convolution_convert_fusion.2
  840.6 6.0 convolution_convert_fusion.3
  846.6 200.1 %collect.1 = (f32[16,128]{1,0:T(8,128)}, f32[64,2048]{1,0:T(8,128)}, f32[64,2048]{1,0:T(8,128)}, f32[64,2048]{1,0:T(8,128)}, f32[64,2048]{1,0:T(8,128)}, /*index=5*/bf16[256,2048]{1,0:T(8,128)(2,1)}, f32[8,2048]{1,0:T(8,128)}) custom-call(f32[2,2,4,16,128]{4,3,2,1,0:T(8,128)} %bitcast.161, bf16[2,2,4,128,1024]{4,3,2,1,0:T(8,128)(2,1)} %bitcast.183, ...), custom_call_target="tpu_custom_call" | custom-call | flops 160000000000 | bytes 320000000 | tf_op jit(solution)/shard_map/collect/pallas_call | solution.py:441
  1049.8 1.4 fusion.94
  1051.2 4.1 convert_element_type.286
  1055.3 2.5 convert_element_type.287
  1057.7 2.5 convert_element_type.288
  1060.3 1.3 fusion.63
  (211 shorter events, 26.8 us)
Async XLA Ops:
  7.2 353.9 %all-gather.4.cloned.1.call-start = ((), (), s32[]{:S(2)}) async-start(), calls=%async_computation.4 | async-start | bytes 10485760 | tf_op jit(solution)/shard_map/all_gather | solution.py:848
  170.9 220.3 %all-gather.6.cloned.1.call-start = ((), (), s32[]{:S(2)}) async-start(), calls=%async_computation.5 | async-start | bytes 10485760 | tf_op jit(solution)/shard_map/all_gather | solution.py:848
  171.6 309.0 %all-gather.8.cloned.1.call-start = ((), (), s32[]{:S(2)}) async-start(), calls=%async_computation.6 | async-start | bytes 10485760 | tf_op jit(solution)/shard_map/all_gather | solution.py:849
  172.4 461.0 %reduce-scatter.5.cloned.1.call-start = ((), (), s32[]{:S(2)}) async-start(), calls=%async_computation.7 | async-start | bytes 10485760 | tf_op jit(solution)/shard_map/reduce_scatter | solution.py:905
  172.6 9.1 copy-start.37
  173.0 8.7 slice-start
  174.3 7.4 slice-start.1
  185.6 7.6 copy-start.2
  185.7 7.5 copy-start.3
  185.7 7.5 copy-start.4
  193.2 89.4 %copy-start = (f32[256,128]{1,0:T(8,128)}, f32[256,128]{1,0:T(8,128)S(1)}, u32[]{:S(2)}) copy-start(f32[256,128]{1,0:T(8,128)S(1)} %get-tuple-element.198.cosine) | copy-start | bytes 393220
  193.2 89.4 %copy-start.1 = (f32[256,128]{1,0:T(8,128)}, f32[256,128]{1,0:T(8,128)S(1)}, u32[]{:S(2)}) copy-start(f32[256,128]{1,0:T(8,128)S(1)} %get-tuple-element.199.sine) | copy-start | bytes 393220
  275.3 7.3 copy-start.5
  275.3 7.3 copy-start.6
  275.3 7.3 copy-start.7
  282.6 76.7 %copy-start.8 = (f32[256,2048]{1,0:T(8,128)}, f32[256,2048]{1,0:T(8,128)S(1)}, u32[]{:S(2)}) copy-start(f32[256,2048]{1,0:T(8,128)S(1)} %get-tuple-element.189) | copy-start | bytes 6291460
  284.5 75.3 %copy-start.46 = (bf16[4,2,16,128]{3,2,1,0:T(8,128)(2,1)S(1)}, bf16[4,2,16,128]{3,2,1,0:T(8,128)(2,1)}, u32[]{:S(2)}) copy-start(bf16[4,2,16,128]{3,2,1,0:T(8,128)(2,1)} %get-tuple-element.73) | copy-start | bytes 98308
  359.8 48.9 %copy-start.12 = (bf16[2048,16]{1,0:T(8,128)(2,1)}, bf16[2048,16]{1,0:T(8,128)(2,1)S(1)}, u32[]{:S(2)}) copy-start(bf16[2048,16]{1,0:T(8,128)(2,1)S(1)} %reshape.293) | copy-start | bytes 196612
  359.8 9.7 copy-start.53
  360.9 55.5 %copy-start.33 = (pred[8,2,256]{2,1,0:T(4,128)(4,1)}, pred[8,2,256]{2,1,0:T(4,128)(4,1)S(1)}, u32[]{:S(2)}) copy-start(pred[8,2,256]{2,1,0:T(4,128)(4,1)S(1)} %compare_reduce_fusion) | copy-start | bytes 12292
  361.1 55.3 %copy-start.25 = (f32[8,2,256]{2,1,0:T(2,128)}, f32[8,2,256]{2,1,0:T(2,128)S(1)}, u32[]{:S(2)}) copy-start(f32[8,2,256]{2,1,0:T(2,128)S(1)} %copy.75) | copy-start | bytes 49156
  414.4 16.1 %copy-start.35 = (f32[2048]{0:T(1024)}, f32[2048]{0:T(1024)S(1)}, u32[]{:S(2)}) copy-start(f32[2048]{0:T(1024)S(1)} %get-tuple-element.192) | copy-start | bytes 24580
  416.3 14.2 %copy-start.44 = (f32[8,2,144]{2,1,0:T(2,128)}, f32[8,2,144]{2,1,0:T(2,128)S(1)}, u32[]{:S(2)}) copy-start(f32[8,2,144]{2,1,0:T(2,128)S(1)} %fusion.39) | copy-start | bytes 27652
  480.7 251.4 %reduce-scatter.7.cloned.1.call-start = ((), (), s32[]{:S(2)}) async-start(), calls=%async_computation.8 | async-start | bytes 10485760 | tf_op jit(solution)/shard_map/reduce_scatter | solution.py:905
  519.3 291.0 %reduce-scatter.9.cloned.1.call-start = ((), (), s32[]{:S(2)}) async-start(), calls=%async_computation.9 | async-start | bytes 10485760 | tf_op jit(solution)/shard_map/reduce_scatter | solution.py:905
  519.6 302.4 %collective-permute-start.3 = (bf16[256,2048]{1,0:T(8,128)(2,1)}, bf16[256,2048]{1,0:T(8,128)(2,1)}, u32[]{:S(2)}, u32[]{:S(2)}) collective-permute-start(bf16[256,2048]{1,0:T(8,128)(2,1)} %fusion.49), channel_id=1, source_target_pairs={{0,1},{1,0},{2,3},{3,2},{4,5},{5,4},{6,7},{7,6},{8,9},{9,8},{10,11... | collective-permute-start | bytes 3145736 | tf_op jit(solution)/shard_map/ppermute | solution.py:933
  520.4 320.3 %collective-permute-start.1 = (bf16[256,2048]{1,0:T(8,128)(2,1)}, bf16[256,2048]{1,0:T(8,128)(2,1)}, u32[]{:S(2)}, u32[]{:S(2)}) collective-permute-start(bf16[256,2048]{1,0:T(8,128)(2,1)} %get-tuple-element.71), channel_id=1, source_target_pairs={{0,1},{1,0},{2,3},{3,2},{4,5},{5,4},{6,7},{7,6},{8,9},{9,8},{10,11... | collective-permute-start | bytes 3145736 | tf_op jit(solution)/shard_map/ppermute | solution.py:933
  538.6 20.0 %copy-start.26 = (f32[8,2,256]{2,1,0:T(2,128)S(1)}, f32[8,2,256]{2,1,0:T(2,128)}, u32[]{:S(2)}) copy-start(f32[8,2,256]{2,1,0:T(2,128)} %copy-done.25) | copy-start | bytes 49156
  538.6 20.0 %copy-start.34 = (pred[8,2,256]{2,1,0:T(4,128)(4,1)S(1)}, pred[8,2,256]{2,1,0:T(4,128)(4,1)}, u32[]{:S(2)}) copy-start(pred[8,2,256]{2,1,0:T(4,128)(4,1)} %copy-done.33) | copy-start | bytes 12292
  538.6 20.8 %copy-start.19 = (f32[2048,16]{0,1:T(8,128)S(1)}, f32[2048,16]{0,1:T(8,128)}, u32[]{:S(2)}) copy-start(f32[2048,16]{0,1:T(8,128)} %copy-done.18) | copy-start | bytes 393220
  538.6 20.8 %copy-start.36 = (f32[2048]{0:T(1024)S(1)}, f32[2048]{0:T(1024)}, u32[]{:S(2)}) copy-start(f32[2048]{0:T(1024)} %copy-done.35) | copy-start | bytes 24580
  538.6 20.8 %copy-start.42 = (f32[2048]{0:T(1024)S(1)}, f32[2048]{0:T(1024)}, u32[]{:S(2)}) copy-start(f32[2048]{0:T(1024)} %copy-done.41) | copy-start | bytes 24580
  538.6 20.9 %copy-start.45 = (f32[8,2,144]{2,1,0:T(2,128)S(1)}, f32[8,2,144]{2,1,0:T(2,128)}, u32[]{:S(2)}) copy-start(f32[8,2,144]{2,1,0:T(2,128)} %copy-done.44) | copy-start | bytes 27652
  588.7 462.5 %reduce-scatter.11.cloned.1.call-start = ((), (), s32[]{:S(2)}) async-start(), calls=%async_computation.10 | async-start | bytes 9437184 | tf_op jit(solution)/shard_map/reduce_scatter | solution.py:922
  595.9 25.8 %copy-start.13 = (bf16[2048,16]{1,0:T(8,128)(2,1)S(1)}, bf16[2048,16]{1,0:T(8,128)(2,1)}, u32[]{:S(2)}) copy-start(bf16[2048,16]{1,0:T(8,128)(2,1)} %copy-done.12) | copy-start | bytes 196612
  633.3 98.8 %copy-start.9 = (f32[256,2048]{1,0:T(8,128)S(1)}, f32[256,2048]{1,0:T(8,128)}, u32[]{:S(2)}) copy-start(f32[256,2048]{1,0:T(8,128)} %copy-done.8) | copy-start | bytes 6291460
  633.3 98.9 %copy-start.40 = (f32[2048]{0:T(1024)S(1)}, f32[2048]{0:T(1024)}, u32[]{:S(2)}) copy-start(f32[2048]{0:T(1024)} %copy-done.39) | copy-start | bytes 24580
  633.3 98.9 %copy-start.51 = (f32[256]{0:T(256)S(1)}, f32[256]{0:T(256)}, u32[]{:S(2)}) copy-start(f32[256]{0:T(256)} %copy-done.50) | copy-start | bytes 3076
  633.3 101.1 %copy-start.48 = (f32[256]{0:T(256)S(1)}, f32[256]{0:T(256)}, u32[]{:S(2)}) copy-start(f32[256]{0:T(256)} %copy-done.47) | copy-start | bytes 3076
  633.3 101.1 %copy-start.52 = (f32[256]{0:T(256)S(1)}, f32[256]{0:T(256)}, u32[]{:S(2)}) copy-start(f32[256]{0:T(256)} %get-tuple-element.186) | copy-start | bytes 3076
  736.8 7.3 copy-start.15
  744.1 74.5 %copy-start.27 = (f32[16,2,1024]{2,1,0:T(2,128)S(1)}, f32[16,2,1024]{2,1,0:T(2,128)}, u32[]{:S(2)}) copy-start(f32[16,2,1024]{2,1,0:T(2,128)} %reshape.301) | copy-start | bytes 393220
  812.6 9.8 collective-permute-start.6
  816.6 12.0 %collective-permute-start.5 = (bf16[256,1024]{1,0:T(8,128)(2,1)}, bf16[256,1024]{1,0:T(8,128)(2,1)}, u32[]{:S(2)}, u32[]{:S(2)}) collective-permute-start(bf16[256,1024]{1,0:T(8,128)(2,1)} %get-tuple-element.169), channel_id=1, source_target_pairs={{0,1},{1,0},{2,3},{3,2},{4,5},{5,4},{6,7},{7,6},{8,9},{9,8},{10,11... | collective-permute-start | bytes 1572872 | tf_op jit(solution)/shard_map/ppermute | solution.py:933
  819.2 1.9 collective-permute-start
  821.1 13.6 %collective-permute-start.4 = (bf16[256,1024]{1,0:T(8,128)(2,1)S(1)}, bf16[256,1024]{1,0:T(8,128)(2,1)S(1)}, u32[]{:S(2)}, u32[]{:S(2)}) collective-permute-start(bf16[256,1024]{1,0:T(8,128)(2,1)S(1)} %get-tuple-element.171), channel_id=1, source_target_pairs={{0,1},{1,0},{2,3},{3,2},{4,5},{5,4},{6,7},{7,6},{8,9},{9,8},{10,11... | collective-permute-start | bytes 1572872 | tf_op jit(solution)/shard_map/ppermute | solution.py:933
  822.0 18.6 %collective-permute-start.2 = (bf16[256,1024]{1,0:T(8,128)(2,1)S(1)}, bf16[256,1024]{1,0:T(8,128)(2,1)S(1)}, u32[]{:S(2)}, u32[]{:S(2)}) collective-permute-start(bf16[256,1024]{1,0:T(8,128)(2,1)S(1)} %get-tuple-element.173), channel_id=1, source_target_pairs={{0,1},{1,0},{2,3},{3,2},{4,5},{5,4},{6,7},{7,6},{8,9},{9,8},{10,11... | collective-permute-start | bytes 1572872 | tf_op jit(solution)/shard_map/ppermute | solution.py:933
  1046.7 8.5 copy-start.21
  (24 other events, 62.0 us)
Sparse Core Ops, SparseCore 0:
  171.0 131.4 all-gather.3
  304.3 86.7 all-gather.5
  393.0 87.6 all-gather.7
  483.6 86.3 reduce-scatter.4
  573.2 86.3 reduce-scatter.6
  662.6 86.3 reduce-scatter.8
  819.9 87.6 reduce-scatter.10

commit v4 on v3

--- a/solution.py
+++ b/solution.py
@@ -62,7 +62,8 @@
 
         @pl.when(sent)
         def _(block=block, to=to, side=side):
-            push(own if step == 0 else block_of(block), block_of(block), send.at[side, step], got.at[side, step], to)
+            src = own if isinstance(step, int) and step == 0 else block_of(block)
+            push(src, block_of(block), send.at[side, step], got.at[side, step], to)
 
 
 def take_along(step, block_of, got, then):
@@ -249,8 +250,10 @@
             matrices[w].at[pl.ds(pl.multiple_of(i * rows, rows), rows), :], chunks.at[slot, w], fetch.at[slot, w]
         )
 
-    def input_side():
-        steps, rows = matrices[0].shape[0] // chunks.shape[2], chunks.shape[2]
+    steps, chunk_rows = matrices[0].shape[0] // chunks.shape[2], chunks.shape[2]
+
+    def input_part(begin, end):
+        rows = chunk_rows
 
         def one(i, carry):
             slot = lax.rem(i, 2)
@@ -267,7 +270,9 @@
             dn1[:, pl.ds(pl.multiple_of(i * rows, rows), rows)] = value
             return carry
 
-        lax.fori_loop(0, steps, one, 0)
+        lax.fori_loop(begin, end, one, 0)
+
+    def input_end():
         tile = 32
         sums[0] = jnp.zeros(sums.shape[1:], jnp.float32)
 
@@ -400,12 +405,9 @@
     for w in range(3):
         chunk(0, 0, w).start()
     first(0)
-    first(1)
-    first(2)
-    input_side()
-    for step in range(count + 3):
-        if 0 < step and step + 2 < count:
-            first(step + 2)
+    for step in range(max(count + 3, 9)):
+        if step + 1 < count:
+            first(step + 1)
         if step < count:
             second(step)
         if 0 <= step - 1 < count:
@@ -413,7 +415,11 @@
         if 0 <= step - 2 < count:
             fourth(step - 2)
         if 1 <= step < 5:
-            gain_stage(step - 1)
+            input_part((step - 1) * steps // 4, step * steps // 4)
+        if step == 4:
+            input_end()
+        if step > 4:
+            gain_stage(step - 5)
     for w in range(count):
         finish(w)
 
@@ -454,103 +460,226 @@
     return outs[1:count], outs[0], outs[count], outs[count + 1]
 
 
-def dispatch_kernel(rows, out, send, got, place, core_send, core_got):
-    ring, r, c, nc = lax.axis_size("ring"), lax.axis_index("ring"), lax.axis_index("core"), turn("core", 1)
-    to_core = {"core": nc}
+def dispatch_kernel(
+    rows, router, hot, g_all, out, picked, grads, gates, probs,
+    rows_in, g_in, picked_low, grads_low, load, store, ring_send, ring_got, place, core_send, core_got,
+):
+    ring = lax.axis_size("ring")
+    r, c, nc = lax.axis_index("ring"), lax.axis_index("core"), turn("core", 1)
+    to_core, experts = {"core": nc}, hot.shape[1]
     greet([to_core] + [{"ring": turn("ring", k)} for k in range(1, ring)])
     block_of = lambda at: out.at[at, c]
+
     own = pltpu.make_async_copy(rows, block_of(r), place)
     own.start()
-    send_along(0, rows, block_of, send, got)
-    push(rows, block_of(r), core_send, core_got, to_core)
-
-    def on(at):
-        push(block_of(at), block_of(at), core_send, core_got, to_core)
-
-    for step in range(ring - 1):
-        if step + 1 < ring - 1:
-            take_along(step, block_of, got, lambda at: None)
-            send_along(step + 1, rows, block_of, send, got)
-            for _, comes, _, block, _, _ in along(step):
-                pl.when(comes)(functools.partial(on, block))
-        else:
-            take_along(step, block_of, got, on)
+    push(rows, block_of(r), core_send, core_got.at[r], to_core)
     own.wait()
-    sent_along(rows, send)
+    send_along(0, block_of(r), block_of, ring_send, ring_got)
+    first = (r * 2 + c) * experts
+    width = rows.shape[1]
+    cols = min(512, width)
+
+    def pick(at, core):
+        source = at * 2 + core
+        copies = (
+            pltpu.make_async_copy(out.at[at, core], rows_in, load.at[0]),
+            pltpu.make_async_copy(g_all.at[at, core], g_in, load.at[1]),
+        )
+        for copy in copies:
+            copy.start()
+        copies[0].wait()
+        logits = times_transposed(router[...], rows_in[...])
+        likely = jnp.exp(logits - jnp.max(logits, axis=0, keepdims=True))
+        probs[source] = likely / jnp.sum(likely, axis=0, keepdims=True)
+        copies[1].wait()
+        for e in range(experts):
+            own_probs = probs[source, pl.ds(first + e, 1), :]
+            gate = jnp.sum(hot[source, e].astype(jnp.float32) * own_probs, axis=-1, keepdims=True)
+            gates[e, source] = gate
+
+            def part(i, carry):
+                lanes = pl.ds(pl.multiple_of(i * cols, cols), cols)
+                chosen = hot[source, e]
+                picked_low[e, :, lanes] = matmul(chosen, rows_in[:, lanes]).astype(picked_low.dtype)
+                grads_low[e, :, lanes] = (matmul(chosen, g_in[:, lanes]) * gate).astype(grads_low.dtype)
+                return carry
+
+            lax.fori_loop(0, width // cols, part, 0)
+        stores = (
+            pltpu.make_async_copy(picked_low, picked.at[:, source], store.at[0]),
+            pltpu.make_async_copy(grads_low, grads.at[:, source], store.at[1]),
+        )
+        for copy in stores:
+            copy.start()
+        for copy in stores:
+            copy.wait()
+
+    pick(r, c)
+    await_bytes(out.at[r, nc], core_got.at[r])
+    pick(r, nc)
+
+    def step_on(step, carry):
+        take_along(step, block_of, ring_got, lambda at: None)
+
+        @pl.when(step + 1 < ring - 1)
+        def _():
+            send_along(step + 1, None, block_of, ring_send, ring_got)
+
+        for _, comes, _, block, _, _ in along(step):
+
+            @pl.when(comes)
+            def _(block=block):
+                push(block_of(block), block_of(block), core_send, core_got.at[block], to_core)
+
+        def four(k, carry):
+            side, other = k // 2, lax.rem(k, 2)
+            (_, comes0, _, block0, _, _), (_, comes1, _, block1, _, _) = along(step)
+            block = jnp.where(side == 0, block0, block1)
+            comes = ((side == 0) & comes0) | ((side == 1) & comes1)
+            core = lax.rem(c + other, 2)
+
+            @pl.when(comes & (other == 1))
+            def _():
+                await_bytes(out.at[block, nc], core_got.at[block])
+
+            @pl.when(comes)
+            def _():
+                pick(block, core)
+
+            return carry
+
+        lax.fori_loop(0, 4, four, 0)
+        return carry
+
+    lax.fori_loop(0, ring - 1, step_on, 0)
+    sent_along(rows, ring_send)
     await_bytes(out.at[:, c], core_send)
-    await_bytes(out.at[:, nc], core_got)
-
-
-def dispatch(rows):
+
+
+def dispatch(rows, router, hot, g_all):
     ring, dma = lax.axis_size("ring"), pltpu.SemaphoreType.DMA
+    sources, experts, slots, count = hot.shape
+    width = rows.shape[1]
+    low = lambda *shape: jax.ShapeDtypeStruct(shape, rows.dtype)
+    f32 = lambda *shape: jax.ShapeDtypeStruct(shape, jnp.float32)
+    vm, anywhere = pl.BlockSpec(memory_space=pltpu.VMEM), pl.BlockSpec(memory_space=pl.ANY)
+    block = pltpu.VMEM((experts, slots, width), rows.dtype)
+    chosen = (experts, sources, slots, width)
     return pl.pallas_call(
         dispatch_kernel,
-        out_shape=jax.ShapeDtypeStruct((ring, 2) + rows.shape, rows.dtype),
-        in_specs=[pl.BlockSpec(memory_space=pltpu.VMEM)],
-        out_specs=pl.BlockSpec(memory_space=pl.ANY),
-        scratch_shapes=[dma((2, ring)), dma((2, ring)), dma, dma, dma],
-        compiler_params=pltpu.CompilerParams(collective_id=2, has_side_effects=True),
+        out_shape=[
+            low(ring, 2, count, width), low(*chosen), low(*chosen), f32(experts, sources, slots, 1),
+            f32(sources, router.shape[0], count),
+        ],
+        in_specs=[vm, vm, vm, anywhere],
+        out_specs=[anywhere, anywhere, anywhere, vm, vm],
+        scratch_shapes=[pltpu.VMEM(rows.shape, rows.dtype)] * 2
+        + [block, block]
+        + [dma((2,)), dma((2,)), dma((2, ring)), dma((2, ring)), dma, dma, dma((ring,))],
+        compiler_params=pltpu.CompilerParams(collective_id=2, has_side_effects=True, vmem_limit_bytes=56 << 20),
         cost_estimate=pl.CostEstimate(flops=1_000_000, bytes_accessed=10_000, transcendentals=0),
         name="dispatch",
-    )(rows)
-
-
-def give_back_kernel(part, out, own, core_in, ring_in, load, core_send, core_got, ring_send, ring_got):
-    ring = lax.axis_size("ring")
+    )(rows, router, hot, g_all)
+
+
+def give_back_kernel(part, out, own, core_in, chain_in, load, core_send, core_got, chain_send, chain_got):
+    ring, pieces, rows, cols = own.shape
     r, c, nc = lax.axis_index("ring"), lax.axis_index("core"), turn("core", 1)
+    to_next, to_last = {"ring": turn("ring", 1)}, {"ring": turn("ring", ring - 1)}
     greet([{"core": nc}] + [{"ring": turn("ring", k)} for k in range(1, ring)])
-    order = list(range(1, ring)) + [0]
-    block_of = lambda k: lax.rem(r + k, ring)
-    for k in order:
-        push(part.at[block_of(k), nc], core_in.at[k], core_send.at[k], core_got.at[k], {"core": nc})
-        pltpu.make_async_copy(part.at[block_of(k), c], own.at[k], load.at[k]).start()
-    rows, cols = own.shape[1:]
+    order = [d for pair in zip(reversed(range(ring)), range(ring)) for d in pair][:ring]
+    for d in order:
+        push(part.at[d, nc], core_in.at[d], core_send.at[d], core_got.at[d], {"core": nc})
+        pltpu.make_async_copy(part.at[d, c], own.at[d], load.at[d]).start()
     tile = 32
-    for k in order:
-        await_bytes(own.at[k], load.at[k])
-        await_bytes(core_in.at[k], core_got.at[k])
-        if k == 0:
-            continue
-
-        def add(i, carry):
+
+    def add(d, piece, other):
+        def one(i, carry):
             at = pl.ds(pl.multiple_of(i * tile, tile), tile)
-            own[k, at] = (own[k, at].astype(jnp.float32) + core_in[k, at].astype(jnp.float32)).astype(own.dtype)
+            own[d, piece, at] = (own[d, piece, at].astype(jnp.float32) + other[at].astype(jnp.float32)).astype(own.dtype)
             return carry
 
-        lax.fori_loop(0, rows // tile, add, 0)
-        push(own.at[k], ring_in.at[k - 1], ring_send.at[k - 1], ring_got.at[k - 1], {"ring": block_of(k)})
-    for k in range(1, ring):
-        await_bytes(ring_in.at[k - 1], ring_got.at[k - 1])
+        lax.fori_loop(0, rows // tile, one, 0)
+
+    def slot(side, d, whose):
+        return d if side == 0 else jnp.where(d == whose, ring, d)
+
+    def pass_on(side, step, d, piece, to):
+        there = chain_in.at[slot(side, d, r - 1), piece]
+        push(own.at[d, piece], there, chain_send.at[side, step, piece], chain_got.at[side, step, piece], to)
+
+    for d in order:
+        await_bytes(own.at[d], load.at[d])
+        await_bytes(core_in.at[d], core_got.at[d])
+        for piece in range(pieces):
+            add(d, piece, core_in.at[d, piece])
+
+            @pl.when((r == 0) & (d != r))
+            def _():
+                pass_on(0, ring - 1 - d, d, piece, to_next)
+
+            @pl.when((r == ring - 1) & (d != r))
+            def _():
+                pass_on(1, d, d, piece, to_last)
+
+    def sides(time):
+        up, down = time - r, time - (ring - 1 - r)
+        return (
+            ((r >= 1) & (up >= 0), jnp.maximum(up, 0), ring - 1 - jnp.maximum(up, 0), to_next, 0),
+            ((r + 1 < ring) & (down >= 0), jnp.maximum(down, 0), jnp.maximum(down, 0), to_last, 1),
+        )
+
+    def on(time, carry):
+        for piece in range(pieces):
+            for comes, step, d, to, side in sides(time):
+
+                @pl.when(comes)
+                def _(step=step, d=d, to=to, side=side):
+                    arrived = chain_in.at[slot(side, d, r), piece]
+                    await_bytes(arrived, chain_got.at[side, step, piece])
+                    add(d, piece, arrived)
+
+                    @pl.when(time < ring - 1)
+                    def _():
+                        pass_on(side, step, d, piece, to)
+
+        return carry
+
+    lax.fori_loop(1, ring, on, 0)
 
     def total(i, carry):
         at = pl.ds(pl.multiple_of(i * tile, tile), tile)
-        value = own[0, at].astype(jnp.float32) + core_in[0, at].astype(jnp.float32)
-        for k in range(ring - 1):
-            value = value + ring_in[k, at].astype(jnp.float32)
-        out[at, :] = value
+        for piece in range(pieces):
+            out[pl.ds(pl.multiple_of(piece * rows + i * tile, tile), tile), :] = own[r, piece, at].astype(jnp.float32)
         return carry
 
     lax.fori_loop(0, rows // tile, total, 0)
-    for k in order:
-        await_bytes(core_in.at[k], core_send.at[k])
-        if k:
-            await_bytes(ring_in.at[k - 1], ring_send.at[k - 1])
+    for d in order:
+        await_bytes(core_in.at[d], core_send.at[d])
+    for step in range(ring - 1):
+        for piece in range(pieces):
+            for sent, side in ((r + step < ring - 1, 0), (step < r, 1)):
+
+                @pl.when(sent)
+                def _(side=side):
+                    await_bytes(own.at[0, 0], chain_send.at[side, step, piece])
 
 
 def give_back(part):
-    ring, dma = lax.axis_size("ring"), pltpu.SemaphoreType.DMA
+    ring, dma, pieces = lax.axis_size("ring"), pltpu.SemaphoreType.DMA, 2
     rows, cols = part.shape[1:]
-    block = lambda n: pltpu.VMEM((n, rows, cols), part.dtype)
+    block = lambda *lead: pltpu.VMEM((*lead, pieces, rows // pieces, cols), part.dtype)
+    chain = dma((2, ring, pieces))
     return pl.pallas_call(
         give_back_kernel,
         out_shape=jax.ShapeDtypeStruct((rows, cols), jnp.float32),
         in_specs=[pl.BlockSpec(memory_space=pl.ANY)],
         out_specs=pl.BlockSpec(memory_space=pltpu.VMEM),
-        scratch_shapes=[block(ring), block(ring), block(ring - 1), dma((ring,)), dma((ring,)), dma((ring,)), dma((ring,)), dma((ring,))],
+        scratch_shapes=[block(ring), block(ring), block(ring + 1), dma((ring,)), dma((ring,)), dma((ring,)), chain, chain],
         compiler_params=pltpu.CompilerParams(collective_id=3, has_side_effects=True, vmem_limit_bytes=60 << 20),
-        cost_estimate=pl.CostEstimate(flops=100000000000, bytes_accessed=200000000, transcendentals=0),
+        cost_estimate=pl.CostEstimate(flops=100_000_000_000, bytes_accessed=200_000_000, transcendentals=0),
         name="give_back",
-    )(part.reshape(ring, 2, rows, cols))
+    )(part.reshape(ring, 2, pieces, rows // pieces, cols))
 
 
 def matmul(left, right):
@@ -837,16 +966,14 @@
     small = jnp.pad(packed, (0, -packed.size % 2048)).reshape(-1, 128)
     ids_low = expert_ids[0].astype(jnp.bfloat16).reshape(-1, 128)
     gathered, (ids_all, g_all) = spread([query_weight, key_weight, value_weight, out_weight, small], [ids_low, grad_total_low])
-    g_all = g_all.reshape(sources, token_count, model_width)
     full_query, full_key, full_value, full_out = (w.reshape(model_width, -1) for w in gathered[:4])
     smalls = gathered[4].reshape(-1, small.size)
     gains = [smalls[:, i * rows_each : (i + 1) * rows_each].reshape(-1).astype(jnp.float32) for i in range(4)]
     gain_first, gain_second, gain_queries, gain_keys = gains
     full_router = smalls[:, 4 * rows_each : packed.size].reshape(model_width, experts)
     ids_all = ids_all.reshape(sources, token_count, top_count).astype(jnp.int32)
-    full_value, gate_weight, up_weight, down_weight = lax.optimization_barrier((full_value, gate_weight, up_weight, down_weight))
+    full_value, gate_weight, up_weight = lax.optimization_barrier((full_value, gate_weight, up_weight))
     gate_all, up_all = (lax.all_gather(w, CTX, axis=2, tiled=True) for w in (gate_weight, up_weight))
-    down_all = lax.all_gather(down_weight, CTX, axis=1, tiled=True)
     cosine, sine = rotary_tables(positions, head_dim)
     normed_one, factor_one = norm_rows(inputs, gain_first)
     normed_one_low = normed_one.astype(jnp.bfloat16)
@@ -858,13 +985,11 @@
     row = lambda g: g.reshape(1, model_width)
     shared = (row(gain_queries), row(gain_keys), *turns)
     attended_low, *saved = attend(query_raw, key_raw, value_low, *shared, keep, score_scale)
+    flip = lambda v, axis: lax.ppermute(v, axis, [(0, 1), (1, 0)])
     hidden_state = inputs + matmul(attended_low, full_out)
     normed_two, factor_two = norm_rows(hidden_state, gain_second)
     normed_two_low = normed_two.astype(jnp.bfloat16)
 
-    n2_all = dispatch(normed_two_low)
-    n2_all, gate_all = lax.optimization_barrier((n2_all, gate_all))
-    n2_all = n2_all.reshape(sources, token_count, model_width)
     first_expert = lax.axis_index(EXP) * local_experts
     own_experts = first_expert + jnp.arange(local_experts, dtype=jnp.int32)
     mask = jnp.any(ids_all[:, None, :, :] == own_experts[None, :, None, None], axis=-1)
@@ -872,25 +997,30 @@
     ranks = jnp.einsum("seu,ut->set", mask.astype(jnp.bfloat16), before, preferred_element_type=jnp.float32)
     slots = jnp.arange(capacity, dtype=jnp.float32)
     hot = (mask[:, :, None, :] & (ranks[:, :, None, :] == slots[None, None, :, None])).astype(jnp.bfloat16)
-    logits = matmul(n2_all.reshape(-1, model_width), full_router)
-    probs = jax.nn.softmax(logits, axis=-1)
-    own_probs = lax.dynamic_slice_in_dim(probs, first_expert, local_experts, 1).reshape(sources, token_count, local_experts)
+    n2_all, x, de, row_gate, probs = dispatch(normed_two_low, full_router.T, hot, g_all)
+    n2_all = n2_all.reshape(sources, token_count, model_width)
+    probs = probs.transpose(0, 2, 1).reshape(-1, experts)
     hot32 = hot.astype(jnp.float32)
-    row_gate = jnp.sum(hot32 * own_probs.transpose(0, 2, 1)[:, :, None, :], axis=-1)
-    x = jnp.einsum("sect,std->escd", hot, n2_all, preferred_element_type=jnp.float32).astype(jnp.bfloat16)
-    row_gate = row_gate.transpose(1, 0, 2)[..., None]
+    x, gate_all, down_weight = lax.optimization_barrier((x, gate_all, down_weight))
+    down_b, down_a = flip(down_weight, "cb"), flip(down_weight, "ca")
+    first_half = local_experts // 2
+    down_corner = [flip(down_b[:first_half], "ca"), flip(down_a[first_half:], "cb")]
     ee = lambda eq, a, b: jnp.einsum(eq, a, b, preferred_element_type=jnp.float32)
     gp = ee("escd,edf->escf", x, gate_all)
     up = ee("escd,edf->escf", x, up_all)
-    up, g_all = lax.optimization_barrier((up, g_all))
-    g_rows = jnp.einsum("sect,std->escd", hot, g_all, preferred_element_type=jnp.float32)
-    de = (g_rows * row_gate).astype(jnp.bfloat16)
     sig = jax.nn.sigmoid(gp)
     hid = (gp * sig * up).astype(jnp.bfloat16)
     down_part = ee("escf,escd->efd", hid, de).astype(jnp.bfloat16)
-    down_all, down_part = lax.optimization_barrier((down_all, down_part))
+    *down_corner, down_part = lax.optimization_barrier((*down_corner, down_part))
+    at_a, at_b = lax.axis_index("ca"), lax.axis_index("cb")
+    units = down_weight.shape[1]
+    down_all = jnp.zeros((local_experts, ctx_size * units, model_width), jnp.bfloat16)
+    for piece, p, q in (
+        (down_weight, at_a, at_b), (down_b, at_a, 1 - at_b), (down_a, 1 - at_a, at_b), (jnp.concatenate(down_corner), 1 - at_a, 1 - at_b)
+    ):
+        down_all = lax.dynamic_update_slice_in_dim(down_all, piece, (2 * p + q) * units, 1)
     eo = ee("escf,efd->escd", hid, down_all).astype(jnp.bfloat16)
-    dgate_rows = jnp.sum(g_rows * eo.astype(jnp.float32), axis=-1)
+    gained = jnp.sum(de.astype(jnp.float32) * eo.astype(jnp.float32), axis=-1)
     mixed_rows = (row_gate * eo.astype(jnp.float32)).astype(jnp.bfloat16)
     mixed_part = jnp.einsum("sect,escd->std", hot, mixed_rows, preferred_element_type=jnp.float32)
     mixed_part = mixed_part.astype(jnp.bfloat16)
@@ -906,11 +1036,11 @@
     down_grad, gate_grad, up_grad = rs_ctx(parts[0], 1), rs_ctx(parts[1], 2), rs_ctx(parts[2], 2)
     dpair = (ee("escf,edf->escd", dgp, gate_all) + ee("escf,edf->escd", dup, up_all)).astype(jnp.bfloat16)
 
-    dprobs_own = jnp.sum(hot32 * dgate_rows.transpose(1, 0, 2)[..., None], axis=2)
-    dprobs_own = dprobs_own.transpose(0, 2, 1).reshape(-1, local_experts)
+    gained = jnp.sum(hot32 * gained.transpose(1, 0, 2)[..., None], axis=2)
+    gained = gained.transpose(0, 2, 1).reshape(-1, local_experts)
     onto = (jnp.arange(experts)[None, :] == own_experts[:, None]).astype(jnp.float32)
-    dprobs = jnp.sum(dprobs_own[:, :, None] * onto[None], axis=1)
-    dlogit_low = (probs * (dprobs - jnp.sum(dprobs * probs, axis=-1, keepdims=True))).astype(jnp.bfloat16)
+    weighed = jnp.sum(gained[:, :, None] * onto[None], axis=1)
+    dlogit_low = (weighed - probs * jnp.sum(gained, axis=-1, keepdims=True)).astype(jnp.bfloat16)
     router_part = transposed_times(n2_all.reshape(-1, model_width), dlogit_low)
     dn2_part = jnp.einsum("sect,escd->std", hot, dpair, preferred_element_type=jnp.float32).reshape(-1, model_width)
     dn2_part = dn2_part + times_transposed(dlogit_low, full_router)
@@ -950,6 +1080,7 @@
     )
     small_parts = jnp.pad(small_parts, ((0, 0), (0, 0), (0, -small_parts.shape[2] % 2048)))
     small_parts = lax.dynamic_index_in_dim(small_parts, core, 1, False) + swap(lax.dynamic_index_in_dim(small_parts, 1 - core, 1, False))
+    small_parts, mixed = lax.optimization_barrier((small_parts, mixed))
     weight_grads, small_grads, input_grad, gain_first_sums = collect(
         parts, small_parts.reshape(ctx_size * sources // 2, -1, 128), (dq_low, dk_low, dv_low),
         (full_query, full_key, full_value), tokens[0], row(gain_first), grad_hidden,

time: 1080 us -> 1060 us (0.981)
  matrix products: 289 us -> 253 us
  Pallas kernels: 676 us -> 662 us
  local copies, waits for them, and re-layouts: 27.6 us -> 40.4 us
    dot_general x2 -> x0, matrix products: 22.6 us -> none  [the longest x1 14.2 us: local(): jnp.einsum('sect,std->escd', hot, g_all, preferred_element_type=jnp.float32)]
    pallas_call x1, Pallas kernels: 200 us -> 188 us  [collect(): pl.pallas_call(functools.partial(collect_kernel, count), out_shape=shapes...]
    dot_general x5 -> x4, matrix products: 31 us -> 21.4 us  [matmul(): return jnp.dot(left, right, preferred_element_type=jnp.float32)]
  transfers between devices with their start and end apart: 14 -> 17, of which waited for: 2 -> 5; matrix products, arithmetic and copies ran while one was open for 29% -> 28% of each run, Pallas kernels for 49% -> 30%
where the time goes in v4:
time: 1060 us; the launch traced here: 1050 us
  Pallas kernels  662 us (62%)
  matrix products  253 us (24%)
  waiting for transfers between devices  41.4 us (4%)
  local copies, waits for them, and re-layouts  40.4 us (4%)
  other arithmetic  32.4 us (3%)
  between operations  16 us (2%)
    pallas_call x1, Pallas kernels, collect(): pl.pallas_call(functools.partial(collect_kernel, count), out_shape=shapes...  188 us
    pallas_call x1, Pallas kernels, spread(): pl.pallas_call(functools.partial(spread_kernel, count, more), out_shape=[...  154 us
    dot_general x8, matrix products, local(): jnp.einsum(eq, a, b, preferred_element_type=jnp.float32)  146 us
    pallas_call x1, Pallas kernels, give_back(): pl.pallas_call(give_back_kernel, out_shape=jax.ShapeDtypeStruct((rows, co...  94.2 us
    pallas_call x1, Pallas kernels, attend(): pl.pallas_call(functools.partial(attend_kernel, scale), out_shape=[jax.Sh...  80.5 us
    pallas_call x1, Pallas kernels, dispatch(): pl.pallas_call(dispatch_kernel, out_shape=[low(ring, 2, count, width), lo...  79.4 us
    pallas_call x1, Pallas kernels, attend_back(): pl.pallas_call(functools.partial(attend_back_kernel, scale), out_shape=[j...  65.9 us
    all_gather x2, waiting for transfers between devices, local(): lax.all_gather(w, CTX, axis=2, tiled=True)  31.8 us
  transfers between devices with their start and end apart: 17, of which 5 were waited for; matrix products, arithmetic and copies ran while one was open for 28% of the time, Pallas kernels for 30%

profile of v4, /device:TPU:9, one launch (start us, length us, event | category | flops | bytes accessed | tf_op | source)
XLA Modules:
  0.0 1053.2 jit_solution(5489421111203932265)
XLA Ops:
  9.5 2.8 concatenate.33
  14.2 2.4 fusion.35.refs_6_
  16.7 154.2 %spread.1 = (bf16[2,2,4,2,64,2048]{5,4,3,2,1,0:T(8,128)(2,1)}, bf16[2,2,4,2,64,2048]{5,4,3,2,1,0:T(8,128)(2,1)}, bf16[2,2,4,2,64,2048]{5,4,3,2,1,0:T(8,128)(2,1)...) custom-call(bf16[64,2048]{1,0:T(8,128)(2,1)} %refs_0_.1, ...), custom_call_target="tpu_custom_call" | custom-call | flops 149999992832 | bytes 300000000 | tf_op jit(solution)/shard_map/spread/pallas_call | solution.py:217
  178.8 6.4 convolution_convert_fusion.5.v
  185.2 3.8 fusion.54.k_raw
  189.0 3.8 fusion.56.q_raw
  192.9 80.5 %attend.1 = (bf16[256,2048]{1,0:T(8,128)(2,1)S(1)}, bf16[1024,512]{1,0:T(8,128)(2,1)S(1)}, bf16[1024,512]{1,0:T(8,128)(2,1)S(1)}, bf16[1024,512]{1,0:T(8,128)(2,1)S(1)}, f32[4,1024,1]{2,1,0:T(8,128)}) custom-call(f32[256,2048]{1,0:T(8,128)} %fusion.56.q_raw, f32[256,2048]{1,0:T(8,128)} %fusion.54.k_raw, bf16[256,2048]{1,0:T(8,128)(2,1)S(1)} %convolution_convert_fusion.5.v, ...), custom_call_target="tpu_custom_call" | custom-call | flops 1000000 | bytes 10000 | tf_op jit(solution)/shard_map/attend/pallas_call | solution.py:829
  273.5 7.4 multiply_reduce_fusion.3
  281.5 1.4 fusion.28.hot
  284.2 79.4 %dispatch.1 = (bf16[4,2,256,2048]{3,2,1,0:T(8,128)(2,1)}, bf16[2,8,144,2048]{3,2,1,0:T(8,128)(2,1)}, bf16[2,8,144,2048]{3,2,1,0:T(8,128)(2,1)}, f32[2,8,144,1]{3,2,1,0:T(8,128)}, f32[8,16,256]{2,1,0:T(8,128)}) custom-call(bf16[256,2048]{1,0:T(8,128)(2,1)} %multiply_convert_fusion.4.rows, bf16[16,2048]{1,0:T(8,128)(2,1)} %bitcast.154, ...), custom_call_target="tpu_custom_call" | custom-call | flops 1000000 | bytes 10000 | tf_op jit(solution)/shard_map/dispatch/pallas_call | solution.py:568
  363.6 1.4 collective-permute-start.1
  365.5 17.5 %fusion.8 = f32[2,8,144,1024]{3,2,1,0:T(8,128)} fusion(bf16[2,8,144,2048]{3,2,1,0:T(8,128)(2,1)} %get-tuple-element.85, bf16[2,2048,1024]{2,1,0:T(8,128)(2,1)} %all-gather.3.cloned.1.call-done), kind=kOutput, calls=%fused_computation.20 | convolution fusion | flops 9663676416 | bytes 27262976 | tf_op jit(solution)/shard_map/escd,edf->escf/dot_general | solution.py:1008
  383.0 31.7 %all-gather.5.cloned.1.call-done = bf16[2,2048,1024]{2,1,0:T(8,128)(2,1)} async-done(((bf16[2,2048,256]{2,1,0:T(8,128)(2,1)}), bf16[2,2048,1024]{2,1,0:T(8,128)(2,1)}) %all-gather.5.cloned.1.call-update) | async-done | bytes 8388624 | tf_op jit(solution)/shard_map/all_gather | solution.py:976
  414.7 19.0 %multiply_convert_fusion.2 = (bf16[2,8,144,1024]{3,2,1,0:T(8,128)(2,1)S(1)}, f32[2,8,144,1024]{3,2,1,0:T(8,128)}) fusion(f32[2,8,144,1024]{3,2,1,0:T(8,128)} %fusion.8, bf16[2,8,144,2048]{3,2,1,0:T(8,128)(2,1)} %get-tuple-element.85, bf16[2,2048,1024]{2,1,0:T(8,128)(2,1)} %all-gather.5.cloned.1.call-done), kind=kOutput, calls=%fused_computation.16 | convolution fusion | flops 9677832192 | bytes 41418752 | tf_op jit(solution)/shard_map/escd,edf->escf/dot_general | solution.py:1008
  433.7 1.6 collective-permute-done.1
  437.6 2.3 slice.53
  440.1 16.8 %bitcast_convert_fusion.3 = bf16[2,1024,2048]{2,1,0:T(8,128)(2,1)} fusion(bf16[2,8,144,1024]{3,2,1,0:T(8,128)(2,1)S(1)} %get-tuple-element.204, bf16[2,8,144,2048]{3,2,1,0:T(8,128)(2,1)} %get-tuple-element.81), kind=kOutput, calls=%fused_computation.10 | convolution fusion | flops 9667870720 | bytes 22544384 | tf_op jit(solution)/shard_map/escf,escd->efd/dot_general | solution.py:1008
  456.9 3.3 collective-permute-done.3
  460.2 3.3 collective-permute-done.2
  463.7 4.3 broadcast_in_dim.6
  468.0 1.5 constant_dynamic-update-slice_fusion.2
  469.6 3.2 constant_dynamic-update-slice_fusion.1
  472.8 1.4 constant_dynamic-update-slice_fusion
  474.2 2.8 maximum_dynamic-update-slice_fusion
  477.0 22.0 %multiply_convert_fusion = (bf16[2,8,144,1024]{3,2,1,0:T(8,128)(2,1)}, bf16[2,8,144,1024]{3,2,1,0:T(8,128)(2,1)}) fusion(f32[2,8,144,1024]{3,2,1,0:T(8,128)} %fusion.8, f32[2,8,144,1024]{3,2,1,0:T(8,128)} %get-tuple-element.205, bf16[2,8,144,2048]{3,2,1,0:T(8,128)(2,1)} %get-tuple-element.81, bf16[2,1024,2048]{2,1,0:T(8,128)(2,1)} %maximum_dynamic-update-slice_fusion), kind=kOutput, calls=%fused_computation.14 | convolution fusion | flops 9694347264 | bytes 46137344 | tf_op jit(solution)/shard_map/escd,efd->escf/dot_general | solution.py:1008
  498.9 17.3 %bitcast_convert_fusion.2 = bf16[2,2048,1024]{2,1,0:T(8,128)(2,1)} fusion(bf16[2,8,144,2048]{3,2,1,0:T(8,128)(2,1)} %get-tuple-element.85, bf16[2,8,144,1024]{3,2,1,0:T(8,128)(2,1)} %get-tuple-element.91), kind=kOutput, calls=%fused_computation.9 | convolution fusion | flops 9667870720 | bytes 22544384 | tf_op jit(solution)/shard_map/escd,escf->edf/dot_general | solution.py:1008
  518.3 18.5 %fusion.1 = (bf16[2,8,144,2048]{3,2,1,0:T(8,128)(2,1)}, f32[2,8,144]{2,1,0:T(8,128)S(1)}) fusion(f32[2,8,144]{2,1,0:T(8,128)S(1)} %reduce.1, bf16[2,8,144,2048]{3,2,1,0:T(8,128)(2,1)} %get-tuple-element.81, bf16[2,8,144,1024]{3,2,1,0:T(8,128)(2,1)} %copy-done.48, bf16[2,1024,2048]{2,1,0:T(8,128)(2,1)} %maximum_dynamic-update-slice_fusion), kind=kOutput, calls=%fused_computation.3 | convolution fusion | flops 9696704512 | bytes 32000000 | tf_op jit(solution)/shard_map/escf,efd->escd/dot_general | solution.py:1008
  536.8 17.3 %bitcast_convert_fusion.1 = bf16[2,2048,1024]{2,1,0:T(8,128)(2,1)} fusion(bf16[2,8,144,2048]{3,2,1,0:T(8,128)(2,1)} %get-tuple-element.85, bf16[2,8,144,1024]{3,2,1,0:T(8,128)(2,1)} %get-tuple-element.92), kind=kOutput, calls=%fused_computation.8 | convolution fusion | flops 9667870720 | bytes 22544384 | tf_op jit(solution)/shard_map/escd,escf->edf/dot_general | solution.py:1008
  554.6 17.5 %fusion.14 = f32[2,8,144,2048]{3,2,0,1:T(8,128)} fusion(bf16[2,2048,1024]{2,1,0:T(8,128)(2,1)} %all-gather.5.cloned.1.call-done, bf16[2,8,144,1024]{3,2,1,0:T(8,128)(2,1)} %get-tuple-element.92), kind=kOutput, calls=%fused_computation.26 | convolution fusion | flops 9663676416 | bytes 31981568 | tf_op jit(solution)/shard_map/escf,edf->escd/dot_general | solution.py:1008
  572.9 25.5 %fusion.3 = f32[8,256,2048,1]{2,1,3,0:T(8,128)} fusion(f32[2,8,144,2048]{3,2,0,1:T(8,128)} %fusion.14, f32[8,2,256]{2,1,0:T(2,128)S(1)} %copy-done.31, pred[8,2,256]{2,1,0:T(4,128)(4,1)S(1)} %copy-done.37, bf16[2,2048,1024]{2,1,0:T(8,128)(2,1)} %all-gather.3.cloned.1.call-done, bf16[2,8,144,1024]{3,2,1,0:T(8,128)(2,1)} %get-tuple-element.91), kind=kOutput, calls=%fused_computation.11 | convolution fusion | flops 12090212352 | bytes 48779264 | tf_op jit(solution)/shard_map/sect,escd->std/dot_general | solution.py:1045
  598.5 11.6 %fusion.2 = bf16[2048,2048]{1,0:T(8,128)(2,1)} fusion(f32[8,256,2048,1]{2,1,3,0:T(8,128)} %fusion.3, bf16[2048,16]{0,1:T(8,128)(2,1)S(1)} %bitcast.155, bf16[2048,16]{1,0:T(8,128)(2,1)S(1)} %copy-done.13), kind=kOutput, calls=%fused_computation.6 | convolution fusion | flops 142606336 | bytes 25296896 | tf_op jit(solution)/shard_map/dot_general | solution.py:690
  610.0 10.6 %bitcast_convert_fusion = bf16[8,256,2048]{2,1,0:T(8,128)(2,1)} fusion(bf16[2,8,144,2048]{3,2,1,0:T(8,128)(2,1)} %get-tuple-element.178, f32[8,2,256]{2,1,0:T(2,128)S(1)} %copy-done.31, pred[8,2,256]{2,1,0:T(4,128)(4,1)S(1)} %copy-done.37), kind=kOutput, calls=%fused_computation.7 | convolution fusion | flops 2421293056 | bytes 17846272 | tf_op jit(solution)/shard_map/sect,escd->std/dot_general | solution.py:1025
  620.6 94.2 %give_back.1 = f32[256,2048]{1,0:T(8,128)} custom-call(bf16[4,2,2,128,2048]{4,3,2,1,0:T(8,128)(2,1)} %bitcast.146), custom_call_target="tpu_custom_call" | custom-call | flops 99999997952 | bytes 200000000 | tf_op jit(solution)/shard_map/give_back/pallas_call | solution.py:673
  717.2 7.1 fusion.80
  724.4 1.8 reshape.303
  726.2 2.2 multiply_reduce_fusion.1
  728.5 4.0 fusion.70
  732.5 7.1 convolution_convert_fusion.4.do
  739.6 65.9 %attend_back.1 = (bf16[256,2048]{1,0:T(8,128)(2,1)}, bf16[256,2048]{1,0:T(8,128)(2,1)}, bf16[256,2048]{1,0:T(8,128)(2,1)}, f32[8,2048]{1,0:T(8,128)}, f32[8,2048]{1,0:T(8,128)}) custom-call(bf16[256,2048]{1,0:T(8,128)(2,1)} %convolution_convert_fusion.4.do, bf16[1024,512]{1,0:T(8,128)(2,1)} %copy-done.7, bf16[1024,512]{1,0:T(8,128)(2,1)} %copy-done.8, ...), custom_call_target="tpu_custom_call" | custom-call | flops 49999998976 | bytes 10000000 | tf_op jit(solution)/shard_map/attend_back/pallas_call | solution.py:904
  814.6 6.0 convolution_convert_fusion.1
  820.6 6.0 convolution_convert_fusion.2
  826.6 5.9 convolution_convert_fusion
  832.5 5.6 convolution_convert_fusion.3
  838.8 188.3 %collect.1 = (f32[16,128]{1,0:T(8,128)}, f32[64,2048]{1,0:T(8,128)}, f32[64,2048]{1,0:T(8,128)}, f32[64,2048]{1,0:T(8,128)}, f32[64,2048]{1,0:T(8,128)}, /*index=5*/bf16[256,2048]{1,0:T(8,128)(2,1)}, f32[8,2048]{1,0:T(8,128)}) custom-call(f32[2,2,4,16,128]{4,3,2,1,0:T(8,128)} %bitcast.160, bf16[2,2,4,128,1024]{4,3,2,1,0:T(8,128)(2,1)} %bitcast.179, ...), custom_call_target="tpu_custom_call" | custom-call | flops 160000000000 | bytes 320000000 | tf_op jit(solution)/shard_map/collect/pallas_call | solution.py:447
  1027.1 3.0 fusion.41
  1033.8 2.5 convert_element_type.283
  1036.3 2.3 convert_element_type.284
  1038.7 2.5 convert_element_type.285
  (212 shorter events, 40.5 us)
Async XLA Ops:
  7.2 356.4 %all-gather.3.cloned.1.call-start = ((), (), s32[]{:S(2)}) async-start(), calls=%async_computation.4 | async-start | bytes 10485760 | tf_op jit(solution)/shard_map/all_gather | solution.py:976
  170.9 243.8 %all-gather.5.cloned.1.call-start = ((), (), s32[]{:S(2)}) async-start(), calls=%async_computation.5 | async-start | bytes 10485760 | tf_op jit(solution)/shard_map/all_gather | solution.py:976
  171.6 449.0 %reduce-scatter.5.cloned.1.call-start = ((), (), s32[]{:S(2)}) async-start(), calls=%async_computation.6 | async-start | bytes 10485760 | tf_op jit(solution)/shard_map/reduce_scatter | solution.py:1035
  172.8 110.2 %copy-start.34 = (f32[2048]{0:T(1024)}, f32[2048]{0:T(1024)S(1)}, u32[]{:S(2)}) copy-start(f32[2048]{0:T(1024)S(1)} %reshape.315) | copy-start | bytes 24580
  173.4 19.4 %copy-start.2 = (f32[1,2048]{1,0:T(1,128)}, f32[1,2048]{1,0:T(1,128)S(1)}, u32[]{:S(2)}) copy-start(f32[1,2048]{1,0:T(1,128)S(1)} %reshape.313.k_gain) | copy-start | bytes 24580
  173.5 19.4 %copy-start.3 = (f32[1,2048]{1,0:T(1,128)}, f32[1,2048]{1,0:T(1,128)S(1)}, u32[]{:S(2)}) copy-start(f32[1,2048]{1,0:T(1,128)S(1)} %reshape.312.q_gain) | copy-start | bytes 24580
  173.9 11.3 %copy-start.12 = (bf16[2048,16]{1,0:T(8,128)(2,1)}, bf16[2048,16]{1,0:T(8,128)(2,1)S(1)}, u32[]{:S(2)}) copy-start(bf16[2048,16]{1,0:T(8,128)(2,1)S(1)} %reshape.296) | copy-start | bytes 196612
  176.3 105.3 %copy-start.36 = (pred[8,2,256]{2,1,0:T(4,128)(4,1)}, pred[8,2,256]{2,1,0:T(4,128)(4,1)S(1)}, u32[]{:S(2)}) copy-start(pred[8,2,256]{2,1,0:T(4,128)(4,1)S(1)} %compare_reduce_fusion) | copy-start | bytes 12292
  176.4 105.1 %copy-start.30 = (f32[8,2,256]{2,1,0:T(2,128)}, f32[8,2,256]{2,1,0:T(2,128)S(1)}, u32[]{:S(2)}) copy-start(f32[8,2,256]{2,1,0:T(2,128)S(1)} %copy.64) | copy-start | bytes 49156
  176.5 16.4 %copy-start.4 = (f32[1,1024]{1,0:T(1,128)}, f32[1,1024]{1,0:T(1,128)S(1)}, u32[]{:S(2)}) copy-start(f32[1,1024]{1,0:T(1,128)S(1)} %compare_convert_fusion.keep) | copy-start | bytes 12292
  177.2 15.7 %copy-start = (f32[256,128]{1,0:T(8,128)}, f32[256,128]{1,0:T(8,128)S(1)}, u32[]{:S(2)}) copy-start(f32[256,128]{1,0:T(8,128)S(1)} %get-tuple-element.206.cosine) | copy-start | bytes 393220
  177.2 15.6 %copy-start.1 = (f32[256,128]{1,0:T(8,128)}, f32[256,128]{1,0:T(8,128)S(1)}, u32[]{:S(2)}) copy-start(f32[256,128]{1,0:T(8,128)S(1)} %get-tuple-element.207.sine) | copy-start | bytes 393220
  177.5 7.7 slice-start.2
  178.8 10.2 slice-start
  273.4 7.4 copy-start.5
  273.4 7.4 copy-start.7
  273.4 7.4 copy-start.8
  273.4 7.4 copy-start.9
  281.5 82.0 %copy-start.43 = (f32[256]{0:T(256)}, f32[256]{0:T(256)S(1)}, u32[]{:S(2)}) copy-start(f32[256]{0:T(256)S(1)} %get-tuple-element.201) | copy-start | bytes 3076
  363.6 71.8 %collective-permute-start.1 = (bf16[2,256,2048]{2,1,0:T(8,128)(2,1)}, bf16[2,256,2048]{2,1,0:T(8,128)(2,1)S(1)}, u32[]{:S(2)}, u32[]{:S(2)}) collective-permute-start(bf16[2,256,2048]{2,1,0:T(8,128)(2,1)} %param.31), channel_id=1, source_target_pairs={{0,16},{16,0},{1,17},{17,1},{2,18},{18,2},{3,19},{19,3},{4,20},{20... | collective-permute-start | bytes 6291464 | tf_op jit(solution)/shard_map/ppermute | solution.py:988
  364.9 72.7 %collective-permute-start = (bf16[2,256,2048]{2,1,0:T(8,128)(2,1)}, bf16[2,256,2048]{2,1,0:T(8,128)(2,1)}, u32[]{:S(2)}, u32[]{:S(2)}) collective-permute-start(bf16[2,256,2048]{2,1,0:T(8,128)(2,1)} %param.31), channel_id=1, source_target_pairs={{0,8},{8,0},{1,9},{9,1},{2,10},{10,2},{3,11},{11,3},{4,12},{12,4},... | collective-permute-start | bytes 6291464 | tf_op jit(solution)/shard_map/ppermute | solution.py:988
  433.7 6.4 copy-start.48
  436.4 23.8 %collective-permute-start.3 = (bf16[1,256,2048]{2,1,0:T(8,128)(2,1)}, bf16[1,256,2048]{2,1,0:T(8,128)(2,1)S(1)}, u32[]{:S(2)}, u32[]{:S(2)}) collective-permute-start(bf16[1,256,2048]{2,1,0:T(8,128)(2,1)} %slice.54), channel_id=1, source_target_pairs={{0,8},{8,0},{1,9},{9,1},{2,10},{10,2},{3,11},{11,3},{4,12},{12,4},... | collective-permute-start | bytes 3145736 | tf_op jit(solution)/shard_map/ppermute | solution.py:988
  439.9 23.5 %collective-permute-start.2 = (bf16[1,256,2048]{2,1,0:T(8,128)(2,1)}, bf16[1,256,2048]{2,1,0:T(8,128)(2,1)}, u32[]{:S(2)}, u32[]{:S(2)}) collective-permute-start(bf16[1,256,2048]{2,1,0:T(8,128)(2,1)} %slice.53), channel_id=1, source_target_pairs={{0,16},{16,0},{1,17},{17,1},{2,18},{18,2},{3,19},{19,3},{4,20},{20... | collective-permute-start | bytes 3145736 | tf_op jit(solution)/shard_map/ppermute | solution.py:988
  463.5 251.4 %reduce-scatter.7.cloned.1.call-start = ((), (), s32[]{:S(2)}) async-start(), calls=%async_computation.7 | async-start | bytes 10485760 | tf_op jit(solution)/shard_map/reduce_scatter | solution.py:1035
  516.3 292.4 %reduce-scatter.11.cloned.1.call-start = ((), (), s32[]{:S(2)}) async-start(), calls=%async_computation.9 | async-start | bytes 10485760 | tf_op jit(solution)/shard_map/reduce_scatter | solution.py:1035
  554.1 17.9 %copy-start.31 = (f32[8,2,256]{2,1,0:T(2,128)S(1)}, f32[8,2,256]{2,1,0:T(2,128)}, u32[]{:S(2)}) copy-start(f32[8,2,256]{2,1,0:T(2,128)} %copy-done.30) | copy-start | bytes 49156
  554.1 17.9 %copy-start.37 = (pred[8,2,256]{2,1,0:T(4,128)(4,1)S(1)}, pred[8,2,256]{2,1,0:T(4,128)(4,1)}, u32[]{:S(2)}) copy-start(pred[8,2,256]{2,1,0:T(4,128)(4,1)} %copy-done.36) | copy-start | bytes 12292
  554.2 18.7 %copy-start.38 = (f32[8,16,256]{2,1,0:T(8,128)S(1)}, f32[8,16,256]{2,1,0:T(8,128)}, u32[]{:S(2)}) copy-start(f32[8,16,256]{2,1,0:T(8,128)} %get-tuple-element.93) | copy-start | bytes 393220
  554.2 283.9 %reduce-scatter.9.cloned.1.call-start = ((), (), s32[]{:S(2)}) async-start(), calls=%async_computation.8 | async-start | bytes 9437184 | tf_op jit(solution)/shard_map/reduce_scatter | solution.py:1052
  572.9 25.5 %copy-start.13 = (bf16[2048,16]{1,0:T(8,128)(2,1)S(1)}, bf16[2048,16]{1,0:T(8,128)(2,1)}, u32[]{:S(2)}) copy-start(bf16[2048,16]{1,0:T(8,128)(2,1)} %copy-done.12) | copy-start | bytes 196612
  714.9 98.6 %collective-permute-start.7 = (bf16[256,2048]{1,0:T(8,128)(2,1)}, bf16[256,2048]{1,0:T(8,128)(2,1)}, u32[]{:S(2)}, u32[]{:S(2)}) collective-permute-start(bf16[256,2048]{1,0:T(8,128)(2,1)} %fusion.31), channel_id=1, source_target_pairs={{0,1},{1,0},{2,3},{3,2},{4,5},{5,4},{6,7},{7,6},{8,9},{9,8},{10,11... | collective-permute-start | bytes 3145736 | tf_op jit(solution)/shard_map/ppermute | solution.py:1063
  716.1 116.3 %collective-permute-start.5 = (bf16[256,2048]{1,0:T(8,128)(2,1)S(1)}, bf16[256,2048]{1,0:T(8,128)(2,1)}, u32[]{:S(2)}, u32[]{:S(2)}) collective-permute-start(bf16[256,2048]{1,0:T(8,128)(2,1)S(1)} %copy-done.6), channel_id=1, source_target_pairs={{0,1},{1,0},{2,3},{3,2},{4,5},{5,4},{6,7},{7,6},{8,9},{9,8},{10,11... | collective-permute-start | bytes 3145736 | tf_op jit(solution)/shard_map/ppermute | solution.py:1063
  717.2 8.9 copy-start.11
  717.2 9.0 copy-start.35
  717.2 9.0 copy-start.44
  732.5 7.1 copy-start.14
  739.6 71.5 %copy-start.15 = (bf16[256,2048]{1,0:T(8,128)(2,1)S(1)}, bf16[256,2048]{1,0:T(8,128)(2,1)}, u32[]{:S(2)}) copy-start(bf16[256,2048]{1,0:T(8,128)(2,1)} %copy-done.14) | copy-start | bytes 3145732
  805.5 7.7 copy-start.24
  809.7 3.6 collective-permute-start.4
  811.2 21.3 %collective-permute-start.6 = (bf16[256,1024]{1,0:T(8,128)(2,1)S(1)}, bf16[256,1024]{1,0:T(8,128)(2,1)S(1)}, u32[]{:S(2)}, u32[]{:S(2)}) collective-permute-start(bf16[256,1024]{1,0:T(8,128)(2,1)S(1)} %get-tuple-element.187), channel_id=1, source_target_pairs={{0,1},{1,0},{2,3},{3,2},{4,5},{5,4},{6,7},{7,6},{8,9},{9,8},{10,11... | collective-permute-start | bytes 1572872 | tf_op jit(solution)/shard_map/ppermute | solution.py:1063
  812.6 2.0 collective-permute-start.9
  813.3 7.3 collective-permute-start.8
  813.5 13.1 %collective-permute-start.10 = (bf16[256,1024]{1,0:T(8,128)(2,1)S(1)}, bf16[256,1024]{1,0:T(8,128)(2,1)S(1)}, u32[]{:S(2)}, u32[]{:S(2)}) collective-permute-start(bf16[256,1024]{1,0:T(8,128)(2,1)S(1)} %get-tuple-element.181), channel_id=1, source_target_pairs={{0,1},{1,0},{2,3},{3,2},{4,5},{5,4},{6,7},{7,6},{8,9},{9,8},{10,11... | collective-permute-start | bytes 1572872 | tf_op jit(solution)/shard_map/ppermute | solution.py:1063
  838.8 188.3 %copy-start.22 = (bf16[256,2048]{1,0:T(8,128)(2,1)S(1)}, bf16[256,2048]{1,0:T(8,128)(2,1)}, u32[]{:S(2)}) copy-start(bf16[256,2048]{1,0:T(8,128)(2,1)} %reduce-scatter.9.cloned.1.call-done) | copy-start | bytes 3145732
  838.8 188.3 %copy-start.42 = (f32[256]{0:T(256)S(1)}, f32[256]{0:T(256)}, u32[]{:S(2)}) copy-start(f32[256]{0:T(256)} %copy-done.40) | copy-start | bytes 3076
  1027.1 6.7 copy-start.18
  1038.6 6.5 copy-start.26
  (22 other events, 71.3 us)
Sparse Core Ops, SparseCore 0:
  171.0 131.4 all-gather.2
  304.3 110.3 all-gather.4
  463.6 87.2 reduce-scatter.4
  554.1 86.3 reduce-scatter.6
  643.4 86.3 reduce-scatter.10
  732.1 88.1 reduce-scatter.8

commit v5 on v4

--- a/solution.py
+++ b/solution.py
@@ -582,37 +582,99 @@
     )(rows, router, hot, g_all)
 
 
-def give_back_kernel(part, out, own, core_in, chain_in, load, core_send, core_got, chain_send, chain_got):
-    ring, pieces, rows, cols = own.shape
+def give_back_kernel(
+    hot, logit, logit_turned, router, pairs, mixed, n2, out, mixed_out, router_part,
+    sums, chain_in, to_core, pair_in, mixed_in, mixed_low, n2_in,
+    load, core_send, core_got, chain_send, chain_got, load_more, store,
+):
+    ring, pieces, rows, width = sums.shape
+    sources, experts = hot.shape[:2]
     r, c, nc = lax.axis_index("ring"), lax.axis_index("core"), turn("core", 1)
     to_next, to_last = {"ring": turn("ring", 1)}, {"ring": turn("ring", ring - 1)}
     greet([{"core": nc}] + [{"ring": turn("ring", k)} for k in range(1, ring)])
-    order = [d for pair in zip(reversed(range(ring)), range(ring)) for d in pair][:ring]
-    for d in order:
-        push(part.at[d, nc], core_in.at[d], core_send.at[d], core_got.at[d], {"core": nc})
-        pltpu.make_async_copy(part.at[d, c], own.at[d], load.at[d]).start()
-    tile = 32
-
-    def add(d, piece, other):
-        def one(i, carry):
-            at = pl.ds(pl.multiple_of(i * tile, tile), tile)
-            own[d, piece, at] = (own[d, piece, at].astype(jnp.float32) + other[at].astype(jnp.float32)).astype(own.dtype)
+    cols, tile = min(512, width), 32
+
+    def whose(i):
+        return (1 - i % 2) * (ring - 1 - i // 2) + (i % 2) * (i // 2)
+
+    def fetch(i, j):
+        return pltpu.make_async_copy(pairs.at[:, whose(i) * 2 + (nc, c)[j]], pair_in.at[j], load.at[j])
+
+    def put_back(source, ref, lanes):
+        return sum(matmul(hot[source, e], ref[e, :, lanes]) for e in range(experts))
+
+    def block(source, j, into, more):
+        def part(k, carry):
+            lanes = pl.ds(pl.multiple_of(k * cols, cols), cols)
+            value = put_back(source, pair_in.at[j], lanes) + matmul(logit[source], router[:, lanes])
+            for piece in range(pieces):
+                got = value[piece * rows : (piece + 1) * rows]
+                if more is not None:
+                    got = got + more[piece, :, lanes].astype(jnp.float32)
+                into[piece, :, lanes] = got.astype(into.dtype)
             return carry
 
-        lax.fori_loop(0, rows // tile, one, 0)
-
-    def slot(side, d, whose):
-        return d if side == 0 else jnp.where(d == whose, ring, d)
+        lax.fori_loop(0, width // cols, part, 0)
+
+    def fetch_beside(source):
+        at = lax.rem(source, 2)
+        return (
+            pltpu.make_async_copy(mixed.at[:, source], mixed_in.at[at], load_more.at[at, 0]),
+            pltpu.make_async_copy(n2.at[source], n2_in.at[at], load_more.at[at, 1]),
+        )
+
+    def beside(source):
+        at = lax.rem(source, 2)
+
+        @pl.when(source + 1 < sources)
+        def _():
+            for copy in fetch_beside(source + 1):
+                copy.start()
+
+        for copy in fetch_beside(source):
+            copy.wait()
+
+        @pl.when(source > 0)
+        def _():
+            await_bytes(mixed_low, store)
+
+        def part(k, carry):
+            lanes = pl.ds(pl.multiple_of(k * cols, cols), cols)
+            mixed_low[:, lanes] = put_back(source, mixed_in.at[at], lanes).astype(mixed_low.dtype)
+            router_part[:, lanes] += matmul(logit_turned[source], n2_in[at, :, lanes])
+            return carry
+
+        lax.fori_loop(0, width // cols, part, 0)
+        pltpu.make_async_copy(mixed_low, mixed_out.at[source], store).start()
+
+    def slot(side, d, at):
+        return d if side == 0 else jnp.where(d == at, ring, d)
 
     def pass_on(side, step, d, piece, to):
         there = chain_in.at[slot(side, d, r - 1), piece]
-        push(own.at[d, piece], there, chain_send.at[side, step, piece], chain_got.at[side, step, piece], to)
-
-    for d in order:
-        await_bytes(own.at[d], load.at[d])
-        await_bytes(core_in.at[d], core_got.at[d])
+        push(sums.at[d, piece], there, chain_send.at[side, step, piece], chain_got.at[side, step, piece], to)
+
+    router_part[...] = jnp.zeros_like(router_part)
+    fetch(0, 0).start()
+    fetch(0, 1).start()
+    for copy in fetch_beside(0):
+        copy.start()
+
+    def start(i, carry):
+        d = whose(i)
+        outgoing = to_core.at[lax.rem(i, 2)]
+        fetch(i, 0).wait()
+
+        @pl.when(i >= 2)
+        def _():
+            await_bytes(outgoing, core_send.at[lax.rem(i, 2)])
+
+        block(d * 2 + nc, 0, outgoing, None)
+        push(outgoing, sums.at[d], core_send.at[lax.rem(i, 2)], core_got.at[d], {"core": nc})
+        fetch(i, 1).wait()
+        await_bytes(sums.at[d], core_got.at[d])
+        block(d * 2 + c, 1, sums.at[d], sums.at[d])
         for piece in range(pieces):
-            add(d, piece, core_in.at[d, piece])
 
             @pl.when((r == 0) & (d != r))
             def _():
@@ -621,6 +683,16 @@
             @pl.when((r == ring - 1) & (d != r))
             def _():
                 pass_on(1, d, d, piece, to_last)
+
+        @pl.when(i + 1 < ring)
+        def _():
+            fetch(i + 1, 0).start()
+            fetch(i + 1, 1).start()
+
+        beside(i)
+        return carry
+
+    lax.fori_loop(0, ring, start, 0)
 
     def sides(time):
         up, down = time - r, time - (ring - 1 - r)
@@ -637,49 +709,76 @@
                 def _(step=step, d=d, to=to, side=side):
                     arrived = chain_in.at[slot(side, d, r), piece]
                     await_bytes(arrived, chain_got.at[side, step, piece])
-                    add(d, piece, arrived)
+
+                    def one(k, carry):
+                        at = pl.ds(pl.multiple_of(k * tile, tile), tile)
+                        total = sums[d, piece, at].astype(jnp.float32) + arrived[at].astype(jnp.float32)
+                        sums[d, piece, at] = total.astype(sums.dtype)
+                        return carry
+
+                    lax.fori_loop(0, rows // tile, one, 0)
 
                     @pl.when(time < ring - 1)
                     def _():
                         pass_on(side, step, d, piece, to)
 
+        @pl.when(time < ring - 1)
+        def _():
+            beside(ring + time - 1)
+
         return carry
 
-    lax.fori_loop(1, ring, on, 0)
-
-    def total(i, carry):
-        at = pl.ds(pl.multiple_of(i * tile, tile), tile)
+    def rest(source, carry):
+        beside(source)
+        return carry
+
+    lax.fori_loop(1, ring - 1, on, 0)
+    lax.fori_loop(2 * ring - 2, sources, rest, 0)
+    on(ring - 1, 0)
+    await_bytes(mixed_low, store)
+
+    def total(k, carry):
+        at = pl.ds(pl.multiple_of(k * tile, tile), tile)
         for piece in range(pieces):
-            out[pl.ds(pl.multiple_of(piece * rows + i * tile, tile), tile), :] = own[r, piece, at].astype(jnp.float32)
+            out[pl.ds(pl.multiple_of(piece * rows + k * tile, tile), tile), :] = sums[r, piece, at].astype(jnp.float32)
         return carry
 
     lax.fori_loop(0, rows // tile, total, 0)
-    for d in order:
-        await_bytes(core_in.at[d], core_send.at[d])
+    for k in range(2):
+        await_bytes(to_core.at[k], core_send.at[k])
     for step in range(ring - 1):
         for piece in range(pieces):
             for sent, side in ((r + step < ring - 1, 0), (step < r, 1)):
 
                 @pl.when(sent)
                 def _(side=side):
-                    await_bytes(own.at[0, 0], chain_send.at[side, step, piece])
-
-
-def give_back(part):
+                    await_bytes(sums.at[0, 0], chain_send.at[side, step, piece])
+
+
+def give_back(hot, logit, router, pairs, mixed, n2):
     ring, dma, pieces = lax.axis_size("ring"), pltpu.SemaphoreType.DMA, 2
-    rows, cols = part.shape[1:]
-    block = lambda *lead: pltpu.VMEM((*lead, pieces, rows // pieces, cols), part.dtype)
+    experts, sources, slots, width = pairs.shape
+    rows, all_experts = hot.shape[2], router.shape[0]
+    vm, anywhere = pl.BlockSpec(memory_space=pltpu.VMEM), pl.BlockSpec(memory_space=pl.ANY)
+    low = lambda *shape: pltpu.VMEM(shape, pairs.dtype)
+    block = lambda n: low(n, pieces, rows // pieces, width)
     chain = dma((2, ring, pieces))
     return pl.pallas_call(
         give_back_kernel,
-        out_shape=jax.ShapeDtypeStruct((rows, cols), jnp.float32),
-        in_specs=[pl.BlockSpec(memory_space=pl.ANY)],
-        out_specs=pl.BlockSpec(memory_space=pltpu.VMEM),
-        scratch_shapes=[block(ring), block(ring), block(ring + 1), dma((ring,)), dma((ring,)), dma((ring,)), chain, chain],
+        out_shape=[
+            jax.ShapeDtypeStruct((rows, width), jnp.float32),
+            jax.ShapeDtypeStruct((sources, rows, width), pairs.dtype),
+            jax.ShapeDtypeStruct((all_experts, width), jnp.float32),
+        ],
+        in_specs=[vm] * 4 + [anywhere] * 3,
+        out_specs=[vm, anywhere, vm],
+        scratch_shapes=[block(ring), block(ring + 1), block(2), low(2, experts, slots, width), low(2, experts, slots, width)]
+        + [low(rows, width), low(2, rows, width)]
+        + [dma((2,)), dma((2,)), dma((ring,)), chain, chain, dma((2, 2)), dma],
         compiler_params=pltpu.CompilerParams(collective_id=3, has_side_effects=True, vmem_limit_bytes=60 << 20),
         cost_estimate=pl.CostEstimate(flops=100_000_000_000, bytes_accessed=200_000_000, transcendentals=0),
         name="give_back",
-    )(part.reshape(ring, 2, pieces, rows // pieces, cols))
+    )(hot, logit, logit.transpose(0, 2, 1), router, pairs, mixed, n2)
 
 
 def matmul(left, right):
@@ -914,6 +1013,44 @@
         cost_estimate=pl.CostEstimate(flops=50_000_000_000, bytes_accessed=10_000_000, transcendentals=0),
         name="attend_back",
     )(do, qh, kh, vh, logs, keep, q_raw, k_raw, q_gain, k_gain, cosine, sine)
+
+
+def join_kernel(own, from_b, from_a, first, second, out, held, load, store):
+    experts, units = own.shape[:2]
+    a, b = lax.axis_index("ca"), lax.axis_index("cb")
+    na, nb = turn("ca", 1), turn("cb", 1)
+    loads, stores = [], []
+    for piece, (p, q) in enumerate(((a, b), (a, nb), (na, b), (na, nb))):
+        for e in range(experts):
+            if piece < 3:
+                src = (own, from_b, from_a)[piece].at[e]
+            else:
+                src = first.at[e] if e < experts // 2 else second.at[e - experts // 2]
+            here = held.at[piece, e]
+            loads.append(pltpu.make_async_copy(src, here, load.at[piece, e]))
+            at = pl.ds(pl.multiple_of((2 * p + q) * units, units), units)
+            stores.append(pltpu.make_async_copy(here, out.at[e, at, :], store.at[piece, e]))
+    for copy in loads:
+        copy.start()
+    for fetch, copy in zip(loads, stores):
+        fetch.wait()
+        copy.start()
+    for copy in stores:
+        copy.wait()
+
+
+def join(own, from_b, from_a, first, second):
+    experts, units, width = own.shape
+    anywhere, dma = pl.BlockSpec(memory_space=pl.ANY), pltpu.SemaphoreType.DMA((4, experts))
+    return pl.pallas_call(
+        join_kernel,
+        out_shape=jax.ShapeDtypeStruct((experts, 4 * units, width), own.dtype),
+        in_specs=[anywhere] * 5,
+        out_specs=anywhere,
+        scratch_shapes=[pltpu.VMEM((4, experts, units, width), own.dtype), dma, dma],
+        cost_estimate=pl.CostEstimate(flops=0, bytes_accessed=8 * experts * units * width * 2, transcendentals=0),
+        name="join",
+    )(own, from_b, from_a, first, second)
 
 
 def norm_rows(values, gain):
@@ -997,7 +1134,8 @@
     ranks = jnp.einsum("seu,ut->set", mask.astype(jnp.bfloat16), before, preferred_element_type=jnp.float32)
     slots = jnp.arange(capacity, dtype=jnp.float32)
     hot = (mask[:, :, None, :] & (ranks[:, :, None, :] == slots[None, None, :, None])).astype(jnp.bfloat16)
-    n2_all, x, de, row_gate, probs = dispatch(normed_two_low, full_router.T, hot, g_all)
+    router_turned = full_router.T
+    n2_all, x, de, row_gate, probs = dispatch(normed_two_low, router_turned, hot, g_all)
     n2_all = n2_all.reshape(sources, token_count, model_width)
     probs = probs.transpose(0, 2, 1).reshape(-1, experts)
     hot32 = hot.astype(jnp.float32)
@@ -1012,19 +1150,10 @@
     hid = (gp * sig * up).astype(jnp.bfloat16)
     down_part = ee("escf,escd->efd", hid, de).astype(jnp.bfloat16)
     *down_corner, down_part = lax.optimization_barrier((*down_corner, down_part))
-    at_a, at_b = lax.axis_index("ca"), lax.axis_index("cb")
-    units = down_weight.shape[1]
-    down_all = jnp.zeros((local_experts, ctx_size * units, model_width), jnp.bfloat16)
-    for piece, p, q in (
-        (down_weight, at_a, at_b), (down_b, at_a, 1 - at_b), (down_a, 1 - at_a, at_b), (jnp.concatenate(down_corner), 1 - at_a, 1 - at_b)
-    ):
-        down_all = lax.dynamic_update_slice_in_dim(down_all, piece, (2 * p + q) * units, 1)
+    down_all = join(down_weight, down_b, down_a, *down_corner)
     eo = ee("escf,efd->escd", hid, down_all).astype(jnp.bfloat16)
     gained = jnp.sum(de.astype(jnp.float32) * eo.astype(jnp.float32), axis=-1)
     mixed_rows = (row_gate * eo.astype(jnp.float32)).astype(jnp.bfloat16)
-    mixed_part = jnp.einsum("sect,escd->std", hot, mixed_rows, preferred_element_type=jnp.float32)
-    mixed_part = mixed_part.astype(jnp.bfloat16)
-
     dhid = ee("escd,efd->escf", de, down_all)
     dgp = (dhid * up * sig * (1.0 + gp * (1.0 - sig))).astype(jnp.bfloat16)
     dup = (dhid * gp * sig).astype(jnp.bfloat16)
@@ -1041,14 +1170,12 @@
     onto = (jnp.arange(experts)[None, :] == own_experts[:, None]).astype(jnp.float32)
     weighed = jnp.sum(gained[:, :, None] * onto[None], axis=1)
     dlogit_low = (weighed - probs * jnp.sum(gained, axis=-1, keepdims=True)).astype(jnp.bfloat16)
-    router_part = transposed_times(n2_all.reshape(-1, model_width), dlogit_low)
-    dn2_part = jnp.einsum("sect,escd->std", hot, dpair, preferred_element_type=jnp.float32).reshape(-1, model_width)
-    dn2_part = dn2_part + times_transposed(dlogit_low, full_router)
-    dn2_part = dn2_part.astype(jnp.bfloat16).reshape(sources, token_count, model_width)
-    dn2_part, down_grad = lax.optimization_barrier((dn2_part, down_grad))
-    dn2 = give_back(dn2_part)
+    dpair, down_grad = lax.optimization_barrier((dpair, down_grad))
+    dn2, mixed_part, router_part = give_back(
+        hot.transpose(0, 1, 3, 2), dlogit_low.reshape(sources, token_count, experts), router_turned, dpair, mixed_rows, n2_all
+    )
+    router_part = router_part.T
     dn2, gate_grad = lax.optimization_barrier((dn2, gate_grad))
-    dn2, mixed_part = lax.optimization_barrier((dn2, mixed_part))
     mixed = lax.psum_scatter(mixed_part.reshape(-1, model_width), EXP, scatter_dimension=0, tiled=True)
 
     dh_norm, gain_second_part = norm_back(dn2, hidden_state, factor_two, gain_second)
@@ -1080,7 +1207,6 @@
     )
     small_parts = jnp.pad(small_parts, ((0, 0), (0, 0), (0, -small_parts.shape[2] % 2048)))
     small_parts = lax.dynamic_index_in_dim(small_parts, core, 1, False) + swap(lax.dynamic_index_in_dim(small_parts, 1 - core, 1, False))
-    small_parts, mixed = lax.optimization_barrier((small_parts, mixed))
     weight_grads, small_grads, input_grad, gain_first_sums = collect(
         parts, small_parts.reshape(ctx_size * sources // 2, -1, 128), (dq_low, dk_low, dv_low),
         (full_query, full_key, full_value), tokens[0], row(gain_first), grad_hidden,

time: 1060 us -> 1040 us (0.981)
  matrix products: 253 us -> 215 us
  Pallas kernels: 662 us -> 690 us
    dot_general x2 -> x0, matrix products: 36.1 us -> none  [the longest x1 25.5 us: local(): jnp.einsum('sect,escd->std', hot, dpair, preferred_element_type=jnp.float32)]
    dot_general x8 -> x9, matrix products: 146 us -> 166 us  [local(): jnp.einsum(eq, a, b, preferred_element_type=jnp.float32)]
    dot_general x2 -> x1, matrix products: 18.6 us -> 3.33 us  [times_transposed(): lax.dot_general(left, right, (((1,), (1,)), ((), ())), preferred_element_...]
    pallas_call x1, Pallas kernels: 65.9 us -> 81.2 us  [attend_back(): pl.pallas_call(functools.partial(attend_back_kernel, scale), out_shape=[j...]
    pallas_call x1 -> x2, Pallas kernels: 94.2 us -> 107 us  [the longest x1 100 us: give_back(): pl.pallas_call(give_back_kernel, out_shape=[jax.ShapeDtypeStruct((rows, w...]
    dot_general x5 -> x4, matrix products: 30.6 us -> 24.2 us  [transposed_times(): lax.dot_general(left, right, (((0,), (0,)), ((), ())), preferred_element_...]
  transfers between devices with their start and end apart: 17 -> 17, of which waited for: 5 -> 4; matrix products, arithmetic and copies ran while one was open for 28% -> 24% of each run, Pallas kernels for 30% -> 52%
where the time goes in v5:
time: 1040 us; the launch traced here: 1030 us
  Pallas kernels  690 us (66%)
  matrix products  215 us (21%)
  waiting for transfers between devices  40.3 us (4%)
  local copies, waits for them, and re-layouts  32.2 us (3%)
  other arithmetic  30.6 us (3%)
  between operations  16 us (2%)
    pallas_call x1, Pallas kernels, collect(): pl.pallas_call(functools.partial(collect_kernel, count), out_shape=shapes...  187 us
    dot_general x9, matrix products, local(): jnp.einsum(eq, a, b, preferred_element_type=jnp.float32)  166 us
    pallas_call x1, Pallas kernels, spread(): pl.pallas_call(functools.partial(spread_kernel, count, more), out_shape=[...  154 us
    pallas_call x1, Pallas kernels, give_back(): pl.pallas_call(give_back_kernel, out_shape=[jax.ShapeDtypeStruct((rows, w...  100 us
    pallas_call x1, Pallas kernels, attend_back(): pl.pallas_call(functools.partial(attend_back_kernel, scale), out_shape=[j...  81.2 us
    pallas_call x1, Pallas kernels, attend(): pl.pallas_call(functools.partial(attend_kernel, scale), out_shape=[jax.Sh...  80.8 us
    pallas_call x1, Pallas kernels, dispatch(): pl.pallas_call(dispatch_kernel, out_shape=[low(ring, 2, count, width), lo...  80 us
    all_gather x2, waiting for transfers between devices, local(): lax.all_gather(w, CTX, axis=2, tiled=True)  30.6 us
  transfers between devices with their start and end apart: 17, of which 4 were waited for; matrix products, arithmetic and copies ran while one was open for 24% of the time, Pallas kernels for 52%

profile of v5, /device:TPU:9, one launch (start us, length us, event | category | flops | bytes accessed | tf_op | source)
XLA Modules:
  0.0 1032.9 jit_solution(712882185238516049)
XLA Ops:
  9.5 2.8 concatenate.30
  14.2 2.4 fusion.29.refs_6_
  16.6 154.2 %spread.1 = (bf16[2,2,4,2,64,2048]{5,4,3,2,1,0:T(8,128)(2,1)}, bf16[2,2,4,2,64,2048]{5,4,3,2,1,0:T(8,128)(2,1)}, bf16[2,2,4,2,64,2048]{5,4,3,2,1,0:T(8,128)(2,1)...) custom-call(bf16[64,2048]{1,0:T(8,128)(2,1)} %refs_0_.1, ...), custom_call_target="tpu_custom_call" | custom-call | flops 149999992832 | bytes 300000000 | tf_op jit(solution)/shard_map/spread/pallas_call | solution.py:217
  177.5 1.3 fusion.25
  178.8 6.4 convolution_convert_fusion.5.v
  185.2 3.8 fusion.44.k_raw
  189.0 3.8 fusion.46.q_raw
  192.8 80.8 %attend.1 = (bf16[256,2048]{1,0:T(8,128)(2,1)}, bf16[1024,512]{1,0:T(8,128)(2,1)S(1)}, bf16[1024,512]{1,0:T(8,128)(2,1)S(1)}, bf16[1024,512]{1,0:T(8,128)(2,1)S(1)}, f32[4,1024,1]{2,1,0:T(8,128)}) custom-call(f32[256,2048]{1,0:T(8,128)} %fusion.46.q_raw, f32[256,2048]{1,0:T(8,128)} %fusion.44.k_raw, bf16[256,2048]{1,0:T(8,128)(2,1)S(1)} %convolution_convert_fusion.5.v, ...), custom_call_target="tpu_custom_call" | custom-call | flops 1000000 | bytes 10000 | tf_op jit(solution)/shard_map/attend/pallas_call | solution.py:928
  273.7 7.3 multiply_reduce_fusion.3
  281.6 1.4 fusion.22.hot
  283.0 1.2 multiply_convert_fusion.4.rows
  284.3 80.0 %dispatch.1 = (bf16[4,2,256,2048]{3,2,1,0:T(8,128)(2,1)}, bf16[2,8,144,2048]{3,2,1,0:T(8,128)(2,1)}, bf16[2,8,144,2048]{3,2,1,0:T(8,128)(2,1)}, f32[2,8,144,1]{3,2,1,0:T(8,128)}, f32[8,16,256]{2,1,0:T(8,128)}) custom-call(bf16[256,2048]{1,0:T(8,128)(2,1)} %multiply_convert_fusion.4.rows, bf16[16,2048]{1,0:T(8,128)(2,1)} %bitcast.134, ...), custom_call_target="tpu_custom_call" | custom-call | flops 1000000 | bytes 10000 | tf_op jit(solution)/shard_map/dispatch/pallas_call | solution.py:568
  365.9 17.6 %fusion.8 = f32[2,8,144,1024]{3,2,1,0:T(8,128)} fusion(bf16[2,8,144,2048]{3,2,1,0:T(8,128)(2,1)} %get-tuple-element.83, bf16[2,2048,1024]{2,1,0:T(8,128)(2,1)} %all-gather.3.cloned.1.call-done), kind=kOutput, calls=%fused_computation.18 | convolution fusion | flops 9663676416 | bytes 27262976 | tf_op jit(solution)/shard_map/escd,edf->escf/dot_general | solution.py:1146
  383.4 30.6 %all-gather.5.cloned.1.call-done = bf16[2,2048,1024]{2,1,0:T(8,128)(2,1)} async-done(((bf16[2,2048,256]{2,1,0:T(8,128)(2,1)}), bf16[2,2048,1024]{2,1,0:T(8,128)(2,1)}) %all-gather.5.cloned.1.call-update) | async-done | bytes 8388624 | tf_op jit(solution)/shard_map/all_gather | solution.py:1113
  414.0 19.0 %multiply_convert_fusion.2 = (bf16[2,8,144,1024]{3,2,1,0:T(8,128)(2,1)S(1)}, f32[2,8,144,1024]{3,2,1,0:T(8,128)}) fusion(f32[2,8,144,1024]{3,2,1,0:T(8,128)} %fusion.8, bf16[2,8,144,2048]{3,2,1,0:T(8,128)(2,1)} %get-tuple-element.83, bf16[2,2048,1024]{2,1,0:T(8,128)(2,1)} %all-gather.5.cloned.1.call-done), kind=kOutput, calls=%fused_computation.10 | convolution fusion | flops 9677832192 | bytes 41418752 | tf_op jit(solution)/shard_map/escd,edf->escf/dot_general | solution.py:1146
  433.0 2.4 collective-permute-done.1.from_a
  437.6 2.3 slice.53
  440.1 16.7 %bitcast_convert_fusion.2 = bf16[2,1024,2048]{2,1,0:T(8,128)(2,1)} fusion(bf16[2,8,144,1024]{3,2,1,0:T(8,128)(2,1)S(1)} %get-tuple-element.202, bf16[2,8,144,2048]{3,2,1,0:T(8,128)(2,1)} %get-tuple-element.80), kind=kOutput, calls=%fused_computation.7 | convolution fusion | flops 9667870720 | bytes 22544384 | tf_op jit(solution)/shard_map/escf,escd->efd/dot_general | solution.py:1146
  456.9 3.4 collective-permute-done.3.second
  460.3 3.1 collective-permute-done.2.first
  463.5 6.4 join.1
  469.9 22.2 %multiply_convert_fusion = (bf16[2,8,144,1024]{3,2,1,0:T(8,128)(2,1)}, bf16[2,8,144,1024]{3,2,1,0:T(8,128)(2,1)}) fusion(f32[2,8,144,1024]{3,2,1,0:T(8,128)} %fusion.8, f32[2,8,144,1024]{3,2,1,0:T(8,128)} %get-tuple-element.203, bf16[2,8,144,2048]{3,2,1,0:T(8,128)(2,1)} %get-tuple-element.80, bf16[2,1024,2048]{2,1,0:T(8,128)(2,1)} %join.1), kind=kOutput, calls=%fused_computation.8 | convolution fusion | flops 9694347264 | bytes 46137344 | tf_op jit(solution)/shard_map/escd,efd->escf/dot_general | solution.py:1146
  492.1 17.3 %bitcast_convert_fusion.1 = bf16[2,2048,1024]{2,1,0:T(8,128)(2,1)} fusion(bf16[2,8,144,2048]{3,2,1,0:T(8,128)(2,1)} %get-tuple-element.83, bf16[2,8,144,1024]{3,2,1,0:T(8,128)(2,1)} %get-tuple-element.91), kind=kOutput, calls=%fused_computation.6 | convolution fusion | flops 9667870720 | bytes 22544384 | tf_op jit(solution)/shard_map/escd,escf->edf/dot_general | solution.py:1146
  509.5 2.1 collective-permute-start.7
  513.1 2.6 fusion.20.hot
  515.7 17.1 %bitcast_convert_fusion = bf16[2,2048,1024]{2,1,0:T(8,128)(2,1)} fusion(bf16[2,8,144,2048]{3,2,1,0:T(8,128)(2,1)} %get-tuple-element.83, bf16[2,8,144,1024]{3,2,1,0:T(8,128)(2,1)} %get-tuple-element.92), kind=kOutput, calls=%fused_computation.5 | convolution fusion | flops 9667870720 | bytes 22544384 | tf_op jit(solution)/shard_map/escd,escf->edf/dot_general | solution.py:1146
  532.9 18.1 %fusion.2 = f32[2,8,144,2048]{3,2,1,0:T(8,128)} fusion(bf16[2,8,144,1024]{3,2,1,0:T(8,128)(2,1)} %get-tuple-element.92, bf16[2,2048,1024]{2,1,0:T(8,128)(2,1)} %all-gather.5.cloned.1.call-done), kind=kOutput, calls=%fused_computation.12 | convolution fusion | flops 9663676416 | bytes 31981568 | tf_op jit(solution)/shard_map/escf,edf->escd/dot_general | solution.py:1146
  550.9 19.0 %add_convert_fusion.pairs = bf16[2,8,144,2048]{3,2,1,0:T(8,128)(2,1)} fusion(f32[2,8,144,2048]{3,2,1,0:T(8,128)} %fusion.2, bf16[2,8,144,1024]{3,2,1,0:T(8,128)(2,1)} %get-tuple-element.91, bf16[2,2048,1024]{2,1,0:T(8,128)(2,1)} %all-gather.3.cloned.1.call-done), kind=kOutput, calls=%fused_computation.4 | convolution fusion | flops 9673113600 | bytes 41418752 | tf_op jit(solution)/shard_map/escf,edf->escd/dot_general | solution.py:1146
  569.9 19.1 %fusion.1 = (bf16[2,8,144,2048]{3,2,1,0:T(8,128)(2,1)}, f32[2,8,144]{2,1,0:T(8,128)S(1)}) fusion(f32[2,8,144]{2,1,0:T(8,128)S(1)} %reduce.1, bf16[2,8,144,2048]{3,2,1,0:T(8,128)(2,1)} %get-tuple-element.80, bf16[2,8,144,1024]{3,2,1,0:T(8,128)(2,1)} %copy-done.48, bf16[2,1024,2048]{2,1,0:T(8,128)(2,1)} %join.1), kind=kOutput, calls=%fused_computation.3 | convolution fusion | flops 9696704512 | bytes 32000000 | tf_op jit(solution)/shard_map/escf,efd->escd/dot_general | solution.py:1146
  591.0 100.3 %give_back.1 = (f32[256,2048]{1,0:T(8,128)}, bf16[8,256,2048]{2,1,0:T(8,128)(2,1)}, f32[16,2048]{1,0:T(8,128)}) custom-call(bf16[8,2,256,144]{3,2,1,0:T(8,128)(2,1)} %fusion.20.hot, bf16[8,256,16]{2,1,0:T(8,128)(2,1)} %copy.71.logit, bf16[8,16,256]{2,1,0:T(8,128)(2,1)} %bitcast.136, bf16[16,2048]{1,0:T(8,128)(2,1)} %bitcast.135, ...), custom_call_target="tpu_custom_call" | custom-call | flops 99999997952 | bytes 200000000 | tf_op jit(solution)/shard_map/give_back/pallas_call | solution.py:766
  691.4 2.3 multiply_reduce_fusion.1
  694.0 2.1 fusion.60
  696.1 2.2 copy-done.47
  698.3 3.3 convolution_convert_fusion.4.do
  701.6 81.2 %attend_back.1 = (bf16[256,2048]{1,0:T(8,128)(2,1)}, bf16[256,2048]{1,0:T(8,128)(2,1)}, bf16[256,2048]{1,0:T(8,128)(2,1)}, f32[8,2048]{1,0:T(8,128)}, f32[8,2048]{1,0:T(8,128)}) custom-call(bf16[256,2048]{1,0:T(8,128)(2,1)} %convolution_convert_fusion.4.do, bf16[1024,512]{1,0:T(8,128)(2,1)} %copy-done.5, bf16[1024,512]{1,0:T(8,128)(2,1)} %copy-done.6, ...), custom_call_target="tpu_custom_call" | custom-call | flops 49999998976 | bytes 10000000 | tf_op jit(solution)/shard_map/attend_back/pallas_call | solution.py:1003
  785.7 2.2 constant_dynamic-slice_fusion.3
  787.9 1.6 collective-permute-start.9
  792.1 1.4 constant_dynamic-slice_fusion.1
  794.9 6.2 convolution_convert_fusion.1
  801.2 6.0 convolution_convert_fusion.2
  807.2 6.0 convolution_convert_fusion
  813.2 6.0 convolution_convert_fusion.3
  819.2 187.3 %collect.1 = (f32[16,128]{1,0:T(8,128)}, f32[64,2048]{1,0:T(8,128)}, f32[64,2048]{1,0:T(8,128)}, f32[64,2048]{1,0:T(8,128)}, f32[64,2048]{1,0:T(8,128)}, /*index=5*/bf16[256,2048]{1,0:T(8,128)(2,1)}, f32[8,2048]{1,0:T(8,128)}) custom-call(f32[2,2,4,16,128]{4,3,2,1,0:T(8,128)} %bitcast.139, bf16[2,2,4,128,1024]{4,3,2,1,0:T(8,128)(2,1)} %bitcast.160, ...), custom_call_target="tpu_custom_call" | custom-call | flops 160000000000 | bytes 320000000 | tf_op jit(solution)/shard_map/collect/pallas_call | solution.py:447
  1009.5 1.4 fusion.61
  1010.9 3.3 fusion.31
  1014.2 2.3 convert_element_type.274
  1016.5 2.3 convert_element_type.275
  1018.9 2.5 convert_element_type.276
  (207 shorter events, 32.7 us)
Async XLA Ops:
  7.2 357.1 %all-gather.3.cloned.1.call-start = ((), (), s32[]{:S(2)}) async-start(), calls=%async_computation.4 | async-start | bytes 10485760 | tf_op jit(solution)/shard_map/all_gather | solution.py:1113
  170.8 6.3 copy-start.15
  170.8 243.2 %all-gather.5.cloned.1.call-start = ((), (), s32[]{:S(2)}) async-start(), calls=%async_computation.5 | async-start | bytes 10485760 | tf_op jit(solution)/shard_map/all_gather | solution.py:1113
  171.6 419.4 %reduce-scatter.5.cloned.1.call-start = ((), (), s32[]{:S(2)}) async-start(), calls=%async_computation.6 | async-start | bytes 10485760 | tf_op jit(solution)/shard_map/reduce_scatter | solution.py:1164
  172.7 110.3 %copy-start.32 = (f32[2048]{0:T(1024)}, f32[2048]{0:T(1024)S(1)}, u32[]{:S(2)}) copy-start(f32[2048]{0:T(1024)S(1)} %reshape.300) | copy-start | bytes 24580
  173.3 19.4 %copy-start.2 = (f32[1,2048]{1,0:T(1,128)}, f32[1,2048]{1,0:T(1,128)S(1)}, u32[]{:S(2)}) copy-start(f32[1,2048]{1,0:T(1,128)S(1)} %reshape.298.k_gain) | copy-start | bytes 24580
  173.4 19.3 %copy-start.3 = (f32[1,2048]{1,0:T(1,128)}, f32[1,2048]{1,0:T(1,128)S(1)}, u32[]{:S(2)}) copy-start(f32[1,2048]{1,0:T(1,128)S(1)} %reshape.297.q_gain) | copy-start | bytes 24580
  176.2 105.4 %copy-start.34 = (pred[8,2,256]{2,1,0:T(4,128)(4,1)}, pred[8,2,256]{2,1,0:T(4,128)(4,1)S(1)}, u32[]{:S(2)}) copy-start(pred[8,2,256]{2,1,0:T(4,128)(4,1)S(1)} %compare_reduce_fusion) | copy-start | bytes 12292
  176.4 105.3 %copy-start.27 = (f32[8,2,256]{2,1,0:T(2,128)}, f32[8,2,256]{2,1,0:T(2,128)S(1)}, u32[]{:S(2)}) copy-start(f32[8,2,256]{2,1,0:T(2,128)S(1)} %copy.66) | copy-start | bytes 49156
  176.4 16.3 %copy-start.4 = (f32[1,1024]{1,0:T(1,128)}, f32[1,1024]{1,0:T(1,128)S(1)}, u32[]{:S(2)}) copy-start(f32[1,1024]{1,0:T(1,128)S(1)} %compare_convert_fusion.keep) | copy-start | bytes 12292
  177.1 15.6 %copy-start = (f32[256,128]{1,0:T(8,128)}, f32[256,128]{1,0:T(8,128)S(1)}, u32[]{:S(2)}) copy-start(f32[256,128]{1,0:T(8,128)S(1)} %get-tuple-element.204.cosine) | copy-start | bytes 393220
  177.2 15.6 %copy-start.1 = (f32[256,128]{1,0:T(8,128)}, f32[256,128]{1,0:T(8,128)S(1)}, u32[]{:S(2)}) copy-start(f32[256,128]{1,0:T(8,128)S(1)} %get-tuple-element.205.sine) | copy-start | bytes 393220
  177.5 7.7 slice-start.2
  178.7 6.4 slice-start.3
  178.8 10.2 slice-start
  273.6 7.3 copy-start.5
  273.6 7.3 copy-start.6
  273.6 7.3 copy-start.7
  281.6 82.6 %copy-start.42 = (f32[256]{0:T(256)}, f32[256]{0:T(256)S(1)}, u32[]{:S(2)}) copy-start(f32[256]{0:T(256)S(1)} %get-tuple-element.199) | copy-start | bytes 3076
  364.3 71.1 %collective-permute-start.1 = (bf16[2,256,2048]{2,1,0:T(8,128)(2,1)}, bf16[2,256,2048]{2,1,0:T(8,128)(2,1)S(1)}, u32[]{:S(2)}, u32[]{:S(2)}) collective-permute-start(bf16[2,256,2048]{2,1,0:T(8,128)(2,1)} %own), channel_id=1, source_target_pairs={{0,16},{16,0},{1,17},{17,1},{2,18},{18,2},{3,19},{19,3},{4,20},{20... | collective-permute-start | bytes 6291464 | tf_op jit(solution)/shard_map/ppermute | solution.py:1125
  365.2 72.4 %collective-permute-start = (bf16[2,256,2048]{2,1,0:T(8,128)(2,1)}, bf16[2,256,2048]{2,1,0:T(8,128)(2,1)}, u32[]{:S(2)}, u32[]{:S(2)}) collective-permute-start(bf16[2,256,2048]{2,1,0:T(8,128)(2,1)} %own), channel_id=1, source_target_pairs={{0,8},{8,0},{1,9},{9,1},{2,10},{10,2},{3,11},{11,3},{4,12},{12,4},... | collective-permute-start | bytes 6291464 | tf_op jit(solution)/shard_map/ppermute | solution.py:1125
  433.0 7.2 copy-start.48
  435.4 21.5 %copy-start.11 = (bf16[2,256,2048]{2,1,0:T(8,128)(2,1)}, bf16[2,256,2048]{2,1,0:T(8,128)(2,1)S(1)}, u32[]{:S(2)}) copy-start(bf16[2,256,2048]{2,1,0:T(8,128)(2,1)S(1)} %collective-permute-done.1.from_a) | copy-start | bytes 6291460
  436.5 23.8 %collective-permute-start.3 = (bf16[1,256,2048]{2,1,0:T(8,128)(2,1)}, bf16[1,256,2048]{2,1,0:T(8,128)(2,1)S(1)}, u32[]{:S(2)}, u32[]{:S(2)}) collective-permute-start(bf16[1,256,2048]{2,1,0:T(8,128)(2,1)} %slice.54), channel_id=1, source_target_pairs={{0,8},{8,0},{1,9},{9,1},{2,10},{10,2},{3,11},{11,3},{4,12},{12,4},... | collective-permute-start | bytes 3145736 | tf_op jit(solution)/shard_map/ppermute | solution.py:1125
  439.9 23.5 %collective-permute-start.2 = (bf16[1,256,2048]{2,1,0:T(8,128)(2,1)}, bf16[1,256,2048]{2,1,0:T(8,128)(2,1)}, u32[]{:S(2)}, u32[]{:S(2)}) collective-permute-start(bf16[1,256,2048]{2,1,0:T(8,128)(2,1)} %slice.53), channel_id=1, source_target_pairs={{0,16},{16,0},{1,17},{17,1},{2,18},{18,2},{3,19},{19,3},{4,20},{20... | collective-permute-start | bytes 3145736 | tf_op jit(solution)/shard_map/ppermute | solution.py:1125
  463.4 227.9 %reduce-scatter.7.cloned.1.call-start = ((), (), s32[]{:S(2)}) async-start(), calls=%async_computation.7 | async-start | bytes 10485760 | tf_op jit(solution)/shard_map/reduce_scatter | solution.py:1164
  509.5 281.5 %reduce-scatter.9.cloned.1.call-start = ((), (), s32[]{:S(2)}) async-start(), calls=%async_computation.8 | async-start | bytes 10485760 | tf_op jit(solution)/shard_map/reduce_scatter | solution.py:1164
  509.5 285.4 %collective-permute-start.7 = (bf16[256,2048]{1,0:T(8,128)(2,1)}, bf16[256,2048]{1,0:T(8,128)(2,1)}, u32[]{:S(2)}, u32[]{:S(2)}) collective-permute-start(bf16[256,2048]{1,0:T(8,128)(2,1)} %fusion.25), channel_id=1, source_target_pairs={{0,1},{1,0},{2,3},{3,2},{4,5},{5,4},{6,7},{7,6},{8,9},{9,8},{10,11... | collective-permute-start | bytes 3145736 | tf_op jit(solution)/shard_map/ppermute | solution.py:1190
  511.6 301.6 %collective-permute-start.5 = (bf16[256,2048]{1,0:T(8,128)(2,1)}, bf16[256,2048]{1,0:T(8,128)(2,1)}, u32[]{:S(2)}, u32[]{:S(2)}) collective-permute-start(bf16[256,2048]{1,0:T(8,128)(2,1)} %get-tuple-element.76), channel_id=1, source_target_pairs={{0,1},{1,0},{2,3},{3,2},{4,5},{5,4},{6,7},{7,6},{8,9},{9,8},{10,11... | collective-permute-start | bytes 3145736 | tf_op jit(solution)/shard_map/ppermute | solution.py:1190
  532.8 478.1 %reduce-scatter.11.cloned.1.call-start = ((), (), s32[]{:S(2)}) async-start(), calls=%async_computation.9 | async-start | bytes 9437184 | tf_op jit(solution)/shard_map/reduce_scatter | solution.py:1179
  569.9 19.9 %copy-start.37 = (f32[8,16,256]{2,1,0:T(8,128)S(1)}, f32[8,16,256]{2,1,0:T(8,128)}, u32[]{:S(2)}) copy-start(f32[8,16,256]{2,1,0:T(8,128)} %get-tuple-element.89) | copy-start | bytes 393220
  590.9 100.4 %copy-start.9 = (f32[256,2048]{1,0:T(8,128)S(1)}, f32[256,2048]{1,0:T(8,128)}, u32[]{:S(2)}) copy-start(f32[256,2048]{1,0:T(8,128)} %copy-done.8) | copy-start | bytes 6291460
  590.9 100.4 %copy-start.33 = (f32[2048]{0:T(1024)S(1)}, f32[2048]{0:T(1024)}, u32[]{:S(2)}) copy-start(f32[2048]{0:T(1024)} %copy-done.32) | copy-start | bytes 24580
  591.0 100.4 %copy-start.43 = (f32[256]{0:T(256)S(1)}, f32[256]{0:T(256)}, u32[]{:S(2)}) copy-start(f32[256]{0:T(256)} %copy-done.42) | copy-start | bytes 3076
  591.0 102.7 %copy-start.40 = (f32[256]{0:T(256)S(1)}, f32[256]{0:T(256)}, u32[]{:S(2)}) copy-start(f32[256]{0:T(256)} %copy-done.39) | copy-start | bytes 3076
  591.0 102.7 %copy-start.44 = (f32[256]{0:T(256)S(1)}, f32[256]{0:T(256)}, u32[]{:S(2)}) copy-start(f32[256]{0:T(256)} %get-tuple-element.198) | copy-start | bytes 3076
  696.1 5.6 copy-start.13
  701.6 81.3 %copy-start.36 = (f32[16,2048]{1,0:T(8,128)S(1)}, f32[16,2048]{1,0:T(8,128)}, u32[]{:S(2)}) copy-start(f32[16,2048]{1,0:T(8,128)} %get-tuple-element.104) | copy-start | bytes 393220
  787.9 7.0 collective-permute-start.9
  791.1 2.5 collective-permute-start.4
  792.0 21.2 %collective-permute-start.6 = (bf16[256,1024]{1,0:T(8,128)(2,1)}, bf16[256,1024]{1,0:T(8,128)(2,1)S(1)}, u32[]{:S(2)}, u32[]{:S(2)}) collective-permute-start(bf16[256,1024]{1,0:T(8,128)(2,1)} %get-tuple-element.185), channel_id=1, source_target_pairs={{0,1},{1,0},{2,3},{3,2},{4,5},{5,4},{6,7},{7,6},{8,9},{9,8},{10,11... | collective-permute-start | bytes 1572872 | tf_op jit(solution)/shard_map/ppermute | solution.py:1190
  793.6 7.6 collective-permute-start.8
  794.9 12.3 %collective-permute-start.10 = (bf16[256,1024]{1,0:T(8,128)(2,1)S(1)}, bf16[256,1024]{1,0:T(8,128)(2,1)S(1)}, u32[]{:S(2)}, u32[]{:S(2)}) collective-permute-start(bf16[256,1024]{1,0:T(8,128)(2,1)S(1)} %get-tuple-element.179), channel_id=1, source_target_pairs={{0,1},{1,0},{2,3},{3,2},{4,5},{5,4},{6,7},{7,6},{8,9},{9,8},{10,11... | collective-permute-start | bytes 1572872 | tf_op jit(solution)/shard_map/ppermute | solution.py:1190
  819.2 191.7 %copy-start.41 = (f32[256]{0:T(256)S(1)}, f32[256]{0:T(256)}, u32[]{:S(2)}) copy-start(f32[256]{0:T(256)} %copy-done.39) | copy-start | bytes 3076
  1006.5 7.7 copy-start.17
  1010.9 5.6 copy-start.18
  1018.9 5.1 copy-start.24
  1018.9 5.9 copy-start.23
  (22 other events, 61.0 us)
Sparse Core Ops, SparseCore 0:
  170.9 131.4 all-gather.2
  304.3 109.6 all-gather.4
  463.5 87.3 reduce-scatter.4
  554.1 86.4 reduce-scatter.6
  643.5 102.8 reduce-scatter.8
  789.7 86.0 reduce-scatter.10

commit v6 on v5

--- a/solution.py
+++ b/solution.py
@@ -233,10 +233,10 @@
 
 def collect_kernel(count, *refs):
     ring = lax.axis_size("ring")
-    parts, refs = refs[:count], refs[count:]
+    small, lefts, rights, refs = refs[0], (refs[1],) + (refs[2],) * (count - 2), refs[3 : count + 2], refs[count + 2 :]
     grads, matrices, (x, gain, passed), refs = refs[:3], refs[3:6], refs[6:9], refs[9:]
     outs, (input_grad, gain_out), refs = refs[:count], refs[count : count + 2], refs[count + 2 :]
-    scratch, refs = refs[: 9 * count], refs[9 * count :]
+    scratch, (out_a, out_b), refs = refs[: 9 * count], refs[9 * count : 9 * count + 2], refs[9 * count + 2 :]
     send, got, ring_send, ring_got, load, chunks, dn1, sums, arrived, ring_arrived, fetch, gain_send, gain_got = refs
     a, b, r, c = (lax.axis_index(n) for n in ALL)
     na, nb, nc = turn("ca", 1), turn("cb", 1), turn("core", 1)
@@ -316,36 +316,68 @@
             return ref.at[(*lead, slice(None), pl.ds(which * (cols // 2), cols // 2))]
         return ref.at[(*lead, pl.ds(which * (rows // 2), rows // 2), slice(None))]
 
-    def loads(w):
-        own_a, own_b = bufs[w][0:2]
-        return (
-            pltpu.make_async_copy(half(parts[w].at[a], 0), own_a, load.at[w, 0]),
-            pltpu.make_async_copy(half(parts[w].at[:, b], 1), own_b, load.at[w, 1]),
-        )
+    own_a, own_b = bufs[0][:2]
+    loads = (
+        pltpu.make_async_copy(half(small.at[a], 0), own_a, load.at[0, 0]),
+        pltpu.make_async_copy(half(small.at[:, b], 1), own_b, load.at[0, 1]),
+    )
+
+    def product(w, block, which):
+        own = bufs[w][0]
+        rows, cols = own.shape[1] * own.shape[2], own.shape[3]
+        left = lefts[w - 1][:, pl.ds(pl.multiple_of(block * rows, rows), rows)]
+        value = transposed_times(left, rights[w - 1][:, pl.ds(which * cols, cols)])
+        return value.reshape(own.shape[1:])
+
+    def sent_first(w):
+        await_bytes(bufs[w][2], send.at[w, 0])
+        await_bytes(bufs[w][3], send.at[w, 1])
 
     def first(w):
-        for copy in loads(w):
-            copy.start()
         in_a, in_b = bufs[w][2:4]
-        push(half(parts[w].at[na], 0), in_a, send.at[w, 0], got.at[w, 0], to_a)
-        push(half(parts[w].at[:, nb], 1), in_b, send.at[w, 1], got.at[w, 1], to_b)
-
-    def add(into, other):
-        def one(k, carry):
-            into[:, k] = (into[:, k].astype(jnp.float32) + other[:, k].astype(jnp.float32)).astype(into.dtype)
+        if w == 0:
+            for copy in loads:
+                copy.start()
+            push(half(small.at[na], 0), in_a, send.at[w, 0], got.at[w, 0], to_a)
+            push(half(small.at[:, nb], 1), in_b, send.at[w, 1], got.at[w, 1], to_b)
+            return
+        if w > 2:
+            sent_first(w - 2)
+
+        def one_a(i, carry):
+            out_a[w % 2, i] = product(w, 2 * na + i, 0).astype(out_a.dtype)
             return carry
 
-        lax.fori_loop(0, ring, one, 0)
+        def one_b(i, carry):
+            out_b[w % 2, i] = product(w, 2 * i + nb, 1).astype(out_b.dtype)
+            return carry
+
+        lax.fori_loop(0, 2, one_a, 0)
+        push(out_a.at[w % 2], in_a, send.at[w, 0], got.at[w, 0], to_a)
+        lax.fori_loop(0, 2, one_b, 0)
+        push(out_b.at[w % 2], in_b, send.at[w, 1], got.at[w, 1], to_b)
 
     def second(w):
         own_a, own_b, in_a, in_b, in_a2, in_b2 = bufs[w][:6]
-        for copy in loads(w):
-            copy.wait()
+        if w == 0:
+            for copy in loads:
+                copy.wait()
+
+        def one_a(i, carry):
+            mine = own_a[i] if w == 0 else product(w, 2 * a + i, 0)
+            own_a[i] = (mine + in_a[i].astype(jnp.float32)).astype(own_a.dtype)
+            return carry
+
+        def one_b(i, carry):
+            mine = own_b[i] if w == 0 else product(w, 2 * i + b, 1)
+            own_b[i] = (mine + in_b[i].astype(jnp.float32)).astype(own_b.dtype)
+            return carry
+
         await_bytes(in_a, got.at[w, 0])
-        add(own_a, in_a)
+        lax.fori_loop(0, 2, one_a, 0)
         push(own_a.at[nb], in_a2, send.at[w, 2], got.at[w, 2], to_b)
         await_bytes(in_b, got.at[w, 1])
-        add(own_b, in_b)
+        lax.fori_loop(0, 2, one_b, 0)
         push(own_b.at[na], in_b2, send.at[w, 3], got.at[w, 3], to_a)
 
     def third(w):
@@ -391,8 +423,8 @@
 
     def finish(w):
         own_a, own_b, in_a, in_b, in_a2, in_b2, total, in_ring, final = bufs[w]
-        await_bytes(in_a, send.at[w, 0])
-        await_bytes(in_b, send.at[w, 1])
+        if w == 0 or w + 2 >= count:
+            sent_first(w)
         await_bytes(in_a2, send.at[w, 2])
         await_bytes(in_b2, send.at[w, 3])
         for k in range(1, ring):
@@ -424,22 +456,22 @@
         finish(w)
 
 
-def collect(parts, small, grads, matrices, x, gain, passed):
-    count, ring = len(parts) + 1, lax.axis_size("ring")
+def collect(small, lefts, rights, grads, matrices, x, gain, passed):
+    count, ring = len(rights) + 1, lax.axis_size("ring")
     chips = lax.axis_size("ca") * lax.axis_size("cb") * ring
     square = (lax.axis_size("ca"), lax.axis_size("cb"), ring)
-    views = [p.reshape(square + (p.shape[0] // chips, p.shape[1])) for p in parts]
-    views = [small.reshape(square + small.shape[1:])] + views
+    view = small.reshape(square + small.shape[1:])
+    forms = [(*view.shape[3:], view.dtype)] + [(lefts[0].shape[1] // chips, r.shape[1], r.dtype) for r in rights]
     shapes, scratch = [], []
-    for v in views:
-        rows, cols = v.shape[3:]
+    for rows, cols, dtype in forms:
         piece = (rows, cols // 2) if cols > 128 else (rows // 2, cols)
         big = cols > 128
-        vm = lambda *shape: pltpu.VMEM(shape, v.dtype)
-        scratch += [vm(2, ring, *piece)] * 4 + [vm(ring, *piece)] * 2
-        scratch += [vm(ring, rows, cols), vm(ring - 1, rows, cols)]
+        vmem = lambda *shape: pltpu.VMEM(shape, dtype)
+        scratch += [vmem(2, ring, *piece)] * 4 + [vmem(ring, *piece)] * 2
+        scratch += [vmem(ring, rows, cols), vmem(ring - 1, rows, cols)]
         scratch += [pltpu.VMEM((2, rows // 2, cols) if big else (1, 8, 128), jnp.float32)]
         shapes.append(jax.ShapeDtypeStruct((rows // 2, 2 * cols) if big else (rows, cols), jnp.float32))
+    scratch += [vmem(2, 2, ring, *piece)] * 2
     dma = pltpu.SemaphoreType.DMA
     vm, anywhere = pl.BlockSpec(memory_space=pltpu.VMEM), pl.BlockSpec(memory_space=pl.ANY)
     wide = (8, gain.shape[1])
@@ -447,16 +479,16 @@
     outs = pl.pallas_call(
         functools.partial(collect_kernel, count),
         out_shape=shapes + [jax.ShapeDtypeStruct(x.shape, x.dtype), jax.ShapeDtypeStruct(wide, jnp.float32)],
-        in_specs=[anywhere] * count + [vm] * 3 + [anywhere] * 3 + [vm] * 3,
+        in_specs=[anywhere] + [vm] * (count + 4) + [anywhere] * 3 + [vm] * 3,
         out_specs=[vm] * (count + 2),
         scratch_shapes=scratch
         + [dma((count, 5)), dma((count, 5)), dma((count, ring - 1)), dma((count, ring - 1)), dma((count, 3))]
-        + [pltpu.VMEM((2, 3, 256, x.shape[1]), x.dtype), f32(*x.shape), f32(4, *wide), f32(3, *wide), f32(ring - 1, *wide)]
+        + [pltpu.VMEM((2, 3, 128, x.shape[1]), x.dtype), f32(*x.shape), f32(4, *wide), f32(3, *wide), f32(ring - 1, *wide)]
         + [dma((2, 3)), dma((2 + ring,)), dma((2 + ring,))],
         compiler_params=pltpu.CompilerParams(collective_id=1, has_side_effects=True, vmem_limit_bytes=62 << 20),
         cost_estimate=pl.CostEstimate(flops=160_000_000_000, bytes_accessed=320_000_000, transcendentals=0),
         name="collect",
-    )(*views, *grads, *matrices, x, gain, passed)
+    )(view, *lefts, *rights, *grads, *matrices, x, gain, passed)
     return outs[1:count], outs[0], outs[count], outs[count + 1]
 
 
@@ -1197,10 +1229,7 @@
 
     both = lambda v: jnp.concatenate([v, swap(v)], axis=0)
     n1_both, att_both = both(normed_one_low), both(attended_low)
-    parts = [
-        transposed_times(l, columns_of_core(r)).astype(jnp.bfloat16)
-        for l, r in ((att_both, dh_low), (n1_both, dq_low), (n1_both, dk_low), (n1_both, dv_low))
-    ]
+    rights = [columns_of_core(v) for v in (dh_low, dv_low, dq_low, dk_low)]
     split = lambda v: v.reshape(ctx_size * sources // 2, 2, -1)
     small_parts = jnp.concatenate(
         [split(v) for v in (gain_second_part, gain_queries_part, gain_keys_part, router_part)], axis=2
@@ -1208,7 +1237,7 @@
     small_parts = jnp.pad(small_parts, ((0, 0), (0, 0), (0, -small_parts.shape[2] % 2048)))
     small_parts = lax.dynamic_index_in_dim(small_parts, core, 1, False) + swap(lax.dynamic_index_in_dim(small_parts, 1 - core, 1, False))
     weight_grads, small_grads, input_grad, gain_first_sums = collect(
-        parts, small_parts.reshape(ctx_size * sources // 2, -1, 128), (dq_low, dk_low, dv_low),
+        small_parts.reshape(ctx_size * sources // 2, -1, 128), (att_both, n1_both), rights, (dq_low, dk_low, dv_low),
         (full_query, full_key, full_value), tokens[0], row(gain_first), grad_hidden,
     )
     weight_grads, mixed, gate_grad, up_grad, down_grad = lax.optimization_barrier(
@@ -1216,7 +1245,7 @@
     )
     layer_out = (row_valid * (hidden_state + mixed.astype(jnp.float32))).astype(jnp.bfloat16)
     gate_grad, up_grad, down_grad = (v.astype(jnp.float32) for v in (gate_grad, up_grad, down_grad))
-    weight_grads = list(weight_grads[1:]) + [weight_grads[0]]
+    weight_grads = [weight_grads[k] for k in (2, 3, 1, 0)]
     small_grads = small_grads.reshape(-1)
     gain_grads = [lax.dynamic_slice_in_dim(jnp.sum(gain_first_sums, axis=0), lax.axis_index(ALL) * rows_each, rows_each)]
     gain_grads += [small_grads[i * rows_each : (i + 1) * rows_each] for i in range(3)]

time: 1040 us -> 1030 us (level)
  matrix products: 215 us -> 190 us
  other arithmetic: 30.6 us -> 41.6 us
    dot_general x4 -> x0, matrix products: 24.2 us -> none  [transposed_times(): lax.dot_general(left, right, (((0,), (0,)), ((), ())), preferred_element_...]
  transfers between devices with their start and end apart: 17 -> 17, of which waited for: 4 -> 4; matrix products, arithmetic and copies ran while one was open for 24% -> 23% of each run, Pallas kernels for 52% -> 52%
where the time goes in v6:
time: 1030 us; the launch traced here: 1020 us
  Pallas kernels  687 us (67%)
  matrix products  190 us (18%)
  waiting for transfers between devices  41.8 us (4%)
  other arithmetic  41.6 us (4%)
  local copies, waits for them, and re-layouts  32.5 us (3%)
  between operations  16 us (2%)
    pallas_call x1, Pallas kernels, collect(): pl.pallas_call(functools.partial(collect_kernel, count), out_shape=shapes...  191 us
    dot_general x9, matrix products, local(): jnp.einsum(eq, a, b, preferred_element_type=jnp.float32)  165 us
    pallas_call x1, Pallas kernels, spread(): pl.pallas_call(functools.partial(spread_kernel, count, more), out_shape=[...  154 us
    pallas_call x1, Pallas kernels, give_back(): pl.pallas_call(give_back_kernel, out_shape=[jax.ShapeDtypeStruct((rows, w...  102 us
    pallas_call x1, Pallas kernels, attend(): pl.pallas_call(functools.partial(attend_kernel, scale), out_shape=[jax.Sh...  80.9 us
    pallas_call x1, Pallas kernels, dispatch(): pl.pallas_call(dispatch_kernel, out_shape=[low(ring, 2, count, width), lo...  79.1 us
    pallas_call x1, Pallas kernels, attend_back(): pl.pallas_call(functools.partial(attend_back_kernel, scale), out_shape=[j...  73.3 us
    all_gather x2, waiting for transfers between devices, local(): lax.all_gather(w, CTX, axis=2, tiled=True)  33.6 us
  transfers between devices with their start and end apart: 17, of which 4 were waited for; matrix products, arithmetic and copies ran while one was open for 23% of the time, Pallas kernels for 52%

profile of v6, /device:TPU:9, one launch (start us, length us, event | category | flops | bytes accessed | tf_op | source)
XLA Modules:
  0.0 1017.9 jit_solution(12705233127561473971)
XLA Ops:
  9.4 2.8 concatenate.30
  14.2 2.4 fusion.26.refs_6_
  16.6 154.2 %spread.1 = (bf16[2,2,4,2,64,2048]{5,4,3,2,1,0:T(8,128)(2,1)}, bf16[2,2,4,2,64,2048]{5,4,3,2,1,0:T(8,128)(2,1)}, bf16[2,2,4,2,64,2048]{5,4,3,2,1,0:T(8,128)(2,1)...) custom-call(bf16[64,2048]{1,0:T(8,128)(2,1)} %refs_0_.1, ...), custom_call_target="tpu_custom_call" | custom-call | flops 149999992832 | bytes 300000000 | tf_op jit(solution)/shard_map/spread/pallas_call | solution.py:217
  177.8 6.3 convolution_convert_fusion.1.v
  184.1 3.8 fusion.29.k_raw
  187.9 3.8 fusion.31.q_raw
  191.7 80.9 %attend.1 = (bf16[256,2048]{1,0:T(8,128)(2,1)S(1)}, bf16[1024,512]{1,0:T(8,128)(2,1)S(1)}, bf16[1024,512]{1,0:T(8,128)(2,1)S(1)}, bf16[1024,512]{1,0:T(8,128)(2,1)S(1)}, f32[4,1024,1]{2,1,0:T(8,128)}) custom-call(f32[256,2048]{1,0:T(8,128)} %fusion.31.q_raw, f32[256,2048]{1,0:T(8,128)} %fusion.29.k_raw, bf16[256,2048]{1,0:T(8,128)(2,1)S(1)} %convolution_convert_fusion.1.v, ...), custom_call_target="tpu_custom_call" | custom-call | flops 1000000 | bytes 10000 | tf_op jit(solution)/shard_map/attend/pallas_call | solution.py:960
  272.7 7.4 multiply_reduce_fusion.3
  280.8 1.4 fusion.22.hot
  282.2 1.2 multiply_convert_fusion.4.rows
  283.4 79.1 %dispatch.1 = (bf16[4,2,256,2048]{3,2,1,0:T(8,128)(2,1)}, bf16[2,8,144,2048]{3,2,1,0:T(8,128)(2,1)}, bf16[2,8,144,2048]{3,2,1,0:T(8,128)(2,1)}, f32[2,8,144,1]{3,2,1,0:T(8,128)}, f32[8,16,256]{2,1,0:T(8,128)}) custom-call(bf16[256,2048]{1,0:T(8,128)(2,1)} %multiply_convert_fusion.4.rows, bf16[16,2048]{1,0:T(8,128)(2,1)} %bitcast.130, ...), custom_call_target="tpu_custom_call" | custom-call | flops 1000000 | bytes 10000 | tf_op jit(solution)/shard_map/dispatch/pallas_call | solution.py:600
  363.6 1.1 collective-permute-start
  364.8 17.2 %fusion.8 = f32[2,8,144,1024]{3,2,1,0:T(8,128)} fusion(bf16[2,8,144,2048]{3,2,1,0:T(8,128)(2,1)} %get-tuple-element.83, bf16[2,2048,1024]{2,1,0:T(8,128)(2,1)} %all-gather.3.cloned.1.call-done), kind=kOutput, calls=%fused_computation.18 | convolution fusion | flops 9663676416 | bytes 27262976 | tf_op jit(solution)/shard_map/escd,edf->escf/dot_general | solution.py:1178
  382.0 33.6 %all-gather.5.cloned.1.call-done = bf16[2,2048,1024]{2,1,0:T(8,128)(2,1)} async-done(((bf16[2,2048,256]{2,1,0:T(8,128)(2,1)}), bf16[2,2048,1024]{2,1,0:T(8,128)(2,1)}) %all-gather.5.cloned.1.call-update) | async-done | bytes 8388624 | tf_op jit(solution)/shard_map/all_gather | solution.py:1145
  415.6 19.0 %multiply_convert_fusion.2 = (bf16[2,8,144,1024]{3,2,1,0:T(8,128)(2,1)S(1)}, f32[2,8,144,1024]{3,2,1,0:T(8,128)}) fusion(f32[2,8,144,1024]{3,2,1,0:T(8,128)} %fusion.8, bf16[2,8,144,2048]{3,2,1,0:T(8,128)(2,1)} %get-tuple-element.83, bf16[2,2048,1024]{2,1,0:T(8,128)(2,1)} %all-gather.5.cloned.1.call-done), kind=kOutput, calls=%fused_computation.10 | convolution fusion | flops 9677832192 | bytes 41418752 | tf_op jit(solution)/shard_map/escd,edf->escf/dot_general | solution.py:1178
  435.3 1.5 slice.54
  436.7 1.1 collective-permute-start.3
  437.9 2.3 slice.53
  440.2 16.7 %bitcast_convert_fusion.2 = bf16[2,1024,2048]{2,1,0:T(8,128)(2,1)} fusion(bf16[2,8,144,1024]{3,2,1,0:T(8,128)(2,1)S(1)} %get-tuple-element.202, bf16[2,8,144,2048]{3,2,1,0:T(8,128)(2,1)} %get-tuple-element.80), kind=kOutput, calls=%fused_computation.7 | convolution fusion | flops 9667870720 | bytes 22544384 | tf_op jit(solution)/shard_map/escf,escd->efd/dot_general | solution.py:1178
  457.0 3.6 collective-permute-done.3.second
  460.5 3.1 collective-permute-done.2.first
  463.7 6.4 join.1
  470.2 22.3 %multiply_convert_fusion = (bf16[2,8,144,1024]{3,2,1,0:T(8,128)(2,1)}, bf16[2,8,144,1024]{3,2,1,0:T(8,128)(2,1)}) fusion(f32[2,8,144,1024]{3,2,1,0:T(8,128)} %fusion.8, f32[2,8,144,1024]{3,2,1,0:T(8,128)} %get-tuple-element.203, bf16[2,8,144,2048]{3,2,1,0:T(8,128)(2,1)} %get-tuple-element.80, bf16[2,1024,2048]{2,1,0:T(8,128)(2,1)} %join.1), kind=kOutput, calls=%fused_computation.8 | convolution fusion | flops 9694347264 | bytes 46137344 | tf_op jit(solution)/shard_map/escd,efd->escf/dot_general | solution.py:1178
  492.5 17.3 %bitcast_convert_fusion.1 = bf16[2,2048,1024]{2,1,0:T(8,128)(2,1)} fusion(bf16[2,8,144,2048]{3,2,1,0:T(8,128)(2,1)} %get-tuple-element.83, bf16[2,8,144,1024]{3,2,1,0:T(8,128)(2,1)} %get-tuple-element.91), kind=kOutput, calls=%fused_computation.6 | convolution fusion | flops 9667870720 | bytes 22544384 | tf_op jit(solution)/shard_map/escd,escf->edf/dot_general | solution.py:1178
  509.9 1.1 copy-done.18
  511.0 2.0 collective-permute-start.6
  514.8 3.1 fusion.20.hot
  517.9 2.8 pad_maximum_fusion.1.refs_2_
  520.7 2.8 pad_maximum_fusion.refs_1_
  523.5 18.2 %fusion.1 = (bf16[2,8,144,2048]{3,2,1,0:T(8,128)(2,1)}, f32[2,8,144]{2,1,0:T(8,128)S(1)}) fusion(f32[2,8,144]{2,1,0:T(8,128)S(1)} %reduce.1, bf16[2,8,144,2048]{3,2,1,0:T(8,128)(2,1)} %get-tuple-element.80, bf16[2,8,144,1024]{3,2,1,0:T(8,128)(2,1)S(1)} %bitcast.154, bf16[2,1024,2048]{2,1,0:T(8,128)(2,1)} %join.1), kind=kOutput, calls=%fused_computation.3 | convolution fusion | flops 9696704512 | bytes 32000000 | tf_op jit(solution)/shard_map/escf,efd->escd/dot_general | solution.py:1178
  543.5 17.1 %bitcast_convert_fusion = bf16[2,2048,1024]{2,1,0:T(8,128)(2,1)} fusion(bf16[2,8,144,2048]{3,2,1,0:T(8,128)(2,1)} %get-tuple-element.83, bf16[2,8,144,1024]{3,2,1,0:T(8,128)(2,1)} %get-tuple-element.92), kind=kOutput, calls=%fused_computation.5 | convolution fusion | flops 9667870720 | bytes 22544384 | tf_op jit(solution)/shard_map/escd,escf->edf/dot_general | solution.py:1178
  560.7 18.3 %fusion.2 = f32[2,8,144,2048]{3,2,1,0:T(8,128)} fusion(bf16[2,8,144,1024]{3,2,1,0:T(8,128)(2,1)} %get-tuple-element.92, bf16[2,2048,1024]{2,1,0:T(8,128)(2,1)} %all-gather.5.cloned.1.call-done), kind=kOutput, calls=%fused_computation.12 | convolution fusion | flops 9663676416 | bytes 31981568 | tf_op jit(solution)/shard_map/escf,edf->escd/dot_general | solution.py:1178
  579.1 19.2 %add_convert_fusion.pairs = bf16[2,8,144,2048]{3,2,1,0:T(8,128)(2,1)} fusion(f32[2,8,144,2048]{3,2,1,0:T(8,128)} %fusion.2, bf16[2,8,144,1024]{3,2,1,0:T(8,128)(2,1)} %get-tuple-element.91, bf16[2,2048,1024]{2,1,0:T(8,128)(2,1)} %all-gather.3.cloned.1.call-done), kind=kOutput, calls=%fused_computation.4 | convolution fusion | flops 9673113600 | bytes 41418752 | tf_op jit(solution)/shard_map/escf,edf->escd/dot_general | solution.py:1178
  598.3 101.6 %give_back.1 = (f32[256,2048]{1,0:T(8,128)}, bf16[8,256,2048]{2,1,0:T(8,128)(2,1)}, f32[16,2048]{1,0:T(8,128)}) custom-call(bf16[8,2,256,144]{3,2,1,0:T(8,128)(2,1)} %fusion.20.hot, bf16[8,256,16]{2,1,0:T(8,128)(2,1)} %copy.71.logit, bf16[8,16,256]{2,1,0:T(8,128)(2,1)} %bitcast.132, bf16[16,2048]{1,0:T(8,128)(2,1)} %bitcast.131, ...), custom_call_target="tpu_custom_call" | custom-call | flops 99999997952 | bytes 200000000 | tf_op jit(solution)/shard_map/give_back/pallas_call | solution.py:798
  700.0 2.2 multiply_reduce_fusion.1
  702.2 2.2 copy.72
  704.5 2.1 reshape.276
  706.6 3.8 fusion.41
  711.4 3.3 convolution_convert_fusion.do
  714.8 73.3 %attend_back.1 = (bf16[256,2048]{1,0:T(8,128)(2,1)}, bf16[256,2048]{1,0:T(8,128)(2,1)}, bf16[256,2048]{1,0:T(8,128)(2,1)}, f32[8,2048]{1,0:T(8,128)}, f32[8,2048]{1,0:T(8,128)}) custom-call(bf16[256,2048]{1,0:T(8,128)(2,1)} %convolution_convert_fusion.do, bf16[1024,512]{1,0:T(8,128)(2,1)} %copy-done.7, bf16[1024,512]{1,0:T(8,128)(2,1)} %copy-done.8, ...), custom_call_target="tpu_custom_call" | custom-call | flops 49999998976 | bytes 10000000 | tf_op jit(solution)/shard_map/attend_back/pallas_call | solution.py:1035
  790.8 1.6 collective-permute-start.4
  792.6 1.3 constant_dynamic-slice_fusion.5
  800.1 191.3 %collect.1 = (f32[16,128]{1,0:T(8,128)}, f32[64,2048]{1,0:T(8,128)}, f32[64,2048]{1,0:T(8,128)}, f32[64,2048]{1,0:T(8,128)}, f32[64,2048]{1,0:T(8,128)}, /*index=5*/bf16[256,2048]{1,0:T(8,128)(2,1)}, f32[8,2048]{1,0:T(8,128)}) custom-call(f32[2,2,4,16,128]{4,3,2,1,0:T(8,128)} %bitcast.135, bf16[512,2048]{1,0:T(8,128)(2,1)} %pad_maximum_fusion.refs_1_, ...), custom_call_target="tpu_custom_call" | custom-call | flops 160000000000 | bytes 320000000 | tf_op jit(solution)/shard_map/collect/pallas_call | solution.py:479
  994.6 1.4 fusion.42
  996.0 3.3 fusion.28
  999.2 2.3 convert_element_type.258
  1001.6 2.3 convert_element_type.259
  1003.9 2.5 convert_element_type.260
  (220 shorter events, 34.0 us)
Async XLA Ops:
  7.2 355.4 %all-gather.3.cloned.1.call-start = ((), (), s32[]{:S(2)}) async-start(), calls=%async_computation.4 | async-start | bytes 10485760 | tf_op jit(solution)/shard_map/all_gather | solution.py:1145
  170.8 6.3 copy-start.16
  170.8 244.7 %all-gather.5.cloned.1.call-start = ((), (), s32[]{:S(2)}) async-start(), calls=%async_computation.5 | async-start | bytes 10485760 | tf_op jit(solution)/shard_map/all_gather | solution.py:1145
  171.6 426.7 %reduce-scatter.5.cloned.1.call-start = ((), (), s32[]{:S(2)}) async-start(), calls=%async_computation.6 | async-start | bytes 10485760 | tf_op jit(solution)/shard_map/reduce_scatter | solution.py:1196
  172.7 109.5 %copy-start.36 = (f32[2048]{0:T(1024)}, f32[2048]{0:T(1024)S(1)}, u32[]{:S(2)}) copy-start(f32[2048]{0:T(1024)S(1)} %reshape.284) | copy-start | bytes 24580
  173.3 18.4 %copy-start.4 = (f32[1,2048]{1,0:T(1,128)}, f32[1,2048]{1,0:T(1,128)S(1)}, u32[]{:S(2)}) copy-start(f32[1,2048]{1,0:T(1,128)S(1)} %reshape.282.k_gain) | copy-start | bytes 24580
  173.4 18.3 %copy-start.5 = (f32[1,2048]{1,0:T(1,128)}, f32[1,2048]{1,0:T(1,128)S(1)}, u32[]{:S(2)}) copy-start(f32[1,2048]{1,0:T(1,128)S(1)} %reshape.281.q_gain) | copy-start | bytes 24580
  176.2 104.6 %copy-start.38 = (pred[8,2,256]{2,1,0:T(4,128)(4,1)}, pred[8,2,256]{2,1,0:T(4,128)(4,1)S(1)}, u32[]{:S(2)}) copy-start(pred[8,2,256]{2,1,0:T(4,128)(4,1)S(1)} %compare_reduce_fusion) | copy-start | bytes 12292
  176.3 104.5 %copy-start.31 = (f32[8,2,256]{2,1,0:T(2,128)}, f32[8,2,256]{2,1,0:T(2,128)S(1)}, u32[]{:S(2)}) copy-start(f32[8,2,256]{2,1,0:T(2,128)S(1)} %copy.66) | copy-start | bytes 49156
  176.4 15.3 %copy-start.6 = (f32[1,1024]{1,0:T(1,128)}, f32[1,1024]{1,0:T(1,128)S(1)}, u32[]{:S(2)}) copy-start(f32[1,1024]{1,0:T(1,128)S(1)} %compare_convert_fusion.keep) | copy-start | bytes 12292
  177.1 14.6 %copy-start.2 = (f32[256,128]{1,0:T(8,128)}, f32[256,128]{1,0:T(8,128)S(1)}, u32[]{:S(2)}) copy-start(f32[256,128]{1,0:T(8,128)S(1)} %get-tuple-element.204.cosine) | copy-start | bytes 393220
  177.1 14.6 %copy-start.3 = (f32[256,128]{1,0:T(8,128)}, f32[256,128]{1,0:T(8,128)S(1)}, u32[]{:S(2)}) copy-start(f32[256,128]{1,0:T(8,128)S(1)} %get-tuple-element.205.sine) | copy-start | bytes 393220
  177.4 6.7 slice-start.2
  177.8 6.3 copy-start.17
  177.8 6.3 slice-start.3
  177.8 10.1 slice-start
  272.7 7.4 copy-start
  272.7 7.4 copy-start.7
  272.7 7.4 copy-start.8
  272.7 7.4 copy-start.9
  280.8 81.7 %copy-start.45 = (f32[256]{0:T(256)}, f32[256]{0:T(256)S(1)}, u32[]{:S(2)}) copy-start(f32[256]{0:T(256)S(1)} %get-tuple-element.199) | copy-start | bytes 3076
  362.6 72.7 %collective-permute-start.1 = (bf16[2,256,2048]{2,1,0:T(8,128)(2,1)}, bf16[2,256,2048]{2,1,0:T(8,128)(2,1)S(1)}, u32[]{:S(2)}, u32[]{:S(2)}) collective-permute-start(bf16[2,256,2048]{2,1,0:T(8,128)(2,1)} %own), channel_id=1, source_target_pairs={{0,16},{16,0},{1,17},{17,1},{2,18},{18,2},{3,19},{19,3},{4,20},{20... | collective-permute-start | bytes 6291464 | tf_op jit(solution)/shard_map/ppermute | solution.py:1157
  363.6 74.3 %collective-permute-start = (bf16[2,256,2048]{2,1,0:T(8,128)(2,1)}, bf16[2,256,2048]{2,1,0:T(8,128)(2,1)}, u32[]{:S(2)}, u32[]{:S(2)}) collective-permute-start(bf16[2,256,2048]{2,1,0:T(8,128)(2,1)} %own), channel_id=1, source_target_pairs={{0,8},{8,0},{1,9},{9,1},{2,10},{10,2},{3,11},{11,3},{4,12},{12,4},... | collective-permute-start | bytes 6291464 | tf_op jit(solution)/shard_map/ppermute | solution.py:1157
  435.3 21.7 %copy-start.12 = (bf16[2,256,2048]{2,1,0:T(8,128)(2,1)}, bf16[2,256,2048]{2,1,0:T(8,128)(2,1)S(1)}, u32[]{:S(2)}) copy-start(bf16[2,256,2048]{2,1,0:T(8,128)(2,1)S(1)} %collective-permute-done.1.from_a) | copy-start | bytes 6291460
  436.7 23.8 %collective-permute-start.3 = (bf16[1,256,2048]{2,1,0:T(8,128)(2,1)}, bf16[1,256,2048]{2,1,0:T(8,128)(2,1)S(1)}, u32[]{:S(2)}, u32[]{:S(2)}) collective-permute-start(bf16[1,256,2048]{2,1,0:T(8,128)(2,1)} %slice.54), channel_id=1, source_target_pairs={{0,8},{8,0},{1,9},{9,1},{2,10},{10,2},{3,11},{11,3},{4,12},{12,4},... | collective-permute-start | bytes 3145736 | tf_op jit(solution)/shard_map/ppermute | solution.py:1157
  440.2 23.5 %collective-permute-start.2 = (bf16[1,256,2048]{2,1,0:T(8,128)(2,1)}, bf16[1,256,2048]{2,1,0:T(8,128)(2,1)}, u32[]{:S(2)}, u32[]{:S(2)}) collective-permute-start(bf16[1,256,2048]{2,1,0:T(8,128)(2,1)} %slice.53), channel_id=1, source_target_pairs={{0,16},{16,0},{1,17},{17,1},{2,18},{18,2},{3,19},{19,3},{4,20},{20... | collective-permute-start | bytes 3145736 | tf_op jit(solution)/shard_map/ppermute | solution.py:1157
  463.7 236.3 %reduce-scatter.7.cloned.1.call-start = ((), (), s32[]{:S(2)}) async-start(), calls=%async_computation.7 | async-start | bytes 10485760 | tf_op jit(solution)/shard_map/reduce_scatter | solution.py:1196
  509.9 278.3 %reduce-scatter.9.cloned.1.call-start = ((), (), s32[]{:S(2)}) async-start(), calls=%async_computation.8 | async-start | bytes 10485760 | tf_op jit(solution)/shard_map/reduce_scatter | solution.py:1196
  511.0 6.9 collective-permute-start.6
  513.0 7.7 collective-permute-start.5
  514.8 8.7 slice-start.4
  523.5 19.0 %copy-start.40 = (f32[8,16,256]{2,1,0:T(8,128)S(1)}, f32[8,16,256]{2,1,0:T(8,128)}, u32[]{:S(2)}) copy-start(f32[8,16,256]{2,1,0:T(8,128)} %get-tuple-element.89) | copy-start | bytes 393220
  542.5 18.1 %copy-start.33 = (bf16[8,256,16]{1,2,0:T(8,128)(2,1)}, bf16[8,256,16]{1,2,0:T(8,128)(2,1)S(1)}, u32[]{:S(2)}) copy-start(bf16[8,256,16]{1,2,0:T(8,128)(2,1)S(1)} %fusion.36) | copy-start | bytes 196612
  560.7 435.3 %reduce-scatter.11.cloned.1.call-start = ((), (), s32[]{:S(2)}) async-start(), calls=%async_computation.9 | async-start | bytes 9437184 | tf_op jit(solution)/shard_map/reduce_scatter | solution.py:1211
  598.3 101.7 %copy-start.11 = (f32[256,2048]{1,0:T(8,128)S(1)}, f32[256,2048]{1,0:T(8,128)}, u32[]{:S(2)}) copy-start(f32[256,2048]{1,0:T(8,128)} %copy-done.10) | copy-start | bytes 6291460
  598.3 101.7 %copy-start.37 = (f32[2048]{0:T(1024)S(1)}, f32[2048]{0:T(1024)}, u32[]{:S(2)}) copy-start(f32[2048]{0:T(1024)} %copy-done.36) | copy-start | bytes 24580
  598.3 101.7 %copy-start.46 = (f32[256]{0:T(256)S(1)}, f32[256]{0:T(256)}, u32[]{:S(2)}) copy-start(f32[256]{0:T(256)} %copy-done.45) | copy-start | bytes 3076
  699.9 6.7 copy-start.13
  699.9 6.7 copy-start.43
  699.9 6.7 copy-start.47
  714.8 77.6 %copy-start.15 = (bf16[256,2048]{1,0:T(8,128)(2,1)S(1)}, bf16[256,2048]{1,0:T(8,128)(2,1)}, u32[]{:S(2)}) copy-start(bf16[256,2048]{1,0:T(8,128)(2,1)} %copy-done.14) | copy-start | bytes 3145732
  790.8 4.4 collective-permute-start.4
  792.5 3.5 collective-permute-start.7
  793.9 3.2 collective-permute-start.8
  794.5 3.5 collective-permute-start.9
  794.7 4.4 collective-permute-start.10
  800.1 195.8 %copy-start.44 = (f32[256]{0:T(256)S(1)}, f32[256]{0:T(256)}, u32[]{:S(2)}) copy-start(f32[256]{0:T(256)} %copy-done.42) | copy-start | bytes 3076
  991.5 7.7 copy-start.20
  (27 other events, 103.0 us)
Sparse Core Ops, SparseCore 0:
  170.9 131.4 all-gather.2
  304.3 111.2 all-gather.4
  463.8 87.6 reduce-scatter.4
  554.8 86.4 reduce-scatter.6
  644.1 91.8 reduce-scatter.8
  738.2 101.7 reduce-scatter.10

commit v7 on v6

--- a/solution.py
+++ b/solution.py
@@ -233,9 +233,10 @@
 
 def collect_kernel(count, *refs):
     ring = lax.axis_size("ring")
-    small, lefts, rights, refs = refs[0], (refs[1],) + (refs[2],) * (count - 2), refs[3 : count + 2], refs[count + 2 :]
+    whole = (count - 1) // 2
+    small, lefts, rights, refs = refs[0], (refs[1],) + (refs[2],) * (whole - 1), refs[3 : whole + 3], refs[whole + 3 :]
     grads, matrices, (x, gain, passed), refs = refs[:3], refs[3:6], refs[6:9], refs[9:]
-    outs, (input_grad, gain_out), refs = refs[:count], refs[count : count + 2], refs[count + 2 :]
+    outs, (input_grad, gain_out), refs = refs[: whole + 1], refs[whole + 1 : whole + 3], refs[whole + 3 :]
     scratch, (out_a, out_b), refs = refs[: 9 * count], refs[9 * count : 9 * count + 2], refs[9 * count + 2 :]
     send, got, ring_send, ring_got, load, chunks, dn1, sums, arrived, ring_arrived, fetch, gain_send, gain_got = refs
     a, b, r, c = (lax.axis_index(n) for n in ALL)
@@ -325,8 +326,9 @@
     def product(w, block, which):
         own = bufs[w][0]
         rows, cols = own.shape[1] * own.shape[2], own.shape[3]
-        left = lefts[w - 1][:, pl.ds(pl.multiple_of(block * rows, rows), rows)]
-        value = transposed_times(left, rights[w - 1][:, pl.ds(which * cols, cols)])
+        at, part = divmod(w - 1, 2)
+        left = lefts[at][:, pl.ds(pl.multiple_of(block * rows, rows), rows)]
+        value = transposed_times(left, rights[at][:, pl.ds((2 * part + which) * cols, cols)])
         return value.reshape(own.shape[1:])
 
     def sent_first(w):
@@ -412,7 +414,8 @@
                     value = value + in_ring[k, at, :].astype(jnp.float32)
                 final[core] = value
             cols = final.shape[2]
-            there = outs[w].at[:, pl.ds(pl.multiple_of(c * cols, cols), cols)]
+            at, part = divmod(w - 1, 2)
+            there = outs[at + 1].at[:, pl.ds(pl.multiple_of((2 * c + part) * cols, cols), cols)]
             push(final.at[nc], there, send.at[w, 4], got.at[w, 4], to_core)
             pltpu.make_async_copy(final.at[c], there, load.at[w, 2]).start()
         else:
@@ -450,19 +453,21 @@
             input_part((step - 1) * steps // 4, step * steps // 4)
         if step == 4:
             input_end()
-        if step > 4:
+        if 4 < step < 9:
             gain_stage(step - 5)
     for w in range(count):
         finish(w)
 
 
 def collect(small, lefts, rights, grads, matrices, x, gain, passed):
-    count, ring = len(rights) + 1, lax.axis_size("ring")
+    count, ring = 2 * len(rights) + 1, lax.axis_size("ring")
     chips = lax.axis_size("ca") * lax.axis_size("cb") * ring
     square = (lax.axis_size("ca"), lax.axis_size("cb"), ring)
     view = small.reshape(square + small.shape[1:])
-    forms = [(*view.shape[3:], view.dtype)] + [(lefts[0].shape[1] // chips, r.shape[1], r.dtype) for r in rights]
-    shapes, scratch = [], []
+    rows = lefts[0].shape[1] // chips
+    forms = [(*view.shape[3:], view.dtype)] + [(rows, r.shape[1] // 2, r.dtype) for r in rights for _ in range(2)]
+    shapes = [view.shape[3:]] + [(rows // 2, 2 * r.shape[1]) for r in rights]
+    shapes, scratch = [jax.ShapeDtypeStruct(shape, jnp.float32) for shape in shapes], []
     for rows, cols, dtype in forms:
         piece = (rows, cols // 2) if cols > 128 else (rows // 2, cols)
         big = cols > 128
@@ -470,7 +475,6 @@
         scratch += [vmem(2, ring, *piece)] * 4 + [vmem(ring, *piece)] * 2
         scratch += [vmem(ring, rows, cols), vmem(ring - 1, rows, cols)]
         scratch += [pltpu.VMEM((2, rows // 2, cols) if big else (1, 8, 128), jnp.float32)]
-        shapes.append(jax.ShapeDtypeStruct((rows // 2, 2 * cols) if big else (rows, cols), jnp.float32))
     scratch += [vmem(2, 2, ring, *piece)] * 2
     dma = pltpu.SemaphoreType.DMA
     vm, anywhere = pl.BlockSpec(memory_space=pltpu.VMEM), pl.BlockSpec(memory_space=pl.ANY)
@@ -479,8 +483,8 @@
     outs = pl.pallas_call(
         functools.partial(collect_kernel, count),
         out_shape=shapes + [jax.ShapeDtypeStruct(x.shape, x.dtype), jax.ShapeDtypeStruct(wide, jnp.float32)],
-        in_specs=[anywhere] + [vm] * (count + 4) + [anywhere] * 3 + [vm] * 3,
-        out_specs=[vm] * (count + 2),
+        in_specs=[anywhere] + [vm] * (len(rights) + 5) + [anywhere] * 3 + [vm] * 3,
+        out_specs=[vm] * (len(rights) + 3),
         scratch_shapes=scratch
         + [dma((count, 5)), dma((count, 5)), dma((count, ring - 1)), dma((count, ring - 1)), dma((count, 3))]
         + [pltpu.VMEM((2, 3, 128, x.shape[1]), x.dtype), f32(*x.shape), f32(4, *wide), f32(3, *wide), f32(ring - 1, *wide)]
@@ -489,7 +493,7 @@
         cost_estimate=pl.CostEstimate(flops=160_000_000_000, bytes_accessed=320_000_000, transcendentals=0),
         name="collect",
     )(view, *lefts, *rights, *grads, *matrices, x, gain, passed)
-    return outs[1:count], outs[0], outs[count], outs[count + 1]
+    return outs[1:-2], outs[0], outs[-2], outs[-1]
 
 
 def dispatch_kernel(

time: 1030 us -> 1010 us (0.981)
  Pallas kernels: 687 us -> 666 us
    pallas_call x1, Pallas kernels: 191 us -> 171 us  [collect(): pl.pallas_call(functools.partial(collect_kernel, count), out_shape=shapes...]
  transfers between devices with their start and end apart: 17 -> 17, of which waited for: 4 -> 4; matrix products, arithmetic and copies ran while one was open for 23% -> 24% of each run, Pallas kernels for 52% -> 51%
where the time goes in v7:
time: 1010 us; the launch traced here: 997 us
  Pallas kernels  666 us (66%)
  matrix products  191 us (19%)
  waiting for transfers between devices  41.7 us (4%)
  other arithmetic  41.4 us (4%)
  local copies, waits for them, and re-layouts  32.6 us (3%)
  between operations  16 us (2%)
    pallas_call x1, Pallas kernels, collect(): pl.pallas_call(functools.partial(collect_kernel, count), out_shape=shapes...  171 us
    dot_general x9, matrix products, local(): jnp.einsum(eq, a, b, preferred_element_type=jnp.float32)  166 us
    pallas_call x1, Pallas kernels, spread(): pl.pallas_call(functools.partial(spread_kernel, count, more), out_shape=[...  154 us
    pallas_call x1, Pallas kernels, give_back(): pl.pallas_call(give_back_kernel, out_shape=[jax.ShapeDtypeStruct((rows, w...  102 us
    pallas_call x1, Pallas kernels, attend(): pl.pallas_call(functools.partial(attend_kernel, scale), out_shape=[jax.Sh...  81 us
    pallas_call x1, Pallas kernels, dispatch(): pl.pallas_call(dispatch_kernel, out_shape=[low(ring, 2, count, width), lo...  79.1 us
    pallas_call x1, Pallas kernels, attend_back(): pl.pallas_call(functools.partial(attend_back_kernel, scale), out_shape=[j...  73.2 us
    all_gather x2, waiting for transfers between devices, local(): lax.all_gather(w, CTX, axis=2, tiled=True)  33.4 us
  transfers between devices with their start and end apart: 17, of which 4 were waited for; matrix products, arithmetic and copies ran while one was open for 24% of the time, Pallas kernels for 51%

profile of v7, /device:TPU:9, one launch (start us, length us, event | category | flops | bytes accessed | tf_op | source)
XLA Modules:
  0.0 997.3 jit_solution(13030996203596688712)
XLA Ops:
  9.4 2.8 concatenate.30
  14.2 2.4 fusion.26.refs_6_
  16.6 154.2 %spread.1 = (bf16[2,2,4,2,64,2048]{5,4,3,2,1,0:T(8,128)(2,1)}, bf16[2,2,4,2,64,2048]{5,4,3,2,1,0:T(8,128)(2,1)}, bf16[2,2,4,2,64,2048]{5,4,3,2,1,0:T(8,128)(2,1)...) custom-call(bf16[64,2048]{1,0:T(8,128)(2,1)} %refs_0_.1, ...), custom_call_target="tpu_custom_call" | custom-call | flops 149999992832 | bytes 300000000 | tf_op jit(solution)/shard_map/spread/pallas_call | solution.py:217
  177.8 6.3 convolution_convert_fusion.1.v
  184.1 3.8 fusion.29.k_raw
  187.9 3.8 fusion.31.q_raw
  191.7 81.0 %attend.1 = (bf16[256,2048]{1,0:T(8,128)(2,1)S(1)}, bf16[1024,512]{1,0:T(8,128)(2,1)S(1)}, bf16[1024,512]{1,0:T(8,128)(2,1)S(1)}, bf16[1024,512]{1,0:T(8,128)(2,1)S(1)}, f32[4,1024,1]{2,1,0:T(8,128)}) custom-call(f32[256,2048]{1,0:T(8,128)} %fusion.31.q_raw, f32[256,2048]{1,0:T(8,128)} %fusion.29.k_raw, bf16[256,2048]{1,0:T(8,128)(2,1)S(1)} %convolution_convert_fusion.1.v, ...), custom_call_target="tpu_custom_call" | custom-call | flops 1000000 | bytes 10000 | tf_op jit(solution)/shard_map/attend/pallas_call | solution.py:964
  272.7 7.4 multiply_reduce_fusion.3
  280.8 1.4 fusion.22.hot
  282.2 1.2 multiply_convert_fusion.4.rows
  283.4 79.1 %dispatch.1 = (bf16[4,2,256,2048]{3,2,1,0:T(8,128)(2,1)}, bf16[2,8,144,2048]{3,2,1,0:T(8,128)(2,1)}, bf16[2,8,144,2048]{3,2,1,0:T(8,128)(2,1)}, f32[2,8,144,1]{3,2,1,0:T(8,128)}, f32[8,16,256]{2,1,0:T(8,128)}) custom-call(bf16[256,2048]{1,0:T(8,128)(2,1)} %multiply_convert_fusion.4.rows, bf16[16,2048]{1,0:T(8,128)(2,1)} %bitcast.130, ...), custom_call_target="tpu_custom_call" | custom-call | flops 1000000 | bytes 10000 | tf_op jit(solution)/shard_map/dispatch/pallas_call | solution.py:604
  363.6 1.1 collective-permute-start
  364.7 17.5 %fusion.8 = f32[2,8,144,1024]{3,2,1,0:T(8,128)} fusion(bf16[2,8,144,2048]{3,2,1,0:T(8,128)(2,1)} %get-tuple-element.83, bf16[2,2048,1024]{2,1,0:T(8,128)(2,1)} %all-gather.3.cloned.1.call-done), kind=kOutput, calls=%fused_computation.18 | convolution fusion | flops 9663676416 | bytes 27262976 | tf_op jit(solution)/shard_map/escd,edf->escf/dot_general | solution.py:1182
  382.2 33.4 %all-gather.5.cloned.1.call-done = bf16[2,2048,1024]{2,1,0:T(8,128)(2,1)} async-done(((bf16[2,2048,256]{2,1,0:T(8,128)(2,1)}), bf16[2,2048,1024]{2,1,0:T(8,128)(2,1)}) %all-gather.5.cloned.1.call-update) | async-done | bytes 8388624 | tf_op jit(solution)/shard_map/all_gather | solution.py:1149
  415.5 19.0 %multiply_convert_fusion.2 = (bf16[2,8,144,1024]{3,2,1,0:T(8,128)(2,1)S(1)}, f32[2,8,144,1024]{3,2,1,0:T(8,128)}) fusion(f32[2,8,144,1024]{3,2,1,0:T(8,128)} %fusion.8, bf16[2,8,144,2048]{3,2,1,0:T(8,128)(2,1)} %get-tuple-element.83, bf16[2,2048,1024]{2,1,0:T(8,128)(2,1)} %all-gather.5.cloned.1.call-done), kind=kOutput, calls=%fused_computation.10 | convolution fusion | flops 9677832192 | bytes 41418752 | tf_op jit(solution)/shard_map/escd,edf->escf/dot_general | solution.py:1182
  435.3 1.5 slice.54
  436.7 1.2 collective-permute-start.3
  437.9 2.3 slice.53
  440.2 16.7 %bitcast_convert_fusion.2 = bf16[2,1024,2048]{2,1,0:T(8,128)(2,1)} fusion(bf16[2,8,144,1024]{3,2,1,0:T(8,128)(2,1)S(1)} %get-tuple-element.202, bf16[2,8,144,2048]{3,2,1,0:T(8,128)(2,1)} %get-tuple-element.80), kind=kOutput, calls=%fused_computation.7 | convolution fusion | flops 9667870720 | bytes 22544384 | tf_op jit(solution)/shard_map/escf,escd->efd/dot_general | solution.py:1182
  457.0 3.6 collective-permute-done.3.second
  460.5 3.2 collective-permute-done.2.first
  463.8 6.4 join.1
  470.2 22.3 %multiply_convert_fusion = (bf16[2,8,144,1024]{3,2,1,0:T(8,128)(2,1)}, bf16[2,8,144,1024]{3,2,1,0:T(8,128)(2,1)}) fusion(f32[2,8,144,1024]{3,2,1,0:T(8,128)} %fusion.8, f32[2,8,144,1024]{3,2,1,0:T(8,128)} %get-tuple-element.203, bf16[2,8,144,2048]{3,2,1,0:T(8,128)(2,1)} %get-tuple-element.80, bf16[2,1024,2048]{2,1,0:T(8,128)(2,1)} %join.1), kind=kOutput, calls=%fused_computation.8 | convolution fusion | flops 9694347264 | bytes 46137344 | tf_op jit(solution)/shard_map/escd,efd->escf/dot_general | solution.py:1182
  492.5 17.3 %bitcast_convert_fusion.1 = bf16[2,2048,1024]{2,1,0:T(8,128)(2,1)} fusion(bf16[2,8,144,2048]{3,2,1,0:T(8,128)(2,1)} %get-tuple-element.83, bf16[2,8,144,1024]{3,2,1,0:T(8,128)(2,1)} %get-tuple-element.91), kind=kOutput, calls=%fused_computation.6 | convolution fusion | flops 9667870720 | bytes 22544384 | tf_op jit(solution)/shard_map/escd,escf->edf/dot_general | solution.py:1182
  509.9 1.1 copy-done.18
  511.0 2.0 collective-permute-start.6
  514.7 2.9 fusion.20.hot
  517.7 2.8 pad_maximum_fusion.1.refs_2_
  520.5 2.8 pad_maximum_fusion.refs_1_
  523.3 18.2 %fusion.1 = (bf16[2,8,144,2048]{3,2,1,0:T(8,128)(2,1)}, f32[2,8,144]{2,1,0:T(8,128)S(1)}) fusion(f32[2,8,144]{2,1,0:T(8,128)S(1)} %reduce.1, bf16[2,8,144,2048]{3,2,1,0:T(8,128)(2,1)} %get-tuple-element.80, bf16[2,8,144,1024]{3,2,1,0:T(8,128)(2,1)S(1)} %bitcast.154, bf16[2,1024,2048]{2,1,0:T(8,128)(2,1)} %join.1), kind=kOutput, calls=%fused_computation.3 | convolution fusion | flops 9696704512 | bytes 32000000 | tf_op jit(solution)/shard_map/escf,efd->escd/dot_general | solution.py:1182
  543.3 17.1 %bitcast_convert_fusion = bf16[2,2048,1024]{2,1,0:T(8,128)(2,1)} fusion(bf16[2,8,144,2048]{3,2,1,0:T(8,128)(2,1)} %get-tuple-element.83, bf16[2,8,144,1024]{3,2,1,0:T(8,128)(2,1)} %get-tuple-element.92), kind=kOutput, calls=%fused_computation.5 | convolution fusion | flops 9667870720 | bytes 22544384 | tf_op jit(solution)/shard_map/escd,escf->edf/dot_general | solution.py:1182
  560.5 18.6 %fusion.2 = f32[2,8,144,2048]{3,2,1,0:T(8,128)} fusion(bf16[2,8,144,1024]{3,2,1,0:T(8,128)(2,1)} %get-tuple-element.92, bf16[2,2048,1024]{2,1,0:T(8,128)(2,1)} %all-gather.5.cloned.1.call-done), kind=kOutput, calls=%fused_computation.12 | convolution fusion | flops 9663676416 | bytes 31981568 | tf_op jit(solution)/shard_map/escf,edf->escd/dot_general | solution.py:1182
  579.1 19.2 %add_convert_fusion.pairs = bf16[2,8,144,2048]{3,2,1,0:T(8,128)(2,1)} fusion(f32[2,8,144,2048]{3,2,1,0:T(8,128)} %fusion.2, bf16[2,8,144,1024]{3,2,1,0:T(8,128)(2,1)} %get-tuple-element.91, bf16[2,2048,1024]{2,1,0:T(8,128)(2,1)} %all-gather.3.cloned.1.call-done), kind=kOutput, calls=%fused_computation.4 | convolution fusion | flops 9673113600 | bytes 41418752 | tf_op jit(solution)/shard_map/escf,edf->escd/dot_general | solution.py:1182
  598.3 101.7 %give_back.1 = (f32[256,2048]{1,0:T(8,128)}, bf16[8,256,2048]{2,1,0:T(8,128)(2,1)}, f32[16,2048]{1,0:T(8,128)}) custom-call(bf16[8,2,256,144]{3,2,1,0:T(8,128)(2,1)} %fusion.20.hot, bf16[8,256,16]{2,1,0:T(8,128)(2,1)} %copy.71.logit, bf16[8,16,256]{2,1,0:T(8,128)(2,1)} %bitcast.132, bf16[16,2048]{1,0:T(8,128)(2,1)} %bitcast.131, ...), custom_call_target="tpu_custom_call" | custom-call | flops 99999997952 | bytes 200000000 | tf_op jit(solution)/shard_map/give_back/pallas_call | solution.py:802
  700.1 2.2 multiply_reduce_fusion.1
  702.3 2.2 copy.72
  704.6 2.1 reshape.276
  706.7 3.8 fusion.41
  711.5 3.3 convolution_convert_fusion.do
  714.9 73.2 %attend_back.1 = (bf16[256,2048]{1,0:T(8,128)(2,1)}, bf16[256,2048]{1,0:T(8,128)(2,1)}, bf16[256,2048]{1,0:T(8,128)(2,1)}, f32[8,2048]{1,0:T(8,128)}, f32[8,2048]{1,0:T(8,128)}) custom-call(bf16[256,2048]{1,0:T(8,128)(2,1)} %convolution_convert_fusion.do, bf16[1024,512]{1,0:T(8,128)(2,1)} %copy-done.7, bf16[1024,512]{1,0:T(8,128)(2,1)} %copy-done.8, ...), custom_call_target="tpu_custom_call" | custom-call | flops 49999998976 | bytes 10000000 | tf_op jit(solution)/shard_map/attend_back/pallas_call | solution.py:1039
  790.8 1.6 collective-permute-start.4
  792.6 1.3 constant_dynamic-slice_fusion.5
  800.2 170.7 %collect.1 = (f32[16,128]{1,0:T(8,128)}, f32[64,2048]{1,0:T(8,128)}, f32[64,2048]{1,0:T(8,128)}, f32[64,2048]{1,0:T(8,128)}, f32[64,2048]{1,0:T(8,128)}, /*index=5*/bf16[256,2048]{1,0:T(8,128)(2,1)}, f32[8,2048]{1,0:T(8,128)}) custom-call(f32[2,2,4,16,128]{4,3,2,1,0:T(8,128)} %bitcast.135, bf16[512,2048]{1,0:T(8,128)(2,1)} %pad_maximum_fusion.refs_1_, ...), custom_call_target="tpu_custom_call" | custom-call | flops 160000000000 | bytes 320000000 | tf_op jit(solution)/shard_map/collect/pallas_call | solution.py:483
  973.9 1.4 fusion.42
  975.3 3.3 fusion.28
  978.6 2.3 convert_element_type.258
  980.9 2.3 convert_element_type.259
  983.3 2.5 convert_element_type.260
  (220 shorter events, 34.0 us)
Async XLA Ops:
  7.2 355.4 %all-gather.3.cloned.1.call-start = ((), (), s32[]{:S(2)}) async-start(), calls=%async_computation.4 | async-start | bytes 10485760 | tf_op jit(solution)/shard_map/all_gather | solution.py:1149
  170.8 6.3 copy-start.16
  170.8 244.7 %all-gather.5.cloned.1.call-start = ((), (), s32[]{:S(2)}) async-start(), calls=%async_computation.5 | async-start | bytes 10485760 | tf_op jit(solution)/shard_map/all_gather | solution.py:1149
  171.6 426.8 %reduce-scatter.5.cloned.1.call-start = ((), (), s32[]{:S(2)}) async-start(), calls=%async_computation.6 | async-start | bytes 10485760 | tf_op jit(solution)/shard_map/reduce_scatter | solution.py:1200
  172.7 109.5 %copy-start.36 = (f32[2048]{0:T(1024)}, f32[2048]{0:T(1024)S(1)}, u32[]{:S(2)}) copy-start(f32[2048]{0:T(1024)S(1)} %reshape.284) | copy-start | bytes 24580
  173.3 18.4 %copy-start.4 = (f32[1,2048]{1,0:T(1,128)}, f32[1,2048]{1,0:T(1,128)S(1)}, u32[]{:S(2)}) copy-start(f32[1,2048]{1,0:T(1,128)S(1)} %reshape.282.k_gain) | copy-start | bytes 24580
  173.4 18.3 %copy-start.5 = (f32[1,2048]{1,0:T(1,128)}, f32[1,2048]{1,0:T(1,128)S(1)}, u32[]{:S(2)}) copy-start(f32[1,2048]{1,0:T(1,128)S(1)} %reshape.281.q_gain) | copy-start | bytes 24580
  176.2 104.7 %copy-start.38 = (pred[8,2,256]{2,1,0:T(4,128)(4,1)}, pred[8,2,256]{2,1,0:T(4,128)(4,1)S(1)}, u32[]{:S(2)}) copy-start(pred[8,2,256]{2,1,0:T(4,128)(4,1)S(1)} %compare_reduce_fusion) | copy-start | bytes 12292
  176.3 104.5 %copy-start.31 = (f32[8,2,256]{2,1,0:T(2,128)}, f32[8,2,256]{2,1,0:T(2,128)S(1)}, u32[]{:S(2)}) copy-start(f32[8,2,256]{2,1,0:T(2,128)S(1)} %copy.66) | copy-start | bytes 49156
  176.4 15.3 %copy-start.6 = (f32[1,1024]{1,0:T(1,128)}, f32[1,1024]{1,0:T(1,128)S(1)}, u32[]{:S(2)}) copy-start(f32[1,1024]{1,0:T(1,128)S(1)} %compare_convert_fusion.keep) | copy-start | bytes 12292
  177.1 14.6 %copy-start.2 = (f32[256,128]{1,0:T(8,128)}, f32[256,128]{1,0:T(8,128)S(1)}, u32[]{:S(2)}) copy-start(f32[256,128]{1,0:T(8,128)S(1)} %get-tuple-element.204.cosine) | copy-start | bytes 393220
  177.1 14.6 %copy-start.3 = (f32[256,128]{1,0:T(8,128)}, f32[256,128]{1,0:T(8,128)S(1)}, u32[]{:S(2)}) copy-start(f32[256,128]{1,0:T(8,128)S(1)} %get-tuple-element.205.sine) | copy-start | bytes 393220
  177.4 6.7 slice-start.2
  177.8 6.3 copy-start.17
  177.8 6.3 slice-start.3
  177.8 10.2 %slice-start = ((s8[8388608]{0:T(1024)(128)(4,1)}), s8[4194304]{0:T(1024)(128)(4,1)S(1)}, s32[]{:S(2)}) async-start(s8[8388608]{0:T(1024)(128)(4,1)} %bitcast.142), calls=%async_computation.10 | async-start | bytes 8388608
  272.7 7.4 copy-start
  272.7 7.4 copy-start.7
  272.7 7.4 copy-start.8
  272.7 7.4 copy-start.9
  280.8 81.7 %copy-start.45 = (f32[256]{0:T(256)}, f32[256]{0:T(256)S(1)}, u32[]{:S(2)}) copy-start(f32[256]{0:T(256)S(1)} %get-tuple-element.199) | copy-start | bytes 3076
  362.6 72.7 %collective-permute-start.1 = (bf16[2,256,2048]{2,1,0:T(8,128)(2,1)}, bf16[2,256,2048]{2,1,0:T(8,128)(2,1)S(1)}, u32[]{:S(2)}, u32[]{:S(2)}) collective-permute-start(bf16[2,256,2048]{2,1,0:T(8,128)(2,1)} %own), channel_id=1, source_target_pairs={{0,16},{16,0},{1,17},{17,1},{2,18},{18,2},{3,19},{19,3},{4,20},{20... | collective-permute-start | bytes 6291464 | tf_op jit(solution)/shard_map/ppermute | solution.py:1161
  363.6 74.3 %collective-permute-start = (bf16[2,256,2048]{2,1,0:T(8,128)(2,1)}, bf16[2,256,2048]{2,1,0:T(8,128)(2,1)}, u32[]{:S(2)}, u32[]{:S(2)}) collective-permute-start(bf16[2,256,2048]{2,1,0:T(8,128)(2,1)} %own), channel_id=1, source_target_pairs={{0,8},{8,0},{1,9},{9,1},{2,10},{10,2},{3,11},{11,3},{4,12},{12,4},... | collective-permute-start | bytes 6291464 | tf_op jit(solution)/shard_map/ppermute | solution.py:1161
  435.3 21.7 %copy-start.12 = (bf16[2,256,2048]{2,1,0:T(8,128)(2,1)}, bf16[2,256,2048]{2,1,0:T(8,128)(2,1)S(1)}, u32[]{:S(2)}) copy-start(bf16[2,256,2048]{2,1,0:T(8,128)(2,1)S(1)} %collective-permute-done.1.from_a) | copy-start | bytes 6291460
  436.7 23.8 %collective-permute-start.3 = (bf16[1,256,2048]{2,1,0:T(8,128)(2,1)}, bf16[1,256,2048]{2,1,0:T(8,128)(2,1)S(1)}, u32[]{:S(2)}, u32[]{:S(2)}) collective-permute-start(bf16[1,256,2048]{2,1,0:T(8,128)(2,1)} %slice.54), channel_id=1, source_target_pairs={{0,8},{8,0},{1,9},{9,1},{2,10},{10,2},{3,11},{11,3},{4,12},{12,4},... | collective-permute-start | bytes 3145736 | tf_op jit(solution)/shard_map/ppermute | solution.py:1161
  440.2 23.5 %collective-permute-start.2 = (bf16[1,256,2048]{2,1,0:T(8,128)(2,1)}, bf16[1,256,2048]{2,1,0:T(8,128)(2,1)}, u32[]{:S(2)}, u32[]{:S(2)}) collective-permute-start(bf16[1,256,2048]{2,1,0:T(8,128)(2,1)} %slice.53), channel_id=1, source_target_pairs={{0,16},{16,0},{1,17},{17,1},{2,18},{18,2},{3,19},{19,3},{4,20},{20... | collective-permute-start | bytes 3145736 | tf_op jit(solution)/shard_map/ppermute | solution.py:1161
  463.7 236.3 %reduce-scatter.7.cloned.1.call-start = ((), (), s32[]{:S(2)}) async-start(), calls=%async_computation.7 | async-start | bytes 10485760 | tf_op jit(solution)/shard_map/reduce_scatter | solution.py:1200
  509.9 278.3 %reduce-scatter.9.cloned.1.call-start = ((), (), s32[]{:S(2)}) async-start(), calls=%async_computation.8 | async-start | bytes 10485760 | tf_op jit(solution)/shard_map/reduce_scatter | solution.py:1200
  511.0 6.6 collective-permute-start.6
  513.0 7.5 collective-permute-start.5
  514.7 8.5 slice-start.4
  523.3 19.0 %copy-start.40 = (f32[8,16,256]{2,1,0:T(8,128)S(1)}, f32[8,16,256]{2,1,0:T(8,128)}, u32[]{:S(2)}) copy-start(f32[8,16,256]{2,1,0:T(8,128)} %get-tuple-element.89) | copy-start | bytes 393220
  542.3 18.1 %copy-start.33 = (bf16[8,256,16]{1,2,0:T(8,128)(2,1)}, bf16[8,256,16]{1,2,0:T(8,128)(2,1)S(1)}, u32[]{:S(2)}) copy-start(bf16[8,256,16]{1,2,0:T(8,128)(2,1)S(1)} %fusion.36) | copy-start | bytes 196612
  560.5 414.8 %reduce-scatter.11.cloned.1.call-start = ((), (), s32[]{:S(2)}) async-start(), calls=%async_computation.9 | async-start | bytes 9437184 | tf_op jit(solution)/shard_map/reduce_scatter | solution.py:1215
  598.3 101.7 %copy-start.11 = (f32[256,2048]{1,0:T(8,128)S(1)}, f32[256,2048]{1,0:T(8,128)}, u32[]{:S(2)}) copy-start(f32[256,2048]{1,0:T(8,128)} %copy-done.10) | copy-start | bytes 6291460
  598.3 101.8 %copy-start.37 = (f32[2048]{0:T(1024)S(1)}, f32[2048]{0:T(1024)}, u32[]{:S(2)}) copy-start(f32[2048]{0:T(1024)} %copy-done.36) | copy-start | bytes 24580
  598.3 101.8 %copy-start.46 = (f32[256]{0:T(256)S(1)}, f32[256]{0:T(256)}, u32[]{:S(2)}) copy-start(f32[256]{0:T(256)} %copy-done.45) | copy-start | bytes 3076
  700.0 6.7 copy-start.13
  700.0 6.7 copy-start.43
  700.0 6.7 copy-start.47
  714.9 77.5 %copy-start.15 = (bf16[256,2048]{1,0:T(8,128)(2,1)S(1)}, bf16[256,2048]{1,0:T(8,128)(2,1)}, u32[]{:S(2)}) copy-start(bf16[256,2048]{1,0:T(8,128)(2,1)} %copy-done.14) | copy-start | bytes 3145732
  790.8 4.4 collective-permute-start.4
  792.5 3.5 collective-permute-start.7
  793.9 3.2 collective-permute-start.8
  794.5 3.5 collective-permute-start.9
  794.7 4.4 collective-permute-start.10
  800.2 175.1 %copy-start.44 = (f32[256]{0:T(256)S(1)}, f32[256]{0:T(256)}, u32[]{:S(2)}) copy-start(f32[256]{0:T(256)} %copy-done.42) | copy-start | bytes 3076
  970.8 7.7 copy-start.20
  (27 other events, 102.9 us)
Sparse Core Ops, SparseCore 0:
  170.9 131.4 all-gather.2
  304.3 111.2 all-gather.4
  463.8 87.6 reduce-scatter.4
  554.8 86.4 reduce-scatter.6
  644.1 91.7 reduce-scatter.8
  738.2 101.5 reduce-scatter.10

commit v8 on v7

--- a/solution.py
+++ b/solution.py
@@ -231,9 +231,17 @@
     return outs[:count], outs[count:]
 
 
-def collect_kernel(count, *refs):
+def column_units(count, width):
+    units = []
+    for at in range(count):
+        pieces = 4 if at == count - 1 else 2
+        units += [(at, part * width // pieces, width // pieces) for part in range(pieces)]
+    return units
+
+
+def collect_kernel(whole, units, *refs):
     ring = lax.axis_size("ring")
-    whole = (count - 1) // 2
+    count = len(units) + 1
     small, lefts, rights, refs = refs[0], (refs[1],) + (refs[2],) * (whole - 1), refs[3 : whole + 3], refs[whole + 3 :]
     grads, matrices, (x, gain, passed), refs = refs[:3], refs[3:6], refs[6:9], refs[9:]
     outs, (input_grad, gain_out), refs = refs[: whole + 1], refs[whole + 1 : whole + 3], refs[whole + 3 :]
@@ -326,9 +334,9 @@
     def product(w, block, which):
         own = bufs[w][0]
         rows, cols = own.shape[1] * own.shape[2], own.shape[3]
-        at, part = divmod(w - 1, 2)
+        at, begin, _ = units[w - 1]
         left = lefts[at][:, pl.ds(pl.multiple_of(block * rows, rows), rows)]
-        value = transposed_times(left, rights[at][:, pl.ds((2 * part + which) * cols, cols)])
+        value = transposed_times(left, rights[at][:, pl.ds(begin + which * cols, cols)])
         return value.reshape(own.shape[1:])
 
     def sent_first(w):
@@ -346,18 +354,20 @@
         if w > 2:
             sent_first(w - 2)
 
+        own_cols = pl.ds(0, bufs[w][0].shape[3])
+
         def one_a(i, carry):
-            out_a[w % 2, i] = product(w, 2 * na + i, 0).astype(out_a.dtype)
+            out_a[w % 2, i, :, :, own_cols] = product(w, 2 * na + i, 0).astype(out_a.dtype)
             return carry
 
         def one_b(i, carry):
-            out_b[w % 2, i] = product(w, 2 * i + nb, 1).astype(out_b.dtype)
+            out_b[w % 2, i, :, :, own_cols] = product(w, 2 * i + nb, 1).astype(out_b.dtype)
             return carry
 
         lax.fori_loop(0, 2, one_a, 0)
-        push(out_a.at[w % 2], in_a, send.at[w, 0], got.at[w, 0], to_a)
+        push(out_a.at[w % 2, :, :, :, own_cols], in_a, send.at[w, 0], got.at[w, 0], to_a)
         lax.fori_loop(0, 2, one_b, 0)
-        push(out_b.at[w % 2], in_b, send.at[w, 1], got.at[w, 1], to_b)
+        push(out_b.at[w % 2, :, :, :, own_cols], in_b, send.at[w, 1], got.at[w, 1], to_b)
 
     def second(w):
         own_a, own_b, in_a, in_b, in_a2, in_b2 = bufs[w][:6]
@@ -414,8 +424,8 @@
                     value = value + in_ring[k, at, :].astype(jnp.float32)
                 final[core] = value
             cols = final.shape[2]
-            at, part = divmod(w - 1, 2)
-            there = outs[at + 1].at[:, pl.ds(pl.multiple_of((2 * c + part) * cols, cols), cols)]
+            at, begin, _ = units[w - 1]
+            there = outs[at + 1].at[:, pl.ds(pl.multiple_of(c * rights[at].shape[1] + begin, 128), cols)]
             push(final.at[nc], there, send.at[w, 4], got.at[w, 4], to_core)
             pltpu.make_async_copy(final.at[c], there, load.at[w, 2]).start()
         else:
@@ -460,12 +470,13 @@
 
 
 def collect(small, lefts, rights, grads, matrices, x, gain, passed):
-    count, ring = 2 * len(rights) + 1, lax.axis_size("ring")
+    units, ring = column_units(len(rights), rights[0].shape[1]), lax.axis_size("ring")
+    count = len(units) + 1
     chips = lax.axis_size("ca") * lax.axis_size("cb") * ring
     square = (lax.axis_size("ca"), lax.axis_size("cb"), ring)
     view = small.reshape(square + small.shape[1:])
     rows = lefts[0].shape[1] // chips
-    forms = [(*view.shape[3:], view.dtype)] + [(rows, r.shape[1] // 2, r.dtype) for r in rights for _ in range(2)]
+    forms = [(*view.shape[3:], view.dtype)] + [(rows, cols, lefts[0].dtype) for _, _, cols in units]
     shapes = [view.shape[3:]] + [(rows // 2, 2 * r.shape[1]) for r in rights]
     shapes, scratch = [jax.ShapeDtypeStruct(shape, jnp.float32) for shape in shapes], []
     for rows, cols, dtype in forms:
@@ -475,13 +486,13 @@
         scratch += [vmem(2, ring, *piece)] * 4 + [vmem(ring, *piece)] * 2
         scratch += [vmem(ring, rows, cols), vmem(ring - 1, rows, cols)]
         scratch += [pltpu.VMEM((2, rows // 2, cols) if big else (1, 8, 128), jnp.float32)]
-    scratch += [vmem(2, 2, ring, *piece)] * 2
+    scratch += [vmem(2, 2, ring, lefts[0].shape[1] // chips, units[0][2] // 2)] * 2
     dma = pltpu.SemaphoreType.DMA
     vm, anywhere = pl.BlockSpec(memory_space=pltpu.VMEM), pl.BlockSpec(memory_space=pl.ANY)
     wide = (8, gain.shape[1])
     f32 = lambda *shape: pltpu.VMEM(shape, jnp.float32)
     outs = pl.pallas_call(
-        functools.partial(collect_kernel, count),
+        functools.partial(collect_kernel, len(rights), units),
         out_shape=shapes + [jax.ShapeDtypeStruct(x.shape, x.dtype), jax.ShapeDtypeStruct(wide, jnp.float32)],
         in_specs=[anywhere] + [vm] * (len(rights) + 5) + [anywhere] * 3 + [vm] * 3,
         out_specs=[vm] * (len(rights) + 3),

time: 1010 us -> 1000 us (0.990)
  no operation moved by 1% of the time
where the time goes in v8:
time: 1000 us; the launch traced here: 993 us
  Pallas kernels  662 us (66%)
  matrix products  191 us (19%)
  waiting for transfers between devices  41.7 us (4%)
  other arithmetic  41.4 us (4%)
  local copies, waits for them, and re-layouts  32.6 us (3%)
  between operations  16 us (2%)
    pallas_call x1, Pallas kernels, collect(): pl.pallas_call(functools.partial(collect_kernel, len(rights), units), out...  166 us
    dot_general x9, matrix products, local(): jnp.einsum(eq, a, b, preferred_element_type=jnp.float32)  166 us
    pallas_call x1, Pallas kernels, spread(): pl.pallas_call(functools.partial(spread_kernel, count, more), out_shape=[...  154 us
    pallas_call x1, Pallas kernels, give_back(): pl.pallas_call(give_back_kernel, out_shape=[jax.ShapeDtypeStruct((rows, w...  102 us
    pallas_call x1, Pallas kernels, attend(): pl.pallas_call(functools.partial(attend_kernel, scale), out_shape=[jax.Sh...  81 us
    pallas_call x1, Pallas kernels, dispatch(): pl.pallas_call(dispatch_kernel, out_shape=[low(ring, 2, count, width), lo...  79.1 us
    pallas_call x1, Pallas kernels, attend_back(): pl.pallas_call(functools.partial(attend_back_kernel, scale), out_shape=[j...  73.2 us
    all_gather x2, waiting for transfers between devices, local(): lax.all_gather(w, CTX, axis=2, tiled=True)  33.4 us
  transfers between devices with their start and end apart: 17, of which 4 were waited for; matrix products, arithmetic and copies ran while one was open for 24% of the time, Pallas kernels for 51%

profile of v8, /device:TPU:9, one launch (start us, length us, event | category | flops | bytes accessed | tf_op | source)
XLA Modules:
  0.0 992.9 jit_solution(13632562626406418797)
XLA Ops:
  9.4 2.8 concatenate.30
  14.2 2.4 fusion.26.refs_6_
  16.6 154.2 %spread.1 = (bf16[2,2,4,2,64,2048]{5,4,3,2,1,0:T(8,128)(2,1)}, bf16[2,2,4,2,64,2048]{5,4,3,2,1,0:T(8,128)(2,1)}, bf16[2,2,4,2,64,2048]{5,4,3,2,1,0:T(8,128)(2,1)...) custom-call(bf16[64,2048]{1,0:T(8,128)(2,1)} %refs_0_.1, ...), custom_call_target="tpu_custom_call" | custom-call | flops 149999992832 | bytes 300000000 | tf_op jit(solution)/shard_map/spread/pallas_call | solution.py:217
  177.8 6.3 convolution_convert_fusion.1.v
  184.1 3.8 fusion.29.k_raw
  187.9 3.8 fusion.31.q_raw
  191.7 81.0 %attend.1 = (bf16[256,2048]{1,0:T(8,128)(2,1)S(1)}, bf16[1024,512]{1,0:T(8,128)(2,1)S(1)}, bf16[1024,512]{1,0:T(8,128)(2,1)S(1)}, bf16[1024,512]{1,0:T(8,128)(2,1)S(1)}, f32[4,1024,1]{2,1,0:T(8,128)}) custom-call(f32[256,2048]{1,0:T(8,128)} %fusion.31.q_raw, f32[256,2048]{1,0:T(8,128)} %fusion.29.k_raw, bf16[256,2048]{1,0:T(8,128)(2,1)S(1)} %convolution_convert_fusion.1.v, ...), custom_call_target="tpu_custom_call" | custom-call | flops 1000000 | bytes 10000 | tf_op jit(solution)/shard_map/attend/pallas_call | solution.py:975
  272.7 7.4 multiply_reduce_fusion.3
  280.8 1.4 fusion.22.hot
  282.2 1.2 multiply_convert_fusion.4.rows
  283.4 79.1 %dispatch.1 = (bf16[4,2,256,2048]{3,2,1,0:T(8,128)(2,1)}, bf16[2,8,144,2048]{3,2,1,0:T(8,128)(2,1)}, bf16[2,8,144,2048]{3,2,1,0:T(8,128)(2,1)}, f32[2,8,144,1]{3,2,1,0:T(8,128)}, f32[8,16,256]{2,1,0:T(8,128)}) custom-call(bf16[256,2048]{1,0:T(8,128)(2,1)} %multiply_convert_fusion.4.rows, bf16[16,2048]{1,0:T(8,128)(2,1)} %bitcast.130, ...), custom_call_target="tpu_custom_call" | custom-call | flops 1000000 | bytes 10000 | tf_op jit(solution)/shard_map/dispatch/pallas_call | solution.py:615
  363.6 1.1 collective-permute-start
  364.7 17.5 %fusion.8 = f32[2,8,144,1024]{3,2,1,0:T(8,128)} fusion(bf16[2,8,144,2048]{3,2,1,0:T(8,128)(2,1)} %get-tuple-element.83, bf16[2,2048,1024]{2,1,0:T(8,128)(2,1)} %all-gather.3.cloned.1.call-done), kind=kOutput, calls=%fused_computation.18 | convolution fusion | flops 9663676416 | bytes 27262976 | tf_op jit(solution)/shard_map/escd,edf->escf/dot_general | solution.py:1193
  382.2 33.4 %all-gather.5.cloned.1.call-done = bf16[2,2048,1024]{2,1,0:T(8,128)(2,1)} async-done(((bf16[2,2048,256]{2,1,0:T(8,128)(2,1)}), bf16[2,2048,1024]{2,1,0:T(8,128)(2,1)}) %all-gather.5.cloned.1.call-update) | async-done | bytes 8388624 | tf_op jit(solution)/shard_map/all_gather | solution.py:1160
  415.5 19.0 %multiply_convert_fusion.2 = (bf16[2,8,144,1024]{3,2,1,0:T(8,128)(2,1)S(1)}, f32[2,8,144,1024]{3,2,1,0:T(8,128)}) fusion(f32[2,8,144,1024]{3,2,1,0:T(8,128)} %fusion.8, bf16[2,8,144,2048]{3,2,1,0:T(8,128)(2,1)} %get-tuple-element.83, bf16[2,2048,1024]{2,1,0:T(8,128)(2,1)} %all-gather.5.cloned.1.call-done), kind=kOutput, calls=%fused_computation.10 | convolution fusion | flops 9677832192 | bytes 41418752 | tf_op jit(solution)/shard_map/escd,edf->escf/dot_general | solution.py:1193
  435.3 1.5 slice.54
  436.7 1.2 collective-permute-start.3
  437.9 2.3 slice.53
  440.2 16.7 %bitcast_convert_fusion.2 = bf16[2,1024,2048]{2,1,0:T(8,128)(2,1)} fusion(bf16[2,8,144,1024]{3,2,1,0:T(8,128)(2,1)S(1)} %get-tuple-element.202, bf16[2,8,144,2048]{3,2,1,0:T(8,128)(2,1)} %get-tuple-element.80), kind=kOutput, calls=%fused_computation.7 | convolution fusion | flops 9667870720 | bytes 22544384 | tf_op jit(solution)/shard_map/escf,escd->efd/dot_general | solution.py:1193
  457.0 3.6 collective-permute-done.3.second
  460.5 3.2 collective-permute-done.2.first
  463.8 6.4 join.1
  470.2 22.3 %multiply_convert_fusion = (bf16[2,8,144,1024]{3,2,1,0:T(8,128)(2,1)}, bf16[2,8,144,1024]{3,2,1,0:T(8,128)(2,1)}) fusion(f32[2,8,144,1024]{3,2,1,0:T(8,128)} %fusion.8, f32[2,8,144,1024]{3,2,1,0:T(8,128)} %get-tuple-element.203, bf16[2,8,144,2048]{3,2,1,0:T(8,128)(2,1)} %get-tuple-element.80, bf16[2,1024,2048]{2,1,0:T(8,128)(2,1)} %join.1), kind=kOutput, calls=%fused_computation.8 | convolution fusion | flops 9694347264 | bytes 46137344 | tf_op jit(solution)/shard_map/escd,efd->escf/dot_general | solution.py:1193
  492.5 17.3 %bitcast_convert_fusion.1 = bf16[2,2048,1024]{2,1,0:T(8,128)(2,1)} fusion(bf16[2,8,144,2048]{3,2,1,0:T(8,128)(2,1)} %get-tuple-element.83, bf16[2,8,144,1024]{3,2,1,0:T(8,128)(2,1)} %get-tuple-element.91), kind=kOutput, calls=%fused_computation.6 | convolution fusion | flops 9667870720 | bytes 22544384 | tf_op jit(solution)/shard_map/escd,escf->edf/dot_general | solution.py:1193
  509.9 1.1 copy-done.18
  511.0 2.0 collective-permute-start.6
  514.7 2.9 fusion.20.hot
  517.7 2.8 pad_maximum_fusion.1.refs_2_
  520.5 2.8 pad_maximum_fusion.refs_1_
  523.3 18.2 %fusion.1 = (bf16[2,8,144,2048]{3,2,1,0:T(8,128)(2,1)}, f32[2,8,144]{2,1,0:T(8,128)S(1)}) fusion(f32[2,8,144]{2,1,0:T(8,128)S(1)} %reduce.1, bf16[2,8,144,2048]{3,2,1,0:T(8,128)(2,1)} %get-tuple-element.80, bf16[2,8,144,1024]{3,2,1,0:T(8,128)(2,1)S(1)} %bitcast.154, bf16[2,1024,2048]{2,1,0:T(8,128)(2,1)} %join.1), kind=kOutput, calls=%fused_computation.3 | convolution fusion | flops 9696704512 | bytes 32000000 | tf_op jit(solution)/shard_map/escf,efd->escd/dot_general | solution.py:1193
  543.3 17.1 %bitcast_convert_fusion = bf16[2,2048,1024]{2,1,0:T(8,128)(2,1)} fusion(bf16[2,8,144,2048]{3,2,1,0:T(8,128)(2,1)} %get-tuple-element.83, bf16[2,8,144,1024]{3,2,1,0:T(8,128)(2,1)} %get-tuple-element.92), kind=kOutput, calls=%fused_computation.5 | convolution fusion | flops 9667870720 | bytes 22544384 | tf_op jit(solution)/shard_map/escd,escf->edf/dot_general | solution.py:1193
  560.5 18.6 %fusion.2 = f32[2,8,144,2048]{3,2,1,0:T(8,128)} fusion(bf16[2,8,144,1024]{3,2,1,0:T(8,128)(2,1)} %get-tuple-element.92, bf16[2,2048,1024]{2,1,0:T(8,128)(2,1)} %all-gather.5.cloned.1.call-done), kind=kOutput, calls=%fused_computation.12 | convolution fusion | flops 9663676416 | bytes 31981568 | tf_op jit(solution)/shard_map/escf,edf->escd/dot_general | solution.py:1193
  579.1 19.2 %add_convert_fusion.pairs = bf16[2,8,144,2048]{3,2,1,0:T(8,128)(2,1)} fusion(f32[2,8,144,2048]{3,2,1,0:T(8,128)} %fusion.2, bf16[2,8,144,1024]{3,2,1,0:T(8,128)(2,1)} %get-tuple-element.91, bf16[2,2048,1024]{2,1,0:T(8,128)(2,1)} %all-gather.3.cloned.1.call-done), kind=kOutput, calls=%fused_computation.4 | convolution fusion | flops 9673113600 | bytes 41418752 | tf_op jit(solution)/shard_map/escf,edf->escd/dot_general | solution.py:1193
  598.3 101.7 %give_back.1 = (f32[256,2048]{1,0:T(8,128)}, bf16[8,256,2048]{2,1,0:T(8,128)(2,1)}, f32[16,2048]{1,0:T(8,128)}) custom-call(bf16[8,2,256,144]{3,2,1,0:T(8,128)(2,1)} %fusion.20.hot, bf16[8,256,16]{2,1,0:T(8,128)(2,1)} %copy.71.logit, bf16[8,16,256]{2,1,0:T(8,128)(2,1)} %bitcast.132, bf16[16,2048]{1,0:T(8,128)(2,1)} %bitcast.131, ...), custom_call_target="tpu_custom_call" | custom-call | flops 99999997952 | bytes 200000000 | tf_op jit(solution)/shard_map/give_back/pallas_call | solution.py:813
  700.1 2.2 multiply_reduce_fusion.1
  702.3 2.2 copy.72
  704.6 2.1 reshape.276
  706.7 3.8 fusion.41
  711.5 3.3 convolution_convert_fusion.do
  714.9 73.2 %attend_back.1 = (bf16[256,2048]{1,0:T(8,128)(2,1)}, bf16[256,2048]{1,0:T(8,128)(2,1)}, bf16[256,2048]{1,0:T(8,128)(2,1)}, f32[8,2048]{1,0:T(8,128)}, f32[8,2048]{1,0:T(8,128)}) custom-call(bf16[256,2048]{1,0:T(8,128)(2,1)} %convolution_convert_fusion.do, bf16[1024,512]{1,0:T(8,128)(2,1)} %copy-done.7, bf16[1024,512]{1,0:T(8,128)(2,1)} %copy-done.8, ...), custom_call_target="tpu_custom_call" | custom-call | flops 49999998976 | bytes 10000000 | tf_op jit(solution)/shard_map/attend_back/pallas_call | solution.py:1050
  790.8 1.6 collective-permute-start.4
  792.6 1.3 constant_dynamic-slice_fusion.5
  800.2 166.3 %collect.1 = (f32[16,128]{1,0:T(8,128)}, f32[64,2048]{1,0:T(8,128)}, f32[64,2048]{1,0:T(8,128)}, f32[64,2048]{1,0:T(8,128)}, f32[64,2048]{1,0:T(8,128)}, /*index=5*/bf16[256,2048]{1,0:T(8,128)(2,1)}, f32[8,2048]{1,0:T(8,128)}) custom-call(f32[2,2,4,16,128]{4,3,2,1,0:T(8,128)} %bitcast.135, bf16[512,2048]{1,0:T(8,128)(2,1)} %pad_maximum_fusion.refs_1_, ...), custom_call_target="tpu_custom_call" | custom-call | flops 160000000000 | bytes 320000000 | tf_op jit(solution)/shard_map/collect/pallas_call | solution.py:494
  969.5 1.4 fusion.42
  970.9 3.3 fusion.28
  974.2 2.3 convert_element_type.258
  976.5 2.3 convert_element_type.259
  978.9 2.5 convert_element_type.260
  (220 shorter events, 34.0 us)
Async XLA Ops:
  7.2 355.4 %all-gather.3.cloned.1.call-start = ((), (), s32[]{:S(2)}) async-start(), calls=%async_computation.4 | async-start | bytes 10485760 | tf_op jit(solution)/shard_map/all_gather | solution.py:1160
  170.8 6.3 copy-start.16
  170.8 244.7 %all-gather.5.cloned.1.call-start = ((), (), s32[]{:S(2)}) async-start(), calls=%async_computation.5 | async-start | bytes 10485760 | tf_op jit(solution)/shard_map/all_gather | solution.py:1160
  171.6 426.8 %reduce-scatter.5.cloned.1.call-start = ((), (), s32[]{:S(2)}) async-start(), calls=%async_computation.6 | async-start | bytes 10485760 | tf_op jit(solution)/shard_map/reduce_scatter | solution.py:1211
  172.7 109.5 %copy-start.36 = (f32[2048]{0:T(1024)}, f32[2048]{0:T(1024)S(1)}, u32[]{:S(2)}) copy-start(f32[2048]{0:T(1024)S(1)} %reshape.284) | copy-start | bytes 24580
  173.3 18.4 %copy-start.4 = (f32[1,2048]{1,0:T(1,128)}, f32[1,2048]{1,0:T(1,128)S(1)}, u32[]{:S(2)}) copy-start(f32[1,2048]{1,0:T(1,128)S(1)} %reshape.282.k_gain) | copy-start | bytes 24580
  173.4 18.3 %copy-start.5 = (f32[1,2048]{1,0:T(1,128)}, f32[1,2048]{1,0:T(1,128)S(1)}, u32[]{:S(2)}) copy-start(f32[1,2048]{1,0:T(1,128)S(1)} %reshape.281.q_gain) | copy-start | bytes 24580
  176.2 104.7 %copy-start.38 = (pred[8,2,256]{2,1,0:T(4,128)(4,1)}, pred[8,2,256]{2,1,0:T(4,128)(4,1)S(1)}, u32[]{:S(2)}) copy-start(pred[8,2,256]{2,1,0:T(4,128)(4,1)S(1)} %compare_reduce_fusion) | copy-start | bytes 12292
  176.3 104.5 %copy-start.31 = (f32[8,2,256]{2,1,0:T(2,128)}, f32[8,2,256]{2,1,0:T(2,128)S(1)}, u32[]{:S(2)}) copy-start(f32[8,2,256]{2,1,0:T(2,128)S(1)} %copy.66) | copy-start | bytes 49156
  176.4 15.3 %copy-start.6 = (f32[1,1024]{1,0:T(1,128)}, f32[1,1024]{1,0:T(1,128)S(1)}, u32[]{:S(2)}) copy-start(f32[1,1024]{1,0:T(1,128)S(1)} %compare_convert_fusion.keep) | copy-start | bytes 12292
  177.1 14.6 %copy-start.2 = (f32[256,128]{1,0:T(8,128)}, f32[256,128]{1,0:T(8,128)S(1)}, u32[]{:S(2)}) copy-start(f32[256,128]{1,0:T(8,128)S(1)} %get-tuple-element.204.cosine) | copy-start | bytes 393220
  177.1 14.6 %copy-start.3 = (f32[256,128]{1,0:T(8,128)}, f32[256,128]{1,0:T(8,128)S(1)}, u32[]{:S(2)}) copy-start(f32[256,128]{1,0:T(8,128)S(1)} %get-tuple-element.205.sine) | copy-start | bytes 393220
  177.4 6.7 slice-start.2
  177.8 6.3 copy-start.17
  177.8 6.3 slice-start.3
  177.8 10.2 %slice-start = ((s8[8388608]{0:T(1024)(128)(4,1)}), s8[4194304]{0:T(1024)(128)(4,1)S(1)}, s32[]{:S(2)}) async-start(s8[8388608]{0:T(1024)(128)(4,1)} %bitcast.142), calls=%async_computation.10 | async-start | bytes 8388608
  272.7 7.4 copy-start
  272.7 7.4 copy-start.7
  272.7 7.4 copy-start.8
  272.7 7.4 copy-start.9
  280.8 81.7 %copy-start.45 = (f32[256]{0:T(256)}, f32[256]{0:T(256)S(1)}, u32[]{:S(2)}) copy-start(f32[256]{0:T(256)S(1)} %get-tuple-element.199) | copy-start | bytes 3076
  362.6 72.7 %collective-permute-start.1 = (bf16[2,256,2048]{2,1,0:T(8,128)(2,1)}, bf16[2,256,2048]{2,1,0:T(8,128)(2,1)S(1)}, u32[]{:S(2)}, u32[]{:S(2)}) collective-permute-start(bf16[2,256,2048]{2,1,0:T(8,128)(2,1)} %own), channel_id=1, source_target_pairs={{0,16},{16,0},{1,17},{17,1},{2,18},{18,2},{3,19},{19,3},{4,20},{20... | collective-permute-start | bytes 6291464 | tf_op jit(solution)/shard_map/ppermute | solution.py:1172
  363.6 74.3 %collective-permute-start = (bf16[2,256,2048]{2,1,0:T(8,128)(2,1)}, bf16[2,256,2048]{2,1,0:T(8,128)(2,1)}, u32[]{:S(2)}, u32[]{:S(2)}) collective-permute-start(bf16[2,256,2048]{2,1,0:T(8,128)(2,1)} %own), channel_id=1, source_target_pairs={{0,8},{8,0},{1,9},{9,1},{2,10},{10,2},{3,11},{11,3},{4,12},{12,4},... | collective-permute-start | bytes 6291464 | tf_op jit(solution)/shard_map/ppermute | solution.py:1172
  435.3 21.7 %copy-start.12 = (bf16[2,256,2048]{2,1,0:T(8,128)(2,1)}, bf16[2,256,2048]{2,1,0:T(8,128)(2,1)S(1)}, u32[]{:S(2)}) copy-start(bf16[2,256,2048]{2,1,0:T(8,128)(2,1)S(1)} %collective-permute-done.1.from_a) | copy-start | bytes 6291460
  436.7 23.8 %collective-permute-start.3 = (bf16[1,256,2048]{2,1,0:T(8,128)(2,1)}, bf16[1,256,2048]{2,1,0:T(8,128)(2,1)S(1)}, u32[]{:S(2)}, u32[]{:S(2)}) collective-permute-start(bf16[1,256,2048]{2,1,0:T(8,128)(2,1)} %slice.54), channel_id=1, source_target_pairs={{0,8},{8,0},{1,9},{9,1},{2,10},{10,2},{3,11},{11,3},{4,12},{12,4},... | collective-permute-start | bytes 3145736 | tf_op jit(solution)/shard_map/ppermute | solution.py:1172
  440.2 23.5 %collective-permute-start.2 = (bf16[1,256,2048]{2,1,0:T(8,128)(2,1)}, bf16[1,256,2048]{2,1,0:T(8,128)(2,1)}, u32[]{:S(2)}, u32[]{:S(2)}) collective-permute-start(bf16[1,256,2048]{2,1,0:T(8,128)(2,1)} %slice.53), channel_id=1, source_target_pairs={{0,16},{16,0},{1,17},{17,1},{2,18},{18,2},{3,19},{19,3},{4,20},{20... | collective-permute-start | bytes 3145736 | tf_op jit(solution)/shard_map/ppermute | solution.py:1172
  463.7 236.3 %reduce-scatter.7.cloned.1.call-start = ((), (), s32[]{:S(2)}) async-start(), calls=%async_computation.7 | async-start | bytes 10485760 | tf_op jit(solution)/shard_map/reduce_scatter | solution.py:1211
  509.9 278.3 %reduce-scatter.9.cloned.1.call-start = ((), (), s32[]{:S(2)}) async-start(), calls=%async_computation.8 | async-start | bytes 10485760 | tf_op jit(solution)/shard_map/reduce_scatter | solution.py:1211
  511.0 6.6 collective-permute-start.6
  513.0 7.5 collective-permute-start.5
  514.7 8.5 slice-start.4
  523.3 19.0 %copy-start.40 = (f32[8,16,256]{2,1,0:T(8,128)S(1)}, f32[8,16,256]{2,1,0:T(8,128)}, u32[]{:S(2)}) copy-start(f32[8,16,256]{2,1,0:T(8,128)} %get-tuple-element.89) | copy-start | bytes 393220
  542.3 18.1 %copy-start.33 = (bf16[8,256,16]{1,2,0:T(8,128)(2,1)}, bf16[8,256,16]{1,2,0:T(8,128)(2,1)S(1)}, u32[]{:S(2)}) copy-start(bf16[8,256,16]{1,2,0:T(8,128)(2,1)S(1)} %fusion.36) | copy-start | bytes 196612
  560.5 410.4 %reduce-scatter.11.cloned.1.call-start = ((), (), s32[]{:S(2)}) async-start(), calls=%async_computation.9 | async-start | bytes 9437184 | tf_op jit(solution)/shard_map/reduce_scatter | solution.py:1226
  598.3 101.7 %copy-start.11 = (f32[256,2048]{1,0:T(8,128)S(1)}, f32[256,2048]{1,0:T(8,128)}, u32[]{:S(2)}) copy-start(f32[256,2048]{1,0:T(8,128)} %copy-done.10) | copy-start | bytes 6291460
  598.3 101.8 %copy-start.37 = (f32[2048]{0:T(1024)S(1)}, f32[2048]{0:T(1024)}, u32[]{:S(2)}) copy-start(f32[2048]{0:T(1024)} %copy-done.36) | copy-start | bytes 24580
  598.3 101.8 %copy-start.46 = (f32[256]{0:T(256)S(1)}, f32[256]{0:T(256)}, u32[]{:S(2)}) copy-start(f32[256]{0:T(256)} %copy-done.45) | copy-start | bytes 3076
  700.0 6.7 copy-start.13
  700.0 6.7 copy-start.43
  700.0 6.7 copy-start.47
  714.9 77.5 %copy-start.15 = (bf16[256,2048]{1,0:T(8,128)(2,1)S(1)}, bf16[256,2048]{1,0:T(8,128)(2,1)}, u32[]{:S(2)}) copy-start(bf16[256,2048]{1,0:T(8,128)(2,1)} %copy-done.14) | copy-start | bytes 3145732
  790.8 4.4 collective-permute-start.4
  792.5 3.5 collective-permute-start.7
  793.9 3.2 collective-permute-start.8
  794.5 3.5 collective-permute-start.9
  794.7 4.4 collective-permute-start.10
  800.2 170.7 %copy-start.44 = (f32[256]{0:T(256)S(1)}, f32[256]{0:T(256)}, u32[]{:S(2)}) copy-start(f32[256]{0:T(256)} %copy-done.42) | copy-start | bytes 3076
  966.5 7.7 copy-start.20
  (27 other events, 102.9 us)
Sparse Core Ops, SparseCore 0:
  170.9 131.4 all-gather.2
  304.3 111.2 all-gather.4
  463.8 87.6 reduce-scatter.4
  554.8 86.4 reduce-scatter.6
  644.1 91.7 reduce-scatter.8
  738.2 101.5 reduce-scatter.10
